TPU v7x, 32 devices: a whole 2x2x4 slice. The times are simulated.
32 devices in a mesh: group: 2 (over x), vox: 4 (over y, core), snp: 4 (over z).
Axes of the slice: x: 2, y: 2, z: 4, core: 2. Of those that a mesh axis runs over, the one named last changes fastest.
Arguments:
- images: bfloat16 [4096, 4, 8, 256], P(('group', 'vox', 'snp')), parts along dimension 0, may hold values from 0 to 1
- genotypes: bfloat16 [4096, 512], P(('group', 'vox', 'snp')), parts along dimension 0, may hold values from 0 to 2
- covariates: bfloat16 [4096, 16], P(('group', 'vox', 'snp')), parts along dimension 0, may hold values from -6 to 6
- site_codes: int32 [4096], P(('group', 'vox', 'snp')), parts along dimension 0, may hold values from 0 to 3, as said below
Outputs:
- t_stats: float32 [1024, 4, 8, 256], P(('group', 'snp'), None, 'vox'), parts along dimension 0
There are 2 independent parts, one for each index of `group`. A program takes and returns all parts, laid end to end along the dimension named above; each array names one. Nothing has to cross between parts.
Inputs may be any that keep to these rules, and one draw needn't show every extreme that they name: `site_codes`: each centre code is held by exactly 512 subjects.
All inputs are finite; a program needn't handle non-finite values.
Results may differ from a plain program's by a relative error of at most 0.0014.
The roundings to bfloat16 on the way count: a program that leaves them out, or rounds other values in their place, can miss the bound.
Values may be sent and summed in bfloat16 or wider, within the bound.
No kernel may reach another device: no remote copies, remote signals or barrier semaphores. Data moves between devices by JAX's collectives and lax.ppermute only.
A program may use at most 192 MiB of HBM per device.

v0:
```python
import math

import jax
import jax.numpy as jnp
from jax import lax
from jax.sharding import PartitionSpec as P

SY = 16
SZ = 16
SITES = 4


smooth_sigma = 1.0
kernel_reach = 2


def kernel_weight(offset):
    weights = jnp.where(
        jnp.abs(offset) <= kernel_reach, jnp.exp(-offset * offset / (2.0 * smooth_sigma**2)), 0.0
    )
    weight_total = sum(
        (
            math.exp(-(lag_value * lag_value) / (2.0 * smooth_sigma**2))
            for lag_value in range(-kernel_reach, kernel_reach + 1)
        )
    )
    return weights / weight_total


def kernel_table(length):
    position = jnp.arange(length)
    offset = (position[:, None] - position[None, :]).astype(jnp.float32)
    return kernel_weight(offset)


def plane_kernel(plane_size):
    row_table = kernel_table(SY)
    depth_table = kernel_table(SZ)
    return (
        (row_table[:, None, :, None] * depth_table[None, :, None, :])
        .reshape(plane_size, plane_size)
        .astype(jnp.bfloat16)
    )


def smooth_with(images, slab_table):
    subj_here, map_count, planes_in, plane_size = images.shape
    plane_table = plane_kernel(plane_size)
    results = []
    for channel in range(map_count):
        flat_map = images[:, channel].reshape(subj_here * planes_in, plane_size)
        inplane = jnp.dot(flat_map, plane_table, preferred_element_type=jnp.float32).reshape(
            subj_here, planes_in, plane_size
        )
        smoothed_map = jnp.einsum(
            "ab,sbp->sap", slab_table, inplane, precision=lax.Precision.HIGHEST
        )
        results.append(smoothed_map.astype(jnp.bfloat16))
    return jnp.stack(results, axis=1)


def build_design(codes, covariates):
    one_hot = (codes[:, None] == jnp.arange(SITES)[None, :]).astype(jnp.bfloat16)
    return jnp.concatenate([one_hot, covariates], axis=1)


def contract(left, right):
    return lax.dot_general(
        left, right, (((0,), (0,)), ((), ())), preferred_element_type=jnp.float32
    )


def contract_exact(left, right):
    return lax.dot_general(left, right, (((0,), (0,)), ((), ())), precision=lax.Precision.HIGHEST)


def on_device(images, genotypes, covariates, site_codes):
    slab_planes = images.shape[2]
    smoothed = smooth_with(images, kernel_table(slab_planes))
    regrouped = lax.all_to_all(smoothed, "vox", split_axis=2, concat_axis=0, tiled=True)
    gene_all, cov_all, codes_all = (
        lax.all_gather(genotypes, "vox", axis=0, tiled=True),
        lax.all_gather(covariates, "vox", axis=0, tiled=True),
        lax.all_gather(site_codes, "vox", axis=0, tiled=True),
    )
    design = build_design(codes_all, cov_all)
    subj_here, map_count, planes_here, plane_size = regrouped.shape
    columns = regrouped.reshape(subj_here, map_count * planes_here * plane_size)
    gram_part = contract(design, design)
    cross_gene_part = contract(design, gene_all)
    gene_sq_part = jnp.sum(jnp.square(gene_all.astype(jnp.float32)), axis=0)
    cross_image_part = contract(design, columns)
    image_sq_part = jnp.sum(jnp.square(columns.astype(jnp.float32)), axis=0)
    gram, cross_gene, gene_sq = lax.psum((gram_part, cross_gene_part, gene_sq_part), "snp")
    cross_image, image_sq = lax.psum((cross_image_part, image_sq_part), "snp")
    factor = jnp.linalg.cholesky(gram)
    gene_coef = jax.scipy.linalg.cho_solve((factor, True), cross_gene)
    gene_rss = gene_sq - jnp.sum(cross_gene * gene_coef, axis=0)
    panel_rows = gene_all.shape[1] // lax.axis_size("snp")
    panel_first = lax.axis_index("snp") * panel_rows
    products = lax.psum_scatter(contract(gene_all, columns), "snp", scatter_dimension=0, tiled=True)
    panel_coef = lax.dynamic_slice_in_dim(gene_coef, panel_first, panel_rows, 1)
    numer = products - contract_exact(panel_coef, cross_image)
    image_coef = jax.scipy.linalg.cho_solve((factor, True), cross_image)
    image_rss = image_sq - jnp.sum(cross_image * image_coef, axis=0)
    panel_rss = lax.dynamic_slice_in_dim(gene_rss, panel_first, panel_rows, 0)
    subjects_all = subj_here * lax.axis_size("snp")
    freedom = float(subjects_all - design.shape[1] - 1)
    ratio = numer * lax.rsqrt(panel_rss[:, None] * image_rss[None, :])
    stats = ratio * jnp.sqrt(freedom / (1.0 - ratio * ratio))
    return stats.reshape(panel_rows, map_count, planes_here, plane_size)


def solution(mesh):
    placed = (
        P(("group", "vox", "snp"), None, None, None),
        P(("group", "vox", "snp"), None),
        P(("group", "vox", "snp"), None),
        P(("group", "vox", "snp")),
    )
    return jax.shard_map(
        on_device,
        mesh=mesh,
        in_specs=placed,
        out_specs=P(("group", "snp"), None, "vox", None),
        check_vma=False,
    )
```

profile of v0, /device:TPU:0, one launch (start us, length us, event | category | flops | bytes accessed | tf_op | source)
XLA Modules:
  0.0 205.9 jit_solution(18131292051315265826)
XLA Ops:
  6.8 1.0 convert_element_type.99
  7.8 2.5 %convolution_bitcast_fusion.1 = f32[1024,256]{0,1:T(8,128)} fusion(bf16[256,256]{1,0:T(8,128)(2,1)S(1)} %convert_element_type.99, bf16[128,4,8,256]{3,2,1,0:T(8,128)(2,1)} %param.4), kind=kOutput, calls=%fused_computation.8 | convolution fusion | flops 134217728 | bytes 1703936 | tf_op jit(solution)/shard_map/dot_general | solution.py:52
  10.3 2.4 %convolution_bitcast_fusion.2 = f32[1024,256]{0,1:T(8,128)} fusion(bf16[256,256]{1,0:T(8,128)(2,1)S(1)} %convert_element_type.99, bf16[128,4,8,256]{3,2,1,0:T(8,128)(2,1)} %param.4), kind=kOutput, calls=%fused_computation.9 | convolution fusion | flops 134217728 | bytes 1703936 | tf_op jit(solution)/shard_map/dot_general | solution.py:52
  13.4 1.6 copy.25
  15.0 1.8 fusion.4
  16.8 1.6 copy.24
  18.3 1.8 fusion.3
  20.5 1.8 fusion.2
  22.6 1.0 fusion.1
  23.6 1.3 pad_maximum_fusion
  24.9 1.8 copy.26
  26.8 4.4 %all-to-all-start = ((bf16[128,4,8,256]{3,0,1,2:T(8,128)(2,1)}), bf16[128,4,8,256]{3,0,1,2:T(8,128)(2,1)S(1)}, u32[]{:S(2)}, u32[]{:S(2)}) async-start(bf16[128,4,8,256]{3,0,1,2:T(8,128)(2,1)} %copy.26), calls=%async_computation | async-start | bytes 4194304 | tf_op jit(solution)/shard_map/all_to_all | solution.py:80
  31.1 26.6 %all-gather = s32[4,1,128]{2,1,0:T(1,128)S(1)} all-gather(s32[1,1,128]{2,1,0:T(1,128)S(1)} %bitcast.106), channel_id=1, replica_groups=mesh['group'=2,'vox'=4,'snp'=4] {'vox'}, dimensions={0}, use_global_device_ids=true | all-gather | bytes 2560 | tf_op jit(solution)/shard_map/all_gather | solution.py:84
  57.7 5.2 %all_gather.11 = bf16[512,16]{0,1:T(8,128)(2,1)S(1)} all-gather(bf16[128,16]{0,1:T(8,128)(2,1)S(1)} %copy-done.6), channel_id=1, replica_groups=mesh['group'=2,'vox'=4,'snp'=4] {'vox'}, dimensions={0}, use_global_device_ids=true | all-gather | bytes 20480 | tf_op jit(solution)/shard_map/all_gather | solution.py:83
  62.9 7.4 %all_gather.9 = bf16[512,512]{1,0:T(8,128)(2,1)S(1)} all-gather(bf16[128,512]{1,0:T(8,128)(2,1)S(1)} %copy-done.5), channel_id=1, replica_groups=mesh['group'=2,'vox'=4,'snp'=4] {'vox'}, dimensions={0}, use_global_device_ids=true | all-gather | bytes 655360 | tf_op jit(solution)/shard_map/all_gather | solution.py:82
  70.3 3.5 %copy.38 = bf16[128,4,4,2,256]{4,3,1,0,2:T(2,128)(2,1)} copy(bf16[128,4,4,2,256]{4,0,1,3,2:T(8,128)(2,1)S(1)} %bitcast.99) | data formatting | bytes 4194304 | tf_op jit(solution)/shard_map/all_to_all | solution.py:80
  73.8 3.3 %reshape.113 = bf16[512,2048]{1,0:T(8,128)(2,1)S(1)} reshape(bf16[4,128,4,2,256]{4,3,2,1,0:T(2,128)(2,1)} %bitcast.101) | data formatting | bytes 4194304 | tf_op jit(solution)/shard_map/reshape | solution.py:88
  77.1 1.1 fusion.28
  78.3 3.2 %convolution_bitcast_fusion = f32[512,2048]{0,1:T(8,128)} fusion(bf16[512,2048]{1,0:T(8,128)(2,1)S(1)} %reshape.113, bf16[512,512]{1,0:T(8,128)(2,1)S(1)} %all_gather.9), kind=kOutput, calls=%fused_computation.1 | convolution fusion | flops 1073741824 | bytes 6815744 | tf_op jit(solution)/shard_map/dot_general | solution.py:68
  82.0 1.1 copy-done.1
  83.1 2.5 %multiply_reduce_fusion = f32[4,2,256]{2,1,0:T(2,128)S(1)} fusion(bf16[128,4,4,2,256]{4,0,1,3,2:T(8,128)(2,1)S(1)} %bitcast.100), kind=kLoop, calls=%fused_computation | loop fusion | flops 3143680 | bytes 2105344 | tf_op jit(solution)/shard_map/reduce_sum | solution.py:93
  85.6 21.4 %all-reduce = (f32[2048]{0:T(1024)S(1)}, f32[20,20]{0,1:T(8,128)S(1)}, f32[512]{0:T(512)S(1)}, f32[20,512]{1,0:T(8,128)S(1)}) all-reduce(f32[2048]{0:T(1024)S(1)} %bitcast.104, f32[20,20]{0,1:T(8,128)S(1)} %fusion.30, f32[512]{0:T(512)S(1)} %multiply_reduce_fusion.1, ...), channel_id=1, replica_groups=mesh['group'=2,'vox'=4,'snp'=4] {'snp'}, use_global_device_ids=true, to_apply=%region_10.11 | all-reduce | flops 13200 | bytes 105600 | tf_op jit(solution)/shard_map/psum | solution.py:95
  107.1 1.8 cholesky.16
  109.0 0.7 compare_reduce_fusion
  109.6 0.6 fusion.18
  110.2 1.5 custom-call.16
  112.3 2.9 %all-reduce.3.cloned.1.call-done = f32[20,2048]{1,0:T(8,128)} async-done(((f32[20,2048]{1,0:T(8,128)}), f32[20,2048]{1,0:T(8,128)}) %all-reduce.3.cloned.1.call-update) | async-done | bytes 163856 | tf_op jit(solution)/shard_map/psum | solution.py:95
  115.2 1.3 fusion.20
  116.5 1.3 fusion.5
  117.8 76.2 %reduce-scatter.2.cloned.1.call-done = f32[128,2048]{0,1:T(8,128)} async-done(((f32[512,2048]{0,1:T(8,128)}), f32[128,2048]{0,1:T(8,128)}) %reduce-scatter.2.cloned.1.call-update) | async-done | bytes 1048592 | tf_op jit(solution)/shard_map/reduce_scatter | solution.py:101
  194.0 3.7 %sqrt_multiply_fusion = f32[128,2048]{0,1:T(8,128)S(1)} fusion(f32[128,2048]{0,1:T(8,128)} %reduce-scatter.2.cloned.1.call-done, f32[20,2048]{1,0:T(8,128)} %all-reduce.3.cloned.1.call-done, f32[2048]{0:T(1024)S(1)} %sub.100, f32[128]{0:T(128)S(1)} %dynamic_slice.7, f32[20,512]{1,0:T(8,128)S(1)} %get-tuple-element.10, s32[]{:T(128)S(6)} %select_n.40), kind=kOutput, calls=%fused_computation.25 | convolution fusion | flops 64749568 | bytes 2281988 | tf_op jit(solution)/shard_map/dot_general | solution.py:74
  197.7 1.3 copy.31
  (39 shorter events, 2.9 us)
Async XLA Ops:
  7.8 4.9 %copy-start.2 = (bf16[128,4,8,256]{3,2,1,0:T(8,128)(2,1)S(1)}, bf16[128,4,8,256]{3,2,1,0:T(8,128)(2,1)}, u32[]{:S(2)}) copy-start(bf16[128,4,8,256]{3,2,1,0:T(8,128)(2,1)} %param.4) | copy-start | bytes 6291460
  22.3 1.3 copy-start.3
  22.3 1.4 copy-start.4
  26.8 4.4 %copy-start.7 = (s32[128]{0:T(128)S(1)}, s32[128]{0:T(128)}, u32[]{:S(2)}) copy-start(s32[128]{0:T(128)} %param.7) | copy-start | bytes 1540
  26.8 31.0 %copy-start.6 = (bf16[128,16]{0,1:T(8,128)(2,1)S(1)}, bf16[128,16]{0,1:T(8,128)(2,1)}, u32[]{:S(2)}) copy-start(bf16[128,16]{0,1:T(8,128)(2,1)} %param.6) | copy-start | bytes 12292
  26.8 36.1 %copy-start.5 = (bf16[128,512]{1,0:T(8,128)(2,1)S(1)}, bf16[128,512]{1,0:T(8,128)(2,1)}, u32[]{:S(2)}) copy-start(bf16[128,512]{1,0:T(8,128)(2,1)} %param.5) | copy-start | bytes 393220
  26.8 43.6 %all-to-all-start = ((bf16[128,4,8,256]{3,0,1,2:T(8,128)(2,1)}), bf16[128,4,8,256]{3,0,1,2:T(8,128)(2,1)S(1)}, u32[]{:S(2)}, u32[]{:S(2)}) async-start(bf16[128,4,8,256]{3,0,1,2:T(8,128)(2,1)} %copy.26), calls=%async_computation | async-start | bytes 4194304 | tf_op jit(solution)/shard_map/all_to_all | solution.py:80
  31.1 84.1 %all-reduce.3.cloned.1.call-start = ((), (), s32[]{:S(2)}) async-start(), calls=%async_computation.3 | async-start | bytes 393216 | tf_op jit(solution)/shard_map/psum | solution.py:95
  70.3 3.5 %copy-start = (bf16[128,4,8,256]{3,0,1,2:T(8,128)(2,1)}, bf16[128,4,8,256]{3,0,1,2:T(8,128)(2,1)S(1)}, u32[]{:S(2)}) copy-start(bf16[128,4,8,256]{3,0,1,2:T(8,128)(2,1)S(1)} %all-to-all-done) | copy-start | bytes 6291460
  78.2 115.8 %reduce-scatter.2.cloned.1.call-start = ((), (), s32[]{:S(2)}) async-start(), calls=%async_computation.2 | async-start | bytes 5242880 | tf_op jit(solution)/shard_map/reduce_scatter | solution.py:101
  81.5 1.6 copy-start.1
Sparse Core Ops, SparseCore 0:
  78.3 36.8 all-reduce.2
  117.6 76.3 reduce-scatter.1
where the time goes:
time: 206 us
  waiting for transfers between devices  79.1 us (38%)
  blocking collectives  60.6 us (29%)
  matrix products  23.3 us (11%)
  local copies, waits for them, and re-layouts  16 us (8%)
  between operations  13.6 us (7%)
  other arithmetic  8.87 us (4%)
  starting transfers between devices  4.41 us (2%)
    reduce_scatter x1, waiting for transfers between devices, on_device(): lax.psum_scatter(contract(gene_all, columns), 'snp', scatter_dimension=0,...  76.2 us
    all_gather x1, blocking collectives, on_device(): lax.all_gather(site_codes, 'vox', axis=0, tiled=True)  26.6 us
    psum x1, blocking collectives, on_device(): cross_image, image_sq = lax.psum((cross_image_part, image_sq_part), 'snp')  21.4 us
    all_gather x1, blocking collectives, on_device(): lax.all_gather(genotypes, 'vox', axis=0, tiled=True)  7.43 us
    dot_general x4, matrix products, smooth_with(): jnp.einsum('ab,sbp->sap', slab_table, inplane, precision=lax.Precision.HI...  6.38 us
    dot_general x4, matrix products, smooth_with(): jnp.dot(flat_map, plane_table, preferred_element_type=jnp.float32)  5.6 us
    all_gather x1, blocking collectives, on_device(): lax.all_gather(covariates, 'vox', axis=0, tiled=True)  5.15 us
    dot_general x4, matrix products, contract(): lax.dot_general(left, right, (((0,), (0,)), ((), ())), preferred_element_...  4.6 us
  transfers between devices with their start and end apart: 3, of which 2 were waited for; matrix products, arithmetic and copies ran while one was open for 7% of the time, Pallas kernels for 0%

commit v1 on v0

v1 whole, which is shorter than its diff:
```python
import functools

import jax
import jax.numpy as jnp
import ml_dtypes
import numpy as np
from jax import lax
from jax.experimental import pallas as pl
from jax.experimental.pallas import tpu as pltpu
from jax.sharding import PartitionSpec as P

SY = 16
SZ = 16
SITES = 4
REACH = 2
DPAD = 24
LANES = 128
SUBJ_TILE = 16
HIGHEST = lax.Precision.HIGHEST
VMEM_LIMIT = 56 * 2**20


def kernel_table(length):
    position = np.arange(length)
    offset = (position[:, None] - position[None, :]).astype(np.float32)
    weights = np.where(np.abs(offset) <= REACH, np.exp(-offset * offset / np.float32(2.0)), np.float32(0.0))
    total = sum(np.exp(-(k * k) / 2.0) for k in range(-REACH, REACH + 1))
    return (weights / np.float32(total)).astype(np.float32)


def plane_kernel(plane):
    row, depth = kernel_table(SY), kernel_table(SZ)
    table = row[:, None, :, None] * depth[None, :, None, :]
    return table.reshape(plane, plane).astype(ml_dtypes.bfloat16)


def row_order(maps, planes):
    rows = SUBJ_TILE * maps * planes
    source = np.arange(rows).reshape(SUBJ_TILE, maps * planes).T.reshape(-1)
    return np.eye(rows, dtype=np.float32)[source].astype(ml_dtypes.bfloat16)


def smooth_kernel(group, planes, per_vox, n_snp, width, images, order, table, out):
    plane = table.shape[0]
    subjects = images.shape[0]
    groups = images.shape[1] // (group * planes)
    near = kernel_table(2 * REACH + 1)[REACH]
    for tile in range(subjects // SUBJ_TILE):
        here = pl.ds(tile * SUBJ_TILE, SUBJ_TILE)
        for part in range(groups):
            rows = images[here, part * group * planes : (part + 1) * group * planes, :]
            rows = rows.reshape(SUBJ_TILE * group * planes, plane)
            rows = jnp.dot(order[...], rows, preferred_element_type=jnp.float32)
            inplane = jnp.dot(
                rows.astype(jnp.bfloat16), table[...], preferred_element_type=jnp.float32
            )
            for m in range(group):
                slabs = [
                    inplane[(m * planes + x) * SUBJ_TILE : (m * planes + x + 1) * SUBJ_TILE]
                    for x in range(planes)
                ]
                for x in range(planes):
                    total = slabs[x] * float(near[REACH])
                    for lag in range(1, REACH + 1):
                        sides = [slabs[i] for i in (x - lag, x + lag) if 0 <= i < planes]
                        if sides:
                            total = total + functools.reduce(jnp.add, sides) * float(
                                near[REACH + lag]
                            )
                    column = ((part * group + m) * per_vox + x % per_vox) * plane
                    target = (x // per_vox) * n_snp + column // width
                    first = column % width
                    out[target, here, first : first + plane] = total.astype(jnp.bfloat16)


def smooth(images, n_vox, n_snp):
    subjects, maps, planes, plane = images.shape
    per_vox = planes // n_vox
    width = maps * per_vox * plane // n_snp
    group = max(1, min(maps, 256 // (SUBJ_TILE * planes)))
    step = 32
    order = jnp.asarray(row_order(group, planes))
    table = jnp.asarray(plane_kernel(plane))
    return pl.pallas_call(
        functools.partial(smooth_kernel, group, planes, per_vox, n_snp, width),
        out_shape=jax.ShapeDtypeStruct((n_vox * n_snp, subjects, width), jnp.bfloat16),
        grid=(subjects // step,),
        in_specs=[
            pl.BlockSpec((step, maps * planes, plane), lambda i: (i, 0, 0)),
            pl.BlockSpec(order.shape, lambda i: (0, 0)),
            pl.BlockSpec(table.shape, lambda i: (0, 0)),
        ],
        out_specs=pl.BlockSpec((n_vox * n_snp, step, width), lambda i: (0, i, 0)),
        compiler_params=pltpu.CompilerParams(vmem_limit_bytes=VMEM_LIMIT),
        name="smooth",
    )(images.reshape(subjects, maps * planes, plane), order, table)


def gene_kernel(snps, design, blocks, joined, coef, inverse, cross, square):
    step = pl.program_id(0)
    rows = jnp.concatenate([blocks[i] for i in range(blocks.shape[0])], axis=1)
    joined[...] = rows
    tail = jnp.concatenate(
        [rows[snps:], jnp.zeros((LANES - DPAD, rows.shape[1]), rows.dtype)], axis=0
    )
    moments = lax.dot_general(
        rows, tail, (((1,), (1,)), ((), ())), preferred_element_type=jnp.float32
    )
    wide = rows[:snps].astype(jnp.float32)
    squares = jnp.sum(wide * wide, axis=1, keepdims=True)

    @pl.when(step == 0)
    def _():
        cross[...] = moments
        square[...] = squares

    @pl.when(step > 0)
    def _():
        cross[...] += moments
        square[...] += squares

    @pl.when(step == pl.num_programs(0) - 1)
    def _():
        lane = lax.broadcasted_iota(jnp.int32, (DPAD, LANES), 1)
        row = lax.broadcasted_iota(jnp.int32, (DPAD, LANES), 0)
        shift = 32
        work = cross[snps:, :]
        work = jnp.where((row >= design) & (lane == row), 1.0, work)
        work = jnp.where(lane == row + shift, 1.0, work)
        for k in range(design):
            pivot = work[k : k + 1, :] / work[k : k + 1, k : k + 1]
            work = jnp.where(row == k, pivot, work - work[:, k : k + 1] * pivot)
        solved = pltpu.roll(work, LANES - shift, 1)
        solved = jnp.where((lane < design) & (row < design), solved, 0.0)
        inverse[...] = solved
        square_inverse = jnp.concatenate(
            [solved, jnp.zeros((LANES - DPAD, LANES), jnp.float32)], axis=0
        )
        cross_gene = cross[:snps, :]
        fitted = jnp.dot(
            cross_gene, square_inverse, precision=HIGHEST, preferred_element_type=jnp.float32
        )
        rss = square[...] - jnp.sum(cross_gene * fitted, axis=1, keepdims=True)
        place = lax.broadcasted_iota(jnp.int32, (snps, LANES), 1)
        coef[...] = jnp.where(place == DPAD, rss, fitted)


def gene_side(blocks, design):
    devices, rows, subjects = blocks.shape
    snps = rows - DPAD
    step = min(devices, 16)
    return pl.pallas_call(
        functools.partial(gene_kernel, snps, design),
        out_shape=(
            jax.ShapeDtypeStruct((rows, devices * subjects), blocks.dtype),
            jax.ShapeDtypeStruct((snps, LANES), jnp.float32),
            jax.ShapeDtypeStruct((DPAD, LANES), jnp.float32),
        ),
        grid=(devices // step,),
        in_specs=[pl.BlockSpec((step, rows, subjects), lambda i: (i, 0, 0))],
        out_specs=(
            pl.BlockSpec((rows, step * subjects), lambda i: (0, i)),
            pl.BlockSpec((snps, LANES), lambda i: (0, 0)),
            pl.BlockSpec((DPAD, LANES), lambda i: (0, 0)),
        ),
        scratch_shapes=[
            pltpu.VMEM((rows, LANES), jnp.float32),
            pltpu.VMEM((snps, 1), jnp.float32),
        ],
        compiler_params=pltpu.CompilerParams(vmem_limit_bytes=VMEM_LIMIT),
        name="gene_side",
    )(blocks)


def test_kernel(snps, freedom, genes, columns, coef, inverse, out, sums, square):
    step = pl.program_id(1)
    values = columns[...]
    wide = values.astype(jnp.float32)
    partial = jnp.dot(genes[...], values, preferred_element_type=jnp.float32)
    partial_square = jnp.sum(wide * wide, axis=0, keepdims=True)

    @pl.when(step == 0)
    def _():
        sums[...] = partial
        square[...] = partial_square

    @pl.when(step > 0)
    def _():
        sums[...] += partial
        square[...] += partial_square

    @pl.when(step == pl.num_programs(1) - 1)
    def _():
        cross_image = sums[snps:, :]
        solved = jnp.dot(
            inverse[:, :DPAD], cross_image, precision=HIGHEST, preferred_element_type=jnp.float32
        )
        image_rss = square[...] - jnp.sum(cross_image * solved, axis=0, keepdims=True)
        numer = sums[:snps, :] - jnp.dot(
            coef[:, :DPAD], cross_image, precision=HIGHEST, preferred_element_type=jnp.float32
        )
        ratio = numer * lax.rsqrt(coef[:, DPAD : DPAD + 1] * image_rss)
        out[...] = ratio * jnp.sqrt(freedom / (1.0 - ratio * ratio))


def test_columns(genes, columns, coef, inverse, design):
    rows, subjects = genes.shape
    snps = rows - DPAD
    width = columns.shape[1]
    step = min(subjects, 2048)
    lanes = min(width, 256)
    freedom = float(subjects - design - 1)
    return pl.pallas_call(
        functools.partial(test_kernel, snps, freedom),
        out_shape=jax.ShapeDtypeStruct((snps, width), jnp.float32),
        grid=(width // lanes, subjects // step),
        in_specs=[
            pl.BlockSpec((rows, step), lambda j, k: (0, k)),
            pl.BlockSpec((step, lanes), lambda j, k: (k, j)),
            pl.BlockSpec((snps, LANES), lambda j, k: (0, 0)),
            pl.BlockSpec((DPAD, LANES), lambda j, k: (0, 0)),
        ],
        out_specs=pl.BlockSpec((snps, lanes), lambda j, k: (0, j)),
        scratch_shapes=[
            pltpu.VMEM((rows, lanes), jnp.float32),
            pltpu.VMEM((1, lanes), jnp.float32),
        ],
        compiler_params=pltpu.CompilerParams(vmem_limit_bytes=VMEM_LIMIT),
        name="test_columns",
    )(genes, columns, coef, inverse)


def on_device(images, genotypes, covariates, site_codes):
    subjects, maps, planes, plane = images.shape
    n_vox, n_snp = lax.axis_size("vox"), lax.axis_size("snp")
    snps = genotypes.shape[1]
    design = SITES + covariates.shape[1]
    per_vox = planes // n_vox
    one_hot = (jnp.arange(SITES)[:, None] == site_codes[None, :]).astype(jnp.bfloat16)
    tall = jnp.concatenate(
        [genotypes.T, one_hot, covariates.T, jnp.zeros((DPAD - design, subjects), jnp.bfloat16)],
        axis=0,
    )
    smoothed = smooth(images, n_vox, n_snp)
    columns = lax.all_to_all(smoothed, ("vox", "snp"), 0, 0, tiled=True)
    tall_all = lax.all_gather(lax.all_gather(tall, "snp"), "vox")
    tall_all = tall_all.reshape(n_vox * n_snp, snps + DPAD, subjects)
    genes, coef, inverse = gene_side(tall_all, design)
    columns = columns.reshape(n_vox * n_snp * subjects, columns.shape[2])
    stats = test_columns(genes, columns, coef, inverse, design)
    width = stats.shape[1]
    panel = snps // n_snp
    stats = lax.all_to_all(stats.reshape(n_snp, panel, width), "snp", 0, 0, tiled=True)
    stats = jnp.swapaxes(stats, 0, 1)
    return stats.reshape(panel, maps, per_vox, plane)


def solution(mesh):
    placed = (
        P(("group", "vox", "snp"), None, None, None),
        P(("group", "vox", "snp"), None),
        P(("group", "vox", "snp"), None),
        P(("group", "vox", "snp")),
    )
    return jax.shard_map(
        on_device,
        mesh=mesh,
        in_specs=placed,
        out_specs=P(("group", "snp"), None, "vox", None),
        check_vma=False,
    )
```

time: 206 us -> 157 us (0.76)
  waiting for transfers between devices: 79.1 us -> 23.9 us
  blocking collectives: 60.6 us -> 90 us
  matrix products: 23.3 us -> 0 us
  Pallas kernels: 0 us -> 17.9 us
  local copies, waits for them, and re-layouts: 16 us -> 3.53 us
  other arithmetic: 8.87 us -> 0.14 us
  starting transfers between devices: 4.41 us -> 7.57 us
    reduce_scatter x1 -> x0, waiting for transfers between devices: 76.2 us -> none  [on_device(): lax.psum_scatter(contract(gene_all, columns), 'snp', scatter_dimension=0,...]
    all_to_all x0 -> x1, blocking collectives: none -> 30.7 us  [on_device(): lax.all_to_all(stats.reshape(n_snp, panel, width), 'snp', 0, 0, tiled=True)]
    all_gather x0 -> x1, waiting for transfers between devices: none -> 23.9 us  [on_device(): tall_all = lax.all_gather(lax.all_gather(tall, 'snp'), 'vox')]
    psum x1 -> x0, blocking collectives: 21.4 us -> none  [on_device(): cross_image, image_sq = lax.psum((cross_image_part, image_sq_part), 'snp')]
    dot_general x13 -> x0, matrix products: 20.3 us -> none  [the longest x4 6.38 us: smooth_with(): jnp.einsum('ab,sbp->sap', slab_table, inplane, precision=lax.Precision.HI...]
    all_gather x3 -> x1, blocking collectives: 39.2 us -> 59.3 us  [on_device(): tall_all = lax.all_gather(lax.all_gather(tall, 'snp'), 'vox')]
    pallas_call x0 -> x3, Pallas kernels: none -> 17.9 us  [the longest x1 7.4 us: test_columns(): pl.pallas_call(functools.partial(test_kernel, snps, freedom), out_shape=j...]
    another operation x6 -> x0, other arithmetic: 5.95 us -> none  [the longest x3 2.5 us: on_device(): factor = jnp.linalg.cholesky(gram)]
  transfers between devices with their start and end apart: 3 -> 2, of which waited for: 2 -> 1; matrix products, arithmetic and copies ran while one was open for 7% -> 0% of each run, Pallas kernels for 0% -> 4%
where the time goes in v1:
time: 157 us
  blocking collectives  90 us (57%)
  waiting for transfers between devices  23.9 us (15%)
  Pallas kernels  17.9 us (11%)
  between operations  13.4 us (9%)
  starting transfers between devices  7.57 us (5%)
  local copies, waits for them, and re-layouts  3.53 us (2%)
    all_gather x1, blocking collectives, on_device(): tall_all = lax.all_gather(lax.all_gather(tall, 'snp'), 'vox')  59.3 us
    all_to_all x1, blocking collectives, on_device(): lax.all_to_all(stats.reshape(n_snp, panel, width), 'snp', 0, 0, tiled=True)  30.7 us
    all_gather x1, waiting for transfers between devices, on_device(): tall_all = lax.all_gather(lax.all_gather(tall, 'snp'), 'vox')  23.9 us
    all_to_all x1, starting transfers between devices, on_device(): columns = lax.all_to_all(smoothed, ('vox', 'snp'), 0, 0, tiled=True)  7.53 us
    pallas_call x1, Pallas kernels, test_columns(): pl.pallas_call(functools.partial(test_kernel, snps, freedom), out_shape=j...  7.4 us
    pallas_call x1, Pallas kernels, gene_side(): pl.pallas_call(functools.partial(gene_kernel, snps, design), out_shape=(j...  5.61 us
    pallas_call x1, Pallas kernels, smooth(): pl.pallas_call(functools.partial(smooth_kernel, group, planes, per_vox, n...  4.9 us
  transfers between devices with their start and end apart: 2, of which 1 were waited for; matrix products, arithmetic and copies ran while one was open for 0% of the time, Pallas kernels for 4%

profile of v1, /device:TPU:0, one launch (start us, length us, event | category | flops | bytes accessed | tf_op | source)
XLA Modules:
  0.0 156.5 jit_solution(5656931391319277995)
XLA Ops:
  6.5 4.9 %smooth.1 = bf16[16,128,512]{2,1,0:T(8,128)(2,1)} custom-call(bf16[128,32,256]{2,1,0:T(8,128)(2,1)} %bitcast.13, bf16[256,256]{1,0:T(8,128)(2,1)} %constant.6.clone.order, bf16[256,256]{1,0:T(8,128)(2,1)} %constant.7.clone.table), custom_call_target="tpu_custom_call" | custom-call | tf_op jit(solution)/shard_map/smooth/pallas_call | solution.py:84
  11.4 0.0 copy-start.1
  11.4 0.0 copy-start.3
  11.4 0.0 copy-start.2
  11.4 7.5 %all-to-all-start = ((bf16[16,128,512]{2,1,0:T(8,128)(2,1)}), bf16[16,128,512]{2,1,0:T(8,128)(2,1)S(1)}, u32[]{:S(2)}, u32[]{:S(2)}) async-start(bf16[16,128,512]{2,1,0:T(8,128)(2,1)} %smooth.1), calls=%async_computation | async-start | bytes 4194304 | tf_op jit(solution)/shard_map/all_to_all | solution.py:245
  19.0 0.0 all-gather.4.cloned.1.call-start
  19.0 0.0 copy-done.1
  19.0 0.1 copy.10
  19.2 0.1 pad.3.clone
  19.3 0.0 copy-done.3
  19.3 0.0 copy-done.2
  19.3 0.1 maximum_maximum_fusion
  19.4 59.3 %all-gather = bf16[2144,128]{1,0:T(8,128)(2,1)} all-gather(bf16[536,128]{1,0:T(8,128)(2,1)S(1)} %maximum_maximum_fusion), channel_id=2, replica_groups=mesh['group'=2,'vox'=4,'snp'=4] {'snp'}, dimensions={0}, use_global_device_ids=true | all-gather | bytes 686080 | tf_op jit(solution)/shard_map/all_gather | solution.py:246
  78.7 0.0 all-gather.4.cloned.1.call-update
  78.7 23.9 %all-gather.4.cloned.1.call-done.blocks = bf16[16,536,128]{2,1,0:T(8,128)(2,1)} async-done(((bf16[4,536,128]{2,1,0:T(8,128)(2,1)}), bf16[16,536,128]{2,1,0:T(8,128)(2,1)}) %all-gather.4.cloned.1.call-update) | async-done | bytes 2195472 | tf_op jit(solution)/shard_map/all_gather | solution.py:246
  102.6 5.6 %gene_side.1 = (bf16[536,2048]{1,0:T(8,128)(2,1)}, f32[512,128]{1,0:T(8,128)}, f32[24,128]{1,0:T(8,128)}) custom-call(bf16[16,536,128]{2,1,0:T(8,128)(2,1)} %all-gather.4.cloned.1.call-done.blocks), custom_call_target="tpu_custom_call" | custom-call | tf_op jit(solution)/shard_map/gene_side/pallas_call | solution.py:152
  108.2 0.0 all-to-all-done
  108.2 0.0 copy-start
  108.2 1.3 copy-done
  109.5 7.4 %test_columns.1 = f32[512,512]{1,0:T(8,128)} custom-call(bf16[536,2048]{1,0:T(8,128)(2,1)} %get-tuple-element.8.genes, bf16[2048,512]{1,0:T(8,128)(2,1)} %bitcast.9, f32[512,128]{1,0:T(8,128)} %get-tuple-element.9.coef, f32[24,128]{1,0:T(8,128)} %get-tuple-element.10.inverse), custom_call_target="tpu_custom_call" | custom-call | tf_op jit(solution)/shard_map/test_columns/pallas_call | solution.py:213
  116.9 30.7 %all_to_all.10 = f32[4,128,512]{2,1,0:T(8,128)S(1)} all-to-all(f32[4,128,512]{2,1,0:T(8,128)} %bitcast.10), channel_id=1, replica_groups=mesh['group'=2,'vox'=4,'snp'=4] {'snp'}, dimensions={0} | all-to-all | bytes 2097152 | tf_op jit(solution)/shard_map/all_to_all | solution.py:253
  147.7 0.7 reshape.24
  148.3 1.3 copy.12
  (2 shorter events, 0.0 us)
Async XLA Ops:
  11.4 7.6 %copy-start.1 = (bf16[128,512]{1,0:T(8,128)(2,1)S(1)}, bf16[128,512]{1,0:T(8,128)(2,1)}, u32[]{:S(2)}) copy-start(bf16[128,512]{1,0:T(8,128)(2,1)} %param.7) | copy-start | bytes 393220
  11.4 7.8 %copy-start.3 = (s32[128]{0:T(128)S(1)}, s32[128]{0:T(128)}, u32[]{:S(2)}) copy-start(s32[128]{0:T(128)} %param.9) | copy-start | bytes 1540
  11.4 7.8 %copy-start.2 = (bf16[128,16]{0,1:T(8,128)(2,1)S(1)}, bf16[128,16]{0,1:T(8,128)(2,1)}, u32[]{:S(2)}) copy-start(bf16[128,16]{0,1:T(8,128)(2,1)} %param.8) | copy-start | bytes 12292
  11.4 96.8 %all-to-all-start = ((bf16[16,128,512]{2,1,0:T(8,128)(2,1)}), bf16[16,128,512]{2,1,0:T(8,128)(2,1)S(1)}, u32[]{:S(2)}, u32[]{:S(2)}) async-start(bf16[16,128,512]{2,1,0:T(8,128)(2,1)} %smooth.1), calls=%async_computation | async-start | bytes 4194304 | tf_op jit(solution)/shard_map/all_to_all | solution.py:245
  19.0 83.6 %all-gather.4.cloned.1.call-start = ((), (), s32[]{:S(2)}) async-start(), calls=%async_computation.2 | async-start | bytes 2744320 | tf_op jit(solution)/shard_map/all_gather | solution.py:246
  108.2 1.3 copy-start
Sparse Core Ops, SparseCore 0:
  78.9 23.6 all-gather.3

commit v2 on v1

v2 whole, which is shorter than its diff:
```python
import functools

import jax
import jax.numpy as jnp
import ml_dtypes
import numpy as np
from jax import lax
from jax.experimental import pallas as pl
from jax.experimental.pallas import tpu as pltpu
from jax.sharding import Mesh
from jax.sharding import PartitionSpec as P

SY = 16
SZ = 16
SITES = 4
REACH = 2
DPAD = 24
LANES = 128
SUBJ_TILE = 16
HIGHEST = lax.Precision.HIGHEST
VMEM_LIMIT = 56 * 2**20
SQUARE_ROW = 20
SCALE_LANE = DPAD
DRIFT_LANE = DPAD + 1
MEAN_ROW = 1
NORM_ROW = 8


def kernel_table(length):
    position = np.arange(length)
    offset = (position[:, None] - position[None, :]).astype(np.float32)
    weights = np.where(np.abs(offset) <= REACH, np.exp(-offset * offset / np.float32(2.0)), np.float32(0.0))
    total = sum(np.exp(-(k * k) / 2.0) for k in range(-REACH, REACH + 1))
    return (weights / np.float32(total)).astype(np.float32)


def plane_kernel(plane):
    row, depth = kernel_table(SY), kernel_table(SZ)
    table = row[:, None, :, None] * depth[None, :, None, :]
    return table.reshape(plane, plane).astype(ml_dtypes.bfloat16)


def row_order(maps, planes):
    rows = SUBJ_TILE * maps * planes
    source = np.arange(rows).reshape(SUBJ_TILE, maps * planes).T.reshape(-1)
    return np.eye(rows, dtype=np.float32)[source].astype(ml_dtypes.bfloat16)


def tree_sum(terms):
    while len(terms) > 1:
        terms = [terms[i] + terms[i + 1] for i in range(0, len(terms), 2)]
    return terms[0]


def params():
    return pltpu.CompilerParams(vmem_limit_bytes=VMEM_LIMIT)


def smooth_kernel(group, planes, per_vox, parts, width, images, order, table, out):
    plane = table.shape[0]
    subjects = images.shape[0]
    groups = images.shape[1] // (group * planes)
    near = kernel_table(2 * REACH + 1)[REACH]
    for tile in range(subjects // SUBJ_TILE):
        here = pl.ds(tile * SUBJ_TILE, SUBJ_TILE)
        for part in range(groups):
            rows = images[here, part * group * planes : (part + 1) * group * planes, :]
            rows = rows.reshape(SUBJ_TILE * group * planes, plane)
            rows = jnp.dot(order[...], rows, preferred_element_type=jnp.float32)
            inplane = jnp.dot(
                rows.astype(jnp.bfloat16), table[...], preferred_element_type=jnp.float32
            )
            for m in range(group):
                slabs = [
                    inplane[(m * planes + x) * SUBJ_TILE : (m * planes + x + 1) * SUBJ_TILE]
                    for x in range(planes)
                ]
                for x in range(planes):
                    total = slabs[x] * float(near[REACH])
                    for lag in range(1, REACH + 1):
                        sides = [slabs[i] for i in (x - lag, x + lag) if 0 <= i < planes]
                        if sides:
                            total = total + functools.reduce(jnp.add, sides) * float(
                                near[REACH + lag]
                            )
                    column = ((part * group + m) * per_vox + x % per_vox) * plane
                    target = (x // per_vox) * parts + column // width
                    first = column % width
                    out[target, here, first : first + plane] = total.astype(jnp.bfloat16)


def smooth(images, n_vox, parts):
    subjects, maps, planes, plane = images.shape
    per_vox = planes // n_vox
    width = maps * per_vox * plane // parts
    group = max(1, min(maps, 256 // (SUBJ_TILE * planes)))
    step = 32
    order = jnp.asarray(row_order(group, planes))
    table = jnp.asarray(plane_kernel(plane))
    return pl.pallas_call(
        functools.partial(smooth_kernel, group, planes, per_vox, parts, width),
        out_shape=jax.ShapeDtypeStruct((n_vox * parts, subjects, width), jnp.bfloat16),
        grid=(subjects // step,),
        in_specs=[
            pl.BlockSpec((step, maps * planes, plane), lambda i: (i, 0, 0)),
            pl.BlockSpec(order.shape, lambda i: (0, 0)),
            pl.BlockSpec(table.shape, lambda i: (0, 0)),
        ],
        out_specs=pl.BlockSpec((n_vox * parts, step, width), lambda i: (0, i, 0)),
        compiler_params=params(),
        name="smooth",
    )(images.reshape(subjects, maps * planes, plane), order, table)


def moments_kernel(snps, bits, me, blocks, joined, out):
    count = blocks.shape[0]
    rows = []
    for source in range(count):
        offset = jnp.bitwise_xor(me[0], source)
        index = 0
        for place, bit in enumerate(bits):
            index = index + ((offset >> bit) & 1) * (1 << place)
        rows.append(blocks[index])
    rows = jnp.concatenate(rows, axis=1)
    joined[...] = rows
    across = (((1,), (1,)), ((), ()))
    out[...] = jnp.zeros(out.shape, jnp.float32)
    out[:DPAD, : snps + DPAD] = lax.dot_general(
        rows[snps:], rows, across, preferred_element_type=jnp.float32
    )
    wide = rows[:snps].astype(jnp.float32)
    wide = wide * wide
    high = wide.astype(jnp.bfloat16)
    low = (wide - high.astype(jnp.float32)).astype(jnp.bfloat16)
    ones = jnp.ones((8, rows.shape[1]), jnp.bfloat16)
    squares = lax.dot_general(ones, high, across, preferred_element_type=jnp.float32)
    squares = squares + lax.dot_general(ones, low, across, preferred_element_type=jnp.float32)
    out[DPAD:, :snps] = squares


def moments(blocks, bits, me):
    count, rows, subjects = blocks.shape
    snps = rows - DPAD
    spread = -(-rows // LANES) * LANES
    return pl.pallas_call(
        functools.partial(moments_kernel, snps, bits),
        out_shape=(
            jax.ShapeDtypeStruct((rows, count * subjects), blocks.dtype),
            jax.ShapeDtypeStruct((DPAD + 8, spread), jnp.float32),
        ),
        in_specs=[
            pl.BlockSpec(memory_space=pltpu.SMEM),
            pl.BlockSpec(memory_space=pltpu.VMEM),
        ],
        compiler_params=params(),
        name="moments",
    )(me, blocks)


def solve_kernel(snps, design, here, *refs):
    parts, (coef, inverse, rows_out) = refs[:-3], refs[-3:]
    total = tree_sum([part[...] for part in parts])
    lane = lax.broadcasted_iota(jnp.int32, (DPAD, LANES), 1)
    row = lax.broadcasted_iota(jnp.int32, (DPAD, LANES), 0)
    shift = 32
    work = total[:DPAD, snps : snps + LANES]
    work = jnp.where((row >= design) & (lane == row), 1.0, work)
    work = jnp.where(lane == row + shift, 1.0, work)
    for k in range(design):
        pivot = work[k : k + 1, :] / work[k : k + 1, k : k + 1]
        work = jnp.where(row == k, pivot, work - work[:, k : k + 1] * pivot)
    solved = pltpu.roll(work, LANES - shift, 1)
    solved = jnp.where((lane < design) & (row < design), solved, 0.0)
    inverse[...] = solved
    cross_gene = total[:DPAD, :snps]
    fitted = jnp.dot(
        solved[:, :DPAD], cross_gene, precision=HIGHEST, preferred_element_type=jnp.float32
    )
    rss = total[DPAD : DPAD + 1, :snps] - jnp.sum(cross_gene * fitted, axis=0, keepdims=True)
    scale = lax.rsqrt(rss)
    site = lax.broadcasted_iota(jnp.int32, (DPAD, snps), 0) < SITES
    rows_out[...] = jnp.zeros(rows_out.shape, jnp.float32)
    for j, part in enumerate(parts):
        mine = part[...]
        count = jnp.sum(
            jnp.where(lane < SITES, mine[:DPAD, snps : snps + LANES], 0.0), axis=1, keepdims=True
        )
        drift = jnp.sum(jnp.where(site, mine[:DPAD, :snps], 0.0), axis=0, keepdims=True)
        drift = (drift - jnp.sum(fitted * count, axis=0, keepdims=True)) * scale
        rows_out[DRIFT_LANE + j : DRIFT_LANE + j + 1, :] = drift
        if j == 0:
            rows_out[:DPAD, :] = fitted * scale + jnp.where(site, drift * (1.0 / here), 0.0)
    rows_out[SCALE_LANE : SCALE_LANE + 1, :] = scale
    coef[...] = jnp.transpose(rows_out[...])


def solve(parts, snps, design, here):
    return pl.pallas_call(
        functools.partial(solve_kernel, snps, design, here),
        out_shape=(
            jax.ShapeDtypeStruct((snps, LANES), jnp.float32),
            jax.ShapeDtypeStruct((DPAD, LANES), jnp.float32),
        ),
        scratch_shapes=[pltpu.VMEM((LANES, snps), jnp.float32)],
        compiler_params=params(),
        name="solve",
    )(*parts)


def column_norm(sums, here):
    square = sums[SQUARE_ROW : SQUARE_ROW + 1, :]
    mean = jnp.sum(sums[:SITES, :], axis=0, keepdims=True) * (1.0 / here)
    spread = jnp.maximum(square - mean * mean * here, square * 2.0**-10)
    return jnp.sqrt(spread + 1e-30), mean


def products_kernel(snps, here, me, genes, columns, coef, own, *refs):
    far, stats, held = refs[:-2], refs[-2], refs[-1]
    values = columns[...]
    wide = values.astype(jnp.float32)
    sums = jnp.dot(genes[...], values, preferred_element_type=jnp.float32)
    square = jnp.sum(wide * wide, axis=0, keepdims=True)
    cross_image = sums[snps:, :]
    row = lax.broadcasted_iota(jnp.int32, cross_image.shape, 0)
    cross_image = jnp.where(row == SQUARE_ROW, square, cross_image)
    stats[...] = cross_image
    norm, _ = column_norm(cross_image, here)
    lanes = lax.broadcasted_iota(jnp.int32, (snps, DPAD), 1)
    fit = jnp.where(lanes < SQUARE_ROW, coef[:, :DPAD], 0.0)
    held[...] = coef[:, SCALE_LANE : SCALE_LANE + 1] * sums[:snps, :] - jnp.dot(
        fit, cross_image, precision=HIGHEST, preferred_element_type=jnp.float32
    )
    size = own.shape[0]
    over = 1.0 / norm
    own[...] = held[pl.ds(pl.multiple_of(me[0] * size, size), size), :]
    for j, out in enumerate(far):
        place = jnp.bitwise_xor(me[0], j + 1)
        out[...] = held[pl.ds(pl.multiple_of(place * size, size), size), :] * over


def products(genes, columns, coef, me, count):
    rows, here = genes.shape
    snps = rows - DPAD
    width = columns.shape[1]
    lanes = min(width, 256)
    size = snps // count
    piece = jax.ShapeDtypeStruct((size, width), jnp.float32)
    piece_spec = pl.BlockSpec((size, lanes), lambda j: (0, j))
    return pl.pallas_call(
        functools.partial(products_kernel, snps, float(here)),
        out_shape=(piece,) * count + (jax.ShapeDtypeStruct((DPAD, width), jnp.float32),),
        grid=(width // lanes,),
        in_specs=[
            pl.BlockSpec(memory_space=pltpu.SMEM),
            pl.BlockSpec((rows, here), lambda j: (0, 0)),
            pl.BlockSpec((here, lanes), lambda j: (0, j)),
            pl.BlockSpec((snps, LANES), lambda j: (0, 0)),
        ],
        out_specs=(piece_spec,) * count + (pl.BlockSpec((DPAD, lanes), lambda j: (0, j)),),
        scratch_shapes=[pltpu.VMEM((snps, lanes), jnp.float32)],
        compiler_params=params(),
        name="products",
    )(me, genes, columns, coef)


def image_kernel(here, design, inverse, *refs):
    parts, out = refs[:-1], refs[-1]
    out[...] = jnp.zeros(out.shape, jnp.float32)
    total = tree_sum([part[...] for part in parts])
    row = lax.broadcasted_iota(jnp.int32, total.shape, 0)
    cross_image = jnp.where(row < design, total, 0.0)
    solved = jnp.dot(
        inverse[:, :DPAD], cross_image, precision=HIGHEST, preferred_element_type=jnp.float32
    )
    rss = total[SQUARE_ROW : SQUARE_ROW + 1, :] - jnp.sum(
        cross_image * solved, axis=0, keepdims=True
    )
    out[0:1, :] = lax.rsqrt(rss)
    for j, part in enumerate(parts):
        norm, mean = column_norm(part[...], here)
        out[MEAN_ROW + j : MEAN_ROW + j + 1, :] = mean
        out[NORM_ROW + j : NORM_ROW + j + 1, :] = norm


def image_side(inverse, parts, here, design):
    return pl.pallas_call(
        functools.partial(image_kernel, float(here), design),
        out_shape=jax.ShapeDtypeStruct((16, parts[0].shape[1]), jnp.float32),
        compiler_params=params(),
        name="image_side",
    )(inverse, *parts)


def permute_xor(value, axis, bits):
    size = lax.axis_size(axis)
    return lax.ppermute(value, axis, [(i, i ^ bits) for i in range(size)])


def on_device(images, genotypes, covariates, site_codes):
    subjects, maps, planes, plane = images.shape
    n_vox, n_far, n_near = (lax.axis_size(name) for name in ("vox", "far", "near"))
    vox, far, near = (lax.axis_index(name) for name in ("vox", "far", "near"))
    snps = genotypes.shape[1]
    design = SITES + covariates.shape[1]
    per_vox = planes // n_vox
    here = n_vox * n_near * subjects

    one_hot = (jnp.arange(SITES)[:, None] == site_codes[None, :]).astype(jnp.bfloat16)
    tall = jnp.concatenate(
        [genotypes.T, one_hot, covariates.T, jnp.zeros((DPAD - design, subjects), jnp.bfloat16)],
        axis=0,
    )[None]
    bits = []
    stages = [("near", b, b) for b in range(n_near.bit_length() - 1)]
    shift = n_near.bit_length() - 1
    stages += [("vox", b, b + shift) for b in reversed(range(n_vox.bit_length() - 1))]
    for axis, bit, place in stages:
        tall = jnp.concatenate([tall, permute_xor(tall, axis, 1 << bit)], axis=0)
        bits.append(place)

    smoothed = smooth(images, n_vox, n_near)
    columns = lax.all_to_all(smoothed, ("vox", "near"), 0, 0, tiled=True)
    columns = columns.reshape(here, columns.shape[2])

    genes, part = moments(tall, tuple(bits), (vox * n_near + near)[None])
    parts = [part] + [permute_xor(part, "far", j) for j in range(1, n_far)]
    coef, inverse = solve(parts, snps, design, float(here))

    *pieces, stats = products(genes, columns, coef, far[None], n_far)
    all_stats = [stats] + [permute_xor(stats, "far", j) for j in range(1, n_far)]
    received = [
        permute_xor(pieces[j].astype(jnp.float16), "far", j) for j in range(1, n_far)
    ]
    rows = image_side(inverse, all_stats, here, design)

    size = snps // n_far
    panel = size // n_near
    freedom = float(subjects * n_vox * n_near * n_far - design - 1)

    def panel_stats(index):
        first = index * panel
        lines = lax.dynamic_slice_in_dim(coef, far * size + first, panel, 0)
        ratio = lax.dynamic_slice_in_dim(pieces[0], first, panel, 0)
        for j in range(n_far):
            ratio = ratio + lines[:, DRIFT_LANE + j, None] * rows[None, MEAN_ROW + j]
            if j:
                piece = lax.dynamic_slice_in_dim(received[j - 1], first, panel, 0)
                ratio = ratio + piece.astype(jnp.float32) * rows[None, NORM_ROW + j]
        ratio = ratio * rows[None, 0]
        return ratio * jnp.sqrt(freedom / (1.0 - ratio * ratio))

    away = permute_xor(panel_stats(jnp.bitwise_xor(near, 1)), "near", 1)
    home = panel_stats(near)
    both = jnp.where(near == 0, jnp.stack([home, away], 1), jnp.stack([away, home], 1))
    return both.reshape(panel, maps, per_vox, plane)


def solution(mesh):
    sizes = dict(mesh.shape)
    devices = mesh.devices.reshape(sizes["group"], sizes["vox"], sizes["snp"] // 2, 2)
    split = Mesh(devices, ("group", "vox", "far", "near"))
    owner = ("group", "vox", "far", "near")
    placed = (P(owner, None, None, None), P(owner, None), P(owner, None), P(owner))
    return jax.shard_map(
        on_device,
        mesh=split,
        in_specs=placed,
        out_specs=P(("group", "far", "near"), None, "vox", None),
        check_vma=False,
    )
```

time: 157 us -> 126 us (0.80)
  blocking collectives: 90 us -> 0 us
  waiting for transfers between devices: 23.9 us -> 78.2 us
  between operations: 13.4 us -> 0.13 us
  starting transfers between devices: 7.57 us -> 14.7 us
  other arithmetic: 0.14 us -> 4.46 us
  Pallas kernels: 17.9 us -> 22 us
  local copies, waits for them, and re-layouts: 3.53 us -> 5.58 us
    ppermute x0 -> x7, waiting for transfers between devices: none -> 78.2 us  [permute_xor(): return lax.ppermute(value, axis, [(i, i ^ bits) for i in range(size)])]
    all_gather x1 -> x0, blocking collectives: 59.3 us -> none  [on_device(): tall_all = lax.all_gather(lax.all_gather(tall, 'snp'), 'vox')]
    all_to_all x1 -> x0, blocking collectives: 30.7 us -> none  [on_device(): lax.all_to_all(stats.reshape(n_snp, panel, width), 'snp', 0, 0, tiled=True)]
    all_gather x1 -> x0, waiting for transfers between devices: 23.9 us -> none  [on_device(): tall_all = lax.all_gather(lax.all_gather(tall, 'snp'), 'vox')]
    ppermute x0 -> x7, starting transfers between devices: none -> 9.26 us  [permute_xor(): return lax.ppermute(value, axis, [(i, i ^ bits) for i in range(size)])]
    pallas_call x3 -> x5, Pallas kernels: 17.9 us -> 22 us  [the longest x1 8.67 us: products(): pl.pallas_call(functools.partial(products_kernel, snps, float(here)), out...]
    all_to_all x1, starting transfers between devices: 7.53 us -> 5.4 us  [on_device(): columns = lax.all_to_all(smoothed, ('vox', 'near'), 0, 0, tiled=True)]
    reshape x2 -> x0, local copies, waits for them, and re-layouts: 2.01 us -> none  [on_device(): return stats.reshape(panel, maps, per_vox, plane)]
  transfers between devices with their start and end apart: 2 -> 8, of which waited for: 1 -> 6; matrix products, arithmetic and copies ran while one was open for 0% -> 3% of each run, Pallas kernels for 4% -> 7%
where the time goes in v2:
time: 126 us; the launch traced here: 125 us
  waiting for transfers between devices  78.2 us (62%)
  Pallas kernels  22 us (17%)
  starting transfers between devices  14.7 us (12%)
  local copies, waits for them, and re-layouts  5.58 us (4%)
  other arithmetic  4.46 us (4%)
    ppermute x7, waiting for transfers between devices, permute_xor(): return lax.ppermute(value, axis, [(i, i ^ bits) for i in range(size)])  78.2 us
    ppermute x7, starting transfers between devices, permute_xor(): return lax.ppermute(value, axis, [(i, i ^ bits) for i in range(size)])  9.26 us
    pallas_call x1, Pallas kernels, products(): pl.pallas_call(functools.partial(products_kernel, snps, float(here)), out...  8.67 us
    all_to_all x1, starting transfers between devices, on_device(): columns = lax.all_to_all(smoothed, ('vox', 'near'), 0, 0, tiled=True)  5.4 us
    pallas_call x1, Pallas kernels, smooth(): pl.pallas_call(functools.partial(smooth_kernel, group, planes, per_vox, p...  4.94 us
    pallas_call x1, Pallas kernels, solve(): pl.pallas_call(functools.partial(solve_kernel, snps, design, here), out_s...  3.65 us
    pallas_call x1, Pallas kernels, moments(): pl.pallas_call(functools.partial(moments_kernel, snps, bits), out_shape=(...  2.92 us
    unnamed x19, local copies, waits for them, and re-layouts  2.73 us
  transfers between devices with their start and end apart: 8, of which 6 were waited for; matrix products, arithmetic and copies ran while one was open for 3% of the time, Pallas kernels for 7%

profile of v2, /device:TPU:0, one launch (start us, length us, event | category | flops | bytes accessed | tf_op | source)
XLA Modules:
  0.0 125.1 jit_solution(16326749288911820236)
XLA Ops:
  0.0 4.9 %smooth.1 = bf16[8,128,1024]{2,1,0:T(8,128)(2,1)} custom-call(bf16[128,32,256]{2,1,0:T(8,128)(2,1)} %bitcast.18, bf16[256,256]{1,0:T(8,128)(2,1)} %constant.33.clone.order, bf16[256,256]{1,0:T(8,128)(2,1)} %constant.34.clone.table), custom_call_target="tpu_custom_call" | custom-call | tf_op jit(solution)/shard_map/smooth/pallas_call | solution.py:100
  4.9 5.4 %all-to-all-start = ((bf16[8,128,1024]{2,1,0:T(8,128)(2,1)}), bf16[8,128,1024]{2,1,0:T(8,128)(2,1)S(1)}, u32[]{:S(2)}, u32[]{:S(2)}) async-start(bf16[8,128,1024]{2,1,0:T(8,128)(2,1)} %smooth.1), calls=%async_computation | async-start | bytes 4194304 | tf_op jit(solution)/shard_map/all_to_all | solution.py:322
  10.4 0.1 copy.8
  10.5 0.1 pad.16.clone
  10.6 0.1 maximum_bitcast_fusion
  10.7 2.1 %collective-permute-start = (bf16[1,536,128]{2,1,0:T(8,128)(2,1)S(1)}, bf16[1,536,128]{2,1,0:T(8,128)(2,1)S(1)}, u32[]{:S(2)}, u32[]{:S(2)}) collective-permute-start(bf16[1,536,128]{2,1,0:T(8,128)(2,1)S(1)} %maximum_bitcast_fusion), channel_id=1, source_target_pairs={{0,1},{1,0},{2,3},{3,2},{4,5},{5,4},{6,7},{7,6},{8,9},{9,8},{10,11... | collective-permute-start | bytes 411656 | tf_op jit(solution)/shard_map/ppermute | solution.py:296
  12.8 26.2 %collective-permute-done = bf16[1,536,128]{2,1,0:T(8,128)(2,1)S(1)} collective-permute-done((bf16[1,536,128]{2,1,0:T(8,128)(2,1)S(1)}, bf16[1,536,128]{2,1,0:T(8,128)(2,1)S(1)}, u32[]{:S(2)}, u32[]{:S(2)}) %collective-permute-start) | collective-permute-done | bytes 137248 | tf_op jit(solution)/shard_map/ppermute | solution.py:296
  39.1 1.5 %collective-permute-start.1 = (bf16[2,536,128]{2,1,0:T(8,128)(2,1)S(1)}, bf16[2,536,128]{2,1,0:T(8,128)(2,1)S(1)}, u32[]{:S(2)}, u32[]{:S(2)}) collective-permute-start(bf16[2,536,128]{2,1,0:T(8,128)(2,1)S(1)} %pad_maximum_fusion.2), channel_id=1, source_target_pairs={{0,8},{4,12},{8,0},{12,4},{1,9},{5,13},{9,1},{13,5},{2,10},{6,14},... | collective-permute-start | bytes 823304 | tf_op jit(solution)/shard_map/ppermute | solution.py:296
  40.6 6.6 %collective-permute-done.1 = bf16[2,536,128]{2,1,0:T(8,128)(2,1)S(1)} collective-permute-done((bf16[2,536,128]{2,1,0:T(8,128)(2,1)S(1)}, bf16[2,536,128]{2,1,0:T(8,128)(2,1)S(1)}, u32[]{:S(2)}, u32[]{:S(2)}) %collective-permute-start.1) | collective-permute-done | bytes 274464 | tf_op jit(solution)/shard_map/ppermute | solution.py:296
  47.2 0.9 pad_maximum_fusion.1
  48.1 2.2 %collective-permute-done.2 = bf16[4,536,128]{2,1,0:T(8,128)(2,1)S(1)} collective-permute-done((bf16[4,536,128]{2,1,0:T(8,128)(2,1)}, bf16[4,536,128]{2,1,0:T(8,128)(2,1)S(1)}, u32[]{:S(2)}, u32[]{:S(2)}) %collective-permute-start.2) | collective-permute-done | bytes 548896 | tf_op jit(solution)/shard_map/ppermute | solution.py:296
  50.3 1.1 pad_maximum_fusion.blocks
  51.4 2.9 %moments.1 = (bf16[536,1024]{1,0:T(8,128)(2,1)}, f32[32,640]{1,0:T(8,128)}) custom-call(s32[1]{0:T(128)} %bitcast.1.me, bf16[8,536,128]{2,1,0:T(8,128)(2,1)} %pad_maximum_fusion.blocks), custom_call_target="tpu_custom_call" | custom-call | tf_op jit(solution)/shard_map/moments/pallas_call | solution.py:145
  54.3 2.6 %collective-permute-start.3 = (f32[32,640]{1,0:T(8,128)}, f32[32,640]{1,0:T(8,128)S(1)}, u32[]{:S(2)}, u32[]{:S(2)}) collective-permute-start(f32[32,640]{1,0:T(8,128)} %get-tuple-element.13.refs_0_), channel_id=1, source_target_pairs={{0,2},{2,0},{1,3},{3,1},{4,6},{6,4},{5,7},{7,5},{8,10},{10,8},{9,1... | collective-permute-start | bytes 245768 | tf_op jit(solution)/shard_map/ppermute | solution.py:296
  56.9 4.8 %collective-permute-done.3.refs_1_ = f32[32,640]{1,0:T(8,128)S(1)} collective-permute-done((f32[32,640]{1,0:T(8,128)}, f32[32,640]{1,0:T(8,128)S(1)}, u32[]{:S(2)}, u32[]{:S(2)}) %collective-permute-start.3) | collective-permute-done | bytes 81952 | tf_op jit(solution)/shard_map/ppermute | solution.py:296
  61.7 0.6 copy-done.6
  62.3 3.6 %solve.1 = (f32[512,128]{1,0:T(8,128)}, f32[24,128]{1,0:T(8,128)}) custom-call(f32[32,640]{1,0:T(8,128)} %get-tuple-element.13.refs_0_, f32[32,640]{1,0:T(8,128)} %copy-done.6), custom_call_target="tpu_custom_call" | custom-call | tf_op jit(solution)/shard_map/solve/pallas_call | solution.py:198
  65.9 1.3 %copy-done = bf16[8,128,1024]{2,1,0:T(8,128)(2,1)} copy-done((bf16[8,128,1024]{2,1,0:T(8,128)(2,1)}, bf16[8,128,1024]{2,1,0:T(8,128)(2,1)S(1)}, u32[]{:S(2)}) %copy-start) | copy-done | bytes 2097176
  67.3 8.7 %products.1 = (f32[256,1024]{1,0:T(8,128)}, f32[256,1024]{1,0:T(8,128)}, f32[24,1024]{1,0:T(8,128)}) custom-call(s32[1]{0:T(128)} %bitcast.me, bf16[536,1024]{1,0:T(8,128)(2,1)} %get-tuple-element.12.genes, bf16[1024,1024]{1,0:T(8,128)(2,1)} %bitcast.16, f32[512,128]{1,0:T(8,128)} %get-tuple-element.14.coef), custom_call_target="tpu_custom_call" | custom-call | tf_op jit(solution)/shard_map/products/pallas_call | solution.py:249
  76.0 1.4 %convert_element_type.13 = f16[256,1024]{1,0:T(8,128)(2,1)S(1)} convert(f32[256,1024]{1,0:T(8,128)} %get-tuple-element.18) | non-fusion elementwise | flops 262144 | bytes 1572864 | tf_op jit(solution)/shard_map/convert_element_type | solution.py:332
  77.4 1.0 collective-permute-start.5
  78.4 2.0 %collective-permute-start.4 = (f32[24,1024]{1,0:T(8,128)S(1)}, f32[24,1024]{1,0:T(8,128)S(1)}, u32[]{:S(2)}, u32[]{:S(2)}) collective-permute-start(f32[24,1024]{1,0:T(8,128)S(1)} %copy-done.4), channel_id=1, source_target_pairs={{0,2},{2,0},{1,3},{3,1},{4,6},{6,4},{5,7},{7,5},{8,10},{10,8},{9,1... | collective-permute-start | bytes 294920 | tf_op jit(solution)/shard_map/ppermute | solution.py:296
  80.4 0.3 dynamic-slice_reduce_fusion.3
  80.6 24.6 %collective-permute-done.4.refs_1_ = f32[24,1024]{1,0:T(8,128)S(1)} collective-permute-done((f32[24,1024]{1,0:T(8,128)S(1)}, f32[24,1024]{1,0:T(8,128)S(1)}, u32[]{:S(2)}, u32[]{:S(2)}) %collective-permute-start.4) | collective-permute-done | bytes 98336 | tf_op jit(solution)/shard_map/ppermute | solution.py:296
  105.2 0.6 copy-done.5
  105.8 1.8 %image_side.1 = f32[16,1024]{1,0:T(8,128)} custom-call(f32[24,128]{1,0:T(8,128)} %get-tuple-element.16.inverse, f32[24,1024]{1,0:T(8,128)} %get-tuple-element.17.refs_0_, f32[24,1024]{1,0:T(8,128)} %copy-done.5), custom_call_target="tpu_custom_call" | custom-call | tf_op jit(solution)/shard_map/image_side/pallas_call | solution.py:286
  107.7 0.9 fusion.1
  108.6 0.8 multiply_bitcast_fusion
  109.5 13.8 %collective-permute-done.6 = f32[128,1024]{1,0:T(8,128)S(1)} collective-permute-done((f32[128,1024]{1,0:T(8,128)S(1)}, f32[128,1024]{1,0:T(8,128)S(1)}, u32[]{:S(2)}, u32[]{:S(2)}) %collective-permute-start.6) | collective-permute-done | bytes 524320 | tf_op jit(solution)/shard_map/ppermute | solution.py:296
  123.3 0.1 maximum_select_fusion
  123.4 0.3 copy.9
  123.7 1.3 %copy.10 = f32[128,4,2,256]{3,2,1,0:T(2,128)} copy(f32[128,4,2,256]{0,3,2,1:T(8,128)S(1)} %bitcast.17) | data formatting | bytes 2097152 | tf_op jit(solution)/shard_map/jit(_where)/select_n | solution.py:354
  (22 shorter events, 0.1 us)
Async XLA Ops:
  4.9 5.4 %copy-start.3 = (bf16[128,512]{1,0:T(8,128)(2,1)S(1)}, bf16[128,512]{1,0:T(8,128)(2,1)}, u32[]{:S(2)}) copy-start(bf16[128,512]{1,0:T(8,128)(2,1)} %param.7) | copy-start | bytes 393220
  4.9 5.6 %copy-start.8 = (s32[128]{0:T(128)S(1)}, s32[128]{0:T(128)}, u32[]{:S(2)}) copy-start(s32[128]{0:T(128)} %param.9) | copy-start | bytes 1540
  4.9 5.6 %copy-start.7 = (bf16[128,16]{0,1:T(8,128)(2,1)S(1)}, bf16[128,16]{0,1:T(8,128)(2,1)}, u32[]{:S(2)}) copy-start(bf16[128,16]{0,1:T(8,128)(2,1)} %param.8) | copy-start | bytes 12292
  4.9 61.0 %all-to-all-start = ((bf16[8,128,1024]{2,1,0:T(8,128)(2,1)}), bf16[8,128,1024]{2,1,0:T(8,128)(2,1)S(1)}, u32[]{:S(2)}, u32[]{:S(2)}) async-start(bf16[8,128,1024]{2,1,0:T(8,128)(2,1)} %smooth.1), calls=%async_computation | async-start | bytes 4194304 | tf_op jit(solution)/shard_map/all_to_all | solution.py:322
  10.7 28.3 %collective-permute-start = (bf16[1,536,128]{2,1,0:T(8,128)(2,1)S(1)}, bf16[1,536,128]{2,1,0:T(8,128)(2,1)S(1)}, u32[]{:S(2)}, u32[]{:S(2)}) collective-permute-start(bf16[1,536,128]{2,1,0:T(8,128)(2,1)S(1)} %maximum_bitcast_fusion), channel_id=1, source_target_pairs={{0,1},{1,0},{2,3},{3,2},{4,5},{5,4},{6,7},{7,6},{8,9},{9,8},{10,11... | collective-permute-start | bytes 411656 | tf_op jit(solution)/shard_map/ppermute | solution.py:296
  39.1 8.2 %collective-permute-start.1 = (bf16[2,536,128]{2,1,0:T(8,128)(2,1)S(1)}, bf16[2,536,128]{2,1,0:T(8,128)(2,1)S(1)}, u32[]{:S(2)}, u32[]{:S(2)}) collective-permute-start(bf16[2,536,128]{2,1,0:T(8,128)(2,1)S(1)} %pad_maximum_fusion.2), channel_id=1, source_target_pairs={{0,8},{4,12},{8,0},{12,4},{1,9},{5,13},{9,1},{13,5},{2,10},{6,14},... | collective-permute-start | bytes 823304 | tf_op jit(solution)/shard_map/ppermute | solution.py:296
  48.1 2.2 %collective-permute-start.2 = (bf16[4,536,128]{2,1,0:T(8,128)(2,1)}, bf16[4,536,128]{2,1,0:T(8,128)(2,1)S(1)}, u32[]{:S(2)}, u32[]{:S(2)}) collective-permute-start(bf16[4,536,128]{2,1,0:T(8,128)(2,1)} %pad_maximum_fusion.1), channel_id=1, source_target_pairs={{0,4},{4,0},{8,12},{12,8},{1,5},{5,1},{9,13},{13,9},{2,6},{6,2},{1... | collective-permute-start | bytes 1646600 | tf_op jit(solution)/shard_map/ppermute | solution.py:296
  54.3 7.4 %collective-permute-start.3 = (f32[32,640]{1,0:T(8,128)}, f32[32,640]{1,0:T(8,128)S(1)}, u32[]{:S(2)}, u32[]{:S(2)}) collective-permute-start(f32[32,640]{1,0:T(8,128)} %get-tuple-element.13.refs_0_), channel_id=1, source_target_pairs={{0,2},{2,0},{1,3},{3,1},{4,6},{6,4},{5,7},{7,5},{8,10},{10,8},{9,1... | collective-permute-start | bytes 245768 | tf_op jit(solution)/shard_map/ppermute | solution.py:296
  61.7 0.6 copy-start.6
  65.9 1.3 %copy-start = (bf16[8,128,1024]{2,1,0:T(8,128)(2,1)}, bf16[8,128,1024]{2,1,0:T(8,128)(2,1)S(1)}, u32[]{:S(2)}) copy-start(bf16[8,128,1024]{2,1,0:T(8,128)(2,1)S(1)} %all-to-all-done) | copy-start | bytes 6291460
  75.9 2.4 %copy-start.4 = (f32[24,1024]{1,0:T(8,128)S(1)}, f32[24,1024]{1,0:T(8,128)}, u32[]{:S(2)}) copy-start(f32[24,1024]{1,0:T(8,128)} %get-tuple-element.17.refs_0_) | copy-start | bytes 294916
  75.9 4.4 %copy-start.1 = (f32[512,128]{1,0:T(8,128)S(1)}, f32[512,128]{1,0:T(8,128)}, u32[]{:S(2)}) copy-start(f32[512,128]{1,0:T(8,128)} %get-tuple-element.14.coef) | copy-start | bytes 786436
  75.9 32.6 %copy-start.2 = (f32[256,1024]{1,0:T(8,128)S(1)}, f32[256,1024]{1,0:T(8,128)}, u32[]{:S(2)}) copy-start(f32[256,1024]{1,0:T(8,128)} %get-tuple-element.15) | copy-start | bytes 3145732
  77.4 31.2 %collective-permute-start.5 = (f16[256,1024]{1,0:T(8,128)(2,1)S(1)}, f16[256,1024]{1,0:T(8,128)(2,1)S(1)}, u32[]{:S(2)}, u32[]{:S(2)}) collective-permute-start(f16[256,1024]{1,0:T(8,128)(2,1)S(1)} %convert_element_type.13), channel_id=1, source_target_pairs={{0,2},{2,0},{1,3},{3,1},{4,6},{6,4},{5,7},{7,5},{8,10},{10,8},{9,1... | collective-permute-start | bytes 1572872 | tf_op jit(solution)/shard_map/ppermute | solution.py:296
  78.4 26.8 %collective-permute-start.4 = (f32[24,1024]{1,0:T(8,128)S(1)}, f32[24,1024]{1,0:T(8,128)S(1)}, u32[]{:S(2)}, u32[]{:S(2)}) collective-permute-start(f32[24,1024]{1,0:T(8,128)S(1)} %copy-done.4), channel_id=1, source_target_pairs={{0,2},{2,0},{1,3},{3,1},{4,6},{6,4},{5,7},{7,5},{8,10},{10,8},{9,1... | collective-permute-start | bytes 294920 | tf_op jit(solution)/shard_map/ppermute | solution.py:296
  105.2 0.6 copy-start.5
  109.4 13.9 %collective-permute-start.6 = (f32[128,1024]{1,0:T(8,128)S(1)}, f32[128,1024]{1,0:T(8,128)S(1)}, u32[]{:S(2)}, u32[]{:S(2)}) collective-permute-start(f32[128,1024]{1,0:T(8,128)S(1)} %get-tuple-element.24), channel_id=1, source_target_pairs={{0,1},{1,0},{2,3},{3,2},{4,5},{5,4},{6,7},{7,6},{8,9},{9,8},{10,11... | collective-permute-start | bytes 1572872 | tf_op jit(solution)/shard_map/ppermute | solution.py:296

commit v3 on v2

--- a/solution.py
+++ b/solution.py
@@ -21,9 +21,7 @@
 VMEM_LIMIT = 56 * 2**20
 SQUARE_ROW = 20
 SCALE_LANE = DPAD
-DRIFT_LANE = DPAD + 1
-MEAN_ROW = 1
-NORM_ROW = 8
+STRIDE = 32
 
 
 def kernel_table(length):
@@ -112,14 +110,13 @@
     )(images.reshape(subjects, maps * planes, plane), order, table)
 
 
-def moments_kernel(snps, bits, me, blocks, joined, out):
-    count = blocks.shape[0]
+def moments_kernel(snps, slots, me, blocks, joined, out):
     rows = []
-    for source in range(count):
+    for source in range(len(slots)):
         offset = jnp.bitwise_xor(me[0], source)
         index = 0
-        for place, bit in enumerate(bits):
-            index = index + ((offset >> bit) & 1) * (1 << place)
+        for place, slot in enumerate(slots):
+            index = index + jnp.where(offset == place, slot, 0)
         rows.append(blocks[index])
     rows = jnp.concatenate(rows, axis=1)
     joined[...] = rows
@@ -138,12 +135,12 @@
     out[DPAD:, :snps] = squares
 
 
-def moments(blocks, bits, me):
+def moments(blocks, slots, me):
     count, rows, subjects = blocks.shape
     snps = rows - DPAD
     spread = -(-rows // LANES) * LANES
     return pl.pallas_call(
-        functools.partial(moments_kernel, snps, bits),
+        functools.partial(moments_kernel, snps, slots),
         out_shape=(
             jax.ShapeDtypeStruct((rows, count * subjects), blocks.dtype),
             jax.ShapeDtypeStruct((DPAD + 8, spread), jnp.float32),
@@ -157,53 +154,79 @@
     )(me, blocks)
 
 
-def solve_kernel(snps, design, here, *refs):
-    parts, (coef, inverse, rows_out) = refs[:-3], refs[-3:]
-    total = tree_sum([part[...] for part in parts])
+def eliminate(total, snps, design, guard):
     lane = lax.broadcasted_iota(jnp.int32, (DPAD, LANES), 1)
     row = lax.broadcasted_iota(jnp.int32, (DPAD, LANES), 0)
     shift = 32
-    work = total[:DPAD, snps : snps + LANES]
-    work = jnp.where((row >= design) & (lane == row), 1.0, work)
+    gram = total[:DPAD, snps : snps + LANES]
+    work = jnp.where((row >= design) & (lane == row), 1.0, gram)
     work = jnp.where(lane == row + shift, 1.0, work)
     for k in range(design):
-        pivot = work[k : k + 1, :] / work[k : k + 1, k : k + 1]
-        work = jnp.where(row == k, pivot, work - work[:, k : k + 1] * pivot)
+        pivot = work[k : k + 1, k : k + 1]
+        line = work[k : k + 1, :] / pivot
+        if guard:
+            line = jnp.where(pivot > gram[k : k + 1, k : k + 1] * 2.0**-14, line, 0.0)
+        work = jnp.where(row == k, line, work - work[:, k : k + 1] * line)
     solved = pltpu.roll(work, LANES - shift, 1)
-    solved = jnp.where((lane < design) & (row < design), solved, 0.0)
-    inverse[...] = solved
+    return jnp.where((lane < design) & (row < design), solved, 0.0)
+
+
+def gene_fit(total, snps, design, guard):
+    solved = eliminate(total, snps, design, guard)
     cross_gene = total[:DPAD, :snps]
     fitted = jnp.dot(
         solved[:, :DPAD], cross_gene, precision=HIGHEST, preferred_element_type=jnp.float32
     )
-    rss = total[DPAD : DPAD + 1, :snps] - jnp.sum(cross_gene * fitted, axis=0, keepdims=True)
-    scale = lax.rsqrt(rss)
-    site = lax.broadcasted_iota(jnp.int32, (DPAD, snps), 0) < SITES
-    rows_out[...] = jnp.zeros(rows_out.shape, jnp.float32)
-    for j, part in enumerate(parts):
-        mine = part[...]
-        count = jnp.sum(
-            jnp.where(lane < SITES, mine[:DPAD, snps : snps + LANES], 0.0), axis=1, keepdims=True
-        )
-        drift = jnp.sum(jnp.where(site, mine[:DPAD, :snps], 0.0), axis=0, keepdims=True)
-        drift = (drift - jnp.sum(fitted * count, axis=0, keepdims=True)) * scale
-        rows_out[DRIFT_LANE + j : DRIFT_LANE + j + 1, :] = drift
-        if j == 0:
-            rows_out[:DPAD, :] = fitted * scale + jnp.where(site, drift * (1.0 / here), 0.0)
-    rows_out[SCALE_LANE : SCALE_LANE + 1, :] = scale
-    coef[...] = jnp.transpose(rows_out[...])
-
-
-def solve(parts, snps, design, here):
-    return pl.pallas_call(
-        functools.partial(solve_kernel, snps, design, here),
+    square = total[DPAD : DPAD + 1, :snps]
+    rss = square - jnp.sum(cross_gene * fitted, axis=0, keepdims=True)
+    if guard:
+        rss = jnp.maximum(rss, square * 2.0**-10) + 1e-30
+    return solved, fitted, lax.rsqrt(rss)
+
+
+def pair_kernel(snps, design, moment, coef, lines):
+    _, fitted, scale = gene_fit(moment[...], snps, design, True)
+    lines[...] = jnp.zeros(lines.shape, jnp.float32)
+    lines[:DPAD, :] = fitted * scale
+    lines[SCALE_LANE : SCALE_LANE + 1, :] = scale
+    coef[...] = jnp.transpose(lines[...])
+
+
+def pair_fit(moment, snps, design):
+    return pl.pallas_call(
+        functools.partial(pair_kernel, snps, design),
+        out_shape=jax.ShapeDtypeStruct((snps, LANES), jnp.float32),
+        scratch_shapes=[pltpu.VMEM((LANES, snps), jnp.float32)],
+        compiler_params=params(),
+        name="pair_fit",
+    )(moment)
+
+
+def cohort_kernel(snps, design, *refs):
+    parts, (coef, inverse, lines) = refs[:-3], refs[-3:]
+    moment = [part[...] for part in parts]
+    solved, fitted, scale = gene_fit(tree_sum(moment), snps, design, False)
+    inverse[...] = solved
+    lines[...] = jnp.zeros(lines.shape, jnp.float32)
+    lines[:DPAD, :] = fitted * -scale
+    lines[SCALE_LANE : SCALE_LANE + 1, :] = scale
+    for j in range(1, len(parts)):
+        _, fit, own_scale = gene_fit(moment[j], snps, design, True)
+        lines[j * STRIDE : j * STRIDE + DPAD, :] = fit * scale
+        lines[SCALE_LANE + j : SCALE_LANE + j + 1, :] = scale / own_scale
+    coef[...] = jnp.transpose(lines[...])
+
+
+def cohort_fit(parts, snps, design):
+    return pl.pallas_call(
+        functools.partial(cohort_kernel, snps, design),
         out_shape=(
             jax.ShapeDtypeStruct((snps, LANES), jnp.float32),
             jax.ShapeDtypeStruct((DPAD, LANES), jnp.float32),
         ),
         scratch_shapes=[pltpu.VMEM((LANES, snps), jnp.float32)],
         compiler_params=params(),
-        name="solve",
+        name="cohort_fit",
     )(*parts)
 
 
@@ -211,31 +234,32 @@
     square = sums[SQUARE_ROW : SQUARE_ROW + 1, :]
     mean = jnp.sum(sums[:SITES, :], axis=0, keepdims=True) * (1.0 / here)
     spread = jnp.maximum(square - mean * mean * here, square * 2.0**-10)
-    return jnp.sqrt(spread + 1e-30), mean
-
-
-def products_kernel(snps, here, me, genes, columns, coef, own, *refs):
+    return jnp.sqrt(spread + 1e-30)
+
+
+def products_kernel(here, me, genes, columns, coef, own, *refs):
     far, stats, held = refs[:-2], refs[-2], refs[-1]
     values = columns[...]
     wide = values.astype(jnp.float32)
     sums = jnp.dot(genes[...], values, preferred_element_type=jnp.float32)
+    snps = held.shape[0]
+    held[...] = sums[:snps, :]
     square = jnp.sum(wide * wide, axis=0, keepdims=True)
     cross_image = sums[snps:, :]
     row = lax.broadcasted_iota(jnp.int32, cross_image.shape, 0)
     cross_image = jnp.where(row == SQUARE_ROW, square, cross_image)
     stats[...] = cross_image
-    norm, _ = column_norm(cross_image, here)
-    lanes = lax.broadcasted_iota(jnp.int32, (snps, DPAD), 1)
-    fit = jnp.where(lanes < SQUARE_ROW, coef[:, :DPAD], 0.0)
-    held[...] = coef[:, SCALE_LANE : SCALE_LANE + 1] * sums[:snps, :] - jnp.dot(
-        fit, cross_image, precision=HIGHEST, preferred_element_type=jnp.float32
-    )
+    over = 1.0 / column_norm(cross_image, here)
     size = own.shape[0]
-    over = 1.0 / norm
     own[...] = held[pl.ds(pl.multiple_of(me[0] * size, size), size), :]
     for j, out in enumerate(far):
-        place = jnp.bitwise_xor(me[0], j + 1)
-        out[...] = held[pl.ds(pl.multiple_of(place * size, size), size), :] * over
+        place = pl.multiple_of(jnp.bitwise_xor(me[0], j + 1) * size, size)
+        line = coef[pl.ds(place, size), :]
+        fit = jnp.dot(
+            line[:, :DPAD], cross_image, precision=HIGHEST, preferred_element_type=jnp.float32
+        )
+        scale = line[:, SCALE_LANE : SCALE_LANE + 1]
+        out[...] = (scale * held[pl.ds(place, size), :] - fit) * over
 
 
 def products(genes, columns, coef, me, count):
@@ -247,7 +271,7 @@
     piece = jax.ShapeDtypeStruct((size, width), jnp.float32)
     piece_spec = pl.BlockSpec((size, lanes), lambda j: (0, j))
     return pl.pallas_call(
-        functools.partial(products_kernel, snps, float(here)),
+        functools.partial(products_kernel, float(here)),
         out_shape=(piece,) * count + (jax.ShapeDtypeStruct((DPAD, width), jnp.float32),),
         grid=(width // lanes,),
         in_specs=[
@@ -263,37 +287,63 @@
     )(me, genes, columns, coef)
 
 
-def image_kernel(here, design, inverse, *refs):
-    parts, out = refs[:-1], refs[-1]
-    out[...] = jnp.zeros(out.shape, jnp.float32)
-    total = tree_sum([part[...] for part in parts])
-    row = lax.broadcasted_iota(jnp.int32, total.shape, 0)
-    cross_image = jnp.where(row < design, total, 0.0)
+def base_kernel(here, me, own, coef, inverse, *refs):
+    parts, (base, factors, stack) = refs[:-3], refs[-3:]
+    stats = [part[...] for part in parts]
+    row = lax.broadcasted_iota(jnp.int32, stats[0].shape, 0)
+    total = tree_sum(stats)
+    cross_image = jnp.where(row < SQUARE_ROW, total, 0.0)
     solved = jnp.dot(
         inverse[:, :DPAD], cross_image, precision=HIGHEST, preferred_element_type=jnp.float32
     )
     rss = total[SQUARE_ROW : SQUARE_ROW + 1, :] - jnp.sum(
         cross_image * solved, axis=0, keepdims=True
     )
-    out[0:1, :] = lax.rsqrt(rss)
-    for j, part in enumerate(parts):
-        norm, mean = column_norm(part[...], here)
-        out[MEAN_ROW + j : MEAN_ROW + j + 1, :] = mean
-        out[NORM_ROW + j : NORM_ROW + j + 1, :] = norm
-
-
-def image_side(inverse, parts, here, design):
-    return pl.pallas_call(
-        functools.partial(image_kernel, float(here), design),
-        out_shape=jax.ShapeDtypeStruct((16, parts[0].shape[1]), jnp.float32),
-        compiler_params=params(),
-        name="image_side",
-    )(inverse, *parts)
-
-
-def permute_xor(value, axis, bits):
-    size = lax.axis_size(axis)
-    return lax.ppermute(value, axis, [(i, i ^ bits) for i in range(size)])
+    scale = lax.rsqrt(rss)
+    stack[...] = jnp.zeros(stack.shape, jnp.float32)
+    stack[:DPAD, :] = cross_image
+    factors[...] = jnp.zeros(factors.shape, jnp.float32)
+    for j in range(1, len(parts)):
+        stack[j * STRIDE : j * STRIDE + DPAD, :] = jnp.where(row < SQUARE_ROW, stats[j], 0.0)
+        factors[j : j + 1, :] = column_norm(stats[j], here) * scale
+    size = own.shape[0]
+    line = coef[pl.ds(pl.multiple_of(me[0] * size, size), size), :]
+    terms = jnp.dot(line, stack[...], precision=HIGHEST, preferred_element_type=jnp.float32)
+    base[...] = (line[:, SCALE_LANE : SCALE_LANE + 1] * own[...] + terms) * scale
+
+
+def base_ratio(me, own, coef, inverse, parts, here):
+    size, width = own.shape
+    lanes = min(width, 256)
+    snps = coef.shape[0]
+    stat_spec = pl.BlockSpec((DPAD, lanes), lambda j: (0, j))
+    return pl.pallas_call(
+        functools.partial(base_kernel, float(here)),
+        out_shape=(
+            jax.ShapeDtypeStruct((size, width), jnp.float32),
+            jax.ShapeDtypeStruct((8, width), jnp.float32),
+        ),
+        grid=(width // lanes,),
+        in_specs=[
+            pl.BlockSpec(memory_space=pltpu.SMEM),
+            pl.BlockSpec((size, lanes), lambda j: (0, j)),
+            pl.BlockSpec((snps, LANES), lambda j: (0, 0)),
+            pl.BlockSpec((DPAD, LANES), lambda j: (0, 0)),
+        ]
+        + [stat_spec] * len(parts),
+        out_specs=(
+            pl.BlockSpec((size, lanes), lambda j: (0, j)),
+            pl.BlockSpec((8, lanes), lambda j: (0, j)),
+        ),
+        scratch_shapes=[pltpu.VMEM((LANES, lanes), jnp.float32)],
+        compiler_params=params(),
+        name="base_ratio",
+    )(me, own, coef, inverse, *parts)
+
+
+def permute_xor(value, axes, bits):
+    size = lax.axis_size(axes)
+    return lax.ppermute(value, axes, [(i, i ^ bits) for i in range(size)])
 
 
 def on_device(images, genotypes, covariates, site_codes):
@@ -303,50 +353,50 @@
     snps = genotypes.shape[1]
     design = SITES + covariates.shape[1]
     per_vox = planes // n_vox
-    here = n_vox * n_near * subjects
+    count = n_vox * n_near
+    here = count * subjects
 
     one_hot = (jnp.arange(SITES)[:, None] == site_codes[None, :]).astype(jnp.bfloat16)
     tall = jnp.concatenate(
         [genotypes.T, one_hot, covariates.T, jnp.zeros((DPAD - design, subjects), jnp.bfloat16)],
         axis=0,
-    )[None]
-    bits = []
-    stages = [("near", b, b) for b in range(n_near.bit_length() - 1)]
-    shift = n_near.bit_length() - 1
-    stages += [("vox", b, b + shift) for b in reversed(range(n_vox.bit_length() - 1))]
-    for axis, bit, place in stages:
-        tall = jnp.concatenate([tall, permute_xor(tall, axis, 1 << bit)], axis=0)
-        bits.append(place)
-
+    )
+    other = n_near
+    offsets = [o for o in range(count) if not o & other]
+    blocks = [tall] + [permute_xor(tall, ("vox", "near"), o) for o in offsets[1:]]
     smoothed = smooth(images, n_vox, n_near)
+    smoothed, *blocks = lax.optimization_barrier((smoothed, *blocks))
     columns = lax.all_to_all(smoothed, ("vox", "near"), 0, 0, tiled=True)
     columns = columns.reshape(here, columns.shape[2])
-
-    genes, part = moments(tall, tuple(bits), (vox * n_near + near)[None])
-    parts = [part] + [permute_xor(part, "far", j) for j in range(1, n_far)]
-    coef, inverse = solve(parts, snps, design, float(here))
-
-    *pieces, stats = products(genes, columns, coef, far[None], n_far)
-    all_stats = [stats] + [permute_xor(stats, "far", j) for j in range(1, n_far)]
-    received = [
-        permute_xor(pieces[j].astype(jnp.float16), "far", j) for j in range(1, n_far)
+    blocks = jnp.stack(blocks)
+    blocks = jnp.concatenate([blocks, permute_xor(blocks, ("vox", "near"), other)], axis=0)
+    order = offsets + [o | other for o in offsets]
+    slots = tuple(order.index(o) for o in range(count))
+
+    genes, moment = moments(blocks, slots, (vox * n_near + near)[None])
+    pair_coef = pair_fit(moment, snps, design)
+    moment_parts = [moment] + [permute_xor(moment, "far", j) for j in range(1, n_far)]
+
+    own, *pieces, stats = products(genes, columns, pair_coef, far[None], n_far)
+    stat_parts = [stats] + [permute_xor(stats, "far", j) for j in range(1, n_far)]
+    pieces = [
+        permute_xor(pieces[j - 1].astype(jnp.float16), "far", j) for j in range(1, n_far)
     ]
-    rows = image_side(inverse, all_stats, here, design)
+    coef, inverse = cohort_fit(moment_parts, snps, design)
+    base, factors = base_ratio(far[None], own, coef, inverse, stat_parts, here)
 
     size = snps // n_far
     panel = size // n_near
-    freedom = float(subjects * n_vox * n_near * n_far - design - 1)
+    freedom = float(here * n_far - design - 1)
 
     def panel_stats(index):
         first = index * panel
-        lines = lax.dynamic_slice_in_dim(coef, far * size + first, panel, 0)
-        ratio = lax.dynamic_slice_in_dim(pieces[0], first, panel, 0)
-        for j in range(n_far):
-            ratio = ratio + lines[:, DRIFT_LANE + j, None] * rows[None, MEAN_ROW + j]
-            if j:
-                piece = lax.dynamic_slice_in_dim(received[j - 1], first, panel, 0)
-                ratio = ratio + piece.astype(jnp.float32) * rows[None, NORM_ROW + j]
-        ratio = ratio * rows[None, 0]
+        line = lax.dynamic_slice_in_dim(coef, far * size + first, panel, 0)
+        ratio = lax.dynamic_slice_in_dim(base, first, panel, 0)
+        for j in range(1, n_far):
+            piece = lax.dynamic_slice_in_dim(pieces[j - 1], first, panel, 0)
+            weight = line[:, SCALE_LANE + j, None] * factors[None, j]
+            ratio = ratio + piece.astype(jnp.float32) * weight
         return ratio * jnp.sqrt(freedom / (1.0 - ratio * ratio))
 
     away = permute_xor(panel_stats(jnp.bitwise_xor(near, 1)), "near", 1)

time: 126 us -> 115 us (0.913)
  waiting for transfers between devices: 78.2 us -> 60.4 us
  Pallas kernels: 22 us -> 26.5 us
  local copies, waits for them, and re-layouts: 5.58 us -> 8.28 us
    ppermute x7 -> x8, waiting for transfers between devices: 78.2 us -> 44.2 us  [permute_xor(): return lax.ppermute(value, axes, [(i, i ^ bits) for i in range(size)])]
    all_to_all x1, waiting for transfers between devices: 0.01 us -> 16.2 us  [on_device(): columns = lax.all_to_all(smoothed, ('vox', 'near'), 0, 0, tiled=True)]
    pallas_call x4 -> x5, Pallas kernels: 17.1 us -> 21.6 us  [the longest x1 6.91 us: products(): pl.pallas_call(functools.partial(products_kernel, float(here)), out_shape...]
    unnamed x19 -> x17, local copies, waits for them, and re-layouts: 2.73 us -> 4.69 us
    all_to_all x1, starting transfers between devices: 5.4 us -> 3.6 us  [on_device(): columns = lax.all_to_all(smoothed, ('vox', 'near'), 0, 0, tiled=True)]
    ppermute x7 -> x8, starting transfers between devices: 9.26 us -> 10.9 us  [permute_xor(): return lax.ppermute(value, axes, [(i, i ^ bits) for i in range(size)])]
  transfers between devices with their start and end apart: 8 -> 9, of which waited for: 6 -> 5; matrix products, arithmetic and copies ran while one was open for 3% -> 2% of each run, Pallas kernels for 7% -> 17%
where the time goes in v3:
time: 115 us
  waiting for transfers between devices  60.4 us (53%)
  Pallas kernels  26.5 us (23%)
  starting transfers between devices  14.5 us (13%)
  local copies, waits for them, and re-layouts  8.28 us (7%)
  other arithmetic  4.86 us (4%)
    ppermute x8, waiting for transfers between devices, permute_xor(): return lax.ppermute(value, axes, [(i, i ^ bits) for i in range(size)])  44.2 us
    all_to_all x1, waiting for transfers between devices, on_device(): columns = lax.all_to_all(smoothed, ('vox', 'near'), 0, 0, tiled=True)  16.2 us
    ppermute x8, starting transfers between devices, permute_xor(): return lax.ppermute(value, axes, [(i, i ^ bits) for i in range(size)])  10.9 us
    pallas_call x1, Pallas kernels, products(): pl.pallas_call(functools.partial(products_kernel, float(here)), out_shape...  6.91 us
    pallas_call x1, Pallas kernels, smooth(): pl.pallas_call(functools.partial(smooth_kernel, group, planes, per_vox, p...  4.92 us
    unnamed x17, local copies, waits for them, and re-layouts  4.69 us
    pallas_call x1, Pallas kernels, base_ratio(): pl.pallas_call(functools.partial(base_kernel, float(here)), out_shape=(ja...  4.33 us
    pallas_call x1, Pallas kernels, cohort_fit(): pl.pallas_call(functools.partial(cohort_kernel, snps, design), out_shape=...  3.78 us
  transfers between devices with their start and end apart: 9, of which 5 were waited for; matrix products, arithmetic and copies ran while one was open for 2% of the time, Pallas kernels for 17%

profile of v3, /device:TPU:0, one launch (start us, length us, event | category | flops | bytes accessed | tf_op | source)
XLA Modules:
  0.0 114.7 jit_solution(10955118191073642563)
XLA Ops:
  0.0 0.7 fusion
  0.7 1.0 copy.8
  1.8 0.8 maximum_maximum_fusion
  2.6 3.1 %collective-permute-start = (bf16[536,128]{1,0:T(8,128)(2,1)S(1)}, bf16[536,128]{1,0:T(8,128)(2,1)S(1)}, u32[]{:S(2)}, u32[]{:S(2)}) collective-permute-start(bf16[536,128]{1,0:T(8,128)(2,1)S(1)} %maximum_maximum_fusion), channel_id=1, source_target_pairs={{0,1},{1,0},{4,5},{5,4},{8,9},{9,8},{12,13},{13,12},{2,3},{3,2},{6... | collective-permute-start | bytes 411656 | tf_op jit(solution)/shard_map/ppermute | solution.py:346
  5.7 1.5 %collective-permute-start.1 = (bf16[536,128]{1,0:T(8,128)(2,1)S(1)}, bf16[536,128]{1,0:T(8,128)(2,1)S(1)}, u32[]{:S(2)}, u32[]{:S(2)}) collective-permute-start(bf16[536,128]{1,0:T(8,128)(2,1)S(1)} %maximum_maximum_fusion), channel_id=1, source_target_pairs={{0,8},{1,9},{4,12},{5,13},{8,0},{9,1},{12,4},{13,5},{2,10},{3,11},... | collective-permute-start | bytes 411656 | tf_op jit(solution)/shard_map/ppermute | solution.py:346
  7.2 4.9 %smooth.1 = bf16[8,128,1024]{2,1,0:T(8,128)(2,1)} custom-call(bf16[128,32,256]{2,1,0:T(8,128)(2,1)} %bitcast.21, bf16[256,256]{1,0:T(8,128)(2,1)} %constant.33.clone.order, bf16[256,256]{1,0:T(8,128)(2,1)} %constant.34.clone.table), custom_call_target="tpu_custom_call" | custom-call | tf_op jit(solution)/shard_map/smooth/pallas_call | solution.py:98
  12.2 1.6 %collective-permute-done.1 = bf16[536,128]{1,0:T(8,128)(2,1)S(1)} collective-permute-done((bf16[536,128]{1,0:T(8,128)(2,1)S(1)}, bf16[536,128]{1,0:T(8,128)(2,1)S(1)}, u32[]{:S(2)}, u32[]{:S(2)}) %collective-permute-start.1) | collective-permute-done | bytes 137248 | tf_op jit(solution)/shard_map/ppermute | solution.py:346
  13.7 3.6 %all-to-all-start = ((bf16[8,128,1024]{2,1,0:T(8,128)(2,1)}), bf16[8,128,1024]{2,1,0:T(8,128)(2,1)S(1)}, u32[]{:S(2)}, u32[]{:S(2)}) async-start(bf16[8,128,1024]{2,1,0:T(8,128)(2,1)} %smooth.1), calls=%async_computation | async-start | bytes 4194304 | tf_op jit(solution)/shard_map/all_to_all | solution.py:369
  17.4 0.5 collective-permute-start.3
  18.0 1.6 %collective-permute-done.3 = bf16[4,536,128]{2,1,0:T(8,128)(2,1)S(1)} collective-permute-done((bf16[4,536,128]{2,1,0:T(8,128)(2,1)S(1)}, bf16[4,536,128]{2,1,0:T(8,128)(2,1)S(1)}, u32[]{:S(2)}, u32[]{:S(2)}) %collective-permute-start.3) | collective-permute-done | bytes 548896 | tf_op jit(solution)/shard_map/ppermute | solution.py:346
  19.6 1.0 copy-done.1
  20.6 2.9 %moments.1 = (bf16[536,1024]{1,0:T(8,128)(2,1)}, f32[32,640]{1,0:T(8,128)}) custom-call(s32[1]{0:T(128)} %bitcast.1.me, bf16[8,536,128]{2,1,0:T(8,128)(2,1)} %copy-done.1), custom_call_target="tpu_custom_call" | custom-call | tf_op jit(solution)/shard_map/moments/pallas_call | solution.py:142
  23.5 3.7 %pair_fit.1.coef = f32[512,128]{1,0:T(8,128)} custom-call(f32[32,640]{1,0:T(8,128)} %get-tuple-element.25.moment.refs_0_), custom_call_target="tpu_custom_call" | custom-call | tf_op jit(solution)/shard_map/pair_fit/pallas_call | solution.py:196
  27.2 16.2 %all-to-all-done = bf16[8,128,1024]{2,1,0:T(8,128)(2,1)S(1)} async-done(((bf16[8,128,1024]{2,1,0:T(8,128)(2,1)}), bf16[8,128,1024]{2,1,0:T(8,128)(2,1)S(1)}, u32[]{:S(2)}, u32[]{:S(2)}) %all-to-all-start) | async-done | bytes 2097184 | tf_op jit(solution)/shard_map/all_to_all | solution.py:369
  43.4 1.3 %copy-done = bf16[8,128,1024]{2,1,0:T(8,128)(2,1)} copy-done((bf16[8,128,1024]{2,1,0:T(8,128)(2,1)}, bf16[8,128,1024]{2,1,0:T(8,128)(2,1)S(1)}, u32[]{:S(2)}) %copy-start) | copy-done | bytes 2097176
  44.8 6.9 %products.1 = (f32[256,1024]{1,0:T(8,128)}, f32[256,1024]{1,0:T(8,128)}, f32[24,1024]{1,0:T(8,128)}) custom-call(s32[1]{0:T(128)} %bitcast.me, bf16[536,1024]{1,0:T(8,128)(2,1)} %get-tuple-element.23.genes, bf16[1024,1024]{1,0:T(8,128)(2,1)} %bitcast.19, f32[512,128]{1,0:T(8,128)} %pair_fit.1.coef), custom_call_target="tpu_custom_call" | custom-call | tf_op jit(solution)/shard_map/products/pallas_call | solution.py:273
  51.7 1.3 %convert_element_type.13 = f16[256,1024]{1,0:T(8,128)(2,1)S(1)} convert(f32[256,1024]{1,0:T(8,128)} %get-tuple-element.31) | non-fusion elementwise | flops 262144 | bytes 1572864 | tf_op jit(solution)/shard_map/convert_element_type | solution.py:383
  53.0 2.7 %collective-permute-start.6 = (f16[256,1024]{1,0:T(8,128)(2,1)S(1)}, f16[256,1024]{1,0:T(8,128)(2,1)S(1)}, u32[]{:S(2)}, u32[]{:S(2)}) collective-permute-start(f16[256,1024]{1,0:T(8,128)(2,1)S(1)} %convert_element_type.13), channel_id=1, source_target_pairs={{0,2},{2,0},{1,3},{3,1},{4,6},{6,4},{5,7},{7,5},{8,10},{10,8},{9,1... | collective-permute-start | bytes 1572872 | tf_op jit(solution)/shard_map/ppermute | solution.py:346
  55.7 0.3 collective-permute-start.5
  56.0 2.6 %collective-permute-start.4 = (f32[32,640]{1,0:T(8,128)S(1)}, f32[32,640]{1,0:T(8,128)S(1)}, u32[]{:S(2)}, u32[]{:S(2)}) collective-permute-start(f32[32,640]{1,0:T(8,128)S(1)} %copy-done.2), channel_id=1, source_target_pairs={{0,2},{2,0},{1,3},{3,1},{4,6},{6,4},{5,7},{7,5},{8,10},{10,8},{9,1... | collective-permute-start | bytes 245768 | tf_op jit(solution)/shard_map/ppermute | solution.py:346
  58.6 27.8 %collective-permute-done.4.refs_1_ = f32[32,640]{1,0:T(8,128)S(1)} collective-permute-done((f32[32,640]{1,0:T(8,128)S(1)}, f32[32,640]{1,0:T(8,128)S(1)}, u32[]{:S(2)}, u32[]{:S(2)}) %collective-permute-start.4) | collective-permute-done | bytes 81952 | tf_op jit(solution)/shard_map/ppermute | solution.py:346
  86.4 0.6 copy-done.5
  87.1 3.8 %cohort_fit.1 = (f32[512,128]{1,0:T(8,128)}, f32[24,128]{1,0:T(8,128)}) custom-call(f32[32,640]{1,0:T(8,128)} %get-tuple-element.25.moment.refs_0_, f32[32,640]{1,0:T(8,128)} %copy-done.5), custom_call_target="tpu_custom_call" | custom-call | tf_op jit(solution)/shard_map/cohort_fit/pallas_call | solution.py:221
  90.9 1.0 dynamic-slice_reduce_fusion.1
  91.9 0.6 copy-done.4
  92.6 4.3 %base_ratio.1 = (f32[256,1024]{1,0:T(8,128)}, f32[8,1024]{1,0:T(8,128)}) custom-call(s32[1]{0:T(128)} %bitcast.me, f32[256,1024]{1,0:T(8,128)} %get-tuple-element.26.own, f32[512,128]{1,0:T(8,128)} %get-tuple-element.27.coef, f32[24,128]{1,0:T(8,128)} %get-tuple-element.28.inverse, f32[24,1024]{1,0:T(8,128)} %get-tuple-element.29.refs_0_, f32[24,1024]{1,0:T(8,128)} %copy-done.4), custom_call_target="tpu_custom_call" | custom-call | tf_op jit(solution)/shard_map/base_ratio/pallas_call | solution.py:320
  96.9 0.8 slice.11
  97.7 1.9 %multiply_bitcast_fusion = (f32[128,1,1024]{2,0,1:T(8,128)S(1)}, f32[128,1024]{1,0:T(8,128)S(1)}) fusion(f32[256,1024]{1,0:T(8,128)} %get-tuple-element.30, s32[]{:T(128)S(6)} %select_n.27, f32[1024]{0:T(1024)S(1)} %bitcast.28, f32[128]{0:T(128)S(1)} %get-tuple-element.33, f16[256,1024]{1,0:T(8,128)(2,1)S(1)} %collective-permute-done.6, ...), kind=kLoop, calls=%fused_computation.3 | loop fusion | flops 2097152 | bytes 2626568 | tf_op jit(solution)/shard_map/stack | solution.py:404
  99.5 0.2 collective-permute-start.7
  99.8 13.2 %collective-permute-done.7 = f32[128,1024]{1,0:T(8,128)S(1)} collective-permute-done((f32[128,1024]{1,0:T(8,128)S(1)}, f32[128,1024]{1,0:T(8,128)S(1)}, u32[]{:S(2)}, u32[]{:S(2)}) %collective-permute-start.7) | collective-permute-done | bytes 524320 | tf_op jit(solution)/shard_map/ppermute | solution.py:346
  113.1 0.3 copy.9
  113.4 1.3 %copy.10 = f32[128,4,2,256]{3,2,1,0:T(2,128)} copy(f32[128,4,2,256]{0,3,2,1:T(8,128)S(1)} %bitcast.20) | data formatting | bytes 2097152 | tf_op jit(solution)/shard_map/jit(_where)/select_n | solution.py:404
  (22 shorter events, 0.5 us)
Async XLA Ops:
  2.6 9.6 %collective-permute-start = (bf16[536,128]{1,0:T(8,128)(2,1)S(1)}, bf16[536,128]{1,0:T(8,128)(2,1)S(1)}, u32[]{:S(2)}, u32[]{:S(2)}) collective-permute-start(bf16[536,128]{1,0:T(8,128)(2,1)S(1)} %maximum_maximum_fusion), channel_id=1, source_target_pairs={{0,1},{1,0},{4,5},{5,4},{8,9},{9,8},{12,13},{13,12},{2,3},{3,2},{6... | collective-permute-start | bytes 411656 | tf_op jit(solution)/shard_map/ppermute | solution.py:346
  5.7 8.0 %collective-permute-start.1 = (bf16[536,128]{1,0:T(8,128)(2,1)S(1)}, bf16[536,128]{1,0:T(8,128)(2,1)S(1)}, u32[]{:S(2)}, u32[]{:S(2)}) collective-permute-start(bf16[536,128]{1,0:T(8,128)(2,1)S(1)} %maximum_maximum_fusion), channel_id=1, source_target_pairs={{0,8},{1,9},{4,12},{5,13},{8,0},{9,1},{12,4},{13,5},{2,10},{3,11},... | collective-permute-start | bytes 411656 | tf_op jit(solution)/shard_map/ppermute | solution.py:346
  7.2 6.5 %collective-permute-start.2 = (bf16[536,128]{1,0:T(8,128)(2,1)S(1)}, bf16[536,128]{1,0:T(8,128)(2,1)S(1)}, u32[]{:S(2)}, u32[]{:S(2)}) collective-permute-start(bf16[536,128]{1,0:T(8,128)(2,1)S(1)} %maximum_maximum_fusion), channel_id=1, source_target_pairs={{0,9},{1,8},{4,13},{5,12},{8,1},{9,0},{12,5},{13,4},{2,11},{3,10},... | collective-permute-start | bytes 411656 | tf_op jit(solution)/shard_map/ppermute | solution.py:346
  13.7 29.7 %all-to-all-start = ((bf16[8,128,1024]{2,1,0:T(8,128)(2,1)}), bf16[8,128,1024]{2,1,0:T(8,128)(2,1)S(1)}, u32[]{:S(2)}, u32[]{:S(2)}) async-start(bf16[8,128,1024]{2,1,0:T(8,128)(2,1)} %smooth.1), calls=%async_computation | async-start | bytes 4194304 | tf_op jit(solution)/shard_map/all_to_all | solution.py:369
  17.4 2.1 %collective-permute-start.3 = (bf16[4,536,128]{2,1,0:T(8,128)(2,1)S(1)}, bf16[4,536,128]{2,1,0:T(8,128)(2,1)S(1)}, u32[]{:S(2)}, u32[]{:S(2)}) collective-permute-start(bf16[4,536,128]{2,1,0:T(8,128)(2,1)S(1)} %pad_maximum_fusion), channel_id=1, source_target_pairs={{0,4},{1,5},{4,0},{5,1},{8,12},{9,13},{12,8},{13,9},{2,6},{3,7},{6... | collective-permute-start | bytes 1646600 | tf_op jit(solution)/shard_map/ppermute | solution.py:346
  19.6 1.0 copy-start.1
  43.4 1.3 %copy-start = (bf16[8,128,1024]{2,1,0:T(8,128)(2,1)}, bf16[8,128,1024]{2,1,0:T(8,128)(2,1)S(1)}, u32[]{:S(2)}) copy-start(bf16[8,128,1024]{2,1,0:T(8,128)(2,1)S(1)} %all-to-all-done) | copy-start | bytes 6291460
  51.7 4.0 %copy-start.3 = (f32[24,1024]{1,0:T(8,128)S(1)}, f32[24,1024]{1,0:T(8,128)}, u32[]{:S(2)}) copy-start(f32[24,1024]{1,0:T(8,128)} %get-tuple-element.29.refs_0_) | copy-start | bytes 294916
  51.7 4.3 %copy-start.2 = (f32[32,640]{1,0:T(8,128)S(1)}, f32[32,640]{1,0:T(8,128)}, u32[]{:S(2)}) copy-start(f32[32,640]{1,0:T(8,128)} %get-tuple-element.25.moment.refs_0_) | copy-start | bytes 245764
  53.0 44.6 %collective-permute-start.6 = (f16[256,1024]{1,0:T(8,128)(2,1)S(1)}, f16[256,1024]{1,0:T(8,128)(2,1)S(1)}, u32[]{:S(2)}, u32[]{:S(2)}) collective-permute-start(f16[256,1024]{1,0:T(8,128)(2,1)S(1)} %convert_element_type.13), channel_id=1, source_target_pairs={{0,2},{2,0},{1,3},{3,1},{4,6},{6,4},{5,7},{7,5},{8,10},{10,8},{9,1... | collective-permute-start | bytes 1572872 | tf_op jit(solution)/shard_map/ppermute | solution.py:346
  55.7 36.2 %collective-permute-start.5 = (f32[24,1024]{1,0:T(8,128)S(1)}, f32[24,1024]{1,0:T(8,128)S(1)}, u32[]{:S(2)}, u32[]{:S(2)}) collective-permute-start(f32[24,1024]{1,0:T(8,128)S(1)} %copy-done.3), channel_id=1, source_target_pairs={{0,2},{2,0},{1,3},{3,1},{4,6},{6,4},{5,7},{7,5},{8,10},{10,8},{9,1... | collective-permute-start | bytes 294920 | tf_op jit(solution)/shard_map/ppermute | solution.py:346
  56.0 30.4 %collective-permute-start.4 = (f32[32,640]{1,0:T(8,128)S(1)}, f32[32,640]{1,0:T(8,128)S(1)}, u32[]{:S(2)}, u32[]{:S(2)}) collective-permute-start(f32[32,640]{1,0:T(8,128)S(1)} %copy-done.2), channel_id=1, source_target_pairs={{0,2},{2,0},{1,3},{3,1},{4,6},{6,4},{5,7},{7,5},{8,10},{10,8},{9,1... | collective-permute-start | bytes 245768 | tf_op jit(solution)/shard_map/ppermute | solution.py:346
  86.4 0.6 copy-start.5
  91.9 0.6 copy-start.4
  99.5 13.5 %collective-permute-start.7 = (f32[128,1024]{1,0:T(8,128)S(1)}, f32[128,1024]{1,0:T(8,128)S(1)}, u32[]{:S(2)}, u32[]{:S(2)}) collective-permute-start(f32[128,1024]{1,0:T(8,128)S(1)} %get-tuple-element.36), channel_id=1, source_target_pairs={{0,1},{1,0},{2,3},{3,2},{4,5},{5,4},{6,7},{7,6},{8,9},{9,8},{10,11... | collective-permute-start | bytes 1572872 | tf_op jit(solution)/shard_map/ppermute | solution.py:346

commit v4 on v3

--- a/solution.py
+++ b/solution.py
@@ -20,6 +20,7 @@
 HIGHEST = lax.Precision.HIGHEST
 VMEM_LIMIT = 56 * 2**20
 SQUARE_ROW = 20
+CHUNKS = 2
 SCALE_LANE = DPAD
 STRIDE = 32
 
@@ -38,10 +39,9 @@
     return table.reshape(plane, plane).astype(ml_dtypes.bfloat16)
 
 
-def row_order(maps, planes):
-    rows = SUBJ_TILE * maps * planes
-    source = np.arange(rows).reshape(SUBJ_TILE, maps * planes).T.reshape(-1)
-    return np.eye(rows, dtype=np.float32)[source].astype(ml_dtypes.bfloat16)
+def row_order(rows, picked, planes):
+    source = [s * rows + m * planes + x for m in picked for x in range(planes) for s in range(SUBJ_TILE)]
+    return np.eye(SUBJ_TILE * rows, dtype=np.float32)[source].astype(ml_dtypes.bfloat16)
 
 
 def tree_sum(terms):
@@ -54,57 +54,63 @@
     return pltpu.CompilerParams(vmem_limit_bytes=VMEM_LIMIT)
 
 
-def smooth_kernel(group, planes, per_vox, parts, width, images, order, table, out):
+def smooth_kernel(groups, planes, per_vox, parts, width, chunks, images, order, table, out):
     plane = table.shape[0]
-    subjects = images.shape[0]
-    groups = images.shape[1] // (group * planes)
+    size = out.shape[2]
     near = kernel_table(2 * REACH + 1)[REACH]
-    for tile in range(subjects // SUBJ_TILE):
+    for tile in range(images.shape[0] // SUBJ_TILE):
         here = pl.ds(tile * SUBJ_TILE, SUBJ_TILE)
-        for part in range(groups):
-            rows = images[here, part * group * planes : (part + 1) * group * planes, :]
-            rows = rows.reshape(SUBJ_TILE * group * planes, plane)
+        for start, stop, maps in groups:
+            rows = images[here, start:stop, :].reshape(SUBJ_TILE * (stop - start), plane)
             rows = jnp.dot(order[...], rows, preferred_element_type=jnp.float32)
             inplane = jnp.dot(
                 rows.astype(jnp.bfloat16), table[...], preferred_element_type=jnp.float32
             )
-            for m in range(group):
+            for i, m in enumerate(maps):
                 slabs = [
-                    inplane[(m * planes + x) * SUBJ_TILE : (m * planes + x + 1) * SUBJ_TILE]
+                    inplane[(i * planes + x) * SUBJ_TILE : (i * planes + x + 1) * SUBJ_TILE]
                     for x in range(planes)
                 ]
                 for x in range(planes):
                     total = slabs[x] * float(near[REACH])
                     for lag in range(1, REACH + 1):
-                        sides = [slabs[i] for i in (x - lag, x + lag) if 0 <= i < planes]
+                        sides = [slabs[k] for k in (x - lag, x + lag) if 0 <= k < planes]
                         if sides:
                             total = total + functools.reduce(jnp.add, sides) * float(
                                 near[REACH + lag]
                             )
-                    column = ((part * group + m) * per_vox + x % per_vox) * plane
+                    column = (m * per_vox + x % per_vox) * plane
                     target = (x // per_vox) * parts + column // width
-                    first = column % width
+                    first = column % size
                     out[target, here, first : first + plane] = total.astype(jnp.bfloat16)
 
 
-def smooth(images, n_vox, parts):
+def smooth(images, n_vox, parts, chunk, chunks):
     subjects, maps, planes, plane = images.shape
     per_vox = planes // n_vox
     width = maps * per_vox * plane // parts
-    group = max(1, min(maps, 256 // (SUBJ_TILE * planes)))
+    size = width // chunks
+    assert size % (per_vox * plane) == 0
+    picked = [m for m in range(maps) if m * per_vox * plane % width // size == chunk]
+    if SUBJ_TILE * planes * len(picked) <= 256:
+        groups = [(0, maps * planes, picked)]
+        order = row_order(maps * planes, picked, planes)
+    else:
+        groups = [(m * planes, (m + 1) * planes, [m]) for m in picked]
+        order = row_order(planes, [0], planes)
     step = 32
-    order = jnp.asarray(row_order(group, planes))
+    order = jnp.asarray(order)
     table = jnp.asarray(plane_kernel(plane))
     return pl.pallas_call(
-        functools.partial(smooth_kernel, group, planes, per_vox, parts, width),
-        out_shape=jax.ShapeDtypeStruct((n_vox * parts, subjects, width), jnp.bfloat16),
+        functools.partial(smooth_kernel, groups, planes, per_vox, parts, width, chunks),
+        out_shape=jax.ShapeDtypeStruct((n_vox * parts, subjects, size), jnp.bfloat16),
         grid=(subjects // step,),
         in_specs=[
             pl.BlockSpec((step, maps * planes, plane), lambda i: (i, 0, 0)),
             pl.BlockSpec(order.shape, lambda i: (0, 0)),
             pl.BlockSpec(table.shape, lambda i: (0, 0)),
         ],
-        out_specs=pl.BlockSpec((n_vox * parts, step, width), lambda i: (0, i, 0)),
+        out_specs=pl.BlockSpec((n_vox * parts, step, size), lambda i: (0, i, 0)),
         compiler_params=params(),
         name="smooth",
     )(images.reshape(subjects, maps * planes, plane), order, table)
@@ -364,32 +370,37 @@
     other = n_near
     offsets = [o for o in range(count) if not o & other]
     blocks = [tall] + [permute_xor(tall, ("vox", "near"), o) for o in offsets[1:]]
-    smoothed = smooth(images, n_vox, n_near)
+    smoothed = smooth(images, n_vox, n_near, 0, CHUNKS)
     smoothed, *blocks = lax.optimization_barrier((smoothed, *blocks))
-    columns = lax.all_to_all(smoothed, ("vox", "near"), 0, 0, tiled=True)
-    columns = columns.reshape(here, columns.shape[2])
+
+    def exchange(value):
+        value = lax.all_to_all(value, ("vox", "near"), 0, 0, tiled=True)
+        return value.reshape(here, value.shape[2])
+
+    columns = [exchange(smoothed)]
     blocks = jnp.stack(blocks)
     blocks = jnp.concatenate([blocks, permute_xor(blocks, ("vox", "near"), other)], axis=0)
     order = offsets + [o | other for o in offsets]
     slots = tuple(order.index(o) for o in range(count))
-
     genes, moment = moments(blocks, slots, (vox * n_near + near)[None])
     pair_coef = pair_fit(moment, snps, design)
     moment_parts = [moment] + [permute_xor(moment, "far", j) for j in range(1, n_far)]
-
-    own, *pieces, stats = products(genes, columns, pair_coef, far[None], n_far)
-    stat_parts = [stats] + [permute_xor(stats, "far", j) for j in range(1, n_far)]
-    pieces = [
-        permute_xor(pieces[j - 1].astype(jnp.float16), "far", j) for j in range(1, n_far)
-    ]
+    for chunk in range(1, CHUNKS):
+        smoothed = smooth(images, n_vox, n_near, chunk, CHUNKS)
+        smoothed, columns[-1], pair_coef, *moment_parts = lax.optimization_barrier(
+            (smoothed, columns[-1], pair_coef, *moment_parts)
+        )
+        columns.append(exchange(smoothed))
     coef, inverse = cohort_fit(moment_parts, snps, design)
-    base, factors = base_ratio(far[None], own, coef, inverse, stat_parts, here)
 
     size = snps // n_far
     panel = size // n_near
     freedom = float(here * n_far - design - 1)
 
-    def panel_stats(index):
+    def send(pieces):
+        return [permute_xor(pieces[j - 1], "far", j) for j in range(1, n_far)]
+
+    def panel_stats(index, base, factors, pieces):
         first = index * panel
         line = lax.dynamic_slice_in_dim(coef, far * size + first, panel, 0)
         ratio = lax.dynamic_slice_in_dim(base, first, panel, 0)
@@ -399,10 +410,31 @@
             ratio = ratio + piece.astype(jnp.float32) * weight
         return ratio * jnp.sqrt(freedom / (1.0 - ratio * ratio))
 
-    away = permute_xor(panel_stats(jnp.bitwise_xor(near, 1)), "near", 1)
-    home = panel_stats(near)
-    both = jnp.where(near == 0, jnp.stack([home, away], 1), jnp.stack([away, home], 1))
-    return both.reshape(panel, maps, per_vox, plane)
+    owns, received, sums = [], [], []
+    for chunk in range(CHUNKS):
+        own, *pieces, stats = products(genes, columns[chunk], pair_coef, far[None], n_far)
+        pieces = [piece.astype(jnp.float16) for piece in pieces]
+        owns.append(own)
+        sums.append([stats] + [permute_xor(stats, "far", j) for j in range(1, n_far)])
+        if chunk == CHUNKS - 1:
+            sums, pieces = lax.optimization_barrier((sums, pieces))
+        received.append(send(pieces))
+    outs = []
+    gate = None
+    for chunk in range(CHUNKS):
+        base, factors = base_ratio(far[None], owns[chunk], coef, inverse, sums[chunk], here)
+        if gate is not None:
+            base, gate = lax.optimization_barrier((base, gate))
+            outs[-1][0] = gate
+        pieces = received[chunk]
+        gate = panel_stats(jnp.bitwise_xor(near, 1), base, factors, pieces)
+        outs.append([gate, panel_stats(near, base, factors, pieces)])
+    outs = [(permute_xor(away, "near", 1), home) for away, home in outs]
+    outs = [
+        jnp.where(near == 0, jnp.stack([home, away], 1), jnp.stack([away, home], 1))
+        for away, home in outs
+    ]
+    return jnp.stack(outs, axis=2).reshape(panel, maps, per_vox, plane)
 
 
 def solution(mesh):

time: 115 us -> 96.2 us (0.84)
  waiting for transfers between devices: 60.4 us -> 27.5 us
  Pallas kernels: 26.5 us -> 34.8 us
  starting transfers between devices: 14.5 us -> 20.5 us
    ppermute x8 -> x11, waiting for transfers between devices: 44.2 us -> 16.8 us  [permute_xor(): return lax.ppermute(value, axes, [(i, i ^ bits) for i in range(size)])]
    all_to_all x1 -> x2, waiting for transfers between devices: 16.2 us -> 10.7 us  [exchange(): value = lax.all_to_all(value, ('vox', 'near'), 0, 0, tiled=True)]
    pallas_call x1 -> x2, Pallas kernels: 4.92 us -> 10.1 us  [smooth(): pl.pallas_call(functools.partial(smooth_kernel, groups, planes, per_vox,...]
    all_to_all x1 -> x2, starting transfers between devices: 3.6 us -> 7.64 us  [exchange(): value = lax.all_to_all(value, ('vox', 'near'), 0, 0, tiled=True)]
    pallas_call x1 -> x2, Pallas kernels: 6.91 us -> 9.17 us  [products(): pl.pallas_call(functools.partial(products_kernel, float(here)), out_shape...]
    reshape x0 -> x2, local copies, waits for them, and re-layouts: none -> 2.01 us  [on_device(): return jnp.stack(outs, axis=2).reshape(panel, maps, per_vox, plane)]
    ppermute x8 -> x11, starting transfers between devices: 10.9 us -> 12.8 us  [permute_xor(): return lax.ppermute(value, axes, [(i, i ^ bits) for i in range(size)])]
    select_n x2 -> x0, local copies, waits for them, and re-layouts: 1.63 us -> none  [on_device(): jnp.where(near == 0, jnp.stack([home, away], 1), jnp.stack([away, home], 1))]
  transfers between devices with their start and end apart: 9 -> 13, of which waited for: 5 -> 6; matrix products, arithmetic and copies ran while one was open for 2% -> 6% of each run, Pallas kernels for 17% -> 37%
where the time goes in v4:
time: 96.2 us; the launch traced here: 95.4 us
  Pallas kernels  34.8 us (36%)
  waiting for transfers between devices  27.5 us (29%)
  starting transfers between devices  20.5 us (21%)
  local copies, waits for them, and re-layouts  7.77 us (8%)
  other arithmetic  4.58 us (5%)
    ppermute x11, waiting for transfers between devices, permute_xor(): return lax.ppermute(value, axes, [(i, i ^ bits) for i in range(size)])  16.8 us
    ppermute x11, starting transfers between devices, permute_xor(): return lax.ppermute(value, axes, [(i, i ^ bits) for i in range(size)])  12.8 us
    all_to_all x2, waiting for transfers between devices, exchange(): value = lax.all_to_all(value, ('vox', 'near'), 0, 0, tiled=True)  10.7 us
    pallas_call x2, Pallas kernels, smooth(): pl.pallas_call(functools.partial(smooth_kernel, groups, planes, per_vox,...  10.1 us
    pallas_call x2, Pallas kernels, products(): pl.pallas_call(functools.partial(products_kernel, float(here)), out_shape...  9.17 us
    all_to_all x2, starting transfers between devices, exchange(): value = lax.all_to_all(value, ('vox', 'near'), 0, 0, tiled=True)  7.64 us
    pallas_call x2, Pallas kernels, base_ratio(): pl.pallas_call(functools.partial(base_kernel, float(here)), out_shape=(ja...  5.2 us
    pallas_call x1, Pallas kernels, cohort_fit(): pl.pallas_call(functools.partial(cohort_kernel, snps, design), out_shape=...  3.77 us
  transfers between devices with their start and end apart: 13, of which 6 were waited for; matrix products, arithmetic and copies ran while one was open for 6% of the time, Pallas kernels for 37%

profile of v4, /device:TPU:0, one launch (start us, length us, event | category | flops | bytes accessed | tf_op | source)
XLA Modules:
  0.0 95.4 jit_solution(16125016528839114220)
XLA Ops:
  0.0 1.0 %copy.11 = bf16[128,512]{0,1:T(8,128)(2,1)S(1)} copy(bf16[128,512]{1,0:T(8,128)(2,1)} %param.9) | data formatting | bytes 262144 | tf_op args[1]
  1.8 0.8 maximum_maximum_fusion
  2.6 3.1 %collective-permute-start = (bf16[536,128]{1,0:T(8,128)(2,1)S(1)}, bf16[536,128]{1,0:T(8,128)(2,1)S(1)}, u32[]{:S(2)}, u32[]{:S(2)}) collective-permute-start(bf16[536,128]{1,0:T(8,128)(2,1)S(1)} %maximum_maximum_fusion), channel_id=1, source_target_pairs={{0,1},{1,0},{4,5},{5,4},{8,9},{9,8},{12,13},{13,12},{2,3},{3,2},{6... | collective-permute-start | bytes 411656 | tf_op jit(solution)/shard_map/ppermute | solution.py:352
  5.7 1.5 %collective-permute-start.1 = (bf16[536,128]{1,0:T(8,128)(2,1)S(1)}, bf16[536,128]{1,0:T(8,128)(2,1)S(1)}, u32[]{:S(2)}, u32[]{:S(2)}) collective-permute-start(bf16[536,128]{1,0:T(8,128)(2,1)S(1)} %maximum_maximum_fusion), channel_id=1, source_target_pairs={{0,8},{1,9},{4,12},{5,13},{8,0},{9,1},{12,4},{13,5},{2,10},{3,11},... | collective-permute-start | bytes 411656 | tf_op jit(solution)/shard_map/ppermute | solution.py:352
  7.2 5.1 %smooth.2 = bf16[8,128,512]{2,1,0:T(8,128)(2,1)} custom-call(bf16[128,32,256]{2,1,0:T(8,128)(2,1)} %bitcast.27, bf16[256,512]{1,0:T(8,128)(2,1)} %constant.35.clone.order, bf16[256,256]{1,0:T(8,128)(2,1)} %constant.36.clone.table), custom_call_target="tpu_custom_call" | custom-call | tf_op jit(solution)/shard_map/smooth/pallas_call | solution.py:104
  12.3 1.4 %collective-permute-done.1 = bf16[536,128]{1,0:T(8,128)(2,1)S(1)} collective-permute-done((bf16[536,128]{1,0:T(8,128)(2,1)S(1)}, bf16[536,128]{1,0:T(8,128)(2,1)S(1)}, u32[]{:S(2)}, u32[]{:S(2)}) %collective-permute-start.1) | collective-permute-done | bytes 137248 | tf_op jit(solution)/shard_map/ppermute | solution.py:352
  13.7 3.6 %all-to-all-start = ((bf16[8,128,512]{2,1,0:T(8,128)(2,1)}), bf16[8,128,512]{2,1,0:T(8,128)(2,1)S(1)}, u32[]{:S(2)}, u32[]{:S(2)}) async-start(bf16[8,128,512]{2,1,0:T(8,128)(2,1)} %smooth.2), calls=%async_computation | async-start | bytes 2097152 | tf_op jit(solution)/shard_map/all_to_all | solution.py:377
  17.9 1.5 %collective-permute-done.3 = bf16[4,536,128]{2,1,0:T(8,128)(2,1)S(1)} collective-permute-done((bf16[4,536,128]{2,1,0:T(8,128)(2,1)S(1)}, bf16[4,536,128]{2,1,0:T(8,128)(2,1)S(1)}, u32[]{:S(2)}, u32[]{:S(2)}) %collective-permute-start.3) | collective-permute-done | bytes 548896 | tf_op jit(solution)/shard_map/ppermute | solution.py:352
  19.5 1.0 %copy-done.2 = bf16[8,536,128]{2,1,0:T(8,128)(2,1)} copy-done((bf16[8,536,128]{2,1,0:T(8,128)(2,1)}, bf16[8,536,128]{2,1,0:T(8,128)(2,1)S(1)}, u32[]{:S(2)}) %copy-start.2) | copy-done | bytes 1097752
  20.5 2.9 %moments.1 = (bf16[536,1024]{1,0:T(8,128)(2,1)}, f32[32,640]{1,0:T(8,128)}) custom-call(s32[1]{0:T(128)} %bitcast.1.me, bf16[8,536,128]{2,1,0:T(8,128)(2,1)} %copy-done.2), custom_call_target="tpu_custom_call" | custom-call | tf_op jit(solution)/shard_map/moments/pallas_call | solution.py:148
  23.4 2.6 %collective-permute-start.4 = (f32[32,640]{1,0:T(8,128)}, f32[32,640]{1,0:T(8,128)S(1)}, u32[]{:S(2)}, u32[]{:S(2)}) collective-permute-start(f32[32,640]{1,0:T(8,128)} %get-tuple-element.46.moment.refs_0_), channel_id=1, source_target_pairs={{0,2},{2,0},{1,3},{3,1},{4,6},{6,4},{5,7},{7,5},{8,10},{10,8},{9,1... | collective-permute-start | bytes 245768 | tf_op jit(solution)/shard_map/ppermute | solution.py:352
  26.0 5.1 %smooth.3 = bf16[8,128,512]{2,1,0:T(8,128)(2,1)} custom-call(bf16[128,32,256]{2,1,0:T(8,128)(2,1)} %bitcast.28, bf16[256,512]{1,0:T(8,128)(2,1)} %constant.37.clone.order, bf16[256,256]{1,0:T(8,128)(2,1)} %constant.36.clone.table), custom_call_target="tpu_custom_call" | custom-call | tf_op jit(solution)/shard_map/smooth/pallas_call | solution.py:104
  31.1 3.6 %pair_fit.1.coef = f32[512,128]{1,0:T(8,128)} custom-call(f32[32,640]{1,0:T(8,128)} %get-tuple-element.46.moment.refs_0_), custom_call_target="tpu_custom_call" | custom-call | tf_op jit(solution)/shard_map/pair_fit/pallas_call | solution.py:202
  34.7 4.1 %all-to-all-start.1 = ((bf16[8,128,512]{2,1,0:T(8,128)(2,1)}), bf16[8,128,512]{2,1,0:T(8,128)(2,1)S(1)}, u32[]{:S(2)}, u32[]{:S(2)}) async-start(bf16[8,128,512]{2,1,0:T(8,128)(2,1)} %smooth.3), calls=%async_computation.1 | async-start | bytes 2097152 | tf_op jit(solution)/shard_map/all_to_all | solution.py:377
  38.8 4.6 %products.2 = (f32[256,512]{1,0:T(8,128)}, f32[256,512]{1,0:T(8,128)}, f32[24,512]{1,0:T(8,128)}) custom-call(s32[1]{0:T(128)} %bitcast.me, bf16[536,1024]{1,0:T(8,128)(2,1)} %get-tuple-element.40.genes, bf16[1024,512]{1,0:T(8,128)(2,1)} %bitcast.29, f32[512,128]{1,0:T(8,128)} %pair_fit.1.coef), custom_call_target="tpu_custom_call" | custom-call | tf_op jit(solution)/shard_map/products/pallas_call | solution.py:279
  43.4 1.1 %convert_element_type.23 = f16[256,512]{1,0:T(8,128)(2,1)S(1)} convert(f32[256,512]{1,0:T(8,128)} %get-tuple-element.57) | non-fusion elementwise | flops 131072 | bytes 786432 | tf_op jit(solution)/shard_map/convert_element_type | solution.py:416
  44.9 2.6 %collective-permute-start.5 = (f32[24,512]{1,0:T(8,128)}, f32[24,512]{1,0:T(8,128)S(1)}, u32[]{:S(2)}, u32[]{:S(2)}) collective-permute-start(f32[24,512]{1,0:T(8,128)} %get-tuple-element.54.refs_0_), channel_id=1, source_target_pairs={{0,2},{2,0},{1,3},{3,1},{4,6},{6,4},{5,7},{7,5},{8,10},{10,8},{9,1... | collective-permute-start | bytes 147464 | tf_op jit(solution)/shard_map/ppermute | solution.py:352
  47.5 10.7 %all-to-all-done.1 = bf16[8,128,512]{2,1,0:T(8,128)(2,1)S(1)} async-done(((bf16[8,128,512]{2,1,0:T(8,128)(2,1)}), bf16[8,128,512]{2,1,0:T(8,128)(2,1)S(1)}, u32[]{:S(2)}, u32[]{:S(2)}) %all-to-all-start.1) | async-done | bytes 1048608 | tf_op jit(solution)/shard_map/all_to_all | solution.py:377
  58.1 1.0 %copy-done.1 = bf16[8,128,512]{2,1,0:T(8,128)(2,1)} copy-done((bf16[8,128,512]{2,1,0:T(8,128)(2,1)}, bf16[8,128,512]{2,1,0:T(8,128)(2,1)S(1)}, u32[]{:S(2)}) %copy-start.1) | copy-done | bytes 1048600
  59.1 4.6 %products.3 = (f32[256,512]{1,0:T(8,128)}, f32[256,512]{1,0:T(8,128)}, f32[24,512]{1,0:T(8,128)}) custom-call(s32[1]{0:T(128)} %bitcast.me, bf16[536,1024]{1,0:T(8,128)(2,1)} %get-tuple-element.40.genes, bf16[1024,512]{1,0:T(8,128)(2,1)} %bitcast.30, f32[512,128]{1,0:T(8,128)} %pair_fit.1.coef), custom_call_target="tpu_custom_call" | custom-call | tf_op jit(solution)/shard_map/products/pallas_call | solution.py:279
  63.7 1.1 %convert_element_type.22 = f16[256,512]{1,0:T(8,128)(2,1)S(1)} convert(f32[256,512]{1,0:T(8,128)} %get-tuple-element.53) | non-fusion elementwise | flops 131072 | bytes 786432 | tf_op jit(solution)/shard_map/convert_element_type | solution.py:416
  64.8 4.1 %collective-permute-done.6.refs_1_ = f32[24,512]{1,0:T(8,128)S(1)} collective-permute-done((f32[24,512]{1,0:T(8,128)}, f32[24,512]{1,0:T(8,128)S(1)}, u32[]{:S(2)}, u32[]{:S(2)}) %collective-permute-start.6) | collective-permute-done | bytes 49184 | tf_op jit(solution)/shard_map/ppermute | solution.py:352
  68.9 3.8 %cohort_fit.1 = (f32[512,128]{1,0:T(8,128)}, f32[24,128]{1,0:T(8,128)}) custom-call(f32[32,640]{1,0:T(8,128)} %get-tuple-element.46.moment.refs_0_, f32[32,640]{1,0:T(8,128)} %copy-done.5), custom_call_target="tpu_custom_call" | custom-call | tf_op jit(solution)/shard_map/cohort_fit/pallas_call | solution.py:227
  72.7 1.0 %dynamic-slice_reduce_fusion.1 = (f32[128]{0:T(128)S(1)}, f32[128]{0:T(128)S(1)}) fusion(f32[512,128]{1,0:T(8,128)} %get-tuple-element.48.coef, s32[]{:T(128)S(6)} %select_n.48, s32[]{:T(128)S(6)} %add.56, s32[]{:T(128)S(6)} %select_n.50), kind=kLoop, calls=%fused_computation.10 | loop fusion | bytes 2060 | tf_op jit(solution)/shard_map/slice | solution.py:409
  73.7 2.6 %base_ratio.2 = (f32[256,512]{1,0:T(8,128)}, f32[8,512]{1,0:T(8,128)}) custom-call(s32[1]{0:T(128)} %bitcast.me, f32[256,512]{1,0:T(8,128)} %get-tuple-element.45.own, f32[512,128]{1,0:T(8,128)} %get-tuple-element.48.coef, f32[24,128]{1,0:T(8,128)} %get-tuple-element.49.inverse, f32[24,512]{1,0:T(8,128)} %get-tuple-element.54.refs_0_, f32[24,512]{1,0:T(8,128)} %copy-done.6), custom_call_target="tpu_custom_call" | custom-call | tf_op jit(solution)/shard_map/base_ratio/pallas_call | solution.py:326
  76.4 0.8 slice.17
  77.1 2.6 %base_ratio.3 = (f32[256,512]{1,0:T(8,128)}, f32[8,512]{1,0:T(8,128)}) custom-call(s32[1]{0:T(128)} %bitcast.me, f32[256,512]{1,0:T(8,128)} %get-tuple-element.59.own, f32[512,128]{1,0:T(8,128)} %get-tuple-element.48.coef, f32[24,128]{1,0:T(8,128)} %get-tuple-element.49.inverse, f32[24,512]{1,0:T(8,128)} %get-tuple-element.60.refs_0_, f32[24,512]{1,0:T(8,128)} %copy-done.7), custom_call_target="tpu_custom_call" | custom-call | tf_op jit(solution)/shard_map/base_ratio/pallas_call | solution.py:326
  80.1 1.9 %collective-permute-start.8 = (f32[128,512]{1,0:T(8,128)S(1)}, f32[128,512]{1,0:T(8,128)S(1)}, u32[]{:S(2)}, u32[]{:S(2)}) collective-permute-start(f32[128,512]{1,0:T(8,128)S(1)} %get-tuple-element.63), channel_id=1, source_target_pairs={{0,1},{1,0},{2,3},{3,2},{4,5},{5,4},{6,7},{7,6},{8,9},{9,8},{10,11... | collective-permute-start | bytes 786440 | tf_op jit(solution)/shard_map/ppermute | solution.py:352
  82.0 0.7 slice.19
  83.4 6.1 %collective-permute-done.8 = f32[128,512]{1,0:T(8,128)S(1)} collective-permute-done((f32[128,512]{1,0:T(8,128)S(1)}, f32[128,512]{1,0:T(8,128)S(1)}, u32[]{:S(2)}, u32[]{:S(2)}) %collective-permute-start.8) | collective-permute-done | bytes 262176 | tf_op jit(solution)/shard_map/ppermute | solution.py:352
  89.5 3.7 %collective-permute-done.10 = f32[128,512]{1,0:T(8,128)S(1)} collective-permute-done((f32[128,512]{1,0:T(8,128)S(1)}, f32[128,512]{1,0:T(8,128)S(1)}, u32[]{:S(2)}, u32[]{:S(2)}) %collective-permute-start.10) | collective-permute-done | bytes 262176 | tf_op jit(solution)/shard_map/ppermute | solution.py:352
  94.0 1.3 %copy.12 = f32[128,4,2,256]{3,2,1,0:T(2,128)} copy(f32[128,4,2,256]{3,2,0,1:T(2,128)S(1)} %reshape.135) | data formatting | bytes 2097152 | tf_op jit(solution)/shard_map/reshape | solution.py:437
  (42 shorter events, 3.7 us)
Async XLA Ops:
  2.6 9.7 %collective-permute-start = (bf16[536,128]{1,0:T(8,128)(2,1)S(1)}, bf16[536,128]{1,0:T(8,128)(2,1)S(1)}, u32[]{:S(2)}, u32[]{:S(2)}) collective-permute-start(bf16[536,128]{1,0:T(8,128)(2,1)S(1)} %maximum_maximum_fusion), channel_id=1, source_target_pairs={{0,1},{1,0},{4,5},{5,4},{8,9},{9,8},{12,13},{13,12},{2,3},{3,2},{6... | collective-permute-start | bytes 411656 | tf_op jit(solution)/shard_map/ppermute | solution.py:352
  5.7 8.0 %collective-permute-start.1 = (bf16[536,128]{1,0:T(8,128)(2,1)S(1)}, bf16[536,128]{1,0:T(8,128)(2,1)S(1)}, u32[]{:S(2)}, u32[]{:S(2)}) collective-permute-start(bf16[536,128]{1,0:T(8,128)(2,1)S(1)} %maximum_maximum_fusion), channel_id=1, source_target_pairs={{0,8},{1,9},{4,12},{5,13},{8,0},{9,1},{12,4},{13,5},{2,10},{3,11},... | collective-permute-start | bytes 411656 | tf_op jit(solution)/shard_map/ppermute | solution.py:352
  7.2 6.5 %collective-permute-start.2 = (bf16[536,128]{1,0:T(8,128)(2,1)S(1)}, bf16[536,128]{1,0:T(8,128)(2,1)S(1)}, u32[]{:S(2)}, u32[]{:S(2)}) collective-permute-start(bf16[536,128]{1,0:T(8,128)(2,1)S(1)} %maximum_maximum_fusion), channel_id=1, source_target_pairs={{0,9},{1,8},{4,13},{5,12},{8,1},{9,0},{12,5},{13,4},{2,11},{3,10},... | collective-permute-start | bytes 411656 | tf_op jit(solution)/shard_map/ppermute | solution.py:352
  13.7 21.0 %all-to-all-start = ((bf16[8,128,512]{2,1,0:T(8,128)(2,1)}), bf16[8,128,512]{2,1,0:T(8,128)(2,1)S(1)}, u32[]{:S(2)}, u32[]{:S(2)}) async-start(bf16[8,128,512]{2,1,0:T(8,128)(2,1)} %smooth.2), calls=%async_computation | async-start | bytes 2097152 | tf_op jit(solution)/shard_map/all_to_all | solution.py:377
  17.4 2.0 %collective-permute-start.3 = (bf16[4,536,128]{2,1,0:T(8,128)(2,1)S(1)}, bf16[4,536,128]{2,1,0:T(8,128)(2,1)S(1)}, u32[]{:S(2)}, u32[]{:S(2)}) collective-permute-start(bf16[4,536,128]{2,1,0:T(8,128)(2,1)S(1)} %pad_maximum_fusion.1), channel_id=1, source_target_pairs={{0,4},{1,5},{4,0},{5,1},{8,12},{9,13},{12,8},{13,9},{2,6},{3,7},{6... | collective-permute-start | bytes 1646600 | tf_op jit(solution)/shard_map/ppermute | solution.py:352
  19.5 1.0 %copy-start.2 = (bf16[8,536,128]{2,1,0:T(8,128)(2,1)}, bf16[8,536,128]{2,1,0:T(8,128)(2,1)S(1)}, u32[]{:S(2)}) copy-start(bf16[8,536,128]{2,1,0:T(8,128)(2,1)S(1)} %constant_dynamic-update-slice_fusion.blocks) | copy-start | bytes 3293188
  23.4 11.3 %collective-permute-start.4 = (f32[32,640]{1,0:T(8,128)}, f32[32,640]{1,0:T(8,128)S(1)}, u32[]{:S(2)}, u32[]{:S(2)}) collective-permute-start(f32[32,640]{1,0:T(8,128)} %get-tuple-element.46.moment.refs_0_), channel_id=1, source_target_pairs={{0,2},{2,0},{1,3},{3,1},{4,6},{6,4},{5,7},{7,5},{8,10},{10,8},{9,1... | collective-permute-start | bytes 245768 | tf_op jit(solution)/shard_map/ppermute | solution.py:352
  34.7 8.7 %copy-start.5 = (f32[32,640]{1,0:T(8,128)}, f32[32,640]{1,0:T(8,128)S(1)}, u32[]{:S(2)}) copy-start(f32[32,640]{1,0:T(8,128)S(1)} %collective-permute-done.4.refs_1_) | copy-start | bytes 245764
  34.7 4.1 %copy-start = (bf16[8,128,512]{2,1,0:T(8,128)(2,1)}, bf16[8,128,512]{2,1,0:T(8,128)(2,1)S(1)}, u32[]{:S(2)}) copy-start(bf16[8,128,512]{2,1,0:T(8,128)(2,1)S(1)} %all-to-all-done) | copy-start | bytes 3145732
  34.7 23.4 %all-to-all-start.1 = ((bf16[8,128,512]{2,1,0:T(8,128)(2,1)}), bf16[8,128,512]{2,1,0:T(8,128)(2,1)S(1)}, u32[]{:S(2)}, u32[]{:S(2)}) async-start(bf16[8,128,512]{2,1,0:T(8,128)(2,1)} %smooth.3), calls=%async_computation.1 | async-start | bytes 2097152 | tf_op jit(solution)/shard_map/all_to_all | solution.py:377
  44.5 35.2 %collective-permute-start.7 = (f16[256,512]{1,0:T(8,128)(2,1)S(1)}, f16[256,512]{1,0:T(8,128)(2,1)S(1)}, u32[]{:S(2)}, u32[]{:S(2)}) collective-permute-start(f16[256,512]{1,0:T(8,128)(2,1)S(1)} %convert_element_type.23), channel_id=1, source_target_pairs={{0,2},{2,0},{1,3},{3,1},{4,6},{6,4},{5,7},{7,5},{8,10},{10,8},{9,1... | collective-permute-start | bytes 786440 | tf_op jit(solution)/shard_map/ppermute | solution.py:352
  44.9 19.9 %collective-permute-start.5 = (f32[24,512]{1,0:T(8,128)}, f32[24,512]{1,0:T(8,128)S(1)}, u32[]{:S(2)}, u32[]{:S(2)}) collective-permute-start(f32[24,512]{1,0:T(8,128)} %get-tuple-element.54.refs_0_), channel_id=1, source_target_pairs={{0,2},{2,0},{1,3},{3,1},{4,6},{6,4},{5,7},{7,5},{8,10},{10,8},{9,1... | collective-permute-start | bytes 147464 | tf_op jit(solution)/shard_map/ppermute | solution.py:352
  58.1 1.0 %copy-start.1 = (bf16[8,128,512]{2,1,0:T(8,128)(2,1)}, bf16[8,128,512]{2,1,0:T(8,128)(2,1)S(1)}, u32[]{:S(2)}) copy-start(bf16[8,128,512]{2,1,0:T(8,128)(2,1)S(1)} %all-to-all-done.1) | copy-start | bytes 3145732
  63.7 5.2 %collective-permute-start.6 = (f32[24,512]{1,0:T(8,128)}, f32[24,512]{1,0:T(8,128)S(1)}, u32[]{:S(2)}, u32[]{:S(2)}) collective-permute-start(f32[24,512]{1,0:T(8,128)} %get-tuple-element.60.refs_0_), channel_id=1, source_target_pairs={{0,2},{2,0},{1,3},{3,1},{4,6},{6,4},{5,7},{7,5},{8,10},{10,8},{9,1... | collective-permute-start | bytes 147464 | tf_op jit(solution)/shard_map/ppermute | solution.py:352
  64.8 8.9 %copy-start.6 = (f32[24,512]{1,0:T(8,128)}, f32[24,512]{1,0:T(8,128)S(1)}, u32[]{:S(2)}) copy-start(f32[24,512]{1,0:T(8,128)S(1)} %collective-permute-done.5.refs_1_) | copy-start | bytes 147460
  68.9 8.2 %copy-start.7 = (f32[24,512]{1,0:T(8,128)}, f32[24,512]{1,0:T(8,128)S(1)}, u32[]{:S(2)}) copy-start(f32[24,512]{1,0:T(8,128)S(1)} %collective-permute-done.6.refs_1_) | copy-start | bytes 147460
  68.9 13.8 %collective-permute-start.9 = (f16[256,512]{1,0:T(8,128)(2,1)S(1)}, f16[256,512]{1,0:T(8,128)(2,1)S(1)}, u32[]{:S(2)}, u32[]{:S(2)}) collective-permute-start(f16[256,512]{1,0:T(8,128)(2,1)S(1)} %convert_element_type.22), channel_id=1, source_target_pairs={{0,2},{2,0},{1,3},{3,1},{4,6},{6,4},{5,7},{7,5},{8,10},{10,8},{9,1... | collective-permute-start | bytes 786440 | tf_op jit(solution)/shard_map/ppermute | solution.py:352
  76.4 3.4 %copy-start.4 = (f32[256,512]{1,0:T(8,128)S(1)}, f32[256,512]{1,0:T(8,128)}, u32[]{:S(2)}) copy-start(f32[256,512]{1,0:T(8,128)} %get-tuple-element.56) | copy-start | bytes 1572868
  79.7 3.0 %copy-start.3 = (f32[256,512]{1,0:T(8,128)S(1)}, f32[256,512]{1,0:T(8,128)}, u32[]{:S(2)}) copy-start(f32[256,512]{1,0:T(8,128)} %get-tuple-element.64) | copy-start | bytes 1572868
  80.1 9.3 %collective-permute-start.8 = (f32[128,512]{1,0:T(8,128)S(1)}, f32[128,512]{1,0:T(8,128)S(1)}, u32[]{:S(2)}, u32[]{:S(2)}) collective-permute-start(f32[128,512]{1,0:T(8,128)S(1)} %get-tuple-element.63), channel_id=1, source_target_pairs={{0,1},{1,0},{2,3},{3,2},{4,5},{5,4},{6,7},{7,6},{8,9},{9,8},{10,11... | collective-permute-start | bytes 786440 | tf_op jit(solution)/shard_map/ppermute | solution.py:352
  83.1 10.1 %collective-permute-start.10 = (f32[128,512]{1,0:T(8,128)S(1)}, f32[128,512]{1,0:T(8,128)S(1)}, u32[]{:S(2)}, u32[]{:S(2)}) collective-permute-start(f32[128,512]{1,0:T(8,128)S(1)} %get-tuple-element.72), channel_id=1, source_target_pairs={{0,1},{1,0},{2,3},{3,2},{4,5},{5,4},{6,7},{7,6},{8,9},{9,8},{10,11... | collective-permute-start | bytes 786440 | tf_op jit(solution)/shard_map/ppermute | solution.py:352

commit v5 on v4

--- a/solution.py
+++ b/solution.py
@@ -18,7 +18,8 @@
 LANES = 128
 SUBJ_TILE = 16
 HIGHEST = lax.Precision.HIGHEST
-VMEM_LIMIT = 56 * 2**20
+VMEM_MOST = 56 * 2**20
+VMEM_BASE = 12 * 2**20
 SQUARE_ROW = 20
 CHUNKS = 2
 SCALE_LANE = DPAD
@@ -39,9 +40,10 @@
     return table.reshape(plane, plane).astype(ml_dtypes.bfloat16)
 
 
-def row_order(rows, picked, planes):
-    source = [s * rows + m * planes + x for m in picked for x in range(planes) for s in range(SUBJ_TILE)]
-    return np.eye(SUBJ_TILE * rows, dtype=np.float32)[source].astype(ml_dtypes.bfloat16)
+def row_order(maps, planes):
+    rows = SUBJ_TILE * maps * planes
+    source = np.arange(rows).reshape(SUBJ_TILE, maps * planes).T.reshape(-1)
+    return np.eye(rows, dtype=np.float32)[source].astype(ml_dtypes.bfloat16)
 
 
 def tree_sum(terms):
@@ -50,25 +52,91 @@
     return terms[0]
 
 
-def params():
-    return pltpu.CompilerParams(vmem_limit_bytes=VMEM_LIMIT)
-
-
-def smooth_kernel(groups, planes, per_vox, parts, width, chunks, images, order, table, out):
+RESIDENT = 3 * 2**20
+IN_VMEM = pl.BlockSpec(memory_space=pltpu.VMEM)
+IN_SMEM = pl.BlockSpec(memory_space=pltpu.SMEM)
+
+
+def params(extra=0):
+    return pltpu.CompilerParams(vmem_limit_bytes=min(VMEM_MOST, VMEM_BASE + extra))
+
+
+def size_of(value):
+    return int(np.prod(value.shape)) * jnp.dtype(value.dtype).itemsize
+
+
+def small(shape, dtype):
+    return int(np.prod(shape)) * jnp.dtype(dtype).itemsize <= RESIDENT
+
+
+def keep(value):
+    if small(value.shape, value.dtype):
+        return pltpu.with_memory_space_constraint(value, pltpu.VMEM)
+    return value
+
+
+def result(shape, dtype):
+    if small(shape, dtype):
+        return pltpu.VMEM(shape, dtype)
+    return jax.ShapeDtypeStruct(shape, dtype)
+
+
+def call(kernel, name, outs, scalars, arrays, scratch=()):
+    many = isinstance(outs, tuple)
+    sizes = [size_of(value) for value in (*arrays, *(outs if many else (outs,)))]
+    extra = 3 * sum(size for size in sizes if size > RESIDENT)
+    return pl.pallas_call(
+        kernel,
+        out_shape=outs,
+        in_specs=[IN_SMEM] * len(scalars) + [IN_VMEM] * len(arrays),
+        out_specs=(IN_VMEM,) * len(outs) if many else IN_VMEM,
+        scratch_shapes=list(scratch),
+        compiler_params=params(extra),
+        name=name,
+    )(*scalars, *[keep(value) for value in arrays])
+
+
+def tall_kernel(genotypes, codes, covariates, out, rows):
+    snps = genotypes.shape[1]
+    out[:snps, :] = jnp.transpose(genotypes[...])
+    count = covariates.shape[0]
+    site = lax.broadcasted_iota(jnp.int32, (SITES, codes.shape[1]), 0)
+    rows[...] = jnp.zeros(rows.shape, jnp.float32)
+    rows[:SITES, :] = (site == codes[...]).astype(jnp.float32)
+    rows[SITES : SITES + count, :] = covariates[...].astype(jnp.float32)
+    out[snps:, :] = rows[...].astype(jnp.bfloat16)
+
+
+def tall_design(genotypes, covariates, site_codes):
+    subjects, snps = genotypes.shape
+    return pl.pallas_call(
+        tall_kernel,
+        out_shape=result((snps + DPAD, subjects), jnp.bfloat16),
+        in_specs=[IN_VMEM] * 3,
+        out_specs=IN_VMEM,
+        scratch_shapes=[pltpu.VMEM((DPAD, subjects), jnp.float32)],
+        compiler_params=params(),
+        name="tall_design",
+    )(genotypes, site_codes[None, :], covariates.T)
+
+
+def smooth_kernel(group, planes, per_vox, parts, width, images, order, table, *outs):
     plane = table.shape[0]
-    size = out.shape[2]
+    size = width // len(outs)
+    groups = images.shape[1] // (group * planes)
     near = kernel_table(2 * REACH + 1)[REACH]
     for tile in range(images.shape[0] // SUBJ_TILE):
         here = pl.ds(tile * SUBJ_TILE, SUBJ_TILE)
-        for start, stop, maps in groups:
-            rows = images[here, start:stop, :].reshape(SUBJ_TILE * (stop - start), plane)
+        for part in range(groups):
+            rows = images[here, part * group * planes : (part + 1) * group * planes, :]
+            rows = rows.reshape(SUBJ_TILE * group * planes, plane)
             rows = jnp.dot(order[...], rows, preferred_element_type=jnp.float32)
             inplane = jnp.dot(
                 rows.astype(jnp.bfloat16), table[...], preferred_element_type=jnp.float32
             )
-            for i, m in enumerate(maps):
+            for m in range(group):
                 slabs = [
-                    inplane[(i * planes + x) * SUBJ_TILE : (i * planes + x + 1) * SUBJ_TILE]
+                    inplane[(m * planes + x) * SUBJ_TILE : (m * planes + x + 1) * SUBJ_TILE]
                     for x in range(planes)
                 ]
                 for x in range(planes):
@@ -79,51 +147,48 @@
                             total = total + functools.reduce(jnp.add, sides) * float(
                                 near[REACH + lag]
                             )
-                    column = (m * per_vox + x % per_vox) * plane
+                    column = ((part * group + m) * per_vox + x % per_vox) * plane
                     target = (x // per_vox) * parts + column // width
-                    first = column % size
+                    chunk, first = column % width // size, column % size
+                    out = outs[chunk]
                     out[target, here, first : first + plane] = total.astype(jnp.bfloat16)
 
 
-def smooth(images, n_vox, parts, chunk, chunks):
+def smooth(images, n_vox, parts, chunks):
     subjects, maps, planes, plane = images.shape
     per_vox = planes // n_vox
     width = maps * per_vox * plane // parts
     size = width // chunks
-    assert size % (per_vox * plane) == 0
-    picked = [m for m in range(maps) if m * per_vox * plane % width // size == chunk]
-    if SUBJ_TILE * planes * len(picked) <= 256:
-        groups = [(0, maps * planes, picked)]
-        order = row_order(maps * planes, picked, planes)
-    else:
-        groups = [(m * planes, (m + 1) * planes, [m]) for m in picked]
-        order = row_order(planes, [0], planes)
+    assert size % plane == 0
+    group = max(1, min(maps, 256 // (SUBJ_TILE * planes)))
     step = 32
-    order = jnp.asarray(order)
+    order = jnp.asarray(row_order(group, planes))
     table = jnp.asarray(plane_kernel(plane))
     return pl.pallas_call(
-        functools.partial(smooth_kernel, groups, planes, per_vox, parts, width, chunks),
-        out_shape=jax.ShapeDtypeStruct((n_vox * parts, subjects, size), jnp.bfloat16),
+        functools.partial(smooth_kernel, group, planes, per_vox, parts, width),
+        out_shape=[jax.ShapeDtypeStruct((n_vox * parts, subjects, size), jnp.bfloat16)] * chunks,
         grid=(subjects // step,),
         in_specs=[
             pl.BlockSpec((step, maps * planes, plane), lambda i: (i, 0, 0)),
             pl.BlockSpec(order.shape, lambda i: (0, 0)),
             pl.BlockSpec(table.shape, lambda i: (0, 0)),
         ],
-        out_specs=pl.BlockSpec((n_vox * parts, step, size), lambda i: (0, i, 0)),
-        compiler_params=params(),
+        out_specs=[pl.BlockSpec((n_vox * parts, step, size), lambda i: (0, i, 0))] * chunks,
+        compiler_params=params(VMEM_MOST),
         name="smooth",
     )(images.reshape(subjects, maps * planes, plane), order, table)
 
 
-def moments_kernel(snps, slots, me, blocks, joined, out):
+def moments_kernel(snps, slots, me, blocks, others, joined, out):
     rows = []
+    half = len(slots) // 2
     for source in range(len(slots)):
         offset = jnp.bitwise_xor(me[0], source)
         index = 0
         for place, slot in enumerate(slots):
             index = index + jnp.where(offset == place, slot, 0)
-        rows.append(blocks[index])
+        place = lax.rem(index, half)
+        rows.append(jnp.where(index < half, blocks[place], others[place]))
     rows = jnp.concatenate(rows, axis=1)
     joined[...] = rows
     across = (((1,), (1,)), ((), ()))
@@ -141,23 +206,16 @@
     out[DPAD:, :snps] = squares
 
 
-def moments(blocks, slots, me):
+def moments(blocks, others, slots, me):
     count, rows, subjects = blocks.shape
     snps = rows - DPAD
     spread = -(-rows // LANES) * LANES
-    return pl.pallas_call(
-        functools.partial(moments_kernel, snps, slots),
-        out_shape=(
-            jax.ShapeDtypeStruct((rows, count * subjects), blocks.dtype),
-            jax.ShapeDtypeStruct((DPAD + 8, spread), jnp.float32),
-        ),
-        in_specs=[
-            pl.BlockSpec(memory_space=pltpu.SMEM),
-            pl.BlockSpec(memory_space=pltpu.VMEM),
-        ],
-        compiler_params=params(),
-        name="moments",
-    )(me, blocks)
+    outs = (
+        result((rows, 2 * count * subjects), blocks.dtype),
+        result((DPAD + 8, spread), jnp.float32),
+    )
+    kernel = functools.partial(moments_kernel, snps, slots)
+    return call(kernel, "moments", outs, [me], [blocks, others])
 
 
 def eliminate(total, snps, design, guard):
@@ -199,13 +257,9 @@
 
 
 def pair_fit(moment, snps, design):
-    return pl.pallas_call(
-        functools.partial(pair_kernel, snps, design),
-        out_shape=jax.ShapeDtypeStruct((snps, LANES), jnp.float32),
-        scratch_shapes=[pltpu.VMEM((LANES, snps), jnp.float32)],
-        compiler_params=params(),
-        name="pair_fit",
-    )(moment)
+    kernel = functools.partial(pair_kernel, snps, design)
+    scratch = [pltpu.VMEM((LANES, snps), jnp.float32)]
+    return call(kernel, "pair_fit", result((snps, LANES), jnp.float32), [], [moment], scratch)
 
 
 def cohort_kernel(snps, design, *refs):
@@ -224,16 +278,10 @@
 
 
 def cohort_fit(parts, snps, design):
-    return pl.pallas_call(
-        functools.partial(cohort_kernel, snps, design),
-        out_shape=(
-            jax.ShapeDtypeStruct((snps, LANES), jnp.float32),
-            jax.ShapeDtypeStruct((DPAD, LANES), jnp.float32),
-        ),
-        scratch_shapes=[pltpu.VMEM((LANES, snps), jnp.float32)],
-        compiler_params=params(),
-        name="cohort_fit",
-    )(*parts)
+    kernel = functools.partial(cohort_kernel, snps, design)
+    outs = (result((snps, LANES), jnp.float32), result((DPAD, LANES), jnp.float32))
+    scratch = [pltpu.VMEM((LANES, snps), jnp.float32)]
+    return call(kernel, "cohort_fit", outs, [], parts, scratch)
 
 
 def column_norm(sums, here):
@@ -272,25 +320,11 @@
     rows, here = genes.shape
     snps = rows - DPAD
     width = columns.shape[1]
-    lanes = min(width, 256)
-    size = snps // count
-    piece = jax.ShapeDtypeStruct((size, width), jnp.float32)
-    piece_spec = pl.BlockSpec((size, lanes), lambda j: (0, j))
-    return pl.pallas_call(
-        functools.partial(products_kernel, float(here)),
-        out_shape=(piece,) * count + (jax.ShapeDtypeStruct((DPAD, width), jnp.float32),),
-        grid=(width // lanes,),
-        in_specs=[
-            pl.BlockSpec(memory_space=pltpu.SMEM),
-            pl.BlockSpec((rows, here), lambda j: (0, 0)),
-            pl.BlockSpec((here, lanes), lambda j: (0, j)),
-            pl.BlockSpec((snps, LANES), lambda j: (0, 0)),
-        ],
-        out_specs=(piece_spec,) * count + (pl.BlockSpec((DPAD, lanes), lambda j: (0, j)),),
-        scratch_shapes=[pltpu.VMEM((snps, lanes), jnp.float32)],
-        compiler_params=params(),
-        name="products",
-    )(me, genes, columns, coef)
+    outs = (result((snps // count, width), jnp.float32),) * count
+    outs += (result((DPAD, width), jnp.float32),)
+    kernel = functools.partial(products_kernel, float(here))
+    scratch = [pltpu.VMEM((snps, width), jnp.float32)]
+    return call(kernel, "products", outs, [me], [genes, columns, coef], scratch)
 
 
 def base_kernel(here, me, own, coef, inverse, *refs):
@@ -320,31 +354,10 @@
 
 def base_ratio(me, own, coef, inverse, parts, here):
     size, width = own.shape
-    lanes = min(width, 256)
-    snps = coef.shape[0]
-    stat_spec = pl.BlockSpec((DPAD, lanes), lambda j: (0, j))
-    return pl.pallas_call(
-        functools.partial(base_kernel, float(here)),
-        out_shape=(
-            jax.ShapeDtypeStruct((size, width), jnp.float32),
-            jax.ShapeDtypeStruct((8, width), jnp.float32),
-        ),
-        grid=(width // lanes,),
-        in_specs=[
-            pl.BlockSpec(memory_space=pltpu.SMEM),
-            pl.BlockSpec((size, lanes), lambda j: (0, j)),
-            pl.BlockSpec((snps, LANES), lambda j: (0, 0)),
-            pl.BlockSpec((DPAD, LANES), lambda j: (0, 0)),
-        ]
-        + [stat_spec] * len(parts),
-        out_specs=(
-            pl.BlockSpec((size, lanes), lambda j: (0, j)),
-            pl.BlockSpec((8, lanes), lambda j: (0, j)),
-        ),
-        scratch_shapes=[pltpu.VMEM((LANES, lanes), jnp.float32)],
-        compiler_params=params(),
-        name="base_ratio",
-    )(me, own, coef, inverse, *parts)
+    outs = (result((size, width), jnp.float32), result((8, width), jnp.float32))
+    kernel = functools.partial(base_kernel, float(here))
+    scratch = [pltpu.VMEM((LANES, width), jnp.float32)]
+    return call(kernel, "base_ratio", outs, [me], [own, coef, inverse, *parts], scratch)
 
 
 def permute_xor(value, axes, bits):
@@ -362,36 +375,32 @@
     count = n_vox * n_near
     here = count * subjects
 
-    one_hot = (jnp.arange(SITES)[:, None] == site_codes[None, :]).astype(jnp.bfloat16)
-    tall = jnp.concatenate(
-        [genotypes.T, one_hot, covariates.T, jnp.zeros((DPAD - design, subjects), jnp.bfloat16)],
-        axis=0,
-    )
+    tall = tall_design(genotypes, covariates, site_codes)
     other = n_near
     offsets = [o for o in range(count) if not o & other]
     blocks = [tall] + [permute_xor(tall, ("vox", "near"), o) for o in offsets[1:]]
-    smoothed = smooth(images, n_vox, n_near, 0, CHUNKS)
+    smoothed = smooth(images, n_vox, n_near, CHUNKS)
     smoothed, *blocks = lax.optimization_barrier((smoothed, *blocks))
 
     def exchange(value):
         value = lax.all_to_all(value, ("vox", "near"), 0, 0, tiled=True)
         return value.reshape(here, value.shape[2])
 
-    columns = [exchange(smoothed)]
+    columns = [exchange(smoothed[0])]
     blocks = jnp.stack(blocks)
-    blocks = jnp.concatenate([blocks, permute_xor(blocks, ("vox", "near"), other)], axis=0)
+    others = permute_xor(blocks, ("vox", "near"), other)
     order = offsets + [o | other for o in offsets]
     slots = tuple(order.index(o) for o in range(count))
-    genes, moment = moments(blocks, slots, (vox * n_near + near)[None])
+    genes, moment = moments(blocks, others, slots, (vox * n_near + near)[None])
     pair_coef = pair_fit(moment, snps, design)
     moment_parts = [moment] + [permute_xor(moment, "far", j) for j in range(1, n_far)]
     for chunk in range(1, CHUNKS):
-        smoothed = smooth(images, n_vox, n_near, chunk, CHUNKS)
-        smoothed, columns[-1], pair_coef, *moment_parts = lax.optimization_barrier(
-            (smoothed, columns[-1], pair_coef, *moment_parts)
+        value, columns[-1], pair_coef, moment_parts = lax.optimization_barrier(
+            (smoothed[chunk], columns[-1], pair_coef, moment_parts)
         )
-        columns.append(exchange(smoothed))
+        columns.append(exchange(value))
     coef, inverse = cohort_fit(moment_parts, snps, design)
+    columns[-1], coef, inverse = lax.optimization_barrier((columns[-1], coef, inverse))
 
     size = snps // n_far
     panel = size // n_near

time: 96.2 us -> 91.5 us (0.951)
  Pallas kernels: 34.8 us -> 14.9 us
  waiting for transfers between devices: 27.5 us -> 47.1 us
  other arithmetic: 4.58 us -> 2.7 us
  local copies, waits for them, and re-layouts: 7.77 us -> 6.66 us
  starting transfers between devices: 20.5 us -> 19.4 us
    pallas_call x9, Pallas kernels: 34.8 us -> 14.9 us  [the longest x7 9.89 us: call(): pl.pallas_call(kernel, out_shape=outs, in_specs=[IN_SMEM] * len(scalars)...]
    ppermute x11, waiting for transfers between devices: 16.8 us -> 31.8 us  [permute_xor(): return lax.ppermute(value, axes, [(i, i ^ bits) for i in range(size)])]
    all_to_all x2, waiting for transfers between devices: 10.7 us -> 15.4 us  [exchange(): value = lax.all_to_all(value, ('vox', 'near'), 0, 0, tiled=True)]
    slice x3, local copies, waits for them, and re-layouts: 2.55 us -> 0.19 us  [panel_stats(): weight = line[:, SCALE_LANE + j, None] * factors[None, j]]
    ppermute x11, starting transfers between devices: 12.8 us -> 10.8 us  [permute_xor(): return lax.ppermute(value, axes, [(i, i ^ bits) for i in range(size)])]
    unnamed x21 -> x18, local copies, waits for them, and re-layouts: 3.07 us -> 4.46 us
    convert_element_type x2, other arithmetic: 2.16 us -> 0.81 us  [on_device(): pieces = [piece.astype(jnp.float16) for piece in pieces]]
    another operation x2, other arithmetic: 0.71 us -> 1.67 us  [on_device(): jnp.stack([home, away], 1)]
  transfers between devices with their start and end apart: 13 -> 13, of which waited for: 6 -> 10; matrix products, arithmetic and copies ran while one was open for 6% -> 3% of each run, Pallas kernels for 37% -> 16%
where the time goes in v5:
time: 91.5 us; the launch traced here: 91.1 us
  waiting for transfers between devices  47.1 us (51%)
  starting transfers between devices  19.4 us (21%)
  Pallas kernels  14.9 us (16%)
  local copies, waits for them, and re-layouts  6.66 us (7%)
  other arithmetic  2.7 us (3%)
    ppermute x11, waiting for transfers between devices, permute_xor(): return lax.ppermute(value, axes, [(i, i ^ bits) for i in range(size)])  31.8 us
    all_to_all x2, waiting for transfers between devices, exchange(): value = lax.all_to_all(value, ('vox', 'near'), 0, 0, tiled=True)  15.4 us
    ppermute x11, starting transfers between devices, permute_xor(): return lax.ppermute(value, axes, [(i, i ^ bits) for i in range(size)])  10.8 us
    pallas_call x7, Pallas kernels, call(): pl.pallas_call(kernel, out_shape=outs, in_specs=[IN_SMEM] * len(scalars)...  9.89 us
    all_to_all x2, starting transfers between devices, exchange(): value = lax.all_to_all(value, ('vox', 'near'), 0, 0, tiled=True)  8.58 us
    pallas_call x1, Pallas kernels, smooth(): pl.pallas_call(functools.partial(smooth_kernel, group, planes, per_vox, p...  4.94 us
    unnamed x18, local copies, waits for them, and re-layouts  4.46 us
    reshape x2, local copies, waits for them, and re-layouts, on_device(): return jnp.stack(outs, axis=2).reshape(panel, maps, per_vox, plane)  2.01 us
  transfers between devices with their start and end apart: 13, of which 10 were waited for; matrix products, arithmetic and copies ran while one was open for 3% of the time, Pallas kernels for 16%

profile of v5, /device:TPU:0, one launch (start us, length us, event | category | flops | bytes accessed | tf_op | source)
XLA Modules:
  0.0 91.1 jit_solution(12230306493648319532)
XLA Ops:
  0.0 0.9 copy-done.4
  0.9 0.7 copy-done.7
  1.6 0.7 copy-done.8
  2.3 4.0 %collective-permute-start.2 = (bf16[536,128]{1,0:T(8,128)(2,1)S(1)}, bf16[536,128]{1,0:T(8,128)(2,1)S(1)}, u32[]{:S(2)}, u32[]{:S(2)}) collective-permute-start(bf16[536,128]{1,0:T(8,128)(2,1)S(1)} %tall_design.1), channel_id=1, source_target_pairs={{0,9},{1,8},{4,13},{5,12},{8,1},{9,0},{12,5},{13,4},{2,11},{3,10},... | collective-permute-start | bytes 411656 | tf_op jit(solution)/shard_map/ppermute | solution.py:365
  7.0 4.9 %smooth.1 = (bf16[8,128,512]{2,1,0:T(8,128)(2,1)}, bf16[8,128,512]{2,1,0:T(8,128)(2,1)}) custom-call(bf16[128,32,256]{2,1,0:T(8,128)(2,1)} %bitcast.28, bf16[256,256]{1,0:T(8,128)(2,1)} %constant.31.clone.order, bf16[256,256]{1,0:T(8,128)(2,1)} %constant.32.clone.table), custom_call_target="tpu_custom_call" | custom-call | tf_op jit(solution)/shard_map/smooth/pallas_call | solution.py:167
  12.0 1.0 %collective-permute-done.1 = bf16[536,128]{1,0:T(8,128)(2,1)S(1)} collective-permute-done((bf16[536,128]{1,0:T(8,128)(2,1)S(1)}, bf16[536,128]{1,0:T(8,128)(2,1)S(1)}, u32[]{:S(2)}, u32[]{:S(2)}) %collective-permute-start.1) | collective-permute-done | bytes 137248 | tf_op jit(solution)/shard_map/ppermute | solution.py:365
  13.1 3.6 %all-to-all-start = ((bf16[8,128,512]{2,1,0:T(8,128)(2,1)}), bf16[8,128,512]{2,1,0:T(8,128)(2,1)S(1)}, u32[]{:S(2)}, u32[]{:S(2)}) async-start(bf16[8,128,512]{2,1,0:T(8,128)(2,1)} %get-tuple-element.50), calls=%async_computation | async-start | bytes 2097152 | tf_op jit(solution)/shard_map/all_to_all | solution.py:386
  17.2 1.6 %collective-permute-done.3.others = bf16[4,536,128]{2,1,0:T(8,128)(2,1)S(1)} collective-permute-done((bf16[4,536,128]{2,1,0:T(8,128)(2,1)S(1)}, bf16[4,536,128]{2,1,0:T(8,128)(2,1)S(1)}, u32[]{:S(2)}, u32[]{:S(2)}) %collective-permute-start.3) | collective-permute-done | bytes 548896 | tf_op jit(solution)/shard_map/ppermute | solution.py:365
  18.8 1.1 %moments.1 = (bf16[536,1024]{1,0:T(8,128)(2,1)S(1)}, f32[32,640]{1,0:T(8,128)S(1)}) custom-call(s32[1]{0:T(128)} %bitcast.1.me, bf16[4,536,128]{2,1,0:T(8,128)(2,1)S(1)} %pad_maximum_fusion.1.blocks, bf16[4,536,128]{2,1,0:T(8,128)(2,1)S(1)} %collective-permute-done.3.others), custom_call_target="tpu_custom_call" | custom-call | tf_op jit(solution)/shard_map/moments/pallas_call | solution.py:88
  19.9 2.6 %collective-permute-start.4 = (f32[32,640]{1,0:T(8,128)S(1)}, f32[32,640]{1,0:T(8,128)S(1)}, u32[]{:S(2)}, u32[]{:S(2)}) collective-permute-start(f32[32,640]{1,0:T(8,128)S(1)} %get-tuple-element.56.moment.refs_0_), channel_id=1, source_target_pairs={{0,2},{2,0},{1,3},{3,1},{4,6},{6,4},{5,7},{7,5},{8,10},{10,8},{9,1... | collective-permute-start | bytes 245768 | tf_op jit(solution)/shard_map/ppermute | solution.py:365
  22.5 2.0 %pair_fit.1.coef = f32[512,128]{1,0:T(8,128)S(1)} custom-call(f32[32,640]{1,0:T(8,128)S(1)} %get-tuple-element.56.moment.refs_0_), custom_call_target="tpu_custom_call" | custom-call | tf_op jit(solution)/shard_map/pair_fit/pallas_call | solution.py:88
  24.5 6.2 %collective-permute-done.4.refs_1_ = f32[32,640]{1,0:T(8,128)S(1)} collective-permute-done((f32[32,640]{1,0:T(8,128)S(1)}, f32[32,640]{1,0:T(8,128)S(1)}, u32[]{:S(2)}, u32[]{:S(2)}) %collective-permute-start.4) | collective-permute-done | bytes 81952 | tf_op jit(solution)/shard_map/ppermute | solution.py:365
  30.7 0.6 copy-done.5
  31.3 1.9 %all-to-all-done = bf16[8,128,512]{2,1,0:T(8,128)(2,1)S(1)} async-done(((bf16[8,128,512]{2,1,0:T(8,128)(2,1)}), bf16[8,128,512]{2,1,0:T(8,128)(2,1)S(1)}, u32[]{:S(2)}, u32[]{:S(2)}) %all-to-all-start) | async-done | bytes 1048608 | tf_op jit(solution)/shard_map/all_to_all | solution.py:386
  33.2 5.0 %all-to-all-start.1 = ((bf16[8,128,512]{2,1,0:T(8,128)(2,1)}), bf16[8,128,512]{2,1,0:T(8,128)(2,1)S(1)}, u32[]{:S(2)}, u32[]{:S(2)}) async-start(bf16[8,128,512]{2,1,0:T(8,128)(2,1)} %get-tuple-element.55), calls=%async_computation.1 | async-start | bytes 2097152 | tf_op jit(solution)/shard_map/all_to_all | solution.py:386
  38.3 1.4 %products.2 = (f32[256,512]{1,0:T(8,128)S(1)}, f32[256,512]{1,0:T(8,128)S(1)}, f32[24,512]{1,0:T(8,128)}) custom-call(s32[1]{0:T(128)} %bitcast.me, bf16[536,1024]{1,0:T(8,128)(2,1)S(1)} %get-tuple-element.48.genes, bf16[1024,512]{1,0:T(8,128)(2,1)S(1)} %bitcast.23, f32[512,128]{1,0:T(8,128)S(1)} %pair_fit.1.coef), custom_call_target="tpu_custom_call" | custom-call | tf_op jit(solution)/shard_map/products/pallas_call | solution.py:88
  39.7 0.8 copy-done
  40.5 0.8 convert_element_type.19
  41.2 2.9 %collective-permute-start.5 = (f32[24,512]{1,0:T(8,128)}, f32[24,512]{1,0:T(8,128)S(1)}, u32[]{:S(2)}, u32[]{:S(2)}) collective-permute-start(f32[24,512]{1,0:T(8,128)} %get-tuple-element.66.refs_0_), channel_id=1, source_target_pairs={{0,2},{2,0},{1,3},{3,1},{4,6},{6,4},{5,7},{7,5},{8,10},{10,8},{9,1... | collective-permute-start | bytes 147464 | tf_op jit(solution)/shard_map/ppermute | solution.py:365
  44.2 2.1 %cohort_fit.1 = (f32[512,128]{1,0:T(8,128)S(1)}, f32[24,128]{1,0:T(8,128)S(1)}) custom-call(f32[32,640]{1,0:T(8,128)S(1)} %get-tuple-element.56.moment.refs_0_, f32[32,640]{1,0:T(8,128)S(1)} %copy-done.6), custom_call_target="tpu_custom_call" | custom-call | tf_op jit(solution)/shard_map/cohort_fit/pallas_call | solution.py:88
  46.3 13.4 %all-to-all-done.1 = bf16[8,128,512]{2,1,0:T(8,128)(2,1)S(1)} async-done(((bf16[8,128,512]{2,1,0:T(8,128)(2,1)}), bf16[8,128,512]{2,1,0:T(8,128)(2,1)S(1)}, u32[]{:S(2)}, u32[]{:S(2)}) %all-to-all-start.1) | async-done | bytes 1048608 | tf_op jit(solution)/shard_map/all_to_all | solution.py:386
  59.7 1.3 %products.3 = (f32[256,512]{1,0:T(8,128)S(1)}, f32[256,512]{1,0:T(8,128)S(1)}, f32[24,512]{1,0:T(8,128)S(1)}) custom-call(s32[1]{0:T(128)} %bitcast.me, bf16[536,1024]{1,0:T(8,128)(2,1)S(1)} %get-tuple-element.48.genes, bf16[1024,512]{1,0:T(8,128)(2,1)S(1)} %bitcast.24, f32[512,128]{1,0:T(8,128)S(1)} %pair_fit.1.coef), custom_call_target="tpu_custom_call" | custom-call | tf_op jit(solution)/shard_map/products/pallas_call | solution.py:88
  61.0 0.8 copy-done.2
  61.9 4.9 %collective-permute-done.6.refs_1_ = f32[24,512]{1,0:T(8,128)S(1)} collective-permute-done((f32[24,512]{1,0:T(8,128)S(1)}, f32[24,512]{1,0:T(8,128)S(1)}, u32[]{:S(2)}, u32[]{:S(2)}) %collective-permute-start.6) | collective-permute-done | bytes 49184 | tf_op jit(solution)/shard_map/ppermute | solution.py:365
  67.0 1.4 %base_ratio.2 = (f32[256,512]{1,0:T(8,128)S(1)}, f32[8,512]{1,0:T(8,128)S(1)}) custom-call(s32[1]{0:T(128)} %bitcast.me, f32[256,512]{1,0:T(8,128)S(1)} %copy-done.1, f32[512,128]{1,0:T(8,128)S(1)} %get-tuple-element.60.coef, f32[24,128]{1,0:T(8,128)S(1)} %get-tuple-element.61.inverse, f32[24,512]{1,0:T(8,128)} %get-tuple-element.66.refs_0_, ...), custom_call_target="tpu_custom_call" | custom-call | tf_op jit(solution)/shard_map/base_ratio/pallas_call | solution.py:88
  68.4 0.6 base_ratio.3
  69.0 1.3 %multiply_bitcast_fusion.1 = (f32[128,1,1,512]{3,0,2,1:T(8,128)S(1)}, f32[128,512]{1,0:T(8,128)S(1)}) fusion(f32[256,512]{1,0:T(8,128)S(1)} %get-tuple-element.68, s32[]{:T(128)S(6)} %select_n.47, f32[512]{0:T(512)S(1)} %bitcast.34, f32[128]{0:T(128)S(1)} %get-tuple-element.79, f16[256,512]{1,0:T(8,128)(2,1)} %collective-permute-done.7, ...), kind=kLoop, calls=%fused_computation.7 | loop fusion | flops 1048576 | bytes 1313800 | tf_op jit(solution)/shard_map/stack | solution.py:443
  70.5 8.5 %collective-permute-done.9 = f16[256,512]{1,0:T(8,128)(2,1)S(1)} collective-permute-done((f16[256,512]{1,0:T(8,128)(2,1)S(1)}, f16[256,512]{1,0:T(8,128)(2,1)S(1)}, u32[]{:S(2)}, u32[]{:S(2)}) %collective-permute-start.9) | collective-permute-done | bytes 262176 | tf_op jit(solution)/shard_map/ppermute | solution.py:365
  79.4 5.2 %collective-permute-done.8 = f32[128,512]{1,0:T(8,128)S(1)} collective-permute-done((f32[128,512]{1,0:T(8,128)S(1)}, f32[128,512]{1,0:T(8,128)S(1)}, u32[]{:S(2)}, u32[]{:S(2)}) %collective-permute-start.8) | collective-permute-done | bytes 262176 | tf_op jit(solution)/shard_map/ppermute | solution.py:365
  84.6 4.3 %collective-permute-done.10 = f32[128,512]{1,0:T(8,128)S(1)} collective-permute-done((f32[128,512]{1,0:T(8,128)S(1)}, f32[128,512]{1,0:T(8,128)S(1)}, u32[]{:S(2)}, u32[]{:S(2)}) %collective-permute-start.10) | collective-permute-done | bytes 262176 | tf_op jit(solution)/shard_map/ppermute | solution.py:365
  89.0 0.7 reshape.133
  89.7 1.3 %copy.8 = f32[128,4,2,256]{3,2,1,0:T(2,128)} copy(f32[128,4,2,256]{3,2,0,1:T(2,128)S(1)} %reshape.133) | data formatting | bytes 2097152 | tf_op jit(solution)/shard_map/reshape | solution.py:446
  (34 shorter events, 2.3 us)
Async XLA Ops:
  0.0 0.9 copy-start.4
  0.9 0.7 copy-start.7
  1.6 0.7 copy-start.8
  2.3 9.6 %collective-permute-start.2 = (bf16[536,128]{1,0:T(8,128)(2,1)S(1)}, bf16[536,128]{1,0:T(8,128)(2,1)S(1)}, u32[]{:S(2)}, u32[]{:S(2)}) collective-permute-start(bf16[536,128]{1,0:T(8,128)(2,1)S(1)} %tall_design.1), channel_id=1, source_target_pairs={{0,9},{1,8},{4,13},{5,12},{8,1},{9,0},{12,5},{13,4},{2,11},{3,10},... | collective-permute-start | bytes 411656 | tf_op jit(solution)/shard_map/ppermute | solution.py:365
  6.4 6.6 %collective-permute-start.1 = (bf16[536,128]{1,0:T(8,128)(2,1)S(1)}, bf16[536,128]{1,0:T(8,128)(2,1)S(1)}, u32[]{:S(2)}, u32[]{:S(2)}) collective-permute-start(bf16[536,128]{1,0:T(8,128)(2,1)S(1)} %tall_design.1), channel_id=1, source_target_pairs={{0,8},{1,9},{4,12},{5,13},{8,0},{9,1},{12,4},{13,5},{2,10},{3,11},... | collective-permute-start | bytes 411656 | tf_op jit(solution)/shard_map/ppermute | solution.py:365
  6.9 6.2 %collective-permute-start = (bf16[536,128]{1,0:T(8,128)(2,1)S(1)}, bf16[536,128]{1,0:T(8,128)(2,1)S(1)}, u32[]{:S(2)}, u32[]{:S(2)}) collective-permute-start(bf16[536,128]{1,0:T(8,128)(2,1)S(1)} %tall_design.1), channel_id=1, source_target_pairs={{0,1},{1,0},{4,5},{5,4},{8,9},{9,8},{12,13},{13,12},{2,3},{3,2},{6... | collective-permute-start | bytes 411656 | tf_op jit(solution)/shard_map/ppermute | solution.py:365
  13.1 20.1 %all-to-all-start = ((bf16[8,128,512]{2,1,0:T(8,128)(2,1)}), bf16[8,128,512]{2,1,0:T(8,128)(2,1)S(1)}, u32[]{:S(2)}, u32[]{:S(2)}) async-start(bf16[8,128,512]{2,1,0:T(8,128)(2,1)} %get-tuple-element.50), calls=%async_computation | async-start | bytes 2097152 | tf_op jit(solution)/shard_map/all_to_all | solution.py:386
  16.8 2.0 %collective-permute-start.3 = (bf16[4,536,128]{2,1,0:T(8,128)(2,1)S(1)}, bf16[4,536,128]{2,1,0:T(8,128)(2,1)S(1)}, u32[]{:S(2)}, u32[]{:S(2)}) collective-permute-start(bf16[4,536,128]{2,1,0:T(8,128)(2,1)S(1)} %pad_maximum_fusion.1.blocks), channel_id=1, source_target_pairs={{0,4},{1,5},{4,0},{5,1},{8,12},{9,13},{12,8},{13,9},{2,6},{3,7},{6... | collective-permute-start | bytes 1646600 | tf_op jit(solution)/shard_map/ppermute | solution.py:365
  19.9 10.8 %collective-permute-start.4 = (f32[32,640]{1,0:T(8,128)S(1)}, f32[32,640]{1,0:T(8,128)S(1)}, u32[]{:S(2)}, u32[]{:S(2)}) collective-permute-start(f32[32,640]{1,0:T(8,128)S(1)} %get-tuple-element.56.moment.refs_0_), channel_id=1, source_target_pairs={{0,2},{2,0},{1,3},{3,1},{4,6},{6,4},{5,7},{7,5},{8,10},{10,8},{9,1... | collective-permute-start | bytes 245768 | tf_op jit(solution)/shard_map/ppermute | solution.py:365
  30.7 0.6 copy-start.5
  33.2 26.5 %all-to-all-start.1 = ((bf16[8,128,512]{2,1,0:T(8,128)(2,1)}), bf16[8,128,512]{2,1,0:T(8,128)(2,1)S(1)}, u32[]{:S(2)}, u32[]{:S(2)}) async-start(bf16[8,128,512]{2,1,0:T(8,128)(2,1)} %get-tuple-element.55), calls=%async_computation.1 | async-start | bytes 2097152 | tf_op jit(solution)/shard_map/all_to_all | solution.py:386
  38.3 5.9 %copy-start.6 = (f32[32,640]{1,0:T(8,128)S(1)}, f32[32,640]{1,0:T(8,128)}, u32[]{:S(2)}) copy-start(f32[32,640]{1,0:T(8,128)} %copy-done.5) | copy-start | bytes 245764
  39.7 0.8 copy-start
  40.5 26.5 %copy-start.1 = (f32[256,512]{1,0:T(8,128)S(1)}, f32[256,512]{1,0:T(8,128)}, u32[]{:S(2)}) copy-start(f32[256,512]{1,0:T(8,128)} %copy-done) | copy-start | bytes 1572868
  41.2 27.8 %collective-permute-start.7 = (f16[256,512]{1,0:T(8,128)(2,1)}, f16[256,512]{1,0:T(8,128)(2,1)}, u32[]{:S(2)}, u32[]{:S(2)}) collective-permute-start(f16[256,512]{1,0:T(8,128)(2,1)} %convert_element_type.19), channel_id=1, source_target_pairs={{0,2},{2,0},{1,3},{3,1},{4,6},{6,4},{5,7},{7,5},{8,10},{10,8},{9,1... | collective-permute-start | bytes 786440 | tf_op jit(solution)/shard_map/ppermute | solution.py:365
  41.2 20.6 %collective-permute-start.5 = (f32[24,512]{1,0:T(8,128)}, f32[24,512]{1,0:T(8,128)S(1)}, u32[]{:S(2)}, u32[]{:S(2)}) collective-permute-start(f32[24,512]{1,0:T(8,128)} %get-tuple-element.66.refs_0_), channel_id=1, source_target_pairs={{0,2},{2,0},{1,3},{3,1},{4,6},{6,4},{5,7},{7,5},{8,10},{10,8},{9,1... | collective-permute-start | bytes 147464 | tf_op jit(solution)/shard_map/ppermute | solution.py:365
  61.0 0.8 copy-start.2
  61.8 6.6 %copy-start.3 = (f32[256,512]{1,0:T(8,128)S(1)}, f32[256,512]{1,0:T(8,128)}, u32[]{:S(2)}) copy-start(f32[256,512]{1,0:T(8,128)} %copy-done.2) | copy-start | bytes 1572868
  61.8 5.0 %collective-permute-start.6 = (f32[24,512]{1,0:T(8,128)S(1)}, f32[24,512]{1,0:T(8,128)S(1)}, u32[]{:S(2)}, u32[]{:S(2)}) collective-permute-start(f32[24,512]{1,0:T(8,128)S(1)} %get-tuple-element.72.refs_0_), channel_id=1, source_target_pairs={{0,2},{2,0},{1,3},{3,1},{4,6},{6,4},{5,7},{7,5},{8,10},{10,8},{9,1... | collective-permute-start | bytes 147464 | tf_op jit(solution)/shard_map/ppermute | solution.py:365
  66.8 12.1 %collective-permute-start.9 = (f16[256,512]{1,0:T(8,128)(2,1)S(1)}, f16[256,512]{1,0:T(8,128)(2,1)S(1)}, u32[]{:S(2)}, u32[]{:S(2)}) collective-permute-start(f16[256,512]{1,0:T(8,128)(2,1)S(1)} %convert_element_type.18), channel_id=1, source_target_pairs={{0,2},{2,0},{1,3},{3,1},{4,6},{6,4},{5,7},{7,5},{8,10},{10,8},{9,1... | collective-permute-start | bytes 786440 | tf_op jit(solution)/shard_map/ppermute | solution.py:365
  70.4 14.2 %collective-permute-start.8 = (f32[128,512]{1,0:T(8,128)S(1)}, f32[128,512]{1,0:T(8,128)S(1)}, u32[]{:S(2)}, u32[]{:S(2)}) collective-permute-start(f32[128,512]{1,0:T(8,128)S(1)} %get-tuple-element.75), channel_id=1, source_target_pairs={{0,1},{1,0},{2,3},{3,2},{4,5},{5,4},{6,7},{7,6},{8,9},{9,8},{10,11... | collective-permute-start | bytes 786440 | tf_op jit(solution)/shard_map/ppermute | solution.py:365
  79.3 9.7 %collective-permute-start.10 = (f32[128,512]{1,0:T(8,128)S(1)}, f32[128,512]{1,0:T(8,128)S(1)}, u32[]{:S(2)}, u32[]{:S(2)}) collective-permute-start(f32[128,512]{1,0:T(8,128)S(1)} %get-tuple-element.84), channel_id=1, source_target_pairs={{0,1},{1,0},{2,3},{3,2},{4,5},{5,4},{6,7},{7,6},{8,9},{9,8},{10,11... | collective-permute-start | bytes 786440 | tf_op jit(solution)/shard_map/ppermute | solution.py:365

commit v6 on v5

--- a/solution.py
+++ b/solution.py
@@ -22,6 +22,7 @@
 VMEM_BASE = 12 * 2**20
 SQUARE_ROW = 20
 CHUNKS = 2
+NARROW = 2.0**-4
 SCALE_LANE = DPAD
 STRIDE = 32
 
@@ -81,7 +82,7 @@
     return jax.ShapeDtypeStruct(shape, dtype)
 
 
-def call(kernel, name, outs, scalars, arrays, scratch=()):
+def call(kernel, name, outs, scalars, arrays, scratch=(), moved=0):
     many = isinstance(outs, tuple)
     sizes = [size_of(value) for value in (*arrays, *(outs if many else (outs,)))]
     extra = 3 * sum(size for size in sizes if size > RESIDENT)
@@ -93,7 +94,7 @@
         scratch_shapes=list(scratch),
         compiler_params=params(extra),
         name=name,
-    )(*scalars, *[keep(value) for value in arrays])
+    )(*scalars, *arrays[:moved], *[keep(value) for value in arrays[moved:]])
 
 
 def tall_kernel(genotypes, codes, covariates, out, rows):
@@ -320,7 +321,9 @@
     rows, here = genes.shape
     snps = rows - DPAD
     width = columns.shape[1]
-    outs = (result((snps // count, width), jnp.float32),) * count
+    size = snps // count
+    outs = (jax.ShapeDtypeStruct((size, width), jnp.float32),)
+    outs += (result((size, width), jnp.float32),) * (count - 1)
     outs += (result((DPAD, width), jnp.float32),)
     kernel = functools.partial(products_kernel, float(here))
     scratch = [pltpu.VMEM((snps, width), jnp.float32)]
@@ -357,7 +360,7 @@
     outs = (result((size, width), jnp.float32), result((8, width), jnp.float32))
     kernel = functools.partial(base_kernel, float(here))
     scratch = [pltpu.VMEM((LANES, width), jnp.float32)]
-    return call(kernel, "base_ratio", outs, [me], [own, coef, inverse, *parts], scratch)
+    return call(kernel, "base_ratio", outs, [me], [own, coef, inverse, *parts], scratch, 1)
 
 
 def permute_xor(value, axes, bits):
@@ -375,18 +378,22 @@
     count = n_vox * n_near
     here = count * subjects
 
+    def exchange(value):
+        value = lax.all_to_all(value, ("vox", "near"), 0, 0, tiled=True)
+        return value.reshape(here, value.shape[2])
+
+    smoothed = smooth(images, n_vox, n_near, CHUNKS)
+    smoothed, genotypes = lax.optimization_barrier((smoothed, genotypes))
+    columns = [exchange(smoothed[0])]
     tall = tall_design(genotypes, covariates, site_codes)
     other = n_near
     offsets = [o for o in range(count) if not o & other]
     blocks = [tall] + [permute_xor(tall, ("vox", "near"), o) for o in offsets[1:]]
-    smoothed = smooth(images, n_vox, n_near, CHUNKS)
-    smoothed, *blocks = lax.optimization_barrier((smoothed, *blocks))
-
-    def exchange(value):
-        value = lax.all_to_all(value, ("vox", "near"), 0, 0, tiled=True)
-        return value.reshape(here, value.shape[2])
-
-    columns = [exchange(smoothed[0])]
+    for chunk in range(1, CHUNKS):
+        value, columns[-1], *blocks = lax.optimization_barrier(
+            (smoothed[chunk], columns[-1], *blocks)
+        )
+        columns.append(exchange(value))
     blocks = jnp.stack(blocks)
     others = permute_xor(blocks, ("vox", "near"), other)
     order = offsets + [o | other for o in offsets]
@@ -394,14 +401,6 @@
     genes, moment = moments(blocks, others, slots, (vox * n_near + near)[None])
     pair_coef = pair_fit(moment, snps, design)
     moment_parts = [moment] + [permute_xor(moment, "far", j) for j in range(1, n_far)]
-    for chunk in range(1, CHUNKS):
-        value, columns[-1], pair_coef, moment_parts = lax.optimization_barrier(
-            (smoothed[chunk], columns[-1], pair_coef, moment_parts)
-        )
-        columns.append(exchange(value))
-    coef, inverse = cohort_fit(moment_parts, snps, design)
-    columns[-1], coef, inverse = lax.optimization_barrier((columns[-1], coef, inverse))
-
     size = snps // n_far
     panel = size // n_near
     freedom = float(here * n_far - design - 1)
@@ -409,7 +408,7 @@
     def send(pieces):
         return [permute_xor(pieces[j - 1], "far", j) for j in range(1, n_far)]
 
-    def panel_stats(index, base, factors, pieces):
+    def panel_stats(index, coef, base, factors, pieces):
         first = index * panel
         line = lax.dynamic_slice_in_dim(coef, far * size + first, panel, 0)
         ratio = lax.dynamic_slice_in_dim(base, first, panel, 0)
@@ -425,9 +424,9 @@
         pieces = [piece.astype(jnp.float16) for piece in pieces]
         owns.append(own)
         sums.append([stats] + [permute_xor(stats, "far", j) for j in range(1, n_far)])
-        if chunk == CHUNKS - 1:
-            sums, pieces = lax.optimization_barrier((sums, pieces))
         received.append(send(pieces))
+    moment_parts, sums[-1][0] = lax.optimization_barrier((moment_parts, sums[-1][0]))
+    coef, inverse = cohort_fit(moment_parts, snps, design)
     outs = []
     gate = None
     for chunk in range(CHUNKS):
@@ -436,9 +435,12 @@
             base, gate = lax.optimization_barrier((base, gate))
             outs[-1][0] = gate
         pieces = received[chunk]
-        gate = panel_stats(jnp.bitwise_xor(near, 1), base, factors, pieces)
-        outs.append([gate, panel_stats(near, base, factors, pieces)])
-    outs = [(permute_xor(away, "near", 1), home) for away, home in outs]
+        gate = panel_stats(jnp.bitwise_xor(near, 1), coef, base, factors, pieces)
+        outs.append([gate, panel_stats(near, coef, base, factors, pieces)])
+    outs = [
+        (permute_xor((away * NARROW).astype(jnp.float16), "near", 1), home) for away, home in outs
+    ]
+    outs = [(away.astype(jnp.float32) * (1.0 / NARROW), home) for away, home in outs]
     outs = [
         jnp.where(near == 0, jnp.stack([home, away], 1), jnp.stack([away, home], 1))
         for away, home in outs

time: 91.5 us -> 94.2 us (1.030)
  starting transfers between devices: 19.4 us -> 23.1 us
  waiting for transfers between devices: 47.1 us -> 45 us
  Pallas kernels: 14.9 us -> 15.9 us
    all_to_all x2, waiting for transfers between devices: 15.4 us -> 0.01 us  [exchange(): value = lax.all_to_all(value, ('vox', 'near'), 0, 0, tiled=True)]
    ppermute x11, waiting for transfers between devices: 31.8 us -> 45 us  [permute_xor(): return lax.ppermute(value, axes, [(i, i ^ bits) for i in range(size)])]
    ppermute x11, starting transfers between devices: 10.8 us -> 14.3 us  [permute_xor(): return lax.ppermute(value, axes, [(i, i ^ bits) for i in range(size)])]
  transfers between devices with their start and end apart: 13 -> 13, of which waited for: 10 -> 6; matrix products, arithmetic and copies ran while one was open for 3% -> 3% of each run, Pallas kernels for 16% -> 12%
where the time goes in v6:
time: 94.2 us; the launch traced here: 93.7 us
  waiting for transfers between devices  45 us (48%)
  starting transfers between devices  23.1 us (25%)
  Pallas kernels  15.9 us (17%)
  local copies, waits for them, and re-layouts  6.72 us (7%)
  other arithmetic  2.78 us (3%)
    ppermute x11, waiting for transfers between devices, permute_xor(): return lax.ppermute(value, axes, [(i, i ^ bits) for i in range(size)])  45 us
    ppermute x11, starting transfers between devices, permute_xor(): return lax.ppermute(value, axes, [(i, i ^ bits) for i in range(size)])  14.3 us
    pallas_call x7, Pallas kernels, call(): pl.pallas_call(kernel, out_shape=outs, in_specs=[IN_SMEM] * len(scalars)...  10.8 us
    all_to_all x2, starting transfers between devices, exchange(): value = lax.all_to_all(value, ('vox', 'near'), 0, 0, tiled=True)  8.86 us
    pallas_call x1, Pallas kernels, smooth(): pl.pallas_call(functools.partial(smooth_kernel, group, planes, per_vox, p...  4.98 us
    unnamed x18, local copies, waits for them, and re-layouts  4.51 us
    reshape x2, local copies, waits for them, and re-layouts, on_device(): return jnp.stack(outs, axis=2).reshape(panel, maps, per_vox, plane)  2.01 us
  transfers between devices with their start and end apart: 13, of which 6 were waited for; matrix products, arithmetic and copies ran while one was open for 3% of the time, Pallas kernels for 12%

profile of v6, /device:TPU:0, one launch (start us, length us, event | category | flops | bytes accessed | tf_op | source)
XLA Modules:
  0.0 93.7 jit_solution(17214365371969177379)
XLA Ops:
  0.0 5.0 %smooth.1 = (bf16[8,128,512]{2,1,0:T(8,128)(2,1)}, bf16[8,128,512]{2,1,0:T(8,128)(2,1)}) custom-call(bf16[128,32,256]{2,1,0:T(8,128)(2,1)} %bitcast.30, bf16[256,256]{1,0:T(8,128)(2,1)} %constant.35.clone.order, bf16[256,256]{1,0:T(8,128)(2,1)} %constant.36.clone.table), custom_call_target="tpu_custom_call" | custom-call | tf_op jit(solution)/shard_map/smooth/pallas_call | solution.py:168
  5.0 5.3 %all-to-all-start = ((bf16[8,128,512]{2,1,0:T(8,128)(2,1)}), bf16[8,128,512]{2,1,0:T(8,128)(2,1)S(1)}, u32[]{:S(2)}, u32[]{:S(2)}) async-start(bf16[8,128,512]{2,1,0:T(8,128)(2,1)} %get-tuple-element.38), calls=%async_computation | async-start | bytes 2097152 | tf_op jit(solution)/shard_map/all_to_all | solution.py:382
  10.4 2.1 %collective-permute-start = (bf16[536,128]{1,0:T(8,128)(2,1)S(1)}, bf16[536,128]{1,0:T(8,128)(2,1)S(1)}, u32[]{:S(2)}, u32[]{:S(2)}) collective-permute-start(bf16[536,128]{1,0:T(8,128)(2,1)S(1)} %tall_design.1), channel_id=1, source_target_pairs={{0,1},{1,0},{4,5},{5,4},{8,9},{9,8},{12,13},{13,12},{2,3},{3,2},{6... | collective-permute-start | bytes 411656 | tf_op jit(solution)/shard_map/ppermute | solution.py:368
  12.5 1.5 %collective-permute-start.1 = (bf16[536,128]{1,0:T(8,128)(2,1)S(1)}, bf16[536,128]{1,0:T(8,128)(2,1)S(1)}, u32[]{:S(2)}, u32[]{:S(2)}) collective-permute-start(bf16[536,128]{1,0:T(8,128)(2,1)S(1)} %tall_design.1), channel_id=1, source_target_pairs={{0,8},{1,9},{4,12},{5,13},{8,0},{9,1},{12,4},{13,5},{2,10},{3,11},... | collective-permute-start | bytes 411656 | tf_op jit(solution)/shard_map/ppermute | solution.py:368
  14.0 14.2 %collective-permute-done = bf16[536,128]{1,0:T(8,128)(2,1)S(1)} collective-permute-done((bf16[536,128]{1,0:T(8,128)(2,1)S(1)}, bf16[536,128]{1,0:T(8,128)(2,1)S(1)}, u32[]{:S(2)}, u32[]{:S(2)}) %collective-permute-start) | collective-permute-done | bytes 137248 | tf_op jit(solution)/shard_map/ppermute | solution.py:368
  28.2 3.4 %collective-permute-done.2 = bf16[536,128]{1,0:T(8,128)(2,1)S(1)} collective-permute-done((bf16[536,128]{1,0:T(8,128)(2,1)S(1)}, bf16[536,128]{1,0:T(8,128)(2,1)S(1)}, u32[]{:S(2)}, u32[]{:S(2)}) %collective-permute-start.2) | collective-permute-done | bytes 137248 | tf_op jit(solution)/shard_map/ppermute | solution.py:368
  31.6 3.6 %all-to-all-start.1 = ((bf16[8,128,512]{2,1,0:T(8,128)(2,1)}), bf16[8,128,512]{2,1,0:T(8,128)(2,1)S(1)}, u32[]{:S(2)}, u32[]{:S(2)}) async-start(bf16[8,128,512]{2,1,0:T(8,128)(2,1)} %get-tuple-element.48), calls=%async_computation.1 | async-start | bytes 2097152 | tf_op jit(solution)/shard_map/all_to_all | solution.py:382
  35.2 0.5 collective-permute-start.3
  35.7 0.8 copy-done
  36.5 0.8 collective-permute-done.3.others
  37.3 0.8 copy-done.2
  38.1 1.0 %copy-done.1 = bf16[4,536,128]{2,1,0:T(8,128)(2,1)S(1)} copy-done((bf16[4,536,128]{2,1,0:T(8,128)(2,1)S(1)}, bf16[4,536,128]{2,1,0:T(8,128)(2,1)}, u32[]{:S(2)}) %copy-start.1) | copy-done | bytes 548888
  39.1 1.0 %copy-done.3 = bf16[4,536,128]{2,1,0:T(8,128)(2,1)S(1)} copy-done((bf16[4,536,128]{2,1,0:T(8,128)(2,1)S(1)}, bf16[4,536,128]{2,1,0:T(8,128)(2,1)}, u32[]{:S(2)}) %copy-start.3) | copy-done | bytes 548888
  40.2 1.1 %moments.1 = (bf16[536,1024]{1,0:T(8,128)(2,1)S(1)}, f32[32,640]{1,0:T(8,128)S(1)}) custom-call(s32[1]{0:T(128)} %bitcast.1.me, bf16[4,536,128]{2,1,0:T(8,128)(2,1)S(1)} %copy-done.1, bf16[4,536,128]{2,1,0:T(8,128)(2,1)S(1)} %copy-done.3), custom_call_target="tpu_custom_call" | custom-call | tf_op jit(solution)/shard_map/moments/pallas_call | solution.py:89
  41.2 2.1 %pair_fit.1.coef = f32[512,128]{1,0:T(8,128)S(1)} custom-call(f32[32,640]{1,0:T(8,128)S(1)} %get-tuple-element.50.moment.refs_0_), custom_call_target="tpu_custom_call" | custom-call | tf_op jit(solution)/shard_map/pair_fit/pallas_call | solution.py:89
  43.3 1.4 %products.2 = (f32[256,512]{1,0:T(8,128)S(1)}, f32[256,512]{1,0:T(8,128)S(1)}, f32[24,512]{1,0:T(8,128)}) custom-call(s32[1]{0:T(128)} %bitcast.me, bf16[536,1024]{1,0:T(8,128)(2,1)S(1)} %get-tuple-element.44.genes, bf16[1024,512]{1,0:T(8,128)(2,1)S(1)} %bitcast.26, f32[512,128]{1,0:T(8,128)S(1)} %pair_fit.1.coef), custom_call_target="tpu_custom_call" | custom-call | tf_op jit(solution)/shard_map/products/pallas_call | solution.py:89
  44.7 0.8 copy-done.4
  45.5 0.7 convert_element_type.30
  46.2 2.6 %collective-permute-start.6 = (f16[256,512]{1,0:T(8,128)(2,1)}, f16[256,512]{1,0:T(8,128)(2,1)}, u32[]{:S(2)}, u32[]{:S(2)}) collective-permute-start(f16[256,512]{1,0:T(8,128)(2,1)} %convert_element_type.30), channel_id=1, source_target_pairs={{0,2},{2,0},{1,3},{3,1},{4,6},{6,4},{5,7},{7,5},{8,10},{10,8},{9,1... | collective-permute-start | bytes 786440 | tf_op jit(solution)/shard_map/ppermute | solution.py:368
  49.2 2.6 %collective-permute-start.5 = (f32[24,512]{1,0:T(8,128)}, f32[24,512]{1,0:T(8,128)}, u32[]{:S(2)}, u32[]{:S(2)}) collective-permute-start(f32[24,512]{1,0:T(8,128)} %get-tuple-element.54.refs_0_), channel_id=1, source_target_pairs={{0,2},{2,0},{1,3},{3,1},{4,6},{6,4},{5,7},{7,5},{8,10},{10,8},{9,1... | collective-permute-start | bytes 147464 | tf_op jit(solution)/shard_map/ppermute | solution.py:368
  51.8 1.3 %products.3 = (f32[256,512]{1,0:T(8,128)S(1)}, f32[256,512]{1,0:T(8,128)S(1)}, f32[24,512]{1,0:T(8,128)S(1)}) custom-call(s32[1]{0:T(128)} %bitcast.me, bf16[536,1024]{1,0:T(8,128)(2,1)S(1)} %get-tuple-element.44.genes, bf16[1024,512]{1,0:T(8,128)(2,1)S(1)} %bitcast.25, f32[512,128]{1,0:T(8,128)S(1)} %pair_fit.1.coef), custom_call_target="tpu_custom_call" | custom-call | tf_op jit(solution)/shard_map/products/pallas_call | solution.py:89
  53.1 0.9 collective-permute-start.7
  54.0 13.9 %collective-permute-done.4.refs_1_ = f32[32,640]{1,0:T(8,128)} collective-permute-done((f32[32,640]{1,0:T(8,128)S(1)}, f32[32,640]{1,0:T(8,128)}, u32[]{:S(2)}, u32[]{:S(2)}) %collective-permute-start.4) | collective-permute-done | bytes 81952 | tf_op jit(solution)/shard_map/ppermute | solution.py:368
  67.8 3.0 %cohort_fit.1 = (f32[512,128]{1,0:T(8,128)S(1)}, f32[24,128]{1,0:T(8,128)S(1)}) custom-call(f32[32,640]{1,0:T(8,128)S(1)} %get-tuple-element.50.moment.refs_0_, f32[32,640]{1,0:T(8,128)} %collective-permute-done.4.refs_1_), custom_call_target="tpu_custom_call" | custom-call | tf_op jit(solution)/shard_map/cohort_fit/pallas_call | solution.py:89
  70.9 1.4 %base_ratio.2 = (f32[256,512]{1,0:T(8,128)S(1)}, f32[8,512]{1,0:T(8,128)S(1)}) custom-call(s32[1]{0:T(128)} %bitcast.me, f32[256,512]{1,0:T(8,128)S(1)} %copy-done.5, f32[512,128]{1,0:T(8,128)S(1)} %get-tuple-element.52.coef, f32[24,128]{1,0:T(8,128)S(1)} %get-tuple-element.53.inverse, f32[24,512]{1,0:T(8,128)} %get-tuple-element.54.refs_0_, ...), custom_call_target="tpu_custom_call" | custom-call | tf_op jit(solution)/shard_map/base_ratio/pallas_call | solution.py:89
  72.6 1.3 %multiply_bitcast_fusion.3 = (f32[128,1,1,512]{3,0,2,1:T(8,128)S(1)}, f32[128,512]{1,0:T(8,128)S(1)}) fusion(f32[256,512]{1,0:T(8,128)S(1)} %get-tuple-element.55, s32[]{:T(128)S(6)} %select_n.47, f32[512]{0:T(512)S(1)} %bitcast.34, f32[128]{0:T(128)S(1)} %get-tuple-element.65, f16[256,512]{1,0:T(8,128)(2,1)} %collective-permute-done.6, ...), kind=kLoop, calls=%fused_computation.10 | loop fusion | flops 1048576 | bytes 1313800 | tf_op jit(solution)/shard_map/stack | solution.py:445
  74.0 0.6 base_ratio.3
  74.6 3.6 %collective-permute-start.8 = (f16[128,512]{1,0:T(8,128)(2,1)S(1)}, f16[128,512]{1,0:T(8,128)(2,1)S(1)}, u32[]{:S(2)}, u32[]{:S(2)}) collective-permute-start(f16[128,512]{1,0:T(8,128)(2,1)S(1)} %multiply_convert_fusion.1), channel_id=1, source_target_pairs={{0,1},{1,0},{2,3},{3,2},{4,5},{5,4},{6,7},{7,6},{8,9},{9,8},{10,11... | collective-permute-start | bytes 393224 | tf_op jit(solution)/shard_map/ppermute | solution.py:368
  78.2 7.9 %collective-permute-done.9 = f16[256,512]{1,0:T(8,128)(2,1)S(1)} collective-permute-done((f16[256,512]{1,0:T(8,128)(2,1)S(1)}, f16[256,512]{1,0:T(8,128)(2,1)S(1)}, u32[]{:S(2)}, u32[]{:S(2)}) %collective-permute-start.9) | collective-permute-done | bytes 262176 | tf_op jit(solution)/shard_map/ppermute | solution.py:368
  86.7 4.9 %collective-permute-done.10 = f16[128,512]{1,0:T(8,128)(2,1)S(1)} collective-permute-done((f16[128,512]{1,0:T(8,128)(2,1)S(1)}, f16[128,512]{1,0:T(8,128)(2,1)S(1)}, u32[]{:S(2)}, u32[]{:S(2)}) %collective-permute-start.10) | collective-permute-done | bytes 131104 | tf_op jit(solution)/shard_map/ppermute | solution.py:368
  91.7 0.7 reshape.133
  92.4 1.3 %copy.8 = f32[128,4,2,256]{3,2,1,0:T(2,128)} copy(f32[128,4,2,256]{3,2,0,1:T(2,128)S(1)} %reshape.133) | data formatting | bytes 2097152 | tf_op jit(solution)/shard_map/reshape | solution.py:448
  (37 shorter events, 1.6 us)
Async XLA Ops:
  0.0 10.3 %copy-start.6 = (bf16[128,512]{1,0:T(8,128)(2,1)S(1)}, bf16[128,512]{1,0:T(8,128)(2,1)}, u32[]{:S(2)}) copy-start(bf16[128,512]{1,0:T(8,128)(2,1)} %genotypes) | copy-start | bytes 393220
  0.0 10.3 %copy-start.7 = (bf16[128,16]{0,1:T(8,128)(2,1)S(1)}, bf16[128,16]{0,1:T(8,128)(2,1)}, u32[]{:S(2)}) copy-start(bf16[128,16]{0,1:T(8,128)(2,1)} %param.8) | copy-start | bytes 12292
  0.0 10.3 %copy-start.8 = (s32[128]{0:T(128)S(1)}, s32[128]{0:T(128)}, u32[]{:S(2)}) copy-start(s32[128]{0:T(128)} %param.9) | copy-start | bytes 1540
  5.0 26.6 %all-to-all-start = ((bf16[8,128,512]{2,1,0:T(8,128)(2,1)}), bf16[8,128,512]{2,1,0:T(8,128)(2,1)S(1)}, u32[]{:S(2)}, u32[]{:S(2)}) async-start(bf16[8,128,512]{2,1,0:T(8,128)(2,1)} %get-tuple-element.38), calls=%async_computation | async-start | bytes 2097152 | tf_op jit(solution)/shard_map/all_to_all | solution.py:382
  10.4 17.8 %collective-permute-start = (bf16[536,128]{1,0:T(8,128)(2,1)S(1)}, bf16[536,128]{1,0:T(8,128)(2,1)S(1)}, u32[]{:S(2)}, u32[]{:S(2)}) collective-permute-start(bf16[536,128]{1,0:T(8,128)(2,1)S(1)} %tall_design.1), channel_id=1, source_target_pairs={{0,1},{1,0},{4,5},{5,4},{8,9},{9,8},{12,13},{13,12},{2,3},{3,2},{6... | collective-permute-start | bytes 411656 | tf_op jit(solution)/shard_map/ppermute | solution.py:368
  12.5 15.7 %collective-permute-start.1 = (bf16[536,128]{1,0:T(8,128)(2,1)S(1)}, bf16[536,128]{1,0:T(8,128)(2,1)S(1)}, u32[]{:S(2)}, u32[]{:S(2)}) collective-permute-start(bf16[536,128]{1,0:T(8,128)(2,1)S(1)} %tall_design.1), channel_id=1, source_target_pairs={{0,8},{1,9},{4,12},{5,13},{8,0},{9,1},{12,4},{13,5},{2,10},{3,11},... | collective-permute-start | bytes 411656 | tf_op jit(solution)/shard_map/ppermute | solution.py:368
  14.0 17.6 %collective-permute-start.2 = (bf16[536,128]{1,0:T(8,128)(2,1)S(1)}, bf16[536,128]{1,0:T(8,128)(2,1)S(1)}, u32[]{:S(2)}, u32[]{:S(2)}) collective-permute-start(bf16[536,128]{1,0:T(8,128)(2,1)S(1)} %tall_design.1), channel_id=1, source_target_pairs={{0,9},{1,8},{4,13},{5,12},{8,1},{9,0},{12,5},{13,4},{2,11},{3,10},... | collective-permute-start | bytes 411656 | tf_op jit(solution)/shard_map/ppermute | solution.py:368
  31.6 20.2 %all-to-all-start.1 = ((bf16[8,128,512]{2,1,0:T(8,128)(2,1)}), bf16[8,128,512]{2,1,0:T(8,128)(2,1)S(1)}, u32[]{:S(2)}, u32[]{:S(2)}) async-start(bf16[8,128,512]{2,1,0:T(8,128)(2,1)} %get-tuple-element.48), calls=%async_computation.1 | async-start | bytes 2097152 | tf_op jit(solution)/shard_map/all_to_all | solution.py:382
  35.2 2.0 %collective-permute-start.3 = (bf16[4,536,128]{2,1,0:T(8,128)(2,1)S(1)}, bf16[4,536,128]{2,1,0:T(8,128)(2,1)S(1)}, u32[]{:S(2)}, u32[]{:S(2)}) collective-permute-start(bf16[4,536,128]{2,1,0:T(8,128)(2,1)S(1)} %pad_maximum_fusion.1.blocks), channel_id=1, source_target_pairs={{0,4},{1,5},{4,0},{5,1},{8,12},{9,13},{12,8},{13,9},{2,6},{3,7},{6... | collective-permute-start | bytes 1646600 | tf_op jit(solution)/shard_map/ppermute | solution.py:368
  35.7 0.8 copy-start
  37.3 0.8 copy-start.2
  38.1 1.1 %copy-start.1 = (bf16[4,536,128]{2,1,0:T(8,128)(2,1)S(1)}, bf16[4,536,128]{2,1,0:T(8,128)(2,1)}, u32[]{:S(2)}) copy-start(bf16[4,536,128]{2,1,0:T(8,128)(2,1)} %copy-done) | copy-start | bytes 1646596
  39.1 1.1 %copy-start.3 = (bf16[4,536,128]{2,1,0:T(8,128)(2,1)S(1)}, bf16[4,536,128]{2,1,0:T(8,128)(2,1)}, u32[]{:S(2)}) copy-start(bf16[4,536,128]{2,1,0:T(8,128)(2,1)} %copy-done.2) | copy-start | bytes 1646596
  44.7 0.8 copy-start.4
  45.5 25.3 %copy-start.5 = (f32[256,512]{1,0:T(8,128)S(1)}, f32[256,512]{1,0:T(8,128)}, u32[]{:S(2)}) copy-start(f32[256,512]{1,0:T(8,128)} %copy-done.4) | copy-start | bytes 1572868
  46.2 26.4 %collective-permute-start.6 = (f16[256,512]{1,0:T(8,128)(2,1)}, f16[256,512]{1,0:T(8,128)(2,1)}, u32[]{:S(2)}, u32[]{:S(2)}) collective-permute-start(f16[256,512]{1,0:T(8,128)(2,1)} %convert_element_type.30), channel_id=1, source_target_pairs={{0,2},{2,0},{1,3},{3,1},{4,6},{6,4},{5,7},{7,5},{8,10},{10,8},{9,1... | collective-permute-start | bytes 786440 | tf_op jit(solution)/shard_map/ppermute | solution.py:368
  48.9 19.0 %collective-permute-start.4 = (f32[32,640]{1,0:T(8,128)S(1)}, f32[32,640]{1,0:T(8,128)}, u32[]{:S(2)}, u32[]{:S(2)}) collective-permute-start(f32[32,640]{1,0:T(8,128)S(1)} %get-tuple-element.50.moment.refs_0_), channel_id=1, source_target_pairs={{0,2},{2,0},{1,3},{3,1},{4,6},{6,4},{5,7},{7,5},{8,10},{10,8},{9,1... | collective-permute-start | bytes 245768 | tf_op jit(solution)/shard_map/ppermute | solution.py:368
  49.2 21.7 %collective-permute-start.5 = (f32[24,512]{1,0:T(8,128)}, f32[24,512]{1,0:T(8,128)}, u32[]{:S(2)}, u32[]{:S(2)}) collective-permute-start(f32[24,512]{1,0:T(8,128)} %get-tuple-element.54.refs_0_), channel_id=1, source_target_pairs={{0,2},{2,0},{1,3},{3,1},{4,6},{6,4},{5,7},{7,5},{8,10},{10,8},{9,1... | collective-permute-start | bytes 147464 | tf_op jit(solution)/shard_map/ppermute | solution.py:368
  53.1 20.9 %collective-permute-start.7 = (f32[24,512]{1,0:T(8,128)S(1)}, f32[24,512]{1,0:T(8,128)S(1)}, u32[]{:S(2)}, u32[]{:S(2)}) collective-permute-start(f32[24,512]{1,0:T(8,128)S(1)} %get-tuple-element.59.refs_0_), channel_id=1, source_target_pairs={{0,2},{2,0},{1,3},{3,1},{4,6},{6,4},{5,7},{7,5},{8,10},{10,8},{9,1... | collective-permute-start | bytes 147464 | tf_op jit(solution)/shard_map/ppermute | solution.py:368
  72.3 13.8 %collective-permute-start.9 = (f16[256,512]{1,0:T(8,128)(2,1)S(1)}, f16[256,512]{1,0:T(8,128)(2,1)S(1)}, u32[]{:S(2)}, u32[]{:S(2)}) collective-permute-start(f16[256,512]{1,0:T(8,128)(2,1)S(1)} %convert_element_type.35), channel_id=1, source_target_pairs={{0,2},{2,0},{1,3},{3,1},{4,6},{6,4},{5,7},{7,5},{8,10},{10,8},{9,1... | collective-permute-start | bytes 786440 | tf_op jit(solution)/shard_map/ppermute | solution.py:368
  74.6 12.0 %collective-permute-start.8 = (f16[128,512]{1,0:T(8,128)(2,1)S(1)}, f16[128,512]{1,0:T(8,128)(2,1)S(1)}, u32[]{:S(2)}, u32[]{:S(2)}) collective-permute-start(f16[128,512]{1,0:T(8,128)(2,1)S(1)} %multiply_convert_fusion.1), channel_id=1, source_target_pairs={{0,1},{1,0},{2,3},{3,2},{4,5},{5,4},{6,7},{7,6},{8,9},{9,8},{10,11... | collective-permute-start | bytes 393224 | tf_op jit(solution)/shard_map/ppermute | solution.py:368
  86.5 5.0 %collective-permute-start.10 = (f16[128,512]{1,0:T(8,128)(2,1)S(1)}, f16[128,512]{1,0:T(8,128)(2,1)S(1)}, u32[]{:S(2)}, u32[]{:S(2)}) collective-permute-start(f16[128,512]{1,0:T(8,128)(2,1)S(1)} %get-tuple-element.70), channel_id=1, source_target_pairs={{0,1},{1,0},{2,3},{3,2},{4,5},{5,4},{6,7},{7,6},{8,9},{9,8},{10,11... | collective-permute-start | bytes 393224 | tf_op jit(solution)/shard_map/ppermute | solution.py:368

commit v7 on v6

--- a/solution.py
+++ b/solution.py
@@ -116,7 +116,7 @@
         in_specs=[IN_VMEM] * 3,
         out_specs=IN_VMEM,
         scratch_shapes=[pltpu.VMEM((DPAD, subjects), jnp.float32)],
-        compiler_params=params(),
+        compiler_params=params(VMEM_MOST),
         name="tall_design",
     )(genotypes, site_codes[None, :], covariates.T)
 
@@ -216,7 +216,7 @@
         result((DPAD + 8, spread), jnp.float32),
     )
     kernel = functools.partial(moments_kernel, snps, slots)
-    return call(kernel, "moments", outs, [me], [blocks, others])
+    return call(kernel, "moments", outs, [me], [blocks, others], (), 2)
 
 
 def eliminate(total, snps, design, guard):
@@ -292,18 +292,30 @@
     return jnp.sqrt(spread + 1e-30)
 
 
-def products_kernel(here, me, genes, columns, coef, own, *refs):
-    far, stats, held = refs[:-2], refs[-2], refs[-1]
+def sums_kernel(genes, columns, out):
     values = columns[...]
     wide = values.astype(jnp.float32)
-    sums = jnp.dot(genes[...], values, preferred_element_type=jnp.float32)
-    snps = held.shape[0]
-    held[...] = sums[:snps, :]
+    design = genes[genes.shape[0] - DPAD :, :]
+    sums = jnp.dot(design, values, preferred_element_type=jnp.float32)
     square = jnp.sum(wide * wide, axis=0, keepdims=True)
-    cross_image = sums[snps:, :]
-    row = lax.broadcasted_iota(jnp.int32, cross_image.shape, 0)
-    cross_image = jnp.where(row == SQUARE_ROW, square, cross_image)
-    stats[...] = cross_image
+    row = lax.broadcasted_iota(jnp.int32, sums.shape, 0)
+    out[...] = jnp.where(row == SQUARE_ROW, square, sums)
+
+
+def column_sums(genes, columns):
+    outs = result((DPAD, columns.shape[1]), jnp.float32)
+    return call(sums_kernel, "column_sums", outs, [], [genes, columns])
+
+
+def products_kernel(here, first, me, genes, columns, coef, stats, own, *refs):
+    far, held = refs[:-1], refs[-1]
+    snps, width = held.shape
+    held[...] = jnp.dot(
+        genes[:snps, :],
+        columns[:, first : first + width],
+        preferred_element_type=jnp.float32,
+    )
+    cross_image = stats[:, first : first + width]
     over = 1.0 / column_norm(cross_image, here)
     size = own.shape[0]
     own[...] = held[pl.ds(pl.multiple_of(me[0] * size, size), size), :]
@@ -317,22 +329,20 @@
         out[...] = (scale * held[pl.ds(place, size), :] - fit) * over
 
 
-def products(genes, columns, coef, me, count):
+def products(genes, columns, coef, stats, me, count, first, width):
     rows, here = genes.shape
     snps = rows - DPAD
-    width = columns.shape[1]
     size = snps // count
-    outs = (jax.ShapeDtypeStruct((size, width), jnp.float32),)
+    outs = (pltpu.HBM((size, width), jnp.float32),)
     outs += (result((size, width), jnp.float32),) * (count - 1)
-    outs += (result((DPAD, width), jnp.float32),)
-    kernel = functools.partial(products_kernel, float(here))
+    kernel = functools.partial(products_kernel, float(here), first)
     scratch = [pltpu.VMEM((snps, width), jnp.float32)]
-    return call(kernel, "products", outs, [me], [genes, columns, coef], scratch)
-
-
-def base_kernel(here, me, own, coef, inverse, *refs):
+    return call(kernel, "products", outs, [me], [genes, columns, coef, stats], scratch)
+
+
+def base_kernel(here, first, me, own, coef, inverse, *refs):
     parts, (base, factors, stack) = refs[:-3], refs[-3:]
-    stats = [part[...] for part in parts]
+    stats = [part[:, first : first + own.shape[1]] for part in parts]
     row = lax.broadcasted_iota(jnp.int32, stats[0].shape, 0)
     total = tree_sum(stats)
     cross_image = jnp.where(row < SQUARE_ROW, total, 0.0)
@@ -355,10 +365,10 @@
     base[...] = (line[:, SCALE_LANE : SCALE_LANE + 1] * own[...] + terms) * scale
 
 
-def base_ratio(me, own, coef, inverse, parts, here):
+def base_ratio(me, own, coef, inverse, parts, here, first):
     size, width = own.shape
     outs = (result((size, width), jnp.float32), result((8, width), jnp.float32))
-    kernel = functools.partial(base_kernel, float(here))
+    kernel = functools.partial(base_kernel, float(here), first)
     scratch = [pltpu.VMEM((LANES, width), jnp.float32)]
     return call(kernel, "base_ratio", outs, [me], [own, coef, inverse, *parts], scratch, 1)
 
@@ -382,18 +392,13 @@
         value = lax.all_to_all(value, ("vox", "near"), 0, 0, tiled=True)
         return value.reshape(here, value.shape[2])
 
-    smoothed = smooth(images, n_vox, n_near, CHUNKS)
-    smoothed, genotypes = lax.optimization_barrier((smoothed, genotypes))
-    columns = [exchange(smoothed[0])]
     tall = tall_design(genotypes, covariates, site_codes)
     other = n_near
     offsets = [o for o in range(count) if not o & other]
     blocks = [tall] + [permute_xor(tall, ("vox", "near"), o) for o in offsets[1:]]
-    for chunk in range(1, CHUNKS):
-        value, columns[-1], *blocks = lax.optimization_barrier(
-            (smoothed[chunk], columns[-1], *blocks)
-        )
-        columns.append(exchange(value))
+    (smoothed,) = smooth(images, n_vox, n_near, 1)
+    smoothed, *blocks = lax.optimization_barrier((smoothed, *blocks))
+    columns = exchange(smoothed)
     blocks = jnp.stack(blocks)
     others = permute_xor(blocks, ("vox", "near"), other)
     order = offsets + [o | other for o in offsets]
@@ -401,6 +406,10 @@
     genes, moment = moments(blocks, others, slots, (vox * n_near + near)[None])
     pair_coef = pair_fit(moment, snps, design)
     moment_parts = [moment] + [permute_xor(moment, "far", j) for j in range(1, n_far)]
+    columns, moment_parts = lax.optimization_barrier((columns, moment_parts))
+    stats = column_sums(genes, columns)
+    stat_parts = [stats] + [permute_xor(stats, "far", j) for j in range(1, n_far)]
+
     size = snps // n_far
     panel = size // n_near
     freedom = float(here * n_far - design - 1)
@@ -418,19 +427,21 @@
             ratio = ratio + piece.astype(jnp.float32) * weight
         return ratio * jnp.sqrt(freedom / (1.0 - ratio * ratio))
 
-    owns, received, sums = [], [], []
+    owns, received = [], []
+    width = columns.shape[1] // CHUNKS
     for chunk in range(CHUNKS):
-        own, *pieces, stats = products(genes, columns[chunk], pair_coef, far[None], n_far)
-        pieces = [piece.astype(jnp.float16) for piece in pieces]
+        own, *pieces = products(
+            genes, columns, pair_coef, stats, far[None], n_far, chunk * width, width
+        )
         owns.append(own)
-        sums.append([stats] + [permute_xor(stats, "far", j) for j in range(1, n_far)])
-        received.append(send(pieces))
-    moment_parts, sums[-1][0] = lax.optimization_barrier((moment_parts, sums[-1][0]))
+        received.append(send([piece.astype(jnp.float16) for piece in pieces]))
     coef, inverse = cohort_fit(moment_parts, snps, design)
     outs = []
     gate = None
     for chunk in range(CHUNKS):
-        base, factors = base_ratio(far[None], owns[chunk], coef, inverse, sums[chunk], here)
+        base, factors = base_ratio(
+            far[None], owns[chunk], coef, inverse, stat_parts, here, chunk * width
+        )
         if gate is not None:
             base, gate = lax.optimization_barrier((base, gate))
             outs[-1][0] = gate

time: 94.2 us -> 86 us (0.913)
  starting transfers between devices: 23.1 us -> 17.3 us
  waiting for transfers between devices: 45 us -> 40.4 us
  Pallas kernels: 15.9 us -> 19 us
    ppermute x11 -> x10, waiting for transfers between devices: 45 us -> 37.7 us  [permute_xor(): return lax.ppermute(value, axes, [(i, i ^ bits) for i in range(size)])]
    all_to_all x2 -> x1, starting transfers between devices: 8.86 us -> 3.6 us  [exchange(): value = lax.all_to_all(value, ('vox', 'near'), 0, 0, tiled=True)]
    all_to_all x2 -> x1, waiting for transfers between devices: 0.01 us -> 2.65 us  [exchange(): value = lax.all_to_all(value, ('vox', 'near'), 0, 0, tiled=True)]
    pallas_call x7 -> x8, Pallas kernels: 10.8 us -> 13.1 us  [call(): pl.pallas_call(kernel, out_shape=outs, in_specs=[IN_SMEM] * len(scalars)...]
    unnamed x18 -> x16, local copies, waits for them, and re-layouts: 4.51 us -> 3.72 us
    ppermute x11 -> x10, starting transfers between devices: 14.3 us -> 13.7 us  [permute_xor(): return lax.ppermute(value, axes, [(i, i ^ bits) for i in range(size)])]
  transfers between devices with their start and end apart: 13 -> 11, of which waited for: 6 -> 7; matrix products, arithmetic and copies ran while one was open for 3% -> 2% of each run, Pallas kernels for 12% -> 18%
where the time goes in v7:
time: 86 us; the launch traced here: 85.5 us
  waiting for transfers between devices  40.4 us (47%)
  Pallas kernels  19 us (22%)
  starting transfers between devices  17.3 us (20%)
  local copies, waits for them, and re-layouts  5.92 us (7%)
  other arithmetic  2.76 us (3%)
    ppermute x10, waiting for transfers between devices, permute_xor(): return lax.ppermute(value, axes, [(i, i ^ bits) for i in range(size)])  37.7 us
    ppermute x10, starting transfers between devices, permute_xor(): return lax.ppermute(value, axes, [(i, i ^ bits) for i in range(size)])  13.7 us
    pallas_call x8, Pallas kernels, call(): pl.pallas_call(kernel, out_shape=outs, in_specs=[IN_SMEM] * len(scalars)...  13.1 us
    pallas_call x1, Pallas kernels, smooth(): pl.pallas_call(functools.partial(smooth_kernel, group, planes, per_vox, p...  4.91 us
    unnamed x16, local copies, waits for them, and re-layouts  3.72 us
    all_to_all x1, starting transfers between devices, exchange(): value = lax.all_to_all(value, ('vox', 'near'), 0, 0, tiled=True)  3.6 us
    all_to_all x1, waiting for transfers between devices, exchange(): value = lax.all_to_all(value, ('vox', 'near'), 0, 0, tiled=True)  2.65 us
    reshape x2, local copies, waits for them, and re-layouts, on_device(): return jnp.stack(outs, axis=2).reshape(panel, maps, per_vox, plane)  2.01 us
  transfers between devices with their start and end apart: 11, of which 7 were waited for; matrix products, arithmetic and copies ran while one was open for 2% of the time, Pallas kernels for 18%

profile of v7, /device:TPU:0, one launch (start us, length us, event | category | flops | bytes accessed | tf_op | source)
XLA Modules:
  0.0 85.5 jit_solution(8404673455465783055)
XLA Ops:
  0.0 1.0 %tall_design.1 = bf16[536,128]{1,0:T(8,128)(2,1)S(1)} custom-call(bf16[128,512]{1,0:T(8,128)(2,1)} %genotypes.1, s32[1,128]{1,0:T(1,128)} %bitcast.35, bf16[16,128]{1,0:T(8,128)(2,1)} %bitcast.34), custom_call_target="tpu_custom_call" | custom-call | tf_op jit(solution)/shard_map/tall_design/pallas_call | solution.py:113
  1.0 3.1 %collective-permute-start = (bf16[536,128]{1,0:T(8,128)(2,1)S(1)}, bf16[536,128]{1,0:T(8,128)(2,1)S(1)}, u32[]{:S(2)}, u32[]{:S(2)}) collective-permute-start(bf16[536,128]{1,0:T(8,128)(2,1)S(1)} %tall_design.1), channel_id=1, source_target_pairs={{0,1},{1,0},{4,5},{5,4},{8,9},{9,8},{12,13},{13,12},{2,3},{3,2},{6... | collective-permute-start | bytes 411656 | tf_op jit(solution)/shard_map/ppermute | solution.py:378
  4.1 1.5 %collective-permute-start.1 = (bf16[536,128]{1,0:T(8,128)(2,1)S(1)}, bf16[536,128]{1,0:T(8,128)(2,1)S(1)}, u32[]{:S(2)}, u32[]{:S(2)}) collective-permute-start(bf16[536,128]{1,0:T(8,128)(2,1)S(1)} %tall_design.1), channel_id=1, source_target_pairs={{0,8},{1,9},{4,12},{5,13},{8,0},{9,1},{12,4},{13,5},{2,10},{3,11},... | collective-permute-start | bytes 411656 | tf_op jit(solution)/shard_map/ppermute | solution.py:378
  5.6 4.9 %smooth.1 = bf16[8,128,1024]{2,1,0:T(8,128)(2,1)} custom-call(bf16[128,32,256]{2,1,0:T(8,128)(2,1)} %bitcast.28, bf16[256,256]{1,0:T(8,128)(2,1)} %constant.35.clone.order, bf16[256,256]{1,0:T(8,128)(2,1)} %constant.36.clone.table), custom_call_target="tpu_custom_call" | custom-call | tf_op jit(solution)/shard_map/smooth/pallas_call | solution.py:168
  10.6 1.6 %collective-permute-done.1 = bf16[536,128]{1,0:T(8,128)(2,1)S(1)} collective-permute-done((bf16[536,128]{1,0:T(8,128)(2,1)S(1)}, bf16[536,128]{1,0:T(8,128)(2,1)S(1)}, u32[]{:S(2)}, u32[]{:S(2)}) %collective-permute-start.1) | collective-permute-done | bytes 137248 | tf_op jit(solution)/shard_map/ppermute | solution.py:378
  12.1 3.6 %all-to-all-start = ((bf16[8,128,1024]{2,1,0:T(8,128)(2,1)}), bf16[8,128,1024]{2,1,0:T(8,128)(2,1)S(1)}, u32[]{:S(2)}, u32[]{:S(2)}) async-start(bf16[8,128,1024]{2,1,0:T(8,128)(2,1)} %smooth.1), calls=%async_computation | async-start | bytes 4194304 | tf_op jit(solution)/shard_map/all_to_all | solution.py:392
  16.3 0.8 copy-done
  17.1 0.9 %collective-permute-done.3.others = bf16[4,536,128]{2,1,0:T(8,128)(2,1)S(1)} collective-permute-done((bf16[4,536,128]{2,1,0:T(8,128)(2,1)S(1)}, bf16[4,536,128]{2,1,0:T(8,128)(2,1)S(1)}, u32[]{:S(2)}, u32[]{:S(2)}) %collective-permute-start.3) | collective-permute-done | bytes 548896 | tf_op jit(solution)/shard_map/ppermute | solution.py:378
  18.0 0.8 copy-done.2
  18.8 1.0 %copy-done.1 = bf16[4,536,128]{2,1,0:T(8,128)(2,1)S(1)} copy-done((bf16[4,536,128]{2,1,0:T(8,128)(2,1)S(1)}, bf16[4,536,128]{2,1,0:T(8,128)(2,1)}, u32[]{:S(2)}) %copy-start.1) | copy-done | bytes 548888
  19.8 1.0 %copy-done.3 = bf16[4,536,128]{2,1,0:T(8,128)(2,1)S(1)} copy-done((bf16[4,536,128]{2,1,0:T(8,128)(2,1)S(1)}, bf16[4,536,128]{2,1,0:T(8,128)(2,1)}, u32[]{:S(2)}) %copy-start.3) | copy-done | bytes 548888
  20.9 1.1 %moments.1 = (bf16[536,1024]{1,0:T(8,128)(2,1)S(1)}, f32[32,640]{1,0:T(8,128)S(1)}) custom-call(s32[1]{0:T(128)} %bitcast.1.me, bf16[4,536,128]{2,1,0:T(8,128)(2,1)S(1)} %copy-done.1, bf16[4,536,128]{2,1,0:T(8,128)(2,1)S(1)} %copy-done.3), custom_call_target="tpu_custom_call" | custom-call | tf_op jit(solution)/shard_map/moments/pallas_call | solution.py:89
  21.9 2.6 %collective-permute-start.4 = (f32[32,640]{1,0:T(8,128)S(1)}, f32[32,640]{1,0:T(8,128)}, u32[]{:S(2)}, u32[]{:S(2)}) collective-permute-start(f32[32,640]{1,0:T(8,128)S(1)} %get-tuple-element.36.moment.refs_0_), channel_id=1, source_target_pairs={{0,2},{2,0},{1,3},{3,1},{4,6},{6,4},{5,7},{7,5},{8,10},{10,8},{9,1... | collective-permute-start | bytes 245768 | tf_op jit(solution)/shard_map/ppermute | solution.py:378
  24.5 2.0 %pair_fit.1.coef = f32[512,128]{1,0:T(8,128)S(1)} custom-call(f32[32,640]{1,0:T(8,128)S(1)} %get-tuple-element.36.moment.refs_0_), custom_call_target="tpu_custom_call" | custom-call | tf_op jit(solution)/shard_map/pair_fit/pallas_call | solution.py:89
  26.6 14.4 %collective-permute-done.4.refs_1_ = f32[32,640]{1,0:T(8,128)} collective-permute-done((f32[32,640]{1,0:T(8,128)S(1)}, f32[32,640]{1,0:T(8,128)}, u32[]{:S(2)}, u32[]{:S(2)}) %collective-permute-start.4) | collective-permute-done | bytes 81952 | tf_op jit(solution)/shard_map/ppermute | solution.py:378
  41.0 2.6 %all-to-all-done = bf16[8,128,1024]{2,1,0:T(8,128)(2,1)S(1)} async-done(((bf16[8,128,1024]{2,1,0:T(8,128)(2,1)}), bf16[8,128,1024]{2,1,0:T(8,128)(2,1)S(1)}, u32[]{:S(2)}, u32[]{:S(2)}) %all-to-all-start) | async-done | bytes 2097184 | tf_op jit(solution)/shard_map/all_to_all | solution.py:392
  44.1 1.8 %products.2 = (f32[256,512]{1,0:T(8,128)}, f32[256,512]{1,0:T(8,128)S(1)}) custom-call(s32[1]{0:T(128)} %bitcast.me, bf16[536,1024]{1,0:T(8,128)(2,1)S(1)} %get-tuple-element.31.genes, bf16[1024,1024]{1,0:T(8,128)(2,1)S(1)} %bitcast.25, f32[512,128]{1,0:T(8,128)S(1)} %pair_fit.1.coef, f32[24,1024]{1,0:T(8,128)S(1)} %column_sums.1.stats.refs_0_), custom_call_target="tpu_custom_call" | custom-call | tf_op jit(solution)/shard_map/products/pallas_call | solution.py:89
  45.9 0.7 convert_element_type.30
  46.6 0.8 collective-permute-start.6
  47.4 2.1 %collective-permute-start.5 = (f32[24,1024]{1,0:T(8,128)S(1)}, f32[24,1024]{1,0:T(8,128)}, u32[]{:S(2)}, u32[]{:S(2)}) collective-permute-start(f32[24,1024]{1,0:T(8,128)S(1)} %column_sums.1.stats.refs_0_), channel_id=1, source_target_pairs={{0,2},{2,0},{1,3},{3,1},{4,6},{6,4},{5,7},{7,5},{8,10},{10,8},{9,1... | collective-permute-start | bytes 294920 | tf_op jit(solution)/shard_map/ppermute | solution.py:378
  49.5 1.8 %products.3 = (f32[256,512]{1,0:T(8,128)}, f32[256,512]{1,0:T(8,128)S(1)}) custom-call(s32[1]{0:T(128)} %bitcast.me, bf16[536,1024]{1,0:T(8,128)(2,1)S(1)} %get-tuple-element.31.genes, bf16[1024,1024]{1,0:T(8,128)(2,1)S(1)} %bitcast.26, f32[512,128]{1,0:T(8,128)S(1)} %pair_fit.1.coef, f32[24,1024]{1,0:T(8,128)S(1)} %column_sums.1.stats.refs_0_), custom_call_target="tpu_custom_call" | custom-call | tf_op jit(solution)/shard_map/products/pallas_call | solution.py:89
  51.3 0.9 %collective-permute-start.8 = (f16[256,512]{1,0:T(8,128)(2,1)S(1)}, f16[256,512]{1,0:T(8,128)(2,1)S(1)}, u32[]{:S(2)}, u32[]{:S(2)}) collective-permute-start(f16[256,512]{1,0:T(8,128)(2,1)S(1)} %convert_element_type.35), channel_id=1, source_target_pairs={{0,2},{2,0},{1,3},{3,1},{4,6},{6,4},{5,7},{7,5},{8,10},{10,8},{9,1... | collective-permute-start | bytes 786440 | tf_op jit(solution)/shard_map/ppermute | solution.py:378
  52.2 3.0 %cohort_fit.1 = (f32[512,128]{1,0:T(8,128)S(1)}, f32[24,128]{1,0:T(8,128)S(1)}) custom-call(f32[32,640]{1,0:T(8,128)S(1)} %copy-done.7, f32[32,640]{1,0:T(8,128)} %collective-permute-done.4.refs_1_), custom_call_target="tpu_custom_call" | custom-call | tf_op jit(solution)/shard_map/cohort_fit/pallas_call | solution.py:89
  55.4 17.1 %collective-permute-done.5.refs_1_ = f32[24,1024]{1,0:T(8,128)} collective-permute-done((f32[24,1024]{1,0:T(8,128)S(1)}, f32[24,1024]{1,0:T(8,128)}, u32[]{:S(2)}, u32[]{:S(2)}) %collective-permute-start.5) | collective-permute-done | bytes 98336 | tf_op jit(solution)/shard_map/ppermute | solution.py:378
  72.5 1.5 %base_ratio.2 = (f32[256,512]{1,0:T(8,128)S(1)}, f32[8,512]{1,0:T(8,128)S(1)}) custom-call(s32[1]{0:T(128)} %bitcast.me, f32[256,512]{1,0:T(8,128)S(1)} %copy-done.4, f32[512,128]{1,0:T(8,128)S(1)} %get-tuple-element.38.coef, f32[24,128]{1,0:T(8,128)S(1)} %get-tuple-element.39.inverse, f32[24,1024]{1,0:T(8,128)S(1)} %column_sums.1.stats.refs_0_, ...), custom_call_target="tpu_custom_call" | custom-call | tf_op jit(solution)/shard_map/base_ratio/pallas_call | solution.py:89
  74.0 1.5 %base_ratio.3 = (f32[256,512]{1,0:T(8,128)S(1)}, f32[8,512]{1,0:T(8,128)S(1)}) custom-call(s32[1]{0:T(128)} %bitcast.me, f32[256,512]{1,0:T(8,128)S(1)} %copy-done.5, f32[512,128]{1,0:T(8,128)S(1)} %get-tuple-element.38.coef, f32[24,128]{1,0:T(8,128)S(1)} %get-tuple-element.39.inverse, f32[24,1024]{1,0:T(8,128)S(1)} %column_sums.1.stats.refs_0_, ...), custom_call_target="tpu_custom_call" | custom-call | tf_op jit(solution)/shard_map/base_ratio/pallas_call | solution.py:89
  75.5 1.3 %multiply_bitcast_fusion.3 = (f32[128,1,1,512]{3,0,2,1:T(8,128)S(1)}, f32[128,512]{1,0:T(8,128)S(1)}) fusion(f32[256,512]{1,0:T(8,128)S(1)} %get-tuple-element.40, s32[]{:T(128)S(6)} %select_n.47, f32[512]{0:T(512)S(1)} %bitcast.33, f32[128]{0:T(128)S(1)} %get-tuple-element.49, f16[256,512]{1,0:T(8,128)(2,1)} %collective-permute-done.6, ...), kind=kLoop, calls=%fused_computation.10 | loop fusion | flops 1048576 | bytes 1313800 | tf_op jit(solution)/shard_map/stack | solution.py:456
  77.4 2.1 %collective-permute-start.9 = (f16[128,512]{1,0:T(8,128)(2,1)S(1)}, f16[128,512]{1,0:T(8,128)(2,1)S(1)}, u32[]{:S(2)}, u32[]{:S(2)}) collective-permute-start(f16[128,512]{1,0:T(8,128)(2,1)S(1)} %get-tuple-element.54), channel_id=1, source_target_pairs={{0,1},{1,0},{2,3},{3,2},{4,5},{5,4},{6,7},{7,6},{8,9},{9,8},{10,11... | collective-permute-start | bytes 393224 | tf_op jit(solution)/shard_map/ppermute | solution.py:378
  79.4 2.5 %collective-permute-done.7 = f16[128,512]{1,0:T(8,128)(2,1)S(1)} collective-permute-done((f16[128,512]{1,0:T(8,128)(2,1)S(1)}, f16[128,512]{1,0:T(8,128)(2,1)S(1)}, u32[]{:S(2)}, u32[]{:S(2)}) %collective-permute-start.7) | collective-permute-done | bytes 131104 | tf_op jit(solution)/shard_map/ppermute | solution.py:378
  82.0 1.3 %collective-permute-done.9 = f16[128,512]{1,0:T(8,128)(2,1)S(1)} collective-permute-done((f16[128,512]{1,0:T(8,128)(2,1)S(1)}, f16[128,512]{1,0:T(8,128)(2,1)S(1)}, u32[]{:S(2)}, u32[]{:S(2)}) %collective-permute-start.9) | collective-permute-done | bytes 131104 | tf_op jit(solution)/shard_map/ppermute | solution.py:378
  83.5 0.7 reshape.129
  84.2 1.3 %copy.8 = f32[128,4,2,256]{3,2,1,0:T(2,128)} copy(f32[128,4,2,256]{3,2,0,1:T(2,128)S(1)} %reshape.129) | data formatting | bytes 2097152 | tf_op jit(solution)/shard_map/reshape | solution.py:459
  (32 shorter events, 2.0 us)
Async XLA Ops:
  1.0 9.5 %collective-permute-start = (bf16[536,128]{1,0:T(8,128)(2,1)S(1)}, bf16[536,128]{1,0:T(8,128)(2,1)S(1)}, u32[]{:S(2)}, u32[]{:S(2)}) collective-permute-start(bf16[536,128]{1,0:T(8,128)(2,1)S(1)} %tall_design.1), channel_id=1, source_target_pairs={{0,1},{1,0},{4,5},{5,4},{8,9},{9,8},{12,13},{13,12},{2,3},{3,2},{6... | collective-permute-start | bytes 411656 | tf_op jit(solution)/shard_map/ppermute | solution.py:378
  4.1 8.0 %collective-permute-start.1 = (bf16[536,128]{1,0:T(8,128)(2,1)S(1)}, bf16[536,128]{1,0:T(8,128)(2,1)S(1)}, u32[]{:S(2)}, u32[]{:S(2)}) collective-permute-start(bf16[536,128]{1,0:T(8,128)(2,1)S(1)} %tall_design.1), channel_id=1, source_target_pairs={{0,8},{1,9},{4,12},{5,13},{8,0},{9,1},{12,4},{13,5},{2,10},{3,11},... | collective-permute-start | bytes 411656 | tf_op jit(solution)/shard_map/ppermute | solution.py:378
  5.6 6.5 %collective-permute-start.2 = (bf16[536,128]{1,0:T(8,128)(2,1)S(1)}, bf16[536,128]{1,0:T(8,128)(2,1)S(1)}, u32[]{:S(2)}, u32[]{:S(2)}) collective-permute-start(bf16[536,128]{1,0:T(8,128)(2,1)S(1)} %tall_design.1), channel_id=1, source_target_pairs={{0,9},{1,8},{4,13},{5,12},{8,1},{9,0},{12,5},{13,4},{2,11},{3,10},... | collective-permute-start | bytes 411656 | tf_op jit(solution)/shard_map/ppermute | solution.py:378
  12.1 31.5 %all-to-all-start = ((bf16[8,128,1024]{2,1,0:T(8,128)(2,1)}), bf16[8,128,1024]{2,1,0:T(8,128)(2,1)S(1)}, u32[]{:S(2)}, u32[]{:S(2)}) async-start(bf16[8,128,1024]{2,1,0:T(8,128)(2,1)} %smooth.1), calls=%async_computation | async-start | bytes 4194304 | tf_op jit(solution)/shard_map/all_to_all | solution.py:392
  15.8 2.1 %collective-permute-start.3 = (bf16[4,536,128]{2,1,0:T(8,128)(2,1)S(1)}, bf16[4,536,128]{2,1,0:T(8,128)(2,1)S(1)}, u32[]{:S(2)}, u32[]{:S(2)}) collective-permute-start(bf16[4,536,128]{2,1,0:T(8,128)(2,1)S(1)} %pad_maximum_fusion.1.blocks), channel_id=1, source_target_pairs={{0,4},{1,5},{4,0},{5,1},{8,12},{9,13},{12,8},{13,9},{2,6},{3,7},{6... | collective-permute-start | bytes 1646600 | tf_op jit(solution)/shard_map/ppermute | solution.py:378
  16.3 0.8 copy-start
  18.0 0.8 copy-start.2
  18.8 1.1 %copy-start.1 = (bf16[4,536,128]{2,1,0:T(8,128)(2,1)S(1)}, bf16[4,536,128]{2,1,0:T(8,128)(2,1)}, u32[]{:S(2)}) copy-start(bf16[4,536,128]{2,1,0:T(8,128)(2,1)} %copy-done) | copy-start | bytes 1646596
  19.8 1.1 %copy-start.3 = (bf16[4,536,128]{2,1,0:T(8,128)(2,1)S(1)}, bf16[4,536,128]{2,1,0:T(8,128)(2,1)}, u32[]{:S(2)}) copy-start(bf16[4,536,128]{2,1,0:T(8,128)(2,1)} %copy-done.2) | copy-start | bytes 1646596
  21.9 21.7 %copy-start.6 = (f32[32,640]{1,0:T(8,128)}, f32[32,640]{1,0:T(8,128)S(1)}, u32[]{:S(2)}) copy-start(f32[32,640]{1,0:T(8,128)S(1)} %get-tuple-element.36.moment.refs_0_) | copy-start | bytes 245764
  21.9 19.1 %collective-permute-start.4 = (f32[32,640]{1,0:T(8,128)S(1)}, f32[32,640]{1,0:T(8,128)}, u32[]{:S(2)}, u32[]{:S(2)}) collective-permute-start(f32[32,640]{1,0:T(8,128)S(1)} %get-tuple-element.36.moment.refs_0_), channel_id=1, source_target_pairs={{0,2},{2,0},{1,3},{3,1},{4,6},{6,4},{5,7},{7,5},{8,10},{10,8},{9,1... | collective-permute-start | bytes 245768 | tf_op jit(solution)/shard_map/ppermute | solution.py:378
  46.6 28.9 %collective-permute-start.6 = (f16[256,512]{1,0:T(8,128)(2,1)}, f16[256,512]{1,0:T(8,128)(2,1)}, u32[]{:S(2)}, u32[]{:S(2)}) collective-permute-start(f16[256,512]{1,0:T(8,128)(2,1)} %convert_element_type.30), channel_id=1, source_target_pairs={{0,2},{2,0},{1,3},{3,1},{4,6},{6,4},{5,7},{7,5},{8,10},{10,8},{9,1... | collective-permute-start | bytes 786440 | tf_op jit(solution)/shard_map/ppermute | solution.py:378
  47.4 25.0 %collective-permute-start.5 = (f32[24,1024]{1,0:T(8,128)S(1)}, f32[24,1024]{1,0:T(8,128)}, u32[]{:S(2)}, u32[]{:S(2)}) collective-permute-start(f32[24,1024]{1,0:T(8,128)S(1)} %column_sums.1.stats.refs_0_), channel_id=1, source_target_pairs={{0,2},{2,0},{1,3},{3,1},{4,6},{6,4},{5,7},{7,5},{8,10},{10,8},{9,1... | collective-permute-start | bytes 294920 | tf_op jit(solution)/shard_map/ppermute | solution.py:378
  49.5 2.7 %copy-start.7 = (f32[32,640]{1,0:T(8,128)S(1)}, f32[32,640]{1,0:T(8,128)}, u32[]{:S(2)}) copy-start(f32[32,640]{1,0:T(8,128)} %copy-done.6) | copy-start | bytes 245764
  49.5 23.0 %copy-start.4 = (f32[256,512]{1,0:T(8,128)S(1)}, f32[256,512]{1,0:T(8,128)}, u32[]{:S(2)}) copy-start(f32[256,512]{1,0:T(8,128)} %get-tuple-element.35.own) | copy-start | bytes 1572868
  51.3 22.7 %copy-start.5 = (f32[256,512]{1,0:T(8,128)S(1)}, f32[256,512]{1,0:T(8,128)}, u32[]{:S(2)}) copy-start(f32[256,512]{1,0:T(8,128)} %get-tuple-element.43.own) | copy-start | bytes 1572868
  51.3 25.6 %collective-permute-start.8 = (f16[256,512]{1,0:T(8,128)(2,1)S(1)}, f16[256,512]{1,0:T(8,128)(2,1)S(1)}, u32[]{:S(2)}, u32[]{:S(2)}) collective-permute-start(f16[256,512]{1,0:T(8,128)(2,1)S(1)} %convert_element_type.35), channel_id=1, source_target_pairs={{0,2},{2,0},{1,3},{3,1},{4,6},{6,4},{5,7},{7,5},{8,10},{10,8},{9,1... | collective-permute-start | bytes 786440 | tf_op jit(solution)/shard_map/ppermute | solution.py:378
  76.9 5.0 %collective-permute-start.7 = (f16[128,512]{1,0:T(8,128)(2,1)S(1)}, f16[128,512]{1,0:T(8,128)(2,1)S(1)}, u32[]{:S(2)}, u32[]{:S(2)}) collective-permute-start(f16[128,512]{1,0:T(8,128)(2,1)S(1)} %multiply_convert_fusion.1), channel_id=1, source_target_pairs={{0,1},{1,0},{2,3},{3,2},{4,5},{5,4},{6,7},{7,6},{8,9},{9,8},{10,11... | collective-permute-start | bytes 393224 | tf_op jit(solution)/shard_map/ppermute | solution.py:378
  77.4 6.0 %collective-permute-start.9 = (f16[128,512]{1,0:T(8,128)(2,1)S(1)}, f16[128,512]{1,0:T(8,128)(2,1)S(1)}, u32[]{:S(2)}, u32[]{:S(2)}) collective-permute-start(f16[128,512]{1,0:T(8,128)(2,1)S(1)} %get-tuple-element.54), channel_id=1, source_target_pairs={{0,1},{1,0},{2,3},{3,2},{4,5},{5,4},{6,7},{7,6},{8,9},{9,8},{10,11... | collective-permute-start | bytes 393224 | tf_op jit(solution)/shard_map/ppermute | solution.py:378

commit v8 on v7

--- a/solution.py
+++ b/solution.py
@@ -213,7 +213,7 @@
     spread = -(-rows // LANES) * LANES
     outs = (
         result((rows, 2 * count * subjects), blocks.dtype),
-        result((DPAD + 8, spread), jnp.float32),
+        pltpu.HBM((DPAD + 8, spread), jnp.float32),
     )
     kernel = functools.partial(moments_kernel, snps, slots)
     return call(kernel, "moments", outs, [me], [blocks, others], (), 2)
@@ -260,7 +260,7 @@
 def pair_fit(moment, snps, design):
     kernel = functools.partial(pair_kernel, snps, design)
     scratch = [pltpu.VMEM((LANES, snps), jnp.float32)]
-    return call(kernel, "pair_fit", result((snps, LANES), jnp.float32), [], [moment], scratch)
+    return call(kernel, "pair_fit", result((snps, LANES), jnp.float32), [], [moment], scratch, 1)
 
 
 def cohort_kernel(snps, design, *refs):
@@ -282,7 +282,7 @@
     kernel = functools.partial(cohort_kernel, snps, design)
     outs = (result((snps, LANES), jnp.float32), result((DPAD, LANES), jnp.float32))
     scratch = [pltpu.VMEM((LANES, snps), jnp.float32)]
-    return call(kernel, "cohort_fit", outs, [], parts, scratch)
+    return call(kernel, "cohort_fit", outs, [], parts, scratch, len(parts))
 
 
 def column_norm(sums, here):
@@ -406,7 +406,9 @@
     genes, moment = moments(blocks, others, slots, (vox * n_near + near)[None])
     pair_coef = pair_fit(moment, snps, design)
     moment_parts = [moment] + [permute_xor(moment, "far", j) for j in range(1, n_far)]
-    columns, moment_parts = lax.optimization_barrier((columns, moment_parts))
+    columns, pair_coef, moment_parts = lax.optimization_barrier(
+        (columns, pair_coef, moment_parts)
+    )
     stats = column_sums(genes, columns)
     stat_parts = [stats] + [permute_xor(stats, "far", j) for j in range(1, n_far)]
 
@@ -434,7 +436,10 @@
             genes, columns, pair_coef, stats, far[None], n_far, chunk * width, width
         )
         owns.append(own)
-        received.append(send([piece.astype(jnp.float16) for piece in pieces]))
+        pieces = [piece.astype(jnp.float16) for piece in pieces]
+        if chunk == 0:
+            pieces, stat_parts = lax.optimization_barrier((pieces, stat_parts))
+        received.append(send(pieces))
     coef, inverse = cohort_fit(moment_parts, snps, design)
     outs = []
     gate = None

time: 86 us -> 82.9 us (0.964)
  waiting for transfers between devices: 40.4 us -> 36.8 us
  local copies, waits for them, and re-layouts: 5.92 us -> 7.46 us
    ppermute x10, waiting for transfers between devices: 37.7 us -> 34.9 us  [permute_xor(): return lax.ppermute(value, axes, [(i, i ^ bits) for i in range(size)])]
    unnamed x16 -> x20, local copies, waits for them, and re-layouts: 3.72 us -> 5.26 us
  transfers between devices with their start and end apart: 11 -> 11, of which waited for: 7 -> 9; matrix products, arithmetic and copies ran while one was open for 2% -> 3% of each run, Pallas kernels for 18% -> 21%
where the time goes in v8:
time: 82.9 us; the launch traced here: 82.5 us
  waiting for transfers between devices  36.8 us (44%)
  Pallas kernels  18.8 us (23%)
  starting transfers between devices  16.5 us (20%)
  local copies, waits for them, and re-layouts  7.46 us (9%)
  other arithmetic  2.75 us (3%)
    ppermute x10, waiting for transfers between devices, permute_xor(): return lax.ppermute(value, axes, [(i, i ^ bits) for i in range(size)])  34.9 us
    ppermute x10, starting transfers between devices, permute_xor(): return lax.ppermute(value, axes, [(i, i ^ bits) for i in range(size)])  12.9 us
    pallas_call x8, Pallas kernels, call(): pl.pallas_call(kernel, out_shape=outs, in_specs=[IN_SMEM] * len(scalars)...  12.8 us
    unnamed x20, local copies, waits for them, and re-layouts  5.26 us
    pallas_call x1, Pallas kernels, smooth(): pl.pallas_call(functools.partial(smooth_kernel, group, planes, per_vox, p...  4.93 us
    all_to_all x1, starting transfers between devices, exchange(): value = lax.all_to_all(value, ('vox', 'near'), 0, 0, tiled=True)  3.6 us
    reshape x2, local copies, waits for them, and re-layouts, on_device(): return jnp.stack(outs, axis=2).reshape(panel, maps, per_vox, plane)  2.01 us
    all_to_all x1, waiting for transfers between devices, exchange(): value = lax.all_to_all(value, ('vox', 'near'), 0, 0, tiled=True)  1.93 us
  transfers between devices with their start and end apart: 11, of which 9 were waited for; matrix products, arithmetic and copies ran while one was open for 3% of the time, Pallas kernels for 21%

profile of v8, /device:TPU:0, one launch (start us, length us, event | category | flops | bytes accessed | tf_op | source)
XLA Modules:
  0.0 82.5 jit_solution(16533065029466073457)
XLA Ops:
  0.0 1.0 %tall_design.1 = bf16[536,128]{1,0:T(8,128)(2,1)S(1)} custom-call(bf16[128,512]{1,0:T(8,128)(2,1)} %genotypes.1, s32[1,128]{1,0:T(1,128)} %bitcast.35, bf16[16,128]{1,0:T(8,128)(2,1)} %bitcast.34), custom_call_target="tpu_custom_call" | custom-call | tf_op jit(solution)/shard_map/tall_design/pallas_call | solution.py:113
  1.0 3.1 %collective-permute-start = (bf16[536,128]{1,0:T(8,128)(2,1)S(1)}, bf16[536,128]{1,0:T(8,128)(2,1)S(1)}, u32[]{:S(2)}, u32[]{:S(2)}) collective-permute-start(bf16[536,128]{1,0:T(8,128)(2,1)S(1)} %tall_design.1), channel_id=1, source_target_pairs={{0,1},{1,0},{4,5},{5,4},{8,9},{9,8},{12,13},{13,12},{2,3},{3,2},{6... | collective-permute-start | bytes 411656 | tf_op jit(solution)/shard_map/ppermute | solution.py:378
  4.1 1.5 %collective-permute-start.1 = (bf16[536,128]{1,0:T(8,128)(2,1)S(1)}, bf16[536,128]{1,0:T(8,128)(2,1)S(1)}, u32[]{:S(2)}, u32[]{:S(2)}) collective-permute-start(bf16[536,128]{1,0:T(8,128)(2,1)S(1)} %tall_design.1), channel_id=1, source_target_pairs={{0,8},{1,9},{4,12},{5,13},{8,0},{9,1},{12,4},{13,5},{2,10},{3,11},... | collective-permute-start | bytes 411656 | tf_op jit(solution)/shard_map/ppermute | solution.py:378
  5.6 4.9 %smooth.1 = bf16[8,128,1024]{2,1,0:T(8,128)(2,1)} custom-call(bf16[128,32,256]{2,1,0:T(8,128)(2,1)} %bitcast.28, bf16[256,256]{1,0:T(8,128)(2,1)} %constant.35.clone.order, bf16[256,256]{1,0:T(8,128)(2,1)} %constant.36.clone.table), custom_call_target="tpu_custom_call" | custom-call | tf_op jit(solution)/shard_map/smooth/pallas_call | solution.py:168
  10.6 1.6 %collective-permute-done.1 = bf16[536,128]{1,0:T(8,128)(2,1)S(1)} collective-permute-done((bf16[536,128]{1,0:T(8,128)(2,1)S(1)}, bf16[536,128]{1,0:T(8,128)(2,1)S(1)}, u32[]{:S(2)}, u32[]{:S(2)}) %collective-permute-start.1) | collective-permute-done | bytes 137248 | tf_op jit(solution)/shard_map/ppermute | solution.py:378
  12.1 3.6 %all-to-all-start = ((bf16[8,128,1024]{2,1,0:T(8,128)(2,1)}), bf16[8,128,1024]{2,1,0:T(8,128)(2,1)S(1)}, u32[]{:S(2)}, u32[]{:S(2)}) async-start(bf16[8,128,1024]{2,1,0:T(8,128)(2,1)} %smooth.1), calls=%async_computation | async-start | bytes 4194304 | tf_op jit(solution)/shard_map/all_to_all | solution.py:392
  16.3 0.8 copy-done
  17.1 0.9 %collective-permute-done.3.others = bf16[4,536,128]{2,1,0:T(8,128)(2,1)S(1)} collective-permute-done((bf16[4,536,128]{2,1,0:T(8,128)(2,1)S(1)}, bf16[4,536,128]{2,1,0:T(8,128)(2,1)S(1)}, u32[]{:S(2)}, u32[]{:S(2)}) %collective-permute-start.3) | collective-permute-done | bytes 548896 | tf_op jit(solution)/shard_map/ppermute | solution.py:378
  18.0 0.8 copy-done.2
  18.8 1.0 %copy-done.1 = bf16[4,536,128]{2,1,0:T(8,128)(2,1)S(1)} copy-done((bf16[4,536,128]{2,1,0:T(8,128)(2,1)S(1)}, bf16[4,536,128]{2,1,0:T(8,128)(2,1)}, u32[]{:S(2)}) %copy-start.1) | copy-done | bytes 548888
  19.8 1.0 %copy-done.3 = bf16[4,536,128]{2,1,0:T(8,128)(2,1)S(1)} copy-done((bf16[4,536,128]{2,1,0:T(8,128)(2,1)S(1)}, bf16[4,536,128]{2,1,0:T(8,128)(2,1)}, u32[]{:S(2)}) %copy-start.3) | copy-done | bytes 548888
  20.9 1.7 %moments.1 = (bf16[536,1024]{1,0:T(8,128)(2,1)S(1)}, f32[32,640]{1,0:T(8,128)}) custom-call(s32[1]{0:T(128)} %bitcast.1.me, bf16[4,536,128]{2,1,0:T(8,128)(2,1)S(1)} %copy-done.1, bf16[4,536,128]{2,1,0:T(8,128)(2,1)S(1)} %copy-done.3), custom_call_target="tpu_custom_call" | custom-call | tf_op jit(solution)/shard_map/moments/pallas_call | solution.py:89
  22.6 2.6 %collective-permute-start.4 = (f32[32,640]{1,0:T(8,128)}, f32[32,640]{1,0:T(8,128)S(1)}, u32[]{:S(2)}, u32[]{:S(2)}) collective-permute-start(f32[32,640]{1,0:T(8,128)} %get-tuple-element.41.moment.refs_0_), channel_id=1, source_target_pairs={{0,2},{2,0},{1,3},{3,1},{4,6},{6,4},{5,7},{7,5},{8,10},{10,8},{9,1... | collective-permute-start | bytes 245768 | tf_op jit(solution)/shard_map/ppermute | solution.py:378
  25.2 0.9 %copy-done.6 = f32[32,640]{1,0:T(8,128)S(1)} copy-done((f32[32,640]{1,0:T(8,128)S(1)}, f32[32,640]{1,0:T(8,128)}, u32[]{:S(2)}) %copy-start.6) | copy-done | bytes 81944
  26.1 2.0 %pair_fit.1.coef = f32[512,128]{1,0:T(8,128)S(1)} custom-call(f32[32,640]{1,0:T(8,128)S(1)} %copy-done.6), custom_call_target="tpu_custom_call" | custom-call | tf_op jit(solution)/shard_map/pair_fit/pallas_call | solution.py:89
  28.1 12.9 %collective-permute-done.4.refs_1_ = f32[32,640]{1,0:T(8,128)S(1)} collective-permute-done((f32[32,640]{1,0:T(8,128)}, f32[32,640]{1,0:T(8,128)S(1)}, u32[]{:S(2)}, u32[]{:S(2)}) %collective-permute-start.4) | collective-permute-done | bytes 81952 | tf_op jit(solution)/shard_map/ppermute | solution.py:378
  41.7 1.9 %all-to-all-done = bf16[8,128,1024]{2,1,0:T(8,128)(2,1)S(1)} async-done(((bf16[8,128,1024]{2,1,0:T(8,128)(2,1)}), bf16[8,128,1024]{2,1,0:T(8,128)(2,1)S(1)}, u32[]{:S(2)}, u32[]{:S(2)}) %all-to-all-start) | async-done | bytes 2097184 | tf_op jit(solution)/shard_map/all_to_all | solution.py:392
  44.1 1.4 %collective-permute-start.5 = (f32[24,1024]{1,0:T(8,128)S(1)}, f32[24,1024]{1,0:T(8,128)}, u32[]{:S(2)}, u32[]{:S(2)}) collective-permute-start(f32[24,1024]{1,0:T(8,128)S(1)} %column_sums.1.stats.refs_0_), channel_id=1, source_target_pairs={{0,2},{2,0},{1,3},{3,1},{4,6},{6,4},{5,7},{7,5},{8,10},{10,8},{9,1... | collective-permute-start | bytes 294920 | tf_op jit(solution)/shard_map/ppermute | solution.py:378
  45.5 1.8 %products.2 = (f32[256,512]{1,0:T(8,128)}, f32[256,512]{1,0:T(8,128)S(1)}) custom-call(s32[1]{0:T(128)} %bitcast.me, bf16[536,1024]{1,0:T(8,128)(2,1)S(1)} %get-tuple-element.35.genes, bf16[1024,1024]{1,0:T(8,128)(2,1)S(1)} %bitcast.25, f32[512,128]{1,0:T(8,128)S(1)} %pair_fit.1.coef, f32[24,1024]{1,0:T(8,128)S(1)} %column_sums.1.stats.refs_0_), custom_call_target="tpu_custom_call" | custom-call | tf_op jit(solution)/shard_map/products/pallas_call | solution.py:89
  48.0 2.8 %collective-permute-done.5.refs_1_ = f32[24,1024]{1,0:T(8,128)} collective-permute-done((f32[24,1024]{1,0:T(8,128)S(1)}, f32[24,1024]{1,0:T(8,128)}, u32[]{:S(2)}, u32[]{:S(2)}) %collective-permute-start.5) | collective-permute-done | bytes 98336 | tf_op jit(solution)/shard_map/ppermute | solution.py:378
  51.2 1.8 %products.3 = (f32[256,512]{1,0:T(8,128)}, f32[256,512]{1,0:T(8,128)S(1)}) custom-call(s32[1]{0:T(128)} %bitcast.me, bf16[536,1024]{1,0:T(8,128)(2,1)S(1)} %get-tuple-element.35.genes, bf16[1024,1024]{1,0:T(8,128)(2,1)S(1)} %bitcast.26, f32[512,128]{1,0:T(8,128)S(1)} %pair_fit.1.coef, f32[24,1024]{1,0:T(8,128)S(1)} %column_sums.1.stats.refs_0_), custom_call_target="tpu_custom_call" | custom-call | tf_op jit(solution)/shard_map/products/pallas_call | solution.py:89
  53.0 2.6 %collective-permute-start.8 = (f16[256,512]{1,0:T(8,128)(2,1)S(1)}, f16[256,512]{1,0:T(8,128)(2,1)S(1)}, u32[]{:S(2)}, u32[]{:S(2)}) collective-permute-start(f16[256,512]{1,0:T(8,128)(2,1)S(1)} %convert_element_type.35), channel_id=1, source_target_pairs={{0,2},{2,0},{1,3},{3,1},{4,6},{6,4},{5,7},{7,5},{8,10},{10,8},{9,1... | collective-permute-start | bytes 786440 | tf_op jit(solution)/shard_map/ppermute | solution.py:378
  55.6 2.1 %cohort_fit.1 = (f32[512,128]{1,0:T(8,128)S(1)}, f32[24,128]{1,0:T(8,128)S(1)}) custom-call(f32[32,640]{1,0:T(8,128)S(1)} %copy-done.7, f32[32,640]{1,0:T(8,128)S(1)} %copy-done.9), custom_call_target="tpu_custom_call" | custom-call | tf_op jit(solution)/shard_map/cohort_fit/pallas_call | solution.py:89
  57.9 1.5 %base_ratio.2 = (f32[256,512]{1,0:T(8,128)S(1)}, f32[8,512]{1,0:T(8,128)S(1)}) custom-call(s32[1]{0:T(128)} %bitcast.me, f32[256,512]{1,0:T(8,128)S(1)} %copy-done.4, f32[512,128]{1,0:T(8,128)S(1)} %get-tuple-element.43.coef, f32[24,128]{1,0:T(8,128)S(1)} %get-tuple-element.44.inverse, f32[24,1024]{1,0:T(8,128)S(1)} %column_sums.1.stats.refs_0_, ...), custom_call_target="tpu_custom_call" | custom-call | tf_op jit(solution)/shard_map/base_ratio/pallas_call | solution.py:89
  59.4 1.5 %base_ratio.3 = (f32[256,512]{1,0:T(8,128)S(1)}, f32[8,512]{1,0:T(8,128)S(1)}) custom-call(s32[1]{0:T(128)} %bitcast.me, f32[256,512]{1,0:T(8,128)S(1)} %copy-done.5, f32[512,128]{1,0:T(8,128)S(1)} %get-tuple-element.43.coef, f32[24,128]{1,0:T(8,128)S(1)} %get-tuple-element.44.inverse, f32[24,1024]{1,0:T(8,128)S(1)} %column_sums.1.stats.refs_0_, ...), custom_call_target="tpu_custom_call" | custom-call | tf_op jit(solution)/shard_map/base_ratio/pallas_call | solution.py:89
  60.9 11.1 %collective-permute-done.6 = f16[256,512]{1,0:T(8,128)(2,1)} collective-permute-done((f16[256,512]{1,0:T(8,128)(2,1)}, f16[256,512]{1,0:T(8,128)(2,1)}, u32[]{:S(2)}, u32[]{:S(2)}) %collective-permute-start.6) | collective-permute-done | bytes 262176 | tf_op jit(solution)/shard_map/ppermute | solution.py:378
  72.1 1.3 %multiply_bitcast_fusion.3 = (f32[128,1,1,512]{3,0,2,1:T(8,128)S(1)}, f32[128,512]{1,0:T(8,128)S(1)}) fusion(f32[256,512]{1,0:T(8,128)S(1)} %get-tuple-element.48, s32[]{:T(128)S(6)} %select_n.47, f32[512]{0:T(512)S(1)} %bitcast.33, f32[128]{0:T(128)S(1)} %get-tuple-element.57, f16[256,512]{1,0:T(8,128)(2,1)} %collective-permute-done.6, ...), kind=kLoop, calls=%fused_computation.10 | loop fusion | flops 1048576 | bytes 1313800 | tf_op jit(solution)/shard_map/stack | solution.py:461
  73.5 1.3 %collective-permute-done.8 = f16[256,512]{1,0:T(8,128)(2,1)S(1)} collective-permute-done((f16[256,512]{1,0:T(8,128)(2,1)S(1)}, f16[256,512]{1,0:T(8,128)(2,1)S(1)}, u32[]{:S(2)}, u32[]{:S(2)}) %collective-permute-start.8) | collective-permute-done | bytes 262176 | tf_op jit(solution)/shard_map/ppermute | solution.py:378
  75.1 0.8 collective-permute-start.9
  76.0 2.9 %collective-permute-done.7 = f16[128,512]{1,0:T(8,128)(2,1)S(1)} collective-permute-done((f16[128,512]{1,0:T(8,128)(2,1)S(1)}, f16[128,512]{1,0:T(8,128)(2,1)S(1)}, u32[]{:S(2)}, u32[]{:S(2)}) %collective-permute-start.7) | collective-permute-done | bytes 131104 | tf_op jit(solution)/shard_map/ppermute | solution.py:378
  79.0 1.3 %collective-permute-done.9 = f16[128,512]{1,0:T(8,128)(2,1)S(1)} collective-permute-done((f16[128,512]{1,0:T(8,128)(2,1)S(1)}, f16[128,512]{1,0:T(8,128)(2,1)S(1)}, u32[]{:S(2)}, u32[]{:S(2)}) %collective-permute-start.9) | collective-permute-done | bytes 131104 | tf_op jit(solution)/shard_map/ppermute | solution.py:378
  81.1 1.3 %copy.8 = f32[128,4,2,256]{3,2,1,0:T(2,128)} copy(f32[128,4,2,256]{3,2,0,1:T(2,128)S(1)} %reshape.129) | data formatting | bytes 2097152 | tf_op jit(solution)/shard_map/reshape | solution.py:464
  (36 shorter events, 4.3 us)
Async XLA Ops:
  1.0 9.6 %collective-permute-start = (bf16[536,128]{1,0:T(8,128)(2,1)S(1)}, bf16[536,128]{1,0:T(8,128)(2,1)S(1)}, u32[]{:S(2)}, u32[]{:S(2)}) collective-permute-start(bf16[536,128]{1,0:T(8,128)(2,1)S(1)} %tall_design.1), channel_id=1, source_target_pairs={{0,1},{1,0},{4,5},{5,4},{8,9},{9,8},{12,13},{13,12},{2,3},{3,2},{6... | collective-permute-start | bytes 411656 | tf_op jit(solution)/shard_map/ppermute | solution.py:378
  4.1 8.0 %collective-permute-start.1 = (bf16[536,128]{1,0:T(8,128)(2,1)S(1)}, bf16[536,128]{1,0:T(8,128)(2,1)S(1)}, u32[]{:S(2)}, u32[]{:S(2)}) collective-permute-start(bf16[536,128]{1,0:T(8,128)(2,1)S(1)} %tall_design.1), channel_id=1, source_target_pairs={{0,8},{1,9},{4,12},{5,13},{8,0},{9,1},{12,4},{13,5},{2,10},{3,11},... | collective-permute-start | bytes 411656 | tf_op jit(solution)/shard_map/ppermute | solution.py:378
  5.6 6.5 %collective-permute-start.2 = (bf16[536,128]{1,0:T(8,128)(2,1)S(1)}, bf16[536,128]{1,0:T(8,128)(2,1)S(1)}, u32[]{:S(2)}, u32[]{:S(2)}) collective-permute-start(bf16[536,128]{1,0:T(8,128)(2,1)S(1)} %tall_design.1), channel_id=1, source_target_pairs={{0,9},{1,8},{4,13},{5,12},{8,1},{9,0},{12,5},{13,4},{2,11},{3,10},... | collective-permute-start | bytes 411656 | tf_op jit(solution)/shard_map/ppermute | solution.py:378
  12.1 31.5 %all-to-all-start = ((bf16[8,128,1024]{2,1,0:T(8,128)(2,1)}), bf16[8,128,1024]{2,1,0:T(8,128)(2,1)S(1)}, u32[]{:S(2)}, u32[]{:S(2)}) async-start(bf16[8,128,1024]{2,1,0:T(8,128)(2,1)} %smooth.1), calls=%async_computation | async-start | bytes 4194304 | tf_op jit(solution)/shard_map/all_to_all | solution.py:392
  15.8 2.1 %collective-permute-start.3 = (bf16[4,536,128]{2,1,0:T(8,128)(2,1)S(1)}, bf16[4,536,128]{2,1,0:T(8,128)(2,1)S(1)}, u32[]{:S(2)}, u32[]{:S(2)}) collective-permute-start(bf16[4,536,128]{2,1,0:T(8,128)(2,1)S(1)} %pad_maximum_fusion.1.blocks), channel_id=1, source_target_pairs={{0,4},{1,5},{4,0},{5,1},{8,12},{9,13},{12,8},{13,9},{2,6},{3,7},{6... | collective-permute-start | bytes 1646600 | tf_op jit(solution)/shard_map/ppermute | solution.py:378
  16.3 0.8 copy-start
  18.0 0.8 copy-start.2
  18.8 1.1 %copy-start.1 = (bf16[4,536,128]{2,1,0:T(8,128)(2,1)S(1)}, bf16[4,536,128]{2,1,0:T(8,128)(2,1)}, u32[]{:S(2)}) copy-start(bf16[4,536,128]{2,1,0:T(8,128)(2,1)} %copy-done) | copy-start | bytes 1646596
  19.8 1.1 %copy-start.3 = (bf16[4,536,128]{2,1,0:T(8,128)(2,1)S(1)}, bf16[4,536,128]{2,1,0:T(8,128)(2,1)}, u32[]{:S(2)}) copy-start(bf16[4,536,128]{2,1,0:T(8,128)(2,1)} %copy-done.2) | copy-start | bytes 1646596
  22.6 18.5 %collective-permute-start.4 = (f32[32,640]{1,0:T(8,128)}, f32[32,640]{1,0:T(8,128)S(1)}, u32[]{:S(2)}, u32[]{:S(2)}) collective-permute-start(f32[32,640]{1,0:T(8,128)} %get-tuple-element.41.moment.refs_0_), channel_id=1, source_target_pairs={{0,2},{2,0},{1,3},{3,1},{4,6},{6,4},{5,7},{7,5},{8,10},{10,8},{9,1... | collective-permute-start | bytes 245768 | tf_op jit(solution)/shard_map/ppermute | solution.py:378
  25.2 0.9 %copy-start.6 = (f32[32,640]{1,0:T(8,128)S(1)}, f32[32,640]{1,0:T(8,128)}, u32[]{:S(2)}) copy-start(f32[32,640]{1,0:T(8,128)} %get-tuple-element.41.moment.refs_0_) | copy-start | bytes 245764
  41.1 0.6 copy-start.8
  44.1 6.7 %collective-permute-start.5 = (f32[24,1024]{1,0:T(8,128)S(1)}, f32[24,1024]{1,0:T(8,128)}, u32[]{:S(2)}, u32[]{:S(2)}) collective-permute-start(f32[24,1024]{1,0:T(8,128)S(1)} %column_sums.1.stats.refs_0_), channel_id=1, source_target_pairs={{0,2},{2,0},{1,3},{3,1},{4,6},{6,4},{5,7},{7,5},{8,10},{10,8},{9,1... | collective-permute-start | bytes 294920 | tf_op jit(solution)/shard_map/ppermute | solution.py:378
  50.8 21.3 %collective-permute-start.6 = (f16[256,512]{1,0:T(8,128)(2,1)}, f16[256,512]{1,0:T(8,128)(2,1)}, u32[]{:S(2)}, u32[]{:S(2)}) collective-permute-start(f16[256,512]{1,0:T(8,128)(2,1)} %convert_element_type.30), channel_id=1, source_target_pairs={{0,2},{2,0},{1,3},{3,1},{4,6},{6,4},{5,7},{7,5},{8,10},{10,8},{9,1... | collective-permute-start | bytes 786440 | tf_op jit(solution)/shard_map/ppermute | solution.py:378
  51.2 4.4 %copy-start.7 = (f32[32,640]{1,0:T(8,128)S(1)}, f32[32,640]{1,0:T(8,128)}, u32[]{:S(2)}) copy-start(f32[32,640]{1,0:T(8,128)} %get-tuple-element.41.moment.refs_0_) | copy-start | bytes 245764
  51.2 4.4 %copy-start.9 = (f32[32,640]{1,0:T(8,128)S(1)}, f32[32,640]{1,0:T(8,128)}, u32[]{:S(2)}) copy-start(f32[32,640]{1,0:T(8,128)} %copy-done.8) | copy-start | bytes 245764
  51.2 6.7 %copy-start.4 = (f32[256,512]{1,0:T(8,128)S(1)}, f32[256,512]{1,0:T(8,128)}, u32[]{:S(2)}) copy-start(f32[256,512]{1,0:T(8,128)} %get-tuple-element.40.own) | copy-start | bytes 1572868
  52.9 6.5 %copy-start.5 = (f32[256,512]{1,0:T(8,128)S(1)}, f32[256,512]{1,0:T(8,128)}, u32[]{:S(2)}) copy-start(f32[256,512]{1,0:T(8,128)} %get-tuple-element.51.own) | copy-start | bytes 1572868
  53.0 21.8 %collective-permute-start.8 = (f16[256,512]{1,0:T(8,128)(2,1)S(1)}, f16[256,512]{1,0:T(8,128)(2,1)S(1)}, u32[]{:S(2)}, u32[]{:S(2)}) collective-permute-start(f16[256,512]{1,0:T(8,128)(2,1)S(1)} %convert_element_type.35), channel_id=1, source_target_pairs={{0,2},{2,0},{1,3},{3,1},{4,6},{6,4},{5,7},{7,5},{8,10},{10,8},{9,1... | collective-permute-start | bytes 786440 | tf_op jit(solution)/shard_map/ppermute | solution.py:378
  73.4 5.5 %collective-permute-start.7 = (f16[128,512]{1,0:T(8,128)(2,1)S(1)}, f16[128,512]{1,0:T(8,128)(2,1)S(1)}, u32[]{:S(2)}, u32[]{:S(2)}) collective-permute-start(f16[128,512]{1,0:T(8,128)(2,1)S(1)} %multiply_convert_fusion.1), channel_id=1, source_target_pairs={{0,1},{1,0},{2,3},{3,2},{4,5},{5,4},{6,7},{7,6},{8,9},{9,8},{10,11... | collective-permute-start | bytes 393224 | tf_op jit(solution)/shard_map/ppermute | solution.py:378
  75.1 5.1 %collective-permute-start.9 = (f16[128,512]{1,0:T(8,128)(2,1)S(1)}, f16[128,512]{1,0:T(8,128)(2,1)S(1)}, u32[]{:S(2)}, u32[]{:S(2)}) collective-permute-start(f16[128,512]{1,0:T(8,128)(2,1)S(1)} %get-tuple-element.62), channel_id=1, source_target_pairs={{0,1},{1,0},{2,3},{3,2},{4,5},{5,4},{6,7},{7,6},{8,9},{9,8},{10,11... | collective-permute-start | bytes 393224 | tf_op jit(solution)/shard_map/ppermute | solution.py:378

commit v9 on v8

--- a/solution.py
+++ b/solution.py
@@ -21,8 +21,6 @@
 VMEM_MOST = 56 * 2**20
 VMEM_BASE = 12 * 2**20
 SQUARE_ROW = 20
-CHUNKS = 2
-NARROW = 2.0**-4
 SCALE_LANE = DPAD
 STRIDE = 32
 
@@ -271,10 +269,12 @@
     lines[...] = jnp.zeros(lines.shape, jnp.float32)
     lines[:DPAD, :] = fitted * -scale
     lines[SCALE_LANE : SCALE_LANE + 1, :] = scale
-    for j in range(1, len(parts)):
+    for j in range(len(parts)):
         _, fit, own_scale = gene_fit(moment[j], snps, design, True)
-        lines[j * STRIDE : j * STRIDE + DPAD, :] = fit * scale
-        lines[SCALE_LANE + j : SCALE_LANE + j + 1, :] = scale / own_scale
+        lane = SCALE_LANE + 1 + j
+        lines[lane : lane + 1, :] = scale / own_scale
+        if j:
+            lines[j * STRIDE : j * STRIDE + DPAD, :] = fit * scale
     coef[...] = jnp.transpose(lines[...])
 
 
@@ -307,45 +307,48 @@
     return call(sums_kernel, "column_sums", outs, [], [genes, columns])
 
 
-def products_kernel(here, first, me, genes, columns, coef, stats, own, *refs):
-    far, held = refs[:-1], refs[-1]
-    snps, width = held.shape
-    held[...] = jnp.dot(
-        genes[:snps, :],
-        columns[:, first : first + width],
-        preferred_element_type=jnp.float32,
-    )
-    cross_image = stats[:, first : first + width]
+def products_kernel(here, offsets, far, near, genes, columns, coef, stats, *refs):
+    outs, held = list(refs[:-1]), refs[-1]
+    size = held.shape[0]
+    panel = outs[0].shape[0]
+    cross_image = stats[...]
     over = 1.0 / column_norm(cross_image, here)
-    size = own.shape[0]
-    own[...] = held[pl.ds(pl.multiple_of(me[0] * size, size), size), :]
-    for j, out in enumerate(far):
-        place = pl.multiple_of(jnp.bitwise_xor(me[0], j + 1) * size, size)
-        line = coef[pl.ds(place, size), :]
-        fit = jnp.dot(
-            line[:, :DPAD], cross_image, precision=HIGHEST, preferred_element_type=jnp.float32
+    for j in offsets:
+        block = pl.multiple_of(jnp.bitwise_xor(far[0], j) * size, size)
+        held[...] = jnp.dot(
+            genes[pl.ds(block, size), :], columns[...], preferred_element_type=jnp.float32
         )
-        scale = line[:, SCALE_LANE : SCALE_LANE + 1]
-        out[...] = (scale * held[pl.ds(place, size), :] - fit) * over
-
-
-def products(genes, columns, coef, stats, me, count, first, width):
-    rows, here = genes.shape
-    snps = rows - DPAD
-    size = snps // count
-    outs = (pltpu.HBM((size, width), jnp.float32),)
-    outs += (result((size, width), jnp.float32),) * (count - 1)
-    kernel = functools.partial(products_kernel, float(here), first)
-    scratch = [pltpu.VMEM((snps, width), jnp.float32)]
-    return call(kernel, "products", outs, [me], [genes, columns, coef, stats], scratch)
-
-
-def base_kernel(here, first, me, own, coef, inverse, *refs):
-    parts, (base, factors, stack) = refs[:-3], refs[-3:]
-    stats = [part[:, first : first + own.shape[1]] for part in parts]
+        for k in range(size // panel):
+            place = pl.multiple_of(jnp.bitwise_xor(near[0], k) * panel, panel)
+            sums = held[pl.ds(place, panel), :]
+            out = outs.pop(0)
+            if j == 0 and k == 0:
+                out[...] = sums
+                continue
+            line = coef[pl.ds(block + place, panel), :]
+            fit = jnp.dot(
+                line[:, :DPAD], cross_image, precision=HIGHEST, preferred_element_type=jnp.float32
+            )
+            out[...] = (line[:, SCALE_LANE : SCALE_LANE + 1] * sums - fit) * over
+
+
+def products(genes, columns, coef, stats, far, near, offsets, size, count):
+    here, width = columns.shape
+    panel = size // count
+    outs = [result((panel, width), jnp.float32) for _ in range(len(offsets) * count)]
+    if 0 in offsets:
+        outs[0] = pltpu.HBM((panel, width), jnp.float32)
+    kernel = functools.partial(products_kernel, float(here), tuple(offsets))
+    scratch = [pltpu.VMEM((size, width), jnp.float32)]
+    arrays = [genes, columns, coef, stats]
+    return call(kernel, "products", tuple(outs), [far, near], arrays, scratch)
+
+
+def base_half(here, line, inverse, stats, extra, factors, stack):
     row = lax.broadcasted_iota(jnp.int32, stats[0].shape, 0)
     total = tree_sum(stats)
-    cross_image = jnp.where(row < SQUARE_ROW, total, 0.0)
+    known = row < SQUARE_ROW
+    cross_image = jnp.where(known, total, 0.0)
     solved = jnp.dot(
         inverse[:, :DPAD], cross_image, precision=HIGHEST, preferred_element_type=jnp.float32
     )
@@ -353,24 +356,45 @@
         cross_image * solved, axis=0, keepdims=True
     )
     scale = lax.rsqrt(rss)
-    stack[...] = jnp.zeros(stack.shape, jnp.float32)
     stack[:DPAD, :] = cross_image
     factors[...] = jnp.zeros(factors.shape, jnp.float32)
-    for j in range(1, len(parts)):
-        stack[j * STRIDE : j * STRIDE + DPAD, :] = jnp.where(row < SQUARE_ROW, stats[j], 0.0)
-        factors[j : j + 1, :] = column_norm(stats[j], here) * scale
-    size = own.shape[0]
-    line = coef[pl.ds(pl.multiple_of(me[0] * size, size), size), :]
+    for j, stat in enumerate(stats):
+        factors[j : j + 1, :] = column_norm(stat, here) * scale
+        if j:
+            stack[j * STRIDE : j * STRIDE + DPAD, :] = jnp.where(known, stat, 0.0)
     terms = jnp.dot(line, stack[...], precision=HIGHEST, preferred_element_type=jnp.float32)
-    base[...] = (line[:, SCALE_LANE : SCALE_LANE + 1] * own[...] + terms) * scale
-
-
-def base_ratio(me, own, coef, inverse, parts, here, first):
-    size, width = own.shape
-    outs = (result((size, width), jnp.float32), result((8, width), jnp.float32))
-    kernel = functools.partial(base_kernel, float(here), first)
+    return (terms + extra) * scale
+
+
+def base_kernel(here, place, own, coef, inverse, pair_coef, *refs):
+    parts, (home, home_factors, away, away_factors, stack) = refs[:-5], refs[-5:]
+    count = len(parts) // 2
+    stack[...] = jnp.zeros(stack.shape, jnp.float32)
+    panel = own.shape[0]
+    rows = pl.ds(pl.multiple_of(place[0] * panel, panel), panel)
+    line = coef[rows, :]
+    stats = [part[...] for part in parts[:count]]
+    extra = line[:, SCALE_LANE : SCALE_LANE + 1] * own[...]
+    home[...] = base_half(here, line, inverse, stats, extra, home_factors, stack)
+    stats = [part[...] for part in parts[count:]]
+    row = lax.broadcasted_iota(jnp.int32, stats[0].shape, 0)
+    extra = jnp.dot(
+        pair_coef[rows, :][:, :DPAD],
+        jnp.where(row < SQUARE_ROW, stats[0], 0.0),
+        precision=HIGHEST,
+        preferred_element_type=jnp.float32,
+    )
+    extra = line[:, SCALE_LANE + 1 : SCALE_LANE + 2] * extra
+    away[...] = base_half(here, line, inverse, stats, extra, away_factors, stack)
+
+
+def base_ratio(place, own, coef, inverse, pair_coef, parts, here):
+    panel, width = own.shape
+    outs = (result((panel, width), jnp.float32), result((8, width), jnp.float32)) * 2
+    kernel = functools.partial(base_kernel, float(here))
     scratch = [pltpu.VMEM((LANES, width), jnp.float32)]
-    return call(kernel, "base_ratio", outs, [me], [own, coef, inverse, *parts], scratch, 1)
+    arrays = [own, coef, inverse, pair_coef, *parts]
+    return call(kernel, "base_ratio", outs, [place], arrays, scratch, 1)
 
 
 def permute_xor(value, axes, bits):
@@ -406,8 +430,9 @@
     genes, moment = moments(blocks, others, slots, (vox * n_near + near)[None])
     pair_coef = pair_fit(moment, snps, design)
     moment_parts = [moment] + [permute_xor(moment, "far", j) for j in range(1, n_far)]
-    columns, pair_coef, moment_parts = lax.optimization_barrier(
-        (columns, pair_coef, moment_parts)
+    coef, inverse = cohort_fit(moment_parts, snps, design)
+    columns, pair_coef, coef, inverse = lax.optimization_barrier(
+        (columns, pair_coef, coef, inverse)
     )
     stats = column_sums(genes, columns)
     stat_parts = [stats] + [permute_xor(stats, "far", j) for j in range(1, n_far)]
@@ -415,53 +440,42 @@
     size = snps // n_far
     panel = size // n_near
     freedom = float(here * n_far - design - 1)
-
-    def send(pieces):
-        return [permute_xor(pieces[j - 1], "far", j) for j in range(1, n_far)]
-
-    def panel_stats(index, coef, base, factors, pieces):
-        first = index * panel
-        line = lax.dynamic_slice_in_dim(coef, far * size + first, panel, 0)
-        ratio = lax.dynamic_slice_in_dim(base, first, panel, 0)
-        for j in range(1, n_far):
-            piece = lax.dynamic_slice_in_dim(pieces[j - 1], first, panel, 0)
-            weight = line[:, SCALE_LANE + j, None] * factors[None, j]
-            ratio = ratio + piece.astype(jnp.float32) * weight
+    line = ("far", "near")
+    where = [far[None], near[None]]
+
+    def shrink(pieces):
+        return [piece.astype(jnp.float16) for piece in pieces]
+
+    sent = products(
+        genes, columns, pair_coef, stats, *where, list(range(1, n_far)), size, n_near
+    )
+    sent = shrink(sent)
+    sent, stat_parts = lax.optimization_barrier((sent, stat_parts))
+    own, *rest = products(genes, columns, pair_coef, stats, *where, [0], size, n_near)
+    sent = [own, *shrink(rest), *sent]
+    pieces = [None] + [permute_xor(sent[k], line, k) for k in range(1, n_far * n_near)]
+    away_parts = permute_xor(jnp.stack(stat_parts), "near", 1)
+    away_parts = [away_parts[j] for j in range(n_far)]
+
+    place = far * n_near + near
+    columns_scale = lax.dynamic_slice_in_dim(coef, place * panel, panel, 0)
+
+    home, home_factors, away, away_factors = base_ratio(
+        place[None], own, coef, inverse, pair_coef, stat_parts + away_parts, here
+    )
+
+    def t_of(ratio, factors, offset):
+        for j in range(n_far):
+            piece = pieces[j * n_near + offset]
+            if piece is not None:
+                weight = columns_scale[:, SCALE_LANE + 1 + j, None] * factors[None, j]
+                ratio = ratio + piece.astype(jnp.float32) * weight
         return ratio * jnp.sqrt(freedom / (1.0 - ratio * ratio))
 
-    owns, received = [], []
-    width = columns.shape[1] // CHUNKS
-    for chunk in range(CHUNKS):
-        own, *pieces = products(
-            genes, columns, pair_coef, stats, far[None], n_far, chunk * width, width
-        )
-        owns.append(own)
-        pieces = [piece.astype(jnp.float16) for piece in pieces]
-        if chunk == 0:
-            pieces, stat_parts = lax.optimization_barrier((pieces, stat_parts))
-        received.append(send(pieces))
-    coef, inverse = cohort_fit(moment_parts, snps, design)
-    outs = []
-    gate = None
-    for chunk in range(CHUNKS):
-        base, factors = base_ratio(
-            far[None], owns[chunk], coef, inverse, stat_parts, here, chunk * width
-        )
-        if gate is not None:
-            base, gate = lax.optimization_barrier((base, gate))
-            outs[-1][0] = gate
-        pieces = received[chunk]
-        gate = panel_stats(jnp.bitwise_xor(near, 1), coef, base, factors, pieces)
-        outs.append([gate, panel_stats(near, coef, base, factors, pieces)])
-    outs = [
-        (permute_xor((away * NARROW).astype(jnp.float16), "near", 1), home) for away, home in outs
-    ]
-    outs = [(away.astype(jnp.float32) * (1.0 / NARROW), home) for away, home in outs]
-    outs = [
-        jnp.where(near == 0, jnp.stack([home, away], 1), jnp.stack([away, home], 1))
-        for away, home in outs
-    ]
-    return jnp.stack(outs, axis=2).reshape(panel, maps, per_vox, plane)
+    home = t_of(home, home_factors, 0)
+    away = t_of(away, away_factors, 1)
+    both = jnp.where(near == 0, jnp.stack([home, away], 1), jnp.stack([away, home], 1))
+    return both.reshape(panel, maps, per_vox, plane)
 
 
 def solution(mesh):

time: 82.9 us -> 86 us (1.037)
  the two profiles are of different devices: /device:TPU:0 before, /device:TPU:20 now
where the time goes in v9:
time: 86 us; the launch traced here: 85.4 us
  waiting for transfers between devices  38.6 us (45%)
  Pallas kernels  17.9 us (21%)
  starting transfers between devices  15 us (17%)
  local copies, waits for them, and re-layouts  9.76 us (11%)
  other arithmetic  3.99 us (5%)
    ppermute x10, waiting for transfers between devices, permute_xor(): return lax.ppermute(value, axes, [(i, i ^ bits) for i in range(size)])  38.6 us
    pallas_call x7, Pallas kernels, call(): pl.pallas_call(kernel, out_shape=outs, in_specs=[IN_SMEM] * len(scalars)...  12 us
    ppermute x10, starting transfers between devices, permute_xor(): return lax.ppermute(value, axes, [(i, i ^ bits) for i in range(size)])  11 us
    unnamed x24, local copies, waits for them, and re-layouts  6.97 us
    pallas_call x1, Pallas kernels, smooth(): pl.pallas_call(functools.partial(smooth_kernel, group, planes, per_vox, p...  4.94 us
    all_to_all x1, starting transfers between devices, exchange(): value = lax.all_to_all(value, ('vox', 'near'), 0, 0, tiled=True)  4.03 us
  transfers between devices with their start and end apart: 11, of which 8 were waited for; matrix products, arithmetic and copies ran while one was open for 3% of the time, Pallas kernels for 19%

profile of v9, /device:TPU:20, one launch (start us, length us, event | category | flops | bytes accessed | tf_op | source)
XLA Modules:
  0.0 85.4 jit_solution(16843831378404968094)
XLA Ops:
  0.0 1.0 %tall_design.1 = bf16[536,128]{1,0:T(8,128)(2,1)S(1)} custom-call(bf16[128,512]{1,0:T(8,128)(2,1)} %genotypes.1, s32[1,128]{1,0:T(1,128)} %bitcast.40, bf16[16,128]{1,0:T(8,128)(2,1)} %bitcast.39), custom_call_target="tpu_custom_call" | custom-call | tf_op jit(solution)/shard_map/tall_design/pallas_call | solution.py:111
  1.0 1.6 %collective-permute-start = (bf16[536,128]{1,0:T(8,128)(2,1)S(1)}, bf16[536,128]{1,0:T(8,128)(2,1)S(1)}, u32[]{:S(2)}, u32[]{:S(2)}) collective-permute-start(bf16[536,128]{1,0:T(8,128)(2,1)S(1)} %tall_design.1), channel_id=1, source_target_pairs={{0,1},{1,0},{4,5},{5,4},{8,9},{9,8},{12,13},{13,12},{2,3},{3,2},{6... | collective-permute-start | bytes 411656 | tf_op jit(solution)/shard_map/ppermute | solution.py:402
  3.2 1.4 %collective-permute-start.2 = (bf16[536,128]{1,0:T(8,128)(2,1)S(1)}, bf16[536,128]{1,0:T(8,128)(2,1)S(1)}, u32[]{:S(2)}, u32[]{:S(2)}) collective-permute-start(bf16[536,128]{1,0:T(8,128)(2,1)S(1)} %tall_design.1), channel_id=1, source_target_pairs={{0,9},{1,8},{4,13},{5,12},{8,1},{9,0},{12,5},{13,4},{2,11},{3,10},... | collective-permute-start | bytes 411656 | tf_op jit(solution)/shard_map/ppermute | solution.py:402
  4.6 4.9 %smooth.1 = bf16[8,128,1024]{2,1,0:T(8,128)(2,1)} custom-call(bf16[128,32,256]{2,1,0:T(8,128)(2,1)} %bitcast.32, bf16[256,256]{1,0:T(8,128)(2,1)} %constant.27.clone.order, bf16[256,256]{1,0:T(8,128)(2,1)} %constant.28.clone.table), custom_call_target="tpu_custom_call" | custom-call | tf_op jit(solution)/shard_map/smooth/pallas_call | solution.py:166
  9.5 1.2 %collective-permute-done.1 = bf16[536,128]{1,0:T(8,128)(2,1)S(1)} collective-permute-done((bf16[536,128]{1,0:T(8,128)(2,1)S(1)}, bf16[536,128]{1,0:T(8,128)(2,1)S(1)}, u32[]{:S(2)}, u32[]{:S(2)}) %collective-permute-start.1) | collective-permute-done | bytes 137248 | tf_op jit(solution)/shard_map/ppermute | solution.py:402
  10.7 4.0 %all-to-all-start = ((bf16[8,128,1024]{2,1,0:T(8,128)(2,1)}), bf16[8,128,1024]{2,1,0:T(8,128)(2,1)S(1)}, u32[]{:S(2)}, u32[]{:S(2)}) async-start(bf16[8,128,1024]{2,1,0:T(8,128)(2,1)} %smooth.1), calls=%async_computation | async-start | bytes 4194304 | tf_op jit(solution)/shard_map/all_to_all | solution.py:416
  15.0 0.8 copy-done
  15.8 1.0 %collective-permute-done.3.others = bf16[4,536,128]{2,1,0:T(8,128)(2,1)S(1)} collective-permute-done((bf16[4,536,128]{2,1,0:T(8,128)(2,1)S(1)}, bf16[4,536,128]{2,1,0:T(8,128)(2,1)S(1)}, u32[]{:S(2)}, u32[]{:S(2)}) %collective-permute-start.3) | collective-permute-done | bytes 548896 | tf_op jit(solution)/shard_map/ppermute | solution.py:402
  16.8 0.8 copy-done.4
  17.6 1.0 %copy-done.1 = bf16[4,536,128]{2,1,0:T(8,128)(2,1)S(1)} copy-done((bf16[4,536,128]{2,1,0:T(8,128)(2,1)S(1)}, bf16[4,536,128]{2,1,0:T(8,128)(2,1)}, u32[]{:S(2)}) %copy-start.1) | copy-done | bytes 548888
  18.7 1.0 %copy-done.5 = bf16[4,536,128]{2,1,0:T(8,128)(2,1)S(1)} copy-done((bf16[4,536,128]{2,1,0:T(8,128)(2,1)S(1)}, bf16[4,536,128]{2,1,0:T(8,128)(2,1)}, u32[]{:S(2)}) %copy-start.5) | copy-done | bytes 548888
  19.7 1.7 %moments.1 = (bf16[536,1024]{1,0:T(8,128)(2,1)S(1)}, f32[32,640]{1,0:T(8,128)}) custom-call(s32[1]{0:T(128)} %bitcast.3.me, bf16[4,536,128]{2,1,0:T(8,128)(2,1)S(1)} %copy-done.1, bf16[4,536,128]{2,1,0:T(8,128)(2,1)S(1)} %copy-done.5), custom_call_target="tpu_custom_call" | custom-call | tf_op jit(solution)/shard_map/moments/pallas_call | solution.py:87
  21.8 0.9 %copy-done.7 = f32[32,640]{1,0:T(8,128)S(1)} copy-done((f32[32,640]{1,0:T(8,128)S(1)}, f32[32,640]{1,0:T(8,128)}, u32[]{:S(2)}) %copy-start.7) | copy-done | bytes 81944
  22.7 2.0 %pair_fit.1.coef.pair_coef = f32[512,128]{1,0:T(8,128)S(1)} custom-call(f32[32,640]{1,0:T(8,128)S(1)} %copy-done.7), custom_call_target="tpu_custom_call" | custom-call | tf_op jit(solution)/shard_map/pair_fit/pallas_call | solution.py:87
  24.7 15.8 %collective-permute-done.4.refs_1_ = f32[32,640]{1,0:T(8,128)S(1)} collective-permute-done((f32[32,640]{1,0:T(8,128)}, f32[32,640]{1,0:T(8,128)S(1)}, u32[]{:S(2)}, u32[]{:S(2)}) %collective-permute-start.4) | collective-permute-done | bytes 81952 | tf_op jit(solution)/shard_map/ppermute | solution.py:402
  40.5 2.2 %cohort_fit.1 = (f32[512,128]{1,0:T(8,128)S(1)}, f32[24,128]{1,0:T(8,128)S(1)}) custom-call(f32[32,640]{1,0:T(8,128)S(1)} %copy-done.7, f32[32,640]{1,0:T(8,128)S(1)} %collective-permute-done.4.refs_1_), custom_call_target="tpu_custom_call" | custom-call | tf_op jit(solution)/shard_map/cohort_fit/pallas_call | solution.py:87
  44.5 1.5 %products.3 = (f32[128,1024]{1,0:T(8,128)S(1)}, f32[128,1024]{1,0:T(8,128)S(1)}) custom-call(s32[1]{0:T(128)} %bitcast.1.far, s32[1]{0:T(128)} %bitcast.2.near, bf16[536,1024]{1,0:T(8,128)(2,1)S(1)} %get-tuple-element.34.genes, bf16[1024,1024]{1,0:T(8,128)(2,1)S(1)} %bitcast.27, f32[512,128]{1,0:T(8,128)S(1)} %pair_fit.1.coef.pair_coef, ...), custom_call_target="tpu_custom_call" | custom-call | tf_op jit(solution)/shard_map/products/pallas_call | solution.py:87
  47.5 2.6 %collective-permute-done.5.refs_1_ = f32[24,1024]{1,0:T(8,128)} collective-permute-done((f32[24,1024]{1,0:T(8,128)S(1)}, f32[24,1024]{1,0:T(8,128)}, u32[]{:S(2)}, u32[]{:S(2)}) %collective-permute-start.5) | collective-permute-done | bytes 98336 | tf_op jit(solution)/shard_map/ppermute | solution.py:402
  50.1 1.6 %pad_maximum_fusion.1 = f32[2,24,1024]{2,1,0:T(8,128)} fusion(f32[1,24,1024]{2,1,0:T(8,128)} %bitcast.13, f32[1,24,1024]{2,1,0:T(8,128)S(1)} %bitcast.29), kind=kLoop, calls=%fused_computation.4 | loop fusion | flops 49152 | bytes 393216 | tf_op jit(solution)/shard_map/stack | solution.py:457
  51.7 3.3 %collective-permute-start.6 = (f32[2,24,1024]{2,1,0:T(8,128)}, f32[2,24,1024]{2,1,0:T(8,128)}, u32[]{:S(2)}, u32[]{:S(2)}) collective-permute-start(f32[2,24,1024]{2,1,0:T(8,128)} %pad_maximum_fusion.1), channel_id=1, source_target_pairs={{0,1},{1,0},{2,3},{3,2},{4,5},{5,4},{6,7},{7,6},{8,9},{9,8},{10,11... | collective-permute-start | bytes 589832 | tf_op jit(solution)/shard_map/ppermute | solution.py:402
  55.0 1.6 %products.2 = (f32[128,1024]{1,0:T(8,128)}, f32[128,1024]{1,0:T(8,128)S(1)}) custom-call(s32[1]{0:T(128)} %bitcast.1.far, s32[1]{0:T(128)} %bitcast.2.near, bf16[536,1024]{1,0:T(8,128)(2,1)S(1)} %get-tuple-element.34.genes, bf16[1024,1024]{1,0:T(8,128)(2,1)S(1)} %bitcast.28, f32[512,128]{1,0:T(8,128)S(1)} %pair_fit.1.coef.pair_coef, ...), custom_call_target="tpu_custom_call" | custom-call | tf_op jit(solution)/shard_map/products/pallas_call | solution.py:87
  56.9 0.9 %collective-permute-start.7 = (f16[128,1024]{1,0:T(8,128)(2,1)S(1)}, f16[128,1024]{1,0:T(8,128)(2,1)S(1)}, u32[]{:S(2)}, u32[]{:S(2)}) collective-permute-start(f16[128,1024]{1,0:T(8,128)(2,1)S(1)} %copy-done.11), channel_id=1, source_target_pairs={{0,2},{1,3},{2,0},{3,1},{4,6},{5,7},{6,4},{7,5},{8,10},{9,11},{10,... | collective-permute-start | bytes 786440 | tf_op jit(solution)/shard_map/ppermute | solution.py:402
  57.7 2.6 %collective-permute-start.9 = (f16[128,1024]{1,0:T(8,128)(2,1)S(1)}, f16[128,1024]{1,0:T(8,128)(2,1)S(1)}, u32[]{:S(2)}, u32[]{:S(2)}) collective-permute-start(f16[128,1024]{1,0:T(8,128)(2,1)S(1)} %copy-done.10), channel_id=1, source_target_pairs={{0,3},{1,2},{2,1},{3,0},{4,7},{5,6},{6,5},{7,4},{8,11},{9,10},{10,... | collective-permute-start | bytes 786440 | tf_op jit(solution)/shard_map/ppermute | solution.py:402
  60.4 2.9 %collective-permute-done.6 = f32[2,24,1024]{2,1,0:T(8,128)} collective-permute-done((f32[2,24,1024]{2,1,0:T(8,128)}, f32[2,24,1024]{2,1,0:T(8,128)}, u32[]{:S(2)}, u32[]{:S(2)}) %collective-permute-start.6) | collective-permute-done | bytes 196640 | tf_op jit(solution)/shard_map/ppermute | solution.py:402
  63.3 1.0 %slice_bitcast_fusion = (f32[24,1024]{1,0:T(8,128)S(1)}, f32[24,1024]{1,0:T(8,128)S(1)}) fusion(f32[2,24,1024]{2,1,0:T(8,128)} %collective-permute-done.6), kind=kLoop, calls=%fused_computation.5 | loop fusion | bytes 393216 | tf_op jit(solution)/shard_map/squeeze | solution.py:458
  64.3 1.0 %copy-done.6 = f32[128,1024]{1,0:T(8,128)S(1)} copy-done((f32[128,1024]{1,0:T(8,128)S(1)}, f32[128,1024]{1,0:T(8,128)}, u32[]{:S(2)}) %copy-start.6) | copy-done | bytes 524312
  65.3 2.5 %base_ratio.1 = (f32[128,1024]{1,0:T(8,128)S(1)}, f32[8,1024]{1,0:T(8,128)S(1)}, f32[128,1024]{1,0:T(8,128)S(1)}, f32[8,1024]{1,0:T(8,128)S(1)}) custom-call(s32[1]{0:T(128)} %bitcast.place, f32[128,1024]{1,0:T(8,128)S(1)} %copy-done.6, f32[512,128]{1,0:T(8,128)S(1)} %copy-done.3, f32[24,128]{1,0:T(8,128)S(1)} %copy-done.9, ...), custom_call_target="tpu_custom_call" | custom-call | tf_op jit(solution)/shard_map/base_ratio/pallas_call | solution.py:87
  67.8 3.7 %collective-permute-done.8 = f16[128,1024]{1,0:T(8,128)(2,1)S(1)} collective-permute-done((f16[128,1024]{1,0:T(8,128)(2,1)S(1)}, f16[128,1024]{1,0:T(8,128)(2,1)S(1)}, u32[]{:S(2)}, u32[]{:S(2)}) %collective-permute-start.8) | collective-permute-done | bytes 262176 | tf_op jit(solution)/shard_map/ppermute | solution.py:402
  71.5 1.6 %collective-permute-done.7 = f16[128,1024]{1,0:T(8,128)(2,1)S(1)} collective-permute-done((f16[128,1024]{1,0:T(8,128)(2,1)S(1)}, f16[128,1024]{1,0:T(8,128)(2,1)S(1)}, u32[]{:S(2)}, u32[]{:S(2)}) %collective-permute-start.7) | collective-permute-done | bytes 262176 | tf_op jit(solution)/shard_map/ppermute | solution.py:402
  73.1 9.8 %collective-permute-done.9 = f16[128,1024]{1,0:T(8,128)(2,1)S(1)} collective-permute-done((f16[128,1024]{1,0:T(8,128)(2,1)S(1)}, f16[128,1024]{1,0:T(8,128)(2,1)S(1)}, u32[]{:S(2)}, u32[]{:S(2)}) %collective-permute-start.9) | collective-permute-done | bytes 262176 | tf_op jit(solution)/shard_map/ppermute | solution.py:402
  82.9 0.7 multiply_bitcast_fusion.1
  84.1 1.3 %copy.8 = f32[128,4,2,256]{3,2,1,0:T(2,128)} copy(f32[128,4,2,256]{0,3,2,1:T(8,128)S(1)} %bitcast.31) | data formatting | bytes 2097152 | tf_op jit(solution)/shard_map/jit(_where)/select_n | solution.py:477
  (36 shorter events, 5.1 us)
Async XLA Ops:
  1.0 8.5 %collective-permute-start = (bf16[536,128]{1,0:T(8,128)(2,1)S(1)}, bf16[536,128]{1,0:T(8,128)(2,1)S(1)}, u32[]{:S(2)}, u32[]{:S(2)}) collective-permute-start(bf16[536,128]{1,0:T(8,128)(2,1)S(1)} %tall_design.1), channel_id=1, source_target_pairs={{0,1},{1,0},{4,5},{5,4},{8,9},{9,8},{12,13},{13,12},{2,3},{3,2},{6... | collective-permute-start | bytes 411656 | tf_op jit(solution)/shard_map/ppermute | solution.py:402
  2.7 8.0 %collective-permute-start.1 = (bf16[536,128]{1,0:T(8,128)(2,1)S(1)}, bf16[536,128]{1,0:T(8,128)(2,1)S(1)}, u32[]{:S(2)}, u32[]{:S(2)}) collective-permute-start(bf16[536,128]{1,0:T(8,128)(2,1)S(1)} %tall_design.1), channel_id=1, source_target_pairs={{0,8},{1,9},{4,12},{5,13},{8,0},{9,1},{12,4},{13,5},{2,10},{3,11},... | collective-permute-start | bytes 411656 | tf_op jit(solution)/shard_map/ppermute | solution.py:402
  3.2 7.5 %collective-permute-start.2 = (bf16[536,128]{1,0:T(8,128)(2,1)S(1)}, bf16[536,128]{1,0:T(8,128)(2,1)S(1)}, u32[]{:S(2)}, u32[]{:S(2)}) collective-permute-start(bf16[536,128]{1,0:T(8,128)(2,1)S(1)} %tall_design.1), channel_id=1, source_target_pairs={{0,9},{1,8},{4,13},{5,12},{8,1},{9,0},{12,5},{13,4},{2,11},{3,10},... | collective-permute-start | bytes 411656 | tf_op jit(solution)/shard_map/ppermute | solution.py:402
  10.7 33.3 %all-to-all-start = ((bf16[8,128,1024]{2,1,0:T(8,128)(2,1)}), bf16[8,128,1024]{2,1,0:T(8,128)(2,1)S(1)}, u32[]{:S(2)}, u32[]{:S(2)}) async-start(bf16[8,128,1024]{2,1,0:T(8,128)(2,1)} %smooth.1), calls=%async_computation | async-start | bytes 4194304 | tf_op jit(solution)/shard_map/all_to_all | solution.py:416
  14.8 2.0 %collective-permute-start.3 = (bf16[4,536,128]{2,1,0:T(8,128)(2,1)S(1)}, bf16[4,536,128]{2,1,0:T(8,128)(2,1)S(1)}, u32[]{:S(2)}, u32[]{:S(2)}) collective-permute-start(bf16[4,536,128]{2,1,0:T(8,128)(2,1)S(1)} %pad_maximum_fusion.blocks), channel_id=1, source_target_pairs={{0,4},{1,5},{4,0},{5,1},{8,12},{9,13},{12,8},{13,9},{2,6},{3,7},{6... | collective-permute-start | bytes 1646600 | tf_op jit(solution)/shard_map/ppermute | solution.py:402
  15.0 0.8 copy-start
  16.8 0.8 copy-start.4
  17.6 1.1 %copy-start.1 = (bf16[4,536,128]{2,1,0:T(8,128)(2,1)S(1)}, bf16[4,536,128]{2,1,0:T(8,128)(2,1)}, u32[]{:S(2)}) copy-start(bf16[4,536,128]{2,1,0:T(8,128)(2,1)} %copy-done) | copy-start | bytes 1646596
  18.7 1.1 %copy-start.5 = (bf16[4,536,128]{2,1,0:T(8,128)(2,1)S(1)}, bf16[4,536,128]{2,1,0:T(8,128)(2,1)}, u32[]{:S(2)}) copy-start(bf16[4,536,128]{2,1,0:T(8,128)(2,1)} %copy-done.4) | copy-start | bytes 1646596
  21.4 19.1 %collective-permute-start.4 = (f32[32,640]{1,0:T(8,128)}, f32[32,640]{1,0:T(8,128)S(1)}, u32[]{:S(2)}, u32[]{:S(2)}) collective-permute-start(f32[32,640]{1,0:T(8,128)} %get-tuple-element.36.moment.refs_0_), channel_id=1, source_target_pairs={{0,2},{2,0},{1,3},{3,1},{4,6},{6,4},{5,7},{7,5},{8,10},{10,8},{9,1... | collective-permute-start | bytes 245768 | tf_op jit(solution)/shard_map/ppermute | solution.py:402
  21.8 0.9 %copy-start.7 = (f32[32,640]{1,0:T(8,128)S(1)}, f32[32,640]{1,0:T(8,128)}, u32[]{:S(2)}) copy-start(f32[32,640]{1,0:T(8,128)} %get-tuple-element.36.moment.refs_0_) | copy-start | bytes 245764
  42.7 0.7 copy-start.2
  43.4 0.6 copy-start.8
  44.5 5.6 %collective-permute-start.5 = (f32[24,1024]{1,0:T(8,128)S(1)}, f32[24,1024]{1,0:T(8,128)}, u32[]{:S(2)}, u32[]{:S(2)}) collective-permute-start(f32[24,1024]{1,0:T(8,128)S(1)} %column_sums.1.stats.refs_0_), channel_id=1, source_target_pairs={{0,2},{2,0},{1,3},{3,1},{4,6},{6,4},{5,7},{7,5},{8,10},{10,8},{9,1... | collective-permute-start | bytes 294920 | tf_op jit(solution)/shard_map/ppermute | solution.py:402
  51.7 11.6 %collective-permute-start.6 = (f32[2,24,1024]{2,1,0:T(8,128)}, f32[2,24,1024]{2,1,0:T(8,128)}, u32[]{:S(2)}, u32[]{:S(2)}) collective-permute-start(f32[2,24,1024]{2,1,0:T(8,128)} %pad_maximum_fusion.1), channel_id=1, source_target_pairs={{0,1},{1,0},{2,3},{3,2},{4,5},{5,4},{6,7},{7,6},{8,9},{9,8},{10,11... | collective-permute-start | bytes 589832 | tf_op jit(solution)/shard_map/ppermute | solution.py:402
  55.0 1.7 %copy-start.3 = (f32[512,128]{1,0:T(8,128)S(1)}, f32[512,128]{1,0:T(8,128)}, u32[]{:S(2)}) copy-start(f32[512,128]{1,0:T(8,128)} %copy-done.2) | copy-start | bytes 786436
  55.0 1.9 %copy-start.11 = (f16[128,1024]{1,0:T(8,128)(2,1)S(1)}, f16[128,1024]{1,0:T(8,128)(2,1)}, u32[]{:S(2)}) copy-start(f16[128,1024]{1,0:T(8,128)(2,1)} %convert_element_type.18) | copy-start | bytes 786436
  55.0 2.8 %copy-start.10 = (f16[128,1024]{1,0:T(8,128)(2,1)S(1)}, f16[128,1024]{1,0:T(8,128)(2,1)}, u32[]{:S(2)}) copy-start(f16[128,1024]{1,0:T(8,128)(2,1)} %convert_element_type.19) | copy-start | bytes 786436
  55.0 9.3 %copy-start.9 = (f32[24,128]{1,0:T(8,128)S(1)}, f32[24,128]{1,0:T(8,128)}, u32[]{:S(2)}) copy-start(f32[24,128]{1,0:T(8,128)} %copy-done.8) | copy-start | bytes 36868
  56.6 15.0 %collective-permute-start.8 = (f16[128,1024]{1,0:T(8,128)(2,1)S(1)}, f16[128,1024]{1,0:T(8,128)(2,1)S(1)}, u32[]{:S(2)}, u32[]{:S(2)}) collective-permute-start(f16[128,1024]{1,0:T(8,128)(2,1)S(1)} %convert_element_type.21), channel_id=1, source_target_pairs={{0,1},{1,0},{2,3},{3,2},{4,5},{5,4},{6,7},{7,6},{8,9},{9,8},{10,11... | collective-permute-start | bytes 786440 | tf_op jit(solution)/shard_map/ppermute | solution.py:402
  56.9 16.3 %collective-permute-start.7 = (f16[128,1024]{1,0:T(8,128)(2,1)S(1)}, f16[128,1024]{1,0:T(8,128)(2,1)S(1)}, u32[]{:S(2)}, u32[]{:S(2)}) collective-permute-start(f16[128,1024]{1,0:T(8,128)(2,1)S(1)} %copy-done.11), channel_id=1, source_target_pairs={{0,2},{1,3},{2,0},{3,1},{4,6},{5,7},{6,4},{7,5},{8,10},{9,11},{10,... | collective-permute-start | bytes 786440 | tf_op jit(solution)/shard_map/ppermute | solution.py:402
  57.7 25.2 %collective-permute-start.9 = (f16[128,1024]{1,0:T(8,128)(2,1)S(1)}, f16[128,1024]{1,0:T(8,128)(2,1)S(1)}, u32[]{:S(2)}, u32[]{:S(2)}) collective-permute-start(f16[128,1024]{1,0:T(8,128)(2,1)S(1)} %copy-done.10), channel_id=1, source_target_pairs={{0,3},{1,2},{2,1},{3,0},{4,7},{5,6},{6,5},{7,4},{8,11},{9,10},{10,... | collective-permute-start | bytes 786440 | tf_op jit(solution)/shard_map/ppermute | solution.py:402
  64.3 1.0 %copy-start.6 = (f32[128,1024]{1,0:T(8,128)S(1)}, f32[128,1024]{1,0:T(8,128)}, u32[]{:S(2)}) copy-start(f32[128,1024]{1,0:T(8,128)} %get-tuple-element.41.own) | copy-start | bytes 1572868

commit v10 on v9

--- a/solution.py
+++ b/solution.py
@@ -280,7 +280,7 @@
 
 def cohort_fit(parts, snps, design):
     kernel = functools.partial(cohort_kernel, snps, design)
-    outs = (result((snps, LANES), jnp.float32), result((DPAD, LANES), jnp.float32))
+    outs = (pltpu.HBM((snps, LANES), jnp.float32), pltpu.HBM((DPAD, LANES), jnp.float32))
     scratch = [pltpu.VMEM((LANES, snps), jnp.float32)]
     return call(kernel, "cohort_fit", outs, [], parts, scratch, len(parts))
 
@@ -394,7 +394,7 @@
     kernel = functools.partial(base_kernel, float(here))
     scratch = [pltpu.VMEM((LANES, width), jnp.float32)]
     arrays = [own, coef, inverse, pair_coef, *parts]
-    return call(kernel, "base_ratio", outs, [place], arrays, scratch, 1)
+    return call(kernel, "base_ratio", outs, [place], arrays, scratch, len(arrays))
 
 
 def permute_xor(value, axes, bits):
@@ -446,17 +446,16 @@
     def shrink(pieces):
         return [piece.astype(jnp.float16) for piece in pieces]
 
-    sent = products(
-        genes, columns, pair_coef, stats, *where, list(range(1, n_far)), size, n_near
-    )
-    sent = shrink(sent)
-    sent, stat_parts = lax.optimization_barrier((sent, stat_parts))
-    own, *rest = products(genes, columns, pair_coef, stats, *where, [0], size, n_near)
-    sent = [own, *shrink(rest), *sent]
-    pieces = [None] + [permute_xor(sent[k], line, k) for k in range(1, n_far * n_near)]
-    away_parts = permute_xor(jnp.stack(stat_parts), "near", 1)
-    away_parts = [away_parts[j] for j in range(n_far)]
-
+    own, *sent = products(
+        genes, columns, pair_coef, stats, *where, list(range(n_far)), size, n_near
+    )
+    away_parts = [permute_xor(stats, "near", 1)]
+    sent, stat_parts, away_parts = lax.optimization_barrier(
+        (shrink(sent), stat_parts, away_parts)
+    )
+    pieces = [None]
+    pieces += [permute_xor(sent[k - 1], line, k) for k in range(1, n_far * n_near)]
+    away_parts += [permute_xor(part, "near", 1) for part in stat_parts[1:]]
     place = far * n_near + near
     columns_scale = lax.dynamic_slice_in_dim(coef, place * panel, panel, 0)
 

time: 86 us -> 84.5 us (0.983)
  the two profiles are of different devices: /device:TPU:20 before, /device:TPU:0 now
where the time goes in v10:
time: 84.5 us; the launch traced here: 84.1 us
  waiting for transfers between devices  34.2 us (40%)
  starting transfers between devices  23.1 us (27%)
  Pallas kernels  18.1 us (21%)
  local copies, waits for them, and re-layouts  6.46 us (8%)
  other arithmetic  2.06 us (2%)
    ppermute x11, waiting for transfers between devices, permute_xor(): return lax.ppermute(value, axes, [(i, i ^ bits) for i in range(size)])  34.2 us
    ppermute x11, starting transfers between devices, permute_xor(): return lax.ppermute(value, axes, [(i, i ^ bits) for i in range(size)])  19.5 us
    pallas_call x6, Pallas kernels, call(): pl.pallas_call(kernel, out_shape=outs, in_specs=[IN_SMEM] * len(scalars)...  12.1 us
    pallas_call x1, Pallas kernels, smooth(): pl.pallas_call(functools.partial(smooth_kernel, group, planes, per_vox, p...  4.94 us
    unnamed x16, local copies, waits for them, and re-layouts  4.63 us
    all_to_all x1, starting transfers between devices, exchange(): value = lax.all_to_all(value, ('vox', 'near'), 0, 0, tiled=True)  3.6 us
    another operation x1, other arithmetic, on_device(): jnp.stack([home, away], 1)  1.78 us
  transfers between devices with their start and end apart: 12, of which 6 were waited for; matrix products, arithmetic and copies ran while one was open for 0% of the time, Pallas kernels for 20%

profile of v10, /device:TPU:0, one launch (start us, length us, event | category | flops | bytes accessed | tf_op | source)
XLA Modules:
  0.0 84.1 jit_solution(3094910245086723872)
XLA Ops:
  0.0 1.0 %tall_design.1 = bf16[536,128]{1,0:T(8,128)(2,1)S(1)} custom-call(bf16[128,512]{1,0:T(8,128)(2,1)} %genotypes.1, s32[1,128]{1,0:T(1,128)} %bitcast.32, bf16[16,128]{1,0:T(8,128)(2,1)} %bitcast.31), custom_call_target="tpu_custom_call" | custom-call | tf_op jit(solution)/shard_map/tall_design/pallas_call | solution.py:111
  1.0 3.1 %collective-permute-start = (bf16[536,128]{1,0:T(8,128)(2,1)S(1)}, bf16[536,128]{1,0:T(8,128)(2,1)S(1)}, u32[]{:S(2)}, u32[]{:S(2)}) collective-permute-start(bf16[536,128]{1,0:T(8,128)(2,1)S(1)} %tall_design.1), channel_id=1, source_target_pairs={{0,1},{1,0},{4,5},{5,4},{8,9},{9,8},{12,13},{13,12},{2,3},{3,2},{6... | collective-permute-start | bytes 411656 | tf_op jit(solution)/shard_map/ppermute | solution.py:402
  4.1 1.5 %collective-permute-start.1 = (bf16[536,128]{1,0:T(8,128)(2,1)S(1)}, bf16[536,128]{1,0:T(8,128)(2,1)S(1)}, u32[]{:S(2)}, u32[]{:S(2)}) collective-permute-start(bf16[536,128]{1,0:T(8,128)(2,1)S(1)} %tall_design.1), channel_id=1, source_target_pairs={{0,8},{1,9},{4,12},{5,13},{8,0},{9,1},{12,4},{13,5},{2,10},{3,11},... | collective-permute-start | bytes 411656 | tf_op jit(solution)/shard_map/ppermute | solution.py:402
  5.6 4.9 %smooth.1 = bf16[8,128,1024]{2,1,0:T(8,128)(2,1)} custom-call(bf16[128,32,256]{2,1,0:T(8,128)(2,1)} %bitcast.24, bf16[256,256]{1,0:T(8,128)(2,1)} %constant.27.clone.order, bf16[256,256]{1,0:T(8,128)(2,1)} %constant.28.clone.table), custom_call_target="tpu_custom_call" | custom-call | tf_op jit(solution)/shard_map/smooth/pallas_call | solution.py:166
  10.6 1.5 %collective-permute-done.1 = bf16[536,128]{1,0:T(8,128)(2,1)S(1)} collective-permute-done((bf16[536,128]{1,0:T(8,128)(2,1)S(1)}, bf16[536,128]{1,0:T(8,128)(2,1)S(1)}, u32[]{:S(2)}, u32[]{:S(2)}) %collective-permute-start.1) | collective-permute-done | bytes 137248 | tf_op jit(solution)/shard_map/ppermute | solution.py:402
  12.1 3.6 %all-to-all-start = ((bf16[8,128,1024]{2,1,0:T(8,128)(2,1)}), bf16[8,128,1024]{2,1,0:T(8,128)(2,1)S(1)}, u32[]{:S(2)}, u32[]{:S(2)}) async-start(bf16[8,128,1024]{2,1,0:T(8,128)(2,1)} %smooth.1), calls=%async_computation | async-start | bytes 4194304 | tf_op jit(solution)/shard_map/all_to_all | solution.py:416
  15.8 0.5 collective-permute-start.3
  16.3 0.8 copy-done
  17.1 0.9 %collective-permute-done.3.others = bf16[4,536,128]{2,1,0:T(8,128)(2,1)S(1)} collective-permute-done((bf16[4,536,128]{2,1,0:T(8,128)(2,1)S(1)}, bf16[4,536,128]{2,1,0:T(8,128)(2,1)S(1)}, u32[]{:S(2)}, u32[]{:S(2)}) %collective-permute-start.3) | collective-permute-done | bytes 548896 | tf_op jit(solution)/shard_map/ppermute | solution.py:402
  18.0 0.8 copy-done.3
  18.8 1.0 %copy-done.1 = bf16[4,536,128]{2,1,0:T(8,128)(2,1)S(1)} copy-done((bf16[4,536,128]{2,1,0:T(8,128)(2,1)S(1)}, bf16[4,536,128]{2,1,0:T(8,128)(2,1)}, u32[]{:S(2)}) %copy-start.1) | copy-done | bytes 548888
  19.8 1.0 %copy-done.4 = bf16[4,536,128]{2,1,0:T(8,128)(2,1)S(1)} copy-done((bf16[4,536,128]{2,1,0:T(8,128)(2,1)S(1)}, bf16[4,536,128]{2,1,0:T(8,128)(2,1)}, u32[]{:S(2)}) %copy-start.4) | copy-done | bytes 548888
  20.9 1.7 %moments.1 = (bf16[536,1024]{1,0:T(8,128)(2,1)S(1)}, f32[32,640]{1,0:T(8,128)}) custom-call(s32[1]{0:T(128)} %bitcast.3.me, bf16[4,536,128]{2,1,0:T(8,128)(2,1)S(1)} %copy-done.1, bf16[4,536,128]{2,1,0:T(8,128)(2,1)S(1)} %copy-done.4), custom_call_target="tpu_custom_call" | custom-call | tf_op jit(solution)/shard_map/moments/pallas_call | solution.py:87
  22.6 2.6 %collective-permute-start.4 = (f32[32,640]{1,0:T(8,128)}, f32[32,640]{1,0:T(8,128)S(1)}, u32[]{:S(2)}, u32[]{:S(2)}) collective-permute-start(f32[32,640]{1,0:T(8,128)} %get-tuple-element.38.moment.refs_0_), channel_id=1, source_target_pairs={{0,2},{2,0},{1,3},{3,1},{4,6},{6,4},{5,7},{7,5},{8,10},{10,8},{9,1... | collective-permute-start | bytes 245768 | tf_op jit(solution)/shard_map/ppermute | solution.py:402
  25.2 0.9 %copy-done.6 = f32[32,640]{1,0:T(8,128)S(1)} copy-done((f32[32,640]{1,0:T(8,128)S(1)}, f32[32,640]{1,0:T(8,128)}, u32[]{:S(2)}) %copy-start.6) | copy-done | bytes 81944
  26.1 2.0 %pair_fit.1.coef.pair_coef = f32[512,128]{1,0:T(8,128)S(1)} custom-call(f32[32,640]{1,0:T(8,128)S(1)} %copy-done.6), custom_call_target="tpu_custom_call" | custom-call | tf_op jit(solution)/shard_map/pair_fit/pallas_call | solution.py:87
  28.1 13.0 %collective-permute-done.4.refs_1_ = f32[32,640]{1,0:T(8,128)S(1)} collective-permute-done((f32[32,640]{1,0:T(8,128)}, f32[32,640]{1,0:T(8,128)S(1)}, u32[]{:S(2)}, u32[]{:S(2)}) %collective-permute-start.4) | collective-permute-done | bytes 81952 | tf_op jit(solution)/shard_map/ppermute | solution.py:402
  41.1 2.9 %cohort_fit.1 = (f32[512,128]{1,0:T(8,128)}, f32[24,128]{1,0:T(8,128)}) custom-call(f32[32,640]{1,0:T(8,128)S(1)} %copy-done.6, f32[32,640]{1,0:T(8,128)S(1)} %collective-permute-done.4.refs_1_), custom_call_target="tpu_custom_call" | custom-call | tf_op jit(solution)/shard_map/cohort_fit/pallas_call | solution.py:87
  44.0 0.5 column_sums.1.stats.refs_0_
  44.5 3.3 %collective-permute-start.5 = (f32[24,1024]{1,0:T(8,128)S(1)}, f32[24,1024]{1,0:T(8,128)}, u32[]{:S(2)}, u32[]{:S(2)}) collective-permute-start(f32[24,1024]{1,0:T(8,128)S(1)} %column_sums.1.stats.refs_0_), channel_id=1, source_target_pairs={{0,2},{2,0},{1,3},{3,1},{4,6},{6,4},{5,7},{7,5},{8,10},{10,8},{9,1... | collective-permute-start | bytes 294920 | tf_op jit(solution)/shard_map/ppermute | solution.py:402
  47.8 1.4 %collective-permute-start.6 = (f32[24,1024]{1,0:T(8,128)S(1)}, f32[24,1024]{1,0:T(8,128)}, u32[]{:S(2)}, u32[]{:S(2)}) collective-permute-start(f32[24,1024]{1,0:T(8,128)S(1)} %column_sums.1.stats.refs_0_), channel_id=1, source_target_pairs={{0,1},{1,0},{2,3},{3,2},{4,5},{5,4},{6,7},{7,6},{8,9},{9,8},{10,11... | collective-permute-start | bytes 294920 | tf_op jit(solution)/shard_map/ppermute | solution.py:402
  49.2 2.5 %products.1 = (f32[128,1024]{1,0:T(8,128)}, f32[128,1024]{1,0:T(8,128)S(1)}, f32[128,1024]{1,0:T(8,128)S(1)}, f32[128,1024]{1,0:T(8,128)S(1)}) custom-call(s32[1]{0:T(128)} %bitcast.1.far, s32[1]{0:T(128)} %bitcast.2.near, bf16[536,1024]{1,0:T(8,128)(2,1)S(1)} %get-tuple-element.36.genes, bf16[1024,1024]{1,0:T(8,128)(2,1)S(1)} %bitcast.21, ...), custom_call_target="tpu_custom_call" | custom-call | tf_op jit(solution)/shard_map/products/pallas_call | solution.py:87
  51.9 1.0 %collective-permute-done.6.refs_2_ = f32[24,1024]{1,0:T(8,128)} collective-permute-done((f32[24,1024]{1,0:T(8,128)S(1)}, f32[24,1024]{1,0:T(8,128)}, u32[]{:S(2)}, u32[]{:S(2)}) %collective-permute-start.6) | collective-permute-done | bytes 98336 | tf_op jit(solution)/shard_map/ppermute | solution.py:402
  52.8 2.7 %collective-permute-start.7 = (f32[24,1024]{1,0:T(8,128)}, f32[24,1024]{1,0:T(8,128)S(1)}, u32[]{:S(2)}, u32[]{:S(2)}) collective-permute-start(f32[24,1024]{1,0:T(8,128)} %collective-permute-done.5.refs_1_), channel_id=1, source_target_pairs={{0,1},{1,0},{2,3},{3,2},{4,5},{5,4},{6,7},{7,6},{8,9},{9,8},{10,11... | collective-permute-start | bytes 294920 | tf_op jit(solution)/shard_map/ppermute | solution.py:402
  55.5 2.5 %collective-permute-start.10 = (f16[128,1024]{1,0:T(8,128)(2,1)S(1)}, f16[128,1024]{1,0:T(8,128)(2,1)S(1)}, u32[]{:S(2)}, u32[]{:S(2)}) collective-permute-start(f16[128,1024]{1,0:T(8,128)(2,1)S(1)} %convert_element_type.20), channel_id=1, source_target_pairs={{0,3},{1,2},{2,1},{3,0},{4,7},{5,6},{6,5},{7,4},{8,11},{9,10},{10,... | collective-permute-start | bytes 786440 | tf_op jit(solution)/shard_map/ppermute | solution.py:402
  58.1 1.8 %collective-permute-start.9 = (f16[128,1024]{1,0:T(8,128)(2,1)S(1)}, f16[128,1024]{1,0:T(8,128)(2,1)}, u32[]{:S(2)}, u32[]{:S(2)}) collective-permute-start(f16[128,1024]{1,0:T(8,128)(2,1)S(1)} %convert_element_type.18), channel_id=1, source_target_pairs={{0,1},{1,0},{2,3},{3,2},{4,5},{5,4},{6,7},{7,6},{8,9},{9,8},{10,11... | collective-permute-start | bytes 786440 | tf_op jit(solution)/shard_map/ppermute | solution.py:402
  60.2 2.5 %base_ratio.1 = (f32[128,1024]{1,0:T(8,128)S(1)}, f32[8,1024]{1,0:T(8,128)S(1)}, f32[128,1024]{1,0:T(8,128)S(1)}, f32[8,1024]{1,0:T(8,128)S(1)}) custom-call(s32[1]{0:T(128)} %bitcast.place, f32[128,1024]{1,0:T(8,128)S(1)} %copy-done.5, f32[512,128]{1,0:T(8,128)S(1)} %copy-done.2, f32[24,128]{1,0:T(8,128)S(1)} %copy-done.7, ...), custom_call_target="tpu_custom_call" | custom-call | tf_op jit(solution)/shard_map/base_ratio/pallas_call | solution.py:87
  62.7 5.0 %collective-permute-done.10 = f16[128,1024]{1,0:T(8,128)(2,1)S(1)} collective-permute-done((f16[128,1024]{1,0:T(8,128)(2,1)S(1)}, f16[128,1024]{1,0:T(8,128)(2,1)S(1)}, u32[]{:S(2)}, u32[]{:S(2)}) %collective-permute-start.10) | collective-permute-done | bytes 262176 | tf_op jit(solution)/shard_map/ppermute | solution.py:402
  67.7 12.8 %collective-permute-done.8 = f16[128,1024]{1,0:T(8,128)(2,1)} collective-permute-done((f16[128,1024]{1,0:T(8,128)(2,1)S(1)}, f16[128,1024]{1,0:T(8,128)(2,1)}, u32[]{:S(2)}, u32[]{:S(2)}) %collective-permute-start.8) | collective-permute-done | bytes 262176 | tf_op jit(solution)/shard_map/ppermute | solution.py:402
  80.5 1.8 %multiply_bitcast_fusion.1 = (f32[128,1,1024]{2,0,1:T(8,128)S(1)}, f32[128,1,1024]{2,0,1:T(8,128)S(1)}) fusion(f32[128,1024]{1,0:T(8,128)S(1)} %get-tuple-element.52, f16[128,1024]{1,0:T(8,128)(2,1)} %collective-permute-done.8, f32[1024]{0:T(1024)S(1)} %bitcast.28, f32[128]{0:T(128)S(1)} %get-tuple-element.59, f32[1024]{0:T(1024)S(1)} %bitcast.30, ...), kind=kLoop, calls=%fused_computation.3 | loop fusion | flops 2621440 | bytes 2896896 | tf_op jit(solution)/shard_map/stack | solution.py:476
  82.4 0.3 copy.7
  82.7 1.3 %copy.8 = f32[128,4,2,256]{3,2,1,0:T(2,128)} copy(f32[128,4,2,256]{0,3,2,1:T(8,128)S(1)} %bitcast.23) | data formatting | bytes 2097152 | tf_op jit(solution)/shard_map/jit(_where)/select_n | solution.py:476
  (27 shorter events, 0.6 us)
Async XLA Ops:
  1.0 9.6 %collective-permute-start = (bf16[536,128]{1,0:T(8,128)(2,1)S(1)}, bf16[536,128]{1,0:T(8,128)(2,1)S(1)}, u32[]{:S(2)}, u32[]{:S(2)}) collective-permute-start(bf16[536,128]{1,0:T(8,128)(2,1)S(1)} %tall_design.1), channel_id=1, source_target_pairs={{0,1},{1,0},{4,5},{5,4},{8,9},{9,8},{12,13},{13,12},{2,3},{3,2},{6... | collective-permute-start | bytes 411656 | tf_op jit(solution)/shard_map/ppermute | solution.py:402
  4.1 8.0 %collective-permute-start.1 = (bf16[536,128]{1,0:T(8,128)(2,1)S(1)}, bf16[536,128]{1,0:T(8,128)(2,1)S(1)}, u32[]{:S(2)}, u32[]{:S(2)}) collective-permute-start(bf16[536,128]{1,0:T(8,128)(2,1)S(1)} %tall_design.1), channel_id=1, source_target_pairs={{0,8},{1,9},{4,12},{5,13},{8,0},{9,1},{12,4},{13,5},{2,10},{3,11},... | collective-permute-start | bytes 411656 | tf_op jit(solution)/shard_map/ppermute | solution.py:402
  5.6 6.5 %collective-permute-start.2 = (bf16[536,128]{1,0:T(8,128)(2,1)S(1)}, bf16[536,128]{1,0:T(8,128)(2,1)S(1)}, u32[]{:S(2)}, u32[]{:S(2)}) collective-permute-start(bf16[536,128]{1,0:T(8,128)(2,1)S(1)} %tall_design.1), channel_id=1, source_target_pairs={{0,9},{1,8},{4,13},{5,12},{8,1},{9,0},{12,5},{13,4},{2,11},{3,10},... | collective-permute-start | bytes 411656 | tf_op jit(solution)/shard_map/ppermute | solution.py:402
  12.1 31.9 %all-to-all-start = ((bf16[8,128,1024]{2,1,0:T(8,128)(2,1)}), bf16[8,128,1024]{2,1,0:T(8,128)(2,1)S(1)}, u32[]{:S(2)}, u32[]{:S(2)}) async-start(bf16[8,128,1024]{2,1,0:T(8,128)(2,1)} %smooth.1), calls=%async_computation | async-start | bytes 4194304 | tf_op jit(solution)/shard_map/all_to_all | solution.py:416
  15.8 2.1 %collective-permute-start.3 = (bf16[4,536,128]{2,1,0:T(8,128)(2,1)S(1)}, bf16[4,536,128]{2,1,0:T(8,128)(2,1)S(1)}, u32[]{:S(2)}, u32[]{:S(2)}) collective-permute-start(bf16[4,536,128]{2,1,0:T(8,128)(2,1)S(1)} %pad_maximum_fusion.blocks), channel_id=1, source_target_pairs={{0,4},{1,5},{4,0},{5,1},{8,12},{9,13},{12,8},{13,9},{2,6},{3,7},{6... | collective-permute-start | bytes 1646600 | tf_op jit(solution)/shard_map/ppermute | solution.py:402
  16.3 0.8 copy-start
  18.0 0.8 copy-start.3
  18.8 1.1 %copy-start.1 = (bf16[4,536,128]{2,1,0:T(8,128)(2,1)S(1)}, bf16[4,536,128]{2,1,0:T(8,128)(2,1)}, u32[]{:S(2)}) copy-start(bf16[4,536,128]{2,1,0:T(8,128)(2,1)} %copy-done) | copy-start | bytes 1646596
  19.8 1.1 %copy-start.4 = (bf16[4,536,128]{2,1,0:T(8,128)(2,1)S(1)}, bf16[4,536,128]{2,1,0:T(8,128)(2,1)}, u32[]{:S(2)}) copy-start(bf16[4,536,128]{2,1,0:T(8,128)(2,1)} %copy-done.3) | copy-start | bytes 1646596
  22.6 18.5 %collective-permute-start.4 = (f32[32,640]{1,0:T(8,128)}, f32[32,640]{1,0:T(8,128)S(1)}, u32[]{:S(2)}, u32[]{:S(2)}) collective-permute-start(f32[32,640]{1,0:T(8,128)} %get-tuple-element.38.moment.refs_0_), channel_id=1, source_target_pairs={{0,2},{2,0},{1,3},{3,1},{4,6},{6,4},{5,7},{7,5},{8,10},{10,8},{9,1... | collective-permute-start | bytes 245768 | tf_op jit(solution)/shard_map/ppermute | solution.py:402
  25.2 0.9 %copy-start.6 = (f32[32,640]{1,0:T(8,128)S(1)}, f32[32,640]{1,0:T(8,128)}, u32[]{:S(2)}) copy-start(f32[32,640]{1,0:T(8,128)} %get-tuple-element.38.moment.refs_0_) | copy-start | bytes 245764
  44.5 7.3 %collective-permute-start.5 = (f32[24,1024]{1,0:T(8,128)S(1)}, f32[24,1024]{1,0:T(8,128)}, u32[]{:S(2)}, u32[]{:S(2)}) collective-permute-start(f32[24,1024]{1,0:T(8,128)S(1)} %column_sums.1.stats.refs_0_), channel_id=1, source_target_pairs={{0,2},{2,0},{1,3},{3,1},{4,6},{6,4},{5,7},{7,5},{8,10},{10,8},{9,1... | collective-permute-start | bytes 294920 | tf_op jit(solution)/shard_map/ppermute | solution.py:402
  47.8 5.1 %collective-permute-start.6 = (f32[24,1024]{1,0:T(8,128)S(1)}, f32[24,1024]{1,0:T(8,128)}, u32[]{:S(2)}, u32[]{:S(2)}) collective-permute-start(f32[24,1024]{1,0:T(8,128)S(1)} %column_sums.1.stats.refs_0_), channel_id=1, source_target_pairs={{0,1},{1,0},{2,3},{3,2},{4,5},{5,4},{6,7},{7,6},{8,9},{9,8},{10,11... | collective-permute-start | bytes 294920 | tf_op jit(solution)/shard_map/ppermute | solution.py:402
  51.7 8.2 %copy-start.2 = (f32[512,128]{1,0:T(8,128)S(1)}, f32[512,128]{1,0:T(8,128)}, u32[]{:S(2)}) copy-start(f32[512,128]{1,0:T(8,128)} %get-tuple-element.44.coef) | copy-start | bytes 786436
  51.7 8.4 %copy-start.5 = (f32[128,1024]{1,0:T(8,128)S(1)}, f32[128,1024]{1,0:T(8,128)}, u32[]{:S(2)}) copy-start(f32[128,1024]{1,0:T(8,128)} %get-tuple-element.43.own) | copy-start | bytes 1572868
  51.7 8.4 %copy-start.7 = (f32[24,128]{1,0:T(8,128)S(1)}, f32[24,128]{1,0:T(8,128)}, u32[]{:S(2)}) copy-start(f32[24,128]{1,0:T(8,128)} %get-tuple-element.45.inverse) | copy-start | bytes 36868
  52.8 7.3 %collective-permute-start.7 = (f32[24,1024]{1,0:T(8,128)}, f32[24,1024]{1,0:T(8,128)S(1)}, u32[]{:S(2)}, u32[]{:S(2)}) collective-permute-start(f32[24,1024]{1,0:T(8,128)} %collective-permute-done.5.refs_1_), channel_id=1, source_target_pairs={{0,1},{1,0},{2,3},{3,2},{4,5},{5,4},{6,7},{7,6},{8,9},{9,8},{10,11... | collective-permute-start | bytes 294920 | tf_op jit(solution)/shard_map/ppermute | solution.py:402
  55.5 12.1 %collective-permute-start.10 = (f16[128,1024]{1,0:T(8,128)(2,1)S(1)}, f16[128,1024]{1,0:T(8,128)(2,1)S(1)}, u32[]{:S(2)}, u32[]{:S(2)}) collective-permute-start(f16[128,1024]{1,0:T(8,128)(2,1)S(1)} %convert_element_type.20), channel_id=1, source_target_pairs={{0,3},{1,2},{2,1},{3,0},{4,7},{5,6},{6,5},{7,4},{8,11},{9,10},{10,... | collective-permute-start | bytes 786440 | tf_op jit(solution)/shard_map/ppermute | solution.py:402
  58.1 22.4 %collective-permute-start.8 = (f16[128,1024]{1,0:T(8,128)(2,1)S(1)}, f16[128,1024]{1,0:T(8,128)(2,1)}, u32[]{:S(2)}, u32[]{:S(2)}) collective-permute-start(f16[128,1024]{1,0:T(8,128)(2,1)S(1)} %convert_element_type.19), channel_id=1, source_target_pairs={{0,2},{1,3},{2,0},{3,1},{4,6},{5,7},{6,4},{7,5},{8,10},{9,11},{10,... | collective-permute-start | bytes 786440 | tf_op jit(solution)/shard_map/ppermute | solution.py:402
  58.1 22.4 %collective-permute-start.9 = (f16[128,1024]{1,0:T(8,128)(2,1)S(1)}, f16[128,1024]{1,0:T(8,128)(2,1)}, u32[]{:S(2)}, u32[]{:S(2)}) collective-permute-start(f16[128,1024]{1,0:T(8,128)(2,1)S(1)} %convert_element_type.18), channel_id=1, source_target_pairs={{0,1},{1,0},{2,3},{3,2},{4,5},{5,4},{6,7},{7,6},{8,9},{9,8},{10,11... | collective-permute-start | bytes 786440 | tf_op jit(solution)/shard_map/ppermute | solution.py:402

commit v11 on v10

--- a/solution.py
+++ b/solution.py
@@ -21,6 +21,7 @@
 VMEM_MOST = 56 * 2**20
 VMEM_BASE = 12 * 2**20
 SQUARE_ROW = 20
+WIDE = 2.0**8
 SCALE_LANE = DPAD
 STRIDE = 32
 
@@ -307,44 +308,39 @@
     return call(sums_kernel, "column_sums", outs, [], [genes, columns])
 
 
-def products_kernel(here, offsets, far, near, genes, columns, coef, stats, *refs):
+def far_kernel(here, count, far, near, genes, columns, coef, stats, *refs):
     outs, held = list(refs[:-1]), refs[-1]
     size = held.shape[0]
     panel = outs[0].shape[0]
     cross_image = stats[...]
     over = 1.0 / column_norm(cross_image, here)
-    for j in offsets:
+    for j in range(1, count):
         block = pl.multiple_of(jnp.bitwise_xor(far[0], j) * size, size)
         held[...] = jnp.dot(
             genes[pl.ds(block, size), :], columns[...], preferred_element_type=jnp.float32
         )
         for k in range(size // panel):
             place = pl.multiple_of(jnp.bitwise_xor(near[0], k) * panel, panel)
-            sums = held[pl.ds(place, panel), :]
-            out = outs.pop(0)
-            if j == 0 and k == 0:
-                out[...] = sums
-                continue
             line = coef[pl.ds(block + place, panel), :]
             fit = jnp.dot(
                 line[:, :DPAD], cross_image, precision=HIGHEST, preferred_element_type=jnp.float32
             )
-            out[...] = (line[:, SCALE_LANE : SCALE_LANE + 1] * sums - fit) * over
-
-
-def products(genes, columns, coef, stats, far, near, offsets, size, count):
+            scale = line[:, SCALE_LANE : SCALE_LANE + 1]
+            outs.pop(0)[...] = (scale * held[pl.ds(place, panel), :] - fit) * over
+
+
+def far_products(genes, columns, coef, stats, far, near, n_far, n_near):
     here, width = columns.shape
-    panel = size // count
-    outs = [result((panel, width), jnp.float32) for _ in range(len(offsets) * count)]
-    if 0 in offsets:
-        outs[0] = pltpu.HBM((panel, width), jnp.float32)
-    kernel = functools.partial(products_kernel, float(here), tuple(offsets))
+    size = (genes.shape[0] - DPAD) // n_far
+    outs = (result((size // n_near, width), jnp.float32),) * ((n_far - 1) * n_near)
+    kernel = functools.partial(far_kernel, float(here), n_far)
     scratch = [pltpu.VMEM((size, width), jnp.float32)]
-    arrays = [genes, columns, coef, stats]
-    return call(kernel, "products", tuple(outs), [far, near], arrays, scratch)
-
-
-def base_half(here, line, inverse, stats, extra, factors, stack):
+    return call(kernel, "far_products", outs, [far, near], [genes, columns, coef, stats], scratch)
+
+
+def base_kernel(here, count, far, near, genes, columns, coef, inverse, *refs):
+    parts, (home, away, factors, stack, held) = refs[:-5], refs[-5:]
+    stats = [part[...] for part in parts]
     row = lax.broadcasted_iota(jnp.int32, stats[0].shape, 0)
     total = tree_sum(stats)
     known = row < SQUARE_ROW
@@ -356,45 +352,38 @@
         cross_image * solved, axis=0, keepdims=True
     )
     scale = lax.rsqrt(rss)
+    stack[...] = jnp.zeros(stack.shape, jnp.float32)
     stack[:DPAD, :] = cross_image
     factors[...] = jnp.zeros(factors.shape, jnp.float32)
-    for j, stat in enumerate(stats):
-        factors[j : j + 1, :] = column_norm(stat, here) * scale
-        if j:
-            stack[j * STRIDE : j * STRIDE + DPAD, :] = jnp.where(known, stat, 0.0)
+    for j in range(1, len(stats)):
+        factors[j : j + 1, :] = column_norm(stats[j], here) * scale
+        stack[j * STRIDE : j * STRIDE + DPAD, :] = jnp.where(known, stats[j], 0.0)
+    size = held.shape[0]
+    block = pl.ds(pl.multiple_of(far[0] * size, size), size)
+    line = coef[block, :]
+    sums = jnp.dot(genes[block, :], columns[...], preferred_element_type=jnp.float32)
     terms = jnp.dot(line, stack[...], precision=HIGHEST, preferred_element_type=jnp.float32)
-    return (terms + extra) * scale
-
-
-def base_kernel(here, place, own, coef, inverse, pair_coef, *refs):
-    parts, (home, home_factors, away, away_factors, stack) = refs[:-5], refs[-5:]
-    count = len(parts) // 2
-    stack[...] = jnp.zeros(stack.shape, jnp.float32)
-    panel = own.shape[0]
-    rows = pl.ds(pl.multiple_of(place[0] * panel, panel), panel)
-    line = coef[rows, :]
-    stats = [part[...] for part in parts[:count]]
-    extra = line[:, SCALE_LANE : SCALE_LANE + 1] * own[...]
-    home[...] = base_half(here, line, inverse, stats, extra, home_factors, stack)
-    stats = [part[...] for part in parts[count:]]
-    row = lax.broadcasted_iota(jnp.int32, stats[0].shape, 0)
-    extra = jnp.dot(
-        pair_coef[rows, :][:, :DPAD],
-        jnp.where(row < SQUARE_ROW, stats[0], 0.0),
-        precision=HIGHEST,
-        preferred_element_type=jnp.float32,
-    )
-    extra = line[:, SCALE_LANE + 1 : SCALE_LANE + 2] * extra
-    away[...] = base_half(here, line, inverse, stats, extra, away_factors, stack)
-
-
-def base_ratio(place, own, coef, inverse, pair_coef, parts, here):
-    panel, width = own.shape
-    outs = (result((panel, width), jnp.float32), result((8, width), jnp.float32)) * 2
-    kernel = functools.partial(base_kernel, float(here))
-    scratch = [pltpu.VMEM((LANES, width), jnp.float32)]
-    arrays = [own, coef, inverse, pair_coef, *parts]
-    return call(kernel, "base_ratio", outs, [place], arrays, scratch, len(arrays))
+    held[...] = (line[:, SCALE_LANE : SCALE_LANE + 1] * sums + terms) * scale
+    panel = size // count
+    for k, out in enumerate((home, away)):
+        place = pl.multiple_of(jnp.bitwise_xor(near[0], k) * panel, panel)
+        out[...] = held[pl.ds(place, panel), :] * (WIDE if k else 1.0)
+
+
+def base_ratio(genes, columns, coef, inverse, parts, far, near, n_far, n_near):
+    here, width = columns.shape
+    size = (genes.shape[0] - DPAD) // n_far
+    outs = (result((size // n_near, width), jnp.float32),) * 2
+    outs += (result((8, width), jnp.float32),)
+    kernel = functools.partial(base_kernel, float(here), n_near)
+    scratch = [pltpu.VMEM((LANES, width), jnp.float32), pltpu.VMEM((size, width), jnp.float32)]
+    arrays = [coef, inverse, genes, columns, *parts]
+    kernel = functools.partial(reorder, kernel)
+    return call(kernel, "base_ratio", outs, [far, near], arrays, scratch, 2)
+
+
+def reorder(kernel, far, near, coef, inverse, genes, columns, *refs):
+    kernel(far, near, genes, columns, coef, inverse, *refs)
 
 
 def permute_xor(value, axes, bits):
@@ -441,37 +430,27 @@
     panel = size // n_near
     freedom = float(here * n_far - design - 1)
     line = ("far", "near")
-    where = [far[None], near[None]]
-
-    def shrink(pieces):
-        return [piece.astype(jnp.float16) for piece in pieces]
-
-    own, *sent = products(
-        genes, columns, pair_coef, stats, *where, list(range(n_far)), size, n_near
-    )
-    away_parts = [permute_xor(stats, "near", 1)]
-    sent, stat_parts, away_parts = lax.optimization_barrier(
-        (shrink(sent), stat_parts, away_parts)
-    )
-    pieces = [None]
-    pieces += [permute_xor(sent[k - 1], line, k) for k in range(1, n_far * n_near)]
-    away_parts += [permute_xor(part, "near", 1) for part in stat_parts[1:]]
+    where = [far[None], near[None], n_far, n_near]
+    sent = far_products(genes, columns, pair_coef, stats, *where)
+    sent = [piece.astype(jnp.float16) for piece in sent]
+    sent, stat_parts = lax.optimization_barrier((sent, stat_parts))
+    pieces = {
+        k: permute_xor(sent[k - n_near], line, k) for k in range(n_near, n_far * n_near)
+    }
+    home, away, factors = base_ratio(genes, columns, coef, inverse, stat_parts, *where)
+    away = permute_xor(away.astype(jnp.float16), "near", 1)
+    away = away.astype(jnp.float32) * (1.0 / WIDE)
+    away_factors = permute_xor(factors, "near", 1)
     place = far * n_near + near
     columns_scale = lax.dynamic_slice_in_dim(coef, place * panel, panel, 0)
 
-    home, home_factors, away, away_factors = base_ratio(
-        place[None], own, coef, inverse, pair_coef, stat_parts + away_parts, here
-    )
-
     def t_of(ratio, factors, offset):
-        for j in range(n_far):
-            piece = pieces[j * n_near + offset]
-            if piece is not None:
-                weight = columns_scale[:, SCALE_LANE + 1 + j, None] * factors[None, j]
-                ratio = ratio + piece.astype(jnp.float32) * weight
+        for j in range(1, n_far):
+            weight = columns_scale[:, SCALE_LANE + 1 + j, None] * factors[None, j]
+            ratio = ratio + pieces[j * n_near + offset].astype(jnp.float32) * weight
         return ratio * jnp.sqrt(freedom / (1.0 - ratio * ratio))
 
-    home = t_of(home, home_factors, 0)
+    home = t_of(home, factors, 0)
     away = t_of(away, away_factors, 1)
     both = jnp.where(near == 0, jnp.stack([home, away], 1), jnp.stack([away, home], 1))
     return both.reshape(panel, maps, per_vox, plane)

time: 84.5 us -> 80.1 us (0.948)
  waiting for transfers between devices: 34.2 us -> 27.8 us
  local copies, waits for them, and re-layouts: 6.46 us -> 8.03 us
  other arithmetic: 2.06 us -> 3.53 us
  Pallas kernels: 18.1 us -> 17.2 us
    ppermute x11 -> x10, waiting for transfers between devices: 34.2 us -> 27.8 us  [permute_xor(): return lax.ppermute(value, axes, [(i, i ^ bits) for i in range(size)])]
    convert_element_type x3, other arithmetic: 0.09 us -> 1.5 us  [the longest x2 1.47 us: on_device(): sent = [piece.astype(jnp.float16) for piece in sent]]
    pallas_call x6, Pallas kernels: 12.1 us -> 11.3 us  [call(): pl.pallas_call(kernel, out_shape=outs, in_specs=[IN_SMEM] * len(scalars)...]
    ppermute x11 -> x10, starting transfers between devices: 19.5 us -> 19.3 us  [permute_xor(): return lax.ppermute(value, axes, [(i, i ^ bits) for i in range(size)])]
  transfers between devices with their start and end apart: 12 -> 11, of which waited for: 6 -> 4; matrix products, arithmetic and copies ran while one was open for 0% -> 3% of each run, Pallas kernels for 20% -> 20%
where the time goes in v11:
time: 80.1 us; the launch traced here: 79.6 us
  waiting for transfers between devices  27.8 us (35%)
  starting transfers between devices  22.9 us (29%)
  Pallas kernels  17.2 us (21%)
  local copies, waits for them, and re-layouts  8.03 us (10%)
  other arithmetic  3.53 us (4%)
    ppermute x10, waiting for transfers between devices, permute_xor(): return lax.ppermute(value, axes, [(i, i ^ bits) for i in range(size)])  27.8 us
    ppermute x10, starting transfers between devices, permute_xor(): return lax.ppermute(value, axes, [(i, i ^ bits) for i in range(size)])  19.3 us
    pallas_call x6, Pallas kernels, call(): pl.pallas_call(kernel, out_shape=outs, in_specs=[IN_SMEM] * len(scalars)...  11.3 us
    unnamed x16, local copies, waits for them, and re-layouts  5.37 us
    pallas_call x1, Pallas kernels, smooth(): pl.pallas_call(functools.partial(smooth_kernel, group, planes, per_vox, p...  4.94 us
    all_to_all x1, starting transfers between devices, exchange(): value = lax.all_to_all(value, ('vox', 'near'), 0, 0, tiled=True)  3.6 us
    another operation x1, other arithmetic, on_device(): jnp.stack([home, away], 1)  1.84 us
    select_n x2, local copies, waits for them, and re-layouts, on_device(): jnp.where(near == 0, jnp.stack([home, away], 1), jnp.stack([away, home], 1))  1.63 us
  transfers between devices with their start and end apart: 11, of which 4 were waited for; matrix products, arithmetic and copies ran while one was open for 3% of the time, Pallas kernels for 20%

profile of v11, /device:TPU:0, one launch (start us, length us, event | category | flops | bytes accessed | tf_op | source)
XLA Modules:
  0.0 79.6 jit_solution(8962717099924608330)
XLA Ops:
  0.0 1.0 %tall_design.1 = bf16[536,128]{1,0:T(8,128)(2,1)S(1)} custom-call(bf16[128,512]{1,0:T(8,128)(2,1)} %genotypes.1, s32[1,128]{1,0:T(1,128)} %bitcast.30, bf16[16,128]{1,0:T(8,128)(2,1)} %bitcast.29), custom_call_target="tpu_custom_call" | custom-call | tf_op jit(solution)/shard_map/tall_design/pallas_call | solution.py:112
  1.0 3.1 %collective-permute-start = (bf16[536,128]{1,0:T(8,128)(2,1)S(1)}, bf16[536,128]{1,0:T(8,128)(2,1)S(1)}, u32[]{:S(2)}, u32[]{:S(2)}) collective-permute-start(bf16[536,128]{1,0:T(8,128)(2,1)S(1)} %tall_design.1), channel_id=1, source_target_pairs={{0,1},{1,0},{4,5},{5,4},{8,9},{9,8},{12,13},{13,12},{2,3},{3,2},{6... | collective-permute-start | bytes 411656 | tf_op jit(solution)/shard_map/ppermute | solution.py:391
  4.1 1.5 %collective-permute-start.1 = (bf16[536,128]{1,0:T(8,128)(2,1)S(1)}, bf16[536,128]{1,0:T(8,128)(2,1)S(1)}, u32[]{:S(2)}, u32[]{:S(2)}) collective-permute-start(bf16[536,128]{1,0:T(8,128)(2,1)S(1)} %tall_design.1), channel_id=1, source_target_pairs={{0,8},{1,9},{4,12},{5,13},{8,0},{9,1},{12,4},{13,5},{2,10},{3,11},... | collective-permute-start | bytes 411656 | tf_op jit(solution)/shard_map/ppermute | solution.py:391
  5.6 4.9 %smooth.1 = bf16[8,128,1024]{2,1,0:T(8,128)(2,1)} custom-call(bf16[128,32,256]{2,1,0:T(8,128)(2,1)} %bitcast.23, bf16[256,256]{1,0:T(8,128)(2,1)} %constant.29.clone.order, bf16[256,256]{1,0:T(8,128)(2,1)} %constant.30.clone.table), custom_call_target="tpu_custom_call" | custom-call | tf_op jit(solution)/shard_map/smooth/pallas_call | solution.py:167
  10.6 1.5 %collective-permute-done.1 = bf16[536,128]{1,0:T(8,128)(2,1)S(1)} collective-permute-done((bf16[536,128]{1,0:T(8,128)(2,1)S(1)}, bf16[536,128]{1,0:T(8,128)(2,1)S(1)}, u32[]{:S(2)}, u32[]{:S(2)}) %collective-permute-start.1) | collective-permute-done | bytes 137248 | tf_op jit(solution)/shard_map/ppermute | solution.py:391
  12.1 3.6 %all-to-all-start = ((bf16[8,128,1024]{2,1,0:T(8,128)(2,1)}), bf16[8,128,1024]{2,1,0:T(8,128)(2,1)S(1)}, u32[]{:S(2)}, u32[]{:S(2)}) async-start(bf16[8,128,1024]{2,1,0:T(8,128)(2,1)} %smooth.1), calls=%async_computation | async-start | bytes 4194304 | tf_op jit(solution)/shard_map/all_to_all | solution.py:405
  15.8 0.5 collective-permute-start.3
  16.3 0.8 %copy-done = bf16[4,536,128]{2,1,0:T(8,128)(2,1)} copy-done((bf16[4,536,128]{2,1,0:T(8,128)(2,1)}, bf16[4,536,128]{2,1,0:T(8,128)(2,1)S(1)}, u32[]{:S(2)}) %copy-start) | copy-done | bytes 548888
  17.1 0.9 %collective-permute-done.3.others = bf16[4,536,128]{2,1,0:T(8,128)(2,1)S(1)} collective-permute-done((bf16[4,536,128]{2,1,0:T(8,128)(2,1)S(1)}, bf16[4,536,128]{2,1,0:T(8,128)(2,1)S(1)}, u32[]{:S(2)}, u32[]{:S(2)}) %collective-permute-start.3) | collective-permute-done | bytes 548896 | tf_op jit(solution)/shard_map/ppermute | solution.py:391
  18.0 0.8 %copy-done.2 = bf16[4,536,128]{2,1,0:T(8,128)(2,1)} copy-done((bf16[4,536,128]{2,1,0:T(8,128)(2,1)}, bf16[4,536,128]{2,1,0:T(8,128)(2,1)S(1)}, u32[]{:S(2)}) %copy-start.2) | copy-done | bytes 548888
  18.8 1.0 %copy-done.1 = bf16[4,536,128]{2,1,0:T(8,128)(2,1)S(1)} copy-done((bf16[4,536,128]{2,1,0:T(8,128)(2,1)S(1)}, bf16[4,536,128]{2,1,0:T(8,128)(2,1)}, u32[]{:S(2)}) %copy-start.1) | copy-done | bytes 548888
  19.8 1.0 %copy-done.3 = bf16[4,536,128]{2,1,0:T(8,128)(2,1)S(1)} copy-done((bf16[4,536,128]{2,1,0:T(8,128)(2,1)S(1)}, bf16[4,536,128]{2,1,0:T(8,128)(2,1)}, u32[]{:S(2)}) %copy-start.3) | copy-done | bytes 548888
  20.9 1.7 %moments.1 = (bf16[536,1024]{1,0:T(8,128)(2,1)S(1)}, f32[32,640]{1,0:T(8,128)}) custom-call(s32[1]{0:T(128)} %bitcast.6.me, bf16[4,536,128]{2,1,0:T(8,128)(2,1)S(1)} %copy-done.1, bf16[4,536,128]{2,1,0:T(8,128)(2,1)S(1)} %copy-done.3), custom_call_target="tpu_custom_call" | custom-call | tf_op jit(solution)/shard_map/moments/pallas_call | solution.py:88
  22.6 2.6 %collective-permute-start.4 = (f32[32,640]{1,0:T(8,128)}, f32[32,640]{1,0:T(8,128)S(1)}, u32[]{:S(2)}, u32[]{:S(2)}) collective-permute-start(f32[32,640]{1,0:T(8,128)} %get-tuple-element.32.moment.refs_0_), channel_id=1, source_target_pairs={{0,2},{2,0},{1,3},{3,1},{4,6},{6,4},{5,7},{7,5},{8,10},{10,8},{9,1... | collective-permute-start | bytes 245768 | tf_op jit(solution)/shard_map/ppermute | solution.py:391
  25.2 0.9 %copy-done.6 = f32[32,640]{1,0:T(8,128)S(1)} copy-done((f32[32,640]{1,0:T(8,128)S(1)}, f32[32,640]{1,0:T(8,128)}, u32[]{:S(2)}) %copy-start.6) | copy-done | bytes 81944
  26.1 2.0 %pair_fit.1.coef = f32[512,128]{1,0:T(8,128)S(1)} custom-call(f32[32,640]{1,0:T(8,128)S(1)} %copy-done.6), custom_call_target="tpu_custom_call" | custom-call | tf_op jit(solution)/shard_map/pair_fit/pallas_call | solution.py:88
  28.1 13.0 %collective-permute-done.4.refs_1_ = f32[32,640]{1,0:T(8,128)S(1)} collective-permute-done((f32[32,640]{1,0:T(8,128)}, f32[32,640]{1,0:T(8,128)S(1)}, u32[]{:S(2)}, u32[]{:S(2)}) %collective-permute-start.4) | collective-permute-done | bytes 81952 | tf_op jit(solution)/shard_map/ppermute | solution.py:391
  41.1 2.9 %cohort_fit.1 = (f32[512,128]{1,0:T(8,128)}, f32[24,128]{1,0:T(8,128)}) custom-call(f32[32,640]{1,0:T(8,128)S(1)} %copy-done.6, f32[32,640]{1,0:T(8,128)S(1)} %collective-permute-done.4.refs_1_), custom_call_target="tpu_custom_call" | custom-call | tf_op jit(solution)/shard_map/cohort_fit/pallas_call | solution.py:88
  44.0 0.5 column_sums.1.stats.refs_0_
  44.5 3.3 %collective-permute-start.5 = (f32[24,1024]{1,0:T(8,128)S(1)}, f32[24,1024]{1,0:T(8,128)}, u32[]{:S(2)}, u32[]{:S(2)}) collective-permute-start(f32[24,1024]{1,0:T(8,128)S(1)} %column_sums.1.stats.refs_0_), channel_id=1, source_target_pairs={{0,2},{2,0},{1,3},{3,1},{4,6},{6,4},{5,7},{7,5},{8,10},{10,8},{9,1... | collective-permute-start | bytes 294920 | tf_op jit(solution)/shard_map/ppermute | solution.py:391
  47.8 1.5 %far_products.1 = (f32[128,1024]{1,0:T(8,128)S(1)}, f32[128,1024]{1,0:T(8,128)S(1)}) custom-call(s32[1]{0:T(128)} %bitcast.far, s32[1]{0:T(128)} %bitcast.1.near, bf16[536,1024]{1,0:T(8,128)(2,1)S(1)} %get-tuple-element.37.genes, bf16[1024,1024]{1,0:T(8,128)(2,1)S(1)} %bitcast.19, f32[512,128]{1,0:T(8,128)S(1)} %pair_fit.1.coef, ...), custom_call_target="tpu_custom_call" | custom-call | tf_op jit(solution)/shard_map/far_products/pallas_call | solution.py:88
  49.3 0.7 convert_element_type.18
  50.0 0.7 convert_element_type.19
  50.8 2.7 %collective-permute-start.6 = (f16[128,1024]{1,0:T(8,128)(2,1)}, f16[128,1024]{1,0:T(8,128)(2,1)}, u32[]{:S(2)}, u32[]{:S(2)}) collective-permute-start(f16[128,1024]{1,0:T(8,128)(2,1)} %convert_element_type.18), channel_id=1, source_target_pairs={{0,2},{1,3},{2,0},{3,1},{4,6},{5,7},{6,4},{7,5},{8,10},{9,11},{10,... | collective-permute-start | bytes 786440 | tf_op jit(solution)/shard_map/ppermute | solution.py:391
  53.5 3.7 %collective-permute-start.8 = (f16[128,1024]{1,0:T(8,128)(2,1)}, f16[128,1024]{1,0:T(8,128)(2,1)}, u32[]{:S(2)}, u32[]{:S(2)}) collective-permute-start(f16[128,1024]{1,0:T(8,128)(2,1)} %convert_element_type.19), channel_id=1, source_target_pairs={{0,3},{1,2},{2,1},{3,0},{4,7},{5,6},{6,5},{7,4},{8,11},{9,10},{10,... | collective-permute-start | bytes 786440 | tf_op jit(solution)/shard_map/ppermute | solution.py:391
  57.1 2.6 %base_ratio.1 = (f32[128,1024]{1,0:T(8,128)S(1)}, f32[128,1024]{1,0:T(8,128)S(1)}, f32[8,1024]{1,0:T(8,128)S(1)}) custom-call(s32[1]{0:T(128)} %bitcast.far, s32[1]{0:T(128)} %bitcast.1.near, f32[512,128]{1,0:T(8,128)S(1)} %copy-done.5, f32[24,128]{1,0:T(8,128)S(1)} %copy-done.7, bf16[536,1024]{1,0:T(8,128)(2,1)S(1)} %get-tuple-element.37.genes, ...), custom_call_target="tpu_custom_call" | custom-call | tf_op jit(solution)/shard_map/base_ratio/pallas_call | solution.py:88
  59.8 0.7 copy-done.4
  60.5 2.0 %collective-permute-start.9 = (f32[8,1024]{1,0:T(8,128)S(1)}, f32[8,1024]{1,0:T(8,128)S(1)}, u32[]{:S(2)}, u32[]{:S(2)}) collective-permute-start(f32[8,1024]{1,0:T(8,128)S(1)} %get-tuple-element.46), channel_id=1, source_target_pairs={{0,1},{1,0},{2,3},{3,2},{4,5},{5,4},{6,7},{7,6},{8,9},{9,8},{10,11... | collective-permute-start | bytes 98312 | tf_op jit(solution)/shard_map/ppermute | solution.py:391
  62.6 1.0 %dynamic-slice_reduce_fusion = f32[128]{0:T(128)S(1)} fusion(f32[512,128]{1,0:T(8,128)} %get-tuple-element.35.coef, s32[]{:T(128)S(6)} %select_n.16, s32[]{:T(128)S(6)} %add.21), kind=kLoop, calls=%fused_computation.4 | loop fusion | bytes 1032 | tf_op jit(solution)/shard_map/slice | solution.py:449
  63.6 12.4 %collective-permute-done.9 = f32[8,1024]{1,0:T(8,128)S(1)} collective-permute-done((f32[8,1024]{1,0:T(8,128)S(1)}, f32[8,1024]{1,0:T(8,128)S(1)}, u32[]{:S(2)}, u32[]{:S(2)}) %collective-permute-start.9) | collective-permute-done | bytes 32800 | tf_op jit(solution)/shard_map/ppermute | solution.py:391
  76.0 1.8 %multiply_bitcast_fusion.1 = (f32[128,1,1024]{2,0,1:T(8,128)S(1)}, f32[128,1,1024]{2,0,1:T(8,128)S(1)}) fusion(f32[128,1024]{1,0:T(8,128)} %copy-done.4, f16[128,1024]{1,0:T(8,128)(2,1)} %collective-permute-done.6, f32[1024]{0:T(1024)S(1)} %bitcast.27, f32[128]{0:T(128)S(1)} %dynamic-slice_reduce_fusion, f32[1024]{0:T(1024)S(1)} %bitcast.28, ...), kind=kLoop, calls=%fused_computation.3 | loop fusion | flops 2359296 | bytes 2368000 | tf_op jit(solution)/shard_map/stack | solution.py:455
  78.3 1.3 %copy.8 = f32[128,4,2,256]{3,2,1,0:T(2,128)} copy(f32[128,4,2,256]{0,3,2,1:T(8,128)S(1)} %bitcast.22) | data formatting | bytes 2097152 | tf_op jit(solution)/shard_map/jit(_where)/select_n | solution.py:455
  (25 shorter events, 0.6 us)
Async XLA Ops:
  1.0 9.6 %collective-permute-start = (bf16[536,128]{1,0:T(8,128)(2,1)S(1)}, bf16[536,128]{1,0:T(8,128)(2,1)S(1)}, u32[]{:S(2)}, u32[]{:S(2)}) collective-permute-start(bf16[536,128]{1,0:T(8,128)(2,1)S(1)} %tall_design.1), channel_id=1, source_target_pairs={{0,1},{1,0},{4,5},{5,4},{8,9},{9,8},{12,13},{13,12},{2,3},{3,2},{6... | collective-permute-start | bytes 411656 | tf_op jit(solution)/shard_map/ppermute | solution.py:391
  4.1 8.0 %collective-permute-start.1 = (bf16[536,128]{1,0:T(8,128)(2,1)S(1)}, bf16[536,128]{1,0:T(8,128)(2,1)S(1)}, u32[]{:S(2)}, u32[]{:S(2)}) collective-permute-start(bf16[536,128]{1,0:T(8,128)(2,1)S(1)} %tall_design.1), channel_id=1, source_target_pairs={{0,8},{1,9},{4,12},{5,13},{8,0},{9,1},{12,4},{13,5},{2,10},{3,11},... | collective-permute-start | bytes 411656 | tf_op jit(solution)/shard_map/ppermute | solution.py:391
  5.6 6.5 %collective-permute-start.2 = (bf16[536,128]{1,0:T(8,128)(2,1)S(1)}, bf16[536,128]{1,0:T(8,128)(2,1)S(1)}, u32[]{:S(2)}, u32[]{:S(2)}) collective-permute-start(bf16[536,128]{1,0:T(8,128)(2,1)S(1)} %tall_design.1), channel_id=1, source_target_pairs={{0,9},{1,8},{4,13},{5,12},{8,1},{9,0},{12,5},{13,4},{2,11},{3,10},... | collective-permute-start | bytes 411656 | tf_op jit(solution)/shard_map/ppermute | solution.py:391
  12.1 31.9 %all-to-all-start = ((bf16[8,128,1024]{2,1,0:T(8,128)(2,1)}), bf16[8,128,1024]{2,1,0:T(8,128)(2,1)S(1)}, u32[]{:S(2)}, u32[]{:S(2)}) async-start(bf16[8,128,1024]{2,1,0:T(8,128)(2,1)} %smooth.1), calls=%async_computation | async-start | bytes 4194304 | tf_op jit(solution)/shard_map/all_to_all | solution.py:405
  15.8 2.1 %collective-permute-start.3 = (bf16[4,536,128]{2,1,0:T(8,128)(2,1)S(1)}, bf16[4,536,128]{2,1,0:T(8,128)(2,1)S(1)}, u32[]{:S(2)}, u32[]{:S(2)}) collective-permute-start(bf16[4,536,128]{2,1,0:T(8,128)(2,1)S(1)} %pad_maximum_fusion.blocks), channel_id=1, source_target_pairs={{0,4},{1,5},{4,0},{5,1},{8,12},{9,13},{12,8},{13,9},{2,6},{3,7},{6... | collective-permute-start | bytes 1646600 | tf_op jit(solution)/shard_map/ppermute | solution.py:391
  16.3 0.8 %copy-start = (bf16[4,536,128]{2,1,0:T(8,128)(2,1)}, bf16[4,536,128]{2,1,0:T(8,128)(2,1)S(1)}, u32[]{:S(2)}) copy-start(bf16[4,536,128]{2,1,0:T(8,128)(2,1)S(1)} %pad_maximum_fusion.blocks) | copy-start | bytes 1646596
  18.0 0.8 %copy-start.2 = (bf16[4,536,128]{2,1,0:T(8,128)(2,1)}, bf16[4,536,128]{2,1,0:T(8,128)(2,1)S(1)}, u32[]{:S(2)}) copy-start(bf16[4,536,128]{2,1,0:T(8,128)(2,1)S(1)} %collective-permute-done.3.others) | copy-start | bytes 1646596
  18.8 1.1 %copy-start.1 = (bf16[4,536,128]{2,1,0:T(8,128)(2,1)S(1)}, bf16[4,536,128]{2,1,0:T(8,128)(2,1)}, u32[]{:S(2)}) copy-start(bf16[4,536,128]{2,1,0:T(8,128)(2,1)} %copy-done) | copy-start | bytes 1646596
  19.8 1.1 %copy-start.3 = (bf16[4,536,128]{2,1,0:T(8,128)(2,1)S(1)}, bf16[4,536,128]{2,1,0:T(8,128)(2,1)}, u32[]{:S(2)}) copy-start(bf16[4,536,128]{2,1,0:T(8,128)(2,1)} %copy-done.2) | copy-start | bytes 1646596
  22.6 18.5 %collective-permute-start.4 = (f32[32,640]{1,0:T(8,128)}, f32[32,640]{1,0:T(8,128)S(1)}, u32[]{:S(2)}, u32[]{:S(2)}) collective-permute-start(f32[32,640]{1,0:T(8,128)} %get-tuple-element.32.moment.refs_0_), channel_id=1, source_target_pairs={{0,2},{2,0},{1,3},{3,1},{4,6},{6,4},{5,7},{7,5},{8,10},{10,8},{9,1... | collective-permute-start | bytes 245768 | tf_op jit(solution)/shard_map/ppermute | solution.py:391
  25.2 0.9 %copy-start.6 = (f32[32,640]{1,0:T(8,128)S(1)}, f32[32,640]{1,0:T(8,128)}, u32[]{:S(2)}) copy-start(f32[32,640]{1,0:T(8,128)} %get-tuple-element.32.moment.refs_0_) | copy-start | bytes 245764
  44.5 6.3 %collective-permute-start.5 = (f32[24,1024]{1,0:T(8,128)S(1)}, f32[24,1024]{1,0:T(8,128)}, u32[]{:S(2)}, u32[]{:S(2)}) collective-permute-start(f32[24,1024]{1,0:T(8,128)S(1)} %column_sums.1.stats.refs_0_), channel_id=1, source_target_pairs={{0,2},{2,0},{1,3},{3,1},{4,6},{6,4},{5,7},{7,5},{8,10},{10,8},{9,1... | collective-permute-start | bytes 294920 | tf_op jit(solution)/shard_map/ppermute | solution.py:391
  47.8 9.4 %copy-start.5 = (f32[512,128]{1,0:T(8,128)S(1)}, f32[512,128]{1,0:T(8,128)}, u32[]{:S(2)}) copy-start(f32[512,128]{1,0:T(8,128)} %get-tuple-element.35.coef) | copy-start | bytes 786436
  47.8 9.4 %copy-start.7 = (f32[24,128]{1,0:T(8,128)S(1)}, f32[24,128]{1,0:T(8,128)}, u32[]{:S(2)}) copy-start(f32[24,128]{1,0:T(8,128)} %get-tuple-element.36.inverse) | copy-start | bytes 36868
  50.8 25.2 %collective-permute-start.6 = (f16[128,1024]{1,0:T(8,128)(2,1)}, f16[128,1024]{1,0:T(8,128)(2,1)}, u32[]{:S(2)}, u32[]{:S(2)}) collective-permute-start(f16[128,1024]{1,0:T(8,128)(2,1)} %convert_element_type.18), channel_id=1, source_target_pairs={{0,2},{1,3},{2,0},{3,1},{4,6},{5,7},{6,4},{7,5},{8,10},{9,11},{10,... | collective-permute-start | bytes 786440 | tf_op jit(solution)/shard_map/ppermute | solution.py:391
  53.5 22.5 %collective-permute-start.8 = (f16[128,1024]{1,0:T(8,128)(2,1)}, f16[128,1024]{1,0:T(8,128)(2,1)}, u32[]{:S(2)}, u32[]{:S(2)}) collective-permute-start(f16[128,1024]{1,0:T(8,128)(2,1)} %convert_element_type.19), channel_id=1, source_target_pairs={{0,3},{1,2},{2,1},{3,0},{4,7},{5,6},{6,5},{7,4},{8,11},{9,10},{10,... | collective-permute-start | bytes 786440 | tf_op jit(solution)/shard_map/ppermute | solution.py:391
  59.8 0.8 copy-start.4
  60.5 15.4 %collective-permute-start.7 = (f16[128,1024]{1,0:T(8,128)(2,1)S(1)}, f16[128,1024]{1,0:T(8,128)(2,1)S(1)}, u32[]{:S(2)}, u32[]{:S(2)}) collective-permute-start(f16[128,1024]{1,0:T(8,128)(2,1)S(1)} %convert_element_type.21), channel_id=1, source_target_pairs={{0,1},{1,0},{2,3},{3,2},{4,5},{5,4},{6,7},{7,6},{8,9},{9,8},{10,11... | collective-permute-start | bytes 786440 | tf_op jit(solution)/shard_map/ppermute | solution.py:391
  60.5 15.4 %collective-permute-start.9 = (f32[8,1024]{1,0:T(8,128)S(1)}, f32[8,1024]{1,0:T(8,128)S(1)}, u32[]{:S(2)}, u32[]{:S(2)}) collective-permute-start(f32[8,1024]{1,0:T(8,128)S(1)} %get-tuple-element.46), channel_id=1, source_target_pairs={{0,1},{1,0},{2,3},{3,2},{4,5},{5,4},{6,7},{7,6},{8,9},{9,8},{10,11... | collective-permute-start | bytes 98312 | tf_op jit(solution)/shard_map/ppermute | solution.py:391

commit v12 on v11

--- a/solution.py
+++ b/solution.py
@@ -161,7 +161,7 @@
     size = width // chunks
     assert size % plane == 0
     group = max(1, min(maps, 256 // (SUBJ_TILE * planes)))
-    step = 32
+    step = min(subjects, 64)
     order = jnp.asarray(row_order(group, planes))
     table = jnp.asarray(plane_kernel(plane))
     return pl.pallas_call(
@@ -432,8 +432,8 @@
     line = ("far", "near")
     where = [far[None], near[None], n_far, n_near]
     sent = far_products(genes, columns, pair_coef, stats, *where)
+    sent, stat_parts = lax.optimization_barrier((sent, stat_parts))
     sent = [piece.astype(jnp.float16) for piece in sent]
-    sent, stat_parts = lax.optimization_barrier((sent, stat_parts))
     pieces = {
         k: permute_xor(sent[k - n_near], line, k) for k in range(n_near, n_far * n_near)
     }
@@ -450,6 +450,9 @@
             ratio = ratio + pieces[j * n_near + offset].astype(jnp.float32) * weight
         return ratio * jnp.sqrt(freedom / (1.0 - ratio * ratio))
 
+    first = [k for k in pieces if k % n_near]
+    *taken, home = lax.optimization_barrier((*[pieces[k] for k in first], home))
+    pieces.update(zip(first, taken))
     home = t_of(home, factors, 0)
     away = t_of(away, away_factors, 1)
     both = jnp.where(near == 0, jnp.stack([home, away], 1), jnp.stack([away, home], 1))

time: 80.1 us -> 83 us (1.036)
  waiting for transfers between devices: 27.8 us -> 32.4 us
  Pallas kernels: 17.2 us -> 16.2 us
    ppermute x10, waiting for transfers between devices: 27.8 us -> 32.4 us  [permute_xor(): return lax.ppermute(value, axes, [(i, i ^ bits) for i in range(size)])]
    pallas_call x1, Pallas kernels: 4.94 us -> 3.98 us  [smooth(): pl.pallas_call(functools.partial(smooth_kernel, group, planes, per_vox, p...]
  transfers between devices with their start and end apart: 11 -> 11, of which waited for: 4 -> 6; matrix products, arithmetic and copies ran while one was open for 3% -> 2% of each run, Pallas kernels for 20% -> 18%
where the time goes in v12:
time: 83 us; the launch traced here: 82.5 us
  waiting for transfers between devices  32.4 us (39%)
  starting transfers between devices  22.2 us (27%)
  Pallas kernels  16.2 us (20%)
  local copies, waits for them, and re-layouts  8.03 us (10%)
  other arithmetic  3.54 us (4%)
    ppermute x10, waiting for transfers between devices, permute_xor(): return lax.ppermute(value, axes, [(i, i ^ bits) for i in range(size)])  32.4 us
    ppermute x10, starting transfers between devices, permute_xor(): return lax.ppermute(value, axes, [(i, i ^ bits) for i in range(size)])  18.6 us
    pallas_call x6, Pallas kernels, call(): pl.pallas_call(kernel, out_shape=outs, in_specs=[IN_SMEM] * len(scalars)...  11.3 us
    unnamed x16, local copies, waits for them, and re-layouts  5.37 us
    pallas_call x1, Pallas kernels, smooth(): pl.pallas_call(functools.partial(smooth_kernel, group, planes, per_vox, p...  3.98 us
    all_to_all x1, starting transfers between devices, exchange(): value = lax.all_to_all(value, ('vox', 'near'), 0, 0, tiled=True)  3.6 us
    another operation x1, other arithmetic, on_device(): jnp.stack([home, away], 1)  1.84 us
  transfers between devices with their start and end apart: 11, of which 6 were waited for; matrix products, arithmetic and copies ran while one was open for 2% of the time, Pallas kernels for 18%

profile of v12, /device:TPU:0, one launch (start us, length us, event | category | flops | bytes accessed | tf_op | source)
XLA Modules:
  0.0 82.5 jit_solution(12960580330180900460)
XLA Ops:
  0.0 1.0 %tall_design.1 = bf16[536,128]{1,0:T(8,128)(2,1)S(1)} custom-call(bf16[128,512]{1,0:T(8,128)(2,1)} %genotypes.1, s32[1,128]{1,0:T(1,128)} %bitcast.30, bf16[16,128]{1,0:T(8,128)(2,1)} %bitcast.29), custom_call_target="tpu_custom_call" | custom-call | tf_op jit(solution)/shard_map/tall_design/pallas_call | solution.py:112
  1.0 3.1 %collective-permute-start = (bf16[536,128]{1,0:T(8,128)(2,1)S(1)}, bf16[536,128]{1,0:T(8,128)(2,1)S(1)}, u32[]{:S(2)}, u32[]{:S(2)}) collective-permute-start(bf16[536,128]{1,0:T(8,128)(2,1)S(1)} %tall_design.1), channel_id=1, source_target_pairs={{0,1},{1,0},{4,5},{5,4},{8,9},{9,8},{12,13},{13,12},{2,3},{3,2},{6... | collective-permute-start | bytes 411656 | tf_op jit(solution)/shard_map/ppermute | solution.py:391
  4.1 1.5 %collective-permute-start.1 = (bf16[536,128]{1,0:T(8,128)(2,1)S(1)}, bf16[536,128]{1,0:T(8,128)(2,1)S(1)}, u32[]{:S(2)}, u32[]{:S(2)}) collective-permute-start(bf16[536,128]{1,0:T(8,128)(2,1)S(1)} %tall_design.1), channel_id=1, source_target_pairs={{0,8},{1,9},{4,12},{5,13},{8,0},{9,1},{12,4},{13,5},{2,10},{3,11},... | collective-permute-start | bytes 411656 | tf_op jit(solution)/shard_map/ppermute | solution.py:391
  5.6 4.0 %smooth.1 = bf16[8,128,1024]{2,1,0:T(8,128)(2,1)} custom-call(bf16[128,32,256]{2,1,0:T(8,128)(2,1)} %bitcast.23, bf16[256,256]{1,0:T(8,128)(2,1)} %constant.29.clone.order, bf16[256,256]{1,0:T(8,128)(2,1)} %constant.30.clone.table), custom_call_target="tpu_custom_call" | custom-call | tf_op jit(solution)/shard_map/smooth/pallas_call | solution.py:167
  9.6 2.5 %collective-permute-done.1 = bf16[536,128]{1,0:T(8,128)(2,1)S(1)} collective-permute-done((bf16[536,128]{1,0:T(8,128)(2,1)S(1)}, bf16[536,128]{1,0:T(8,128)(2,1)S(1)}, u32[]{:S(2)}, u32[]{:S(2)}) %collective-permute-start.1) | collective-permute-done | bytes 137248 | tf_op jit(solution)/shard_map/ppermute | solution.py:391
  12.1 3.6 %all-to-all-start = ((bf16[8,128,1024]{2,1,0:T(8,128)(2,1)}), bf16[8,128,1024]{2,1,0:T(8,128)(2,1)S(1)}, u32[]{:S(2)}, u32[]{:S(2)}) async-start(bf16[8,128,1024]{2,1,0:T(8,128)(2,1)} %smooth.1), calls=%async_computation | async-start | bytes 4194304 | tf_op jit(solution)/shard_map/all_to_all | solution.py:405
  16.3 0.8 copy-done
  17.1 0.9 %collective-permute-done.3.others = bf16[4,536,128]{2,1,0:T(8,128)(2,1)S(1)} collective-permute-done((bf16[4,536,128]{2,1,0:T(8,128)(2,1)S(1)}, bf16[4,536,128]{2,1,0:T(8,128)(2,1)S(1)}, u32[]{:S(2)}, u32[]{:S(2)}) %collective-permute-start.3) | collective-permute-done | bytes 548896 | tf_op jit(solution)/shard_map/ppermute | solution.py:391
  18.0 0.8 copy-done.2
  18.8 1.0 %copy-done.1 = bf16[4,536,128]{2,1,0:T(8,128)(2,1)S(1)} copy-done((bf16[4,536,128]{2,1,0:T(8,128)(2,1)S(1)}, bf16[4,536,128]{2,1,0:T(8,128)(2,1)}, u32[]{:S(2)}) %copy-start.1) | copy-done | bytes 548888
  19.8 1.0 %copy-done.3 = bf16[4,536,128]{2,1,0:T(8,128)(2,1)S(1)} copy-done((bf16[4,536,128]{2,1,0:T(8,128)(2,1)S(1)}, bf16[4,536,128]{2,1,0:T(8,128)(2,1)}, u32[]{:S(2)}) %copy-start.3) | copy-done | bytes 548888
  20.9 1.7 %moments.1 = (bf16[536,1024]{1,0:T(8,128)(2,1)S(1)}, f32[32,640]{1,0:T(8,128)}) custom-call(s32[1]{0:T(128)} %bitcast.2.me, bf16[4,536,128]{2,1,0:T(8,128)(2,1)S(1)} %copy-done.1, bf16[4,536,128]{2,1,0:T(8,128)(2,1)S(1)} %copy-done.3), custom_call_target="tpu_custom_call" | custom-call | tf_op jit(solution)/shard_map/moments/pallas_call | solution.py:88
  22.6 2.6 %collective-permute-start.4 = (f32[32,640]{1,0:T(8,128)}, f32[32,640]{1,0:T(8,128)S(1)}, u32[]{:S(2)}, u32[]{:S(2)}) collective-permute-start(f32[32,640]{1,0:T(8,128)} %get-tuple-element.35.moment.refs_0_), channel_id=1, source_target_pairs={{0,2},{2,0},{1,3},{3,1},{4,6},{6,4},{5,7},{7,5},{8,10},{10,8},{9,1... | collective-permute-start | bytes 245768 | tf_op jit(solution)/shard_map/ppermute | solution.py:391
  25.2 0.9 %copy-done.6 = f32[32,640]{1,0:T(8,128)S(1)} copy-done((f32[32,640]{1,0:T(8,128)S(1)}, f32[32,640]{1,0:T(8,128)}, u32[]{:S(2)}) %copy-start.6) | copy-done | bytes 81944
  26.1 2.0 %pair_fit.1.coef = f32[512,128]{1,0:T(8,128)S(1)} custom-call(f32[32,640]{1,0:T(8,128)S(1)} %copy-done.6), custom_call_target="tpu_custom_call" | custom-call | tf_op jit(solution)/shard_map/pair_fit/pallas_call | solution.py:88
  28.1 13.0 %collective-permute-done.4.refs_1_ = f32[32,640]{1,0:T(8,128)S(1)} collective-permute-done((f32[32,640]{1,0:T(8,128)}, f32[32,640]{1,0:T(8,128)S(1)}, u32[]{:S(2)}, u32[]{:S(2)}) %collective-permute-start.4) | collective-permute-done | bytes 81952 | tf_op jit(solution)/shard_map/ppermute | solution.py:391
  41.1 2.9 %cohort_fit.1 = (f32[512,128]{1,0:T(8,128)}, f32[24,128]{1,0:T(8,128)}) custom-call(f32[32,640]{1,0:T(8,128)S(1)} %copy-done.6, f32[32,640]{1,0:T(8,128)S(1)} %collective-permute-done.4.refs_1_), custom_call_target="tpu_custom_call" | custom-call | tf_op jit(solution)/shard_map/cohort_fit/pallas_call | solution.py:88
  44.5 3.3 %collective-permute-start.5 = (f32[24,1024]{1,0:T(8,128)S(1)}, f32[24,1024]{1,0:T(8,128)}, u32[]{:S(2)}, u32[]{:S(2)}) collective-permute-start(f32[24,1024]{1,0:T(8,128)S(1)} %column_sums.1.stats.refs_0_), channel_id=1, source_target_pairs={{0,2},{2,0},{1,3},{3,1},{4,6},{6,4},{5,7},{7,5},{8,10},{10,8},{9,1... | collective-permute-start | bytes 294920 | tf_op jit(solution)/shard_map/ppermute | solution.py:391
  47.8 1.5 %far_products.1 = (f32[128,1024]{1,0:T(8,128)S(1)}, f32[128,1024]{1,0:T(8,128)S(1)}) custom-call(s32[1]{0:T(128)} %bitcast.far, s32[1]{0:T(128)} %bitcast.1.near, bf16[536,1024]{1,0:T(8,128)(2,1)S(1)} %get-tuple-element.33.genes, bf16[1024,1024]{1,0:T(8,128)(2,1)S(1)} %bitcast.19, f32[512,128]{1,0:T(8,128)S(1)} %pair_fit.1.coef, ...), custom_call_target="tpu_custom_call" | custom-call | tf_op jit(solution)/shard_map/far_products/pallas_call | solution.py:88
  49.3 1.4 %collective-permute-done.5.refs_1_ = f32[24,1024]{1,0:T(8,128)} collective-permute-done((f32[24,1024]{1,0:T(8,128)S(1)}, f32[24,1024]{1,0:T(8,128)}, u32[]{:S(2)}, u32[]{:S(2)}) %collective-permute-start.5) | collective-permute-done | bytes 98336 | tf_op jit(solution)/shard_map/ppermute | solution.py:391
  50.7 0.7 convert_element_type.18
  51.5 5.6 %collective-permute-start.6 = (f16[128,1024]{1,0:T(8,128)(2,1)}, f16[128,1024]{1,0:T(8,128)(2,1)}, u32[]{:S(2)}, u32[]{:S(2)}) collective-permute-start(f16[128,1024]{1,0:T(8,128)(2,1)} %convert_element_type.18), channel_id=1, source_target_pairs={{0,3},{1,2},{2,1},{3,0},{4,7},{5,6},{6,5},{7,4},{8,11},{9,10},{10,... | collective-permute-start | bytes 786440 | tf_op jit(solution)/shard_map/ppermute | solution.py:391
  57.1 0.7 convert_element_type.19
  57.8 2.6 %base_ratio.1 = (f32[128,1024]{1,0:T(8,128)S(1)}, f32[128,1024]{1,0:T(8,128)S(1)}, f32[8,1024]{1,0:T(8,128)S(1)}) custom-call(s32[1]{0:T(128)} %bitcast.far, s32[1]{0:T(128)} %bitcast.1.near, f32[512,128]{1,0:T(8,128)S(1)} %copy-done.5, f32[24,128]{1,0:T(8,128)S(1)} %copy-done.7, bf16[536,1024]{1,0:T(8,128)(2,1)S(1)} %get-tuple-element.33.genes, ...), custom_call_target="tpu_custom_call" | custom-call | tf_op jit(solution)/shard_map/base_ratio/pallas_call | solution.py:88
  60.5 0.7 copy-done.4
  61.2 0.6 collective-permute-start.8
  61.8 1.5 %collective-permute-start.9 = (f32[8,1024]{1,0:T(8,128)S(1)}, f32[8,1024]{1,0:T(8,128)S(1)}, u32[]{:S(2)}, u32[]{:S(2)}) collective-permute-start(f32[8,1024]{1,0:T(8,128)S(1)} %get-tuple-element.50), channel_id=1, source_target_pairs={{0,1},{1,0},{2,3},{3,2},{4,5},{5,4},{6,7},{7,6},{8,9},{9,8},{10,11... | collective-permute-start | bytes 98312 | tf_op jit(solution)/shard_map/ppermute | solution.py:391
  63.2 1.0 %dynamic-slice_reduce_fusion = f32[128]{0:T(128)S(1)} fusion(f32[512,128]{1,0:T(8,128)} %get-tuple-element.43.coef, s32[]{:T(128)S(6)} %select_n.16, s32[]{:T(128)S(6)} %add.21), kind=kLoop, calls=%fused_computation.4 | loop fusion | bytes 1032 | tf_op jit(solution)/shard_map/slice | solution.py:449
  64.3 10.7 %collective-permute-done.9 = f32[8,1024]{1,0:T(8,128)S(1)} collective-permute-done((f32[8,1024]{1,0:T(8,128)S(1)}, f32[8,1024]{1,0:T(8,128)S(1)}, u32[]{:S(2)}, u32[]{:S(2)}) %collective-permute-start.9) | collective-permute-done | bytes 32800 | tf_op jit(solution)/shard_map/ppermute | solution.py:391
  74.9 4.0 %collective-permute-done.7 = f16[128,1024]{1,0:T(8,128)(2,1)} collective-permute-done((f16[128,1024]{1,0:T(8,128)(2,1)}, f16[128,1024]{1,0:T(8,128)(2,1)}, u32[]{:S(2)}, u32[]{:S(2)}) %collective-permute-start.7) | collective-permute-done | bytes 262176 | tf_op jit(solution)/shard_map/ppermute | solution.py:391
  78.9 1.8 %multiply_bitcast_fusion.1 = (f32[128,1,1024]{2,0,1:T(8,128)S(1)}, f32[128,1,1024]{2,0,1:T(8,128)S(1)}) fusion(f32[128,1024]{1,0:T(8,128)} %copy-done.4, f16[128,1024]{1,0:T(8,128)(2,1)} %collective-permute-done.7, f32[1024]{0:T(1024)S(1)} %bitcast.27, f32[128]{0:T(128)S(1)} %dynamic-slice_reduce_fusion, f32[1024]{0:T(1024)S(1)} %bitcast.28, ...), kind=kLoop, calls=%fused_computation.3 | loop fusion | flops 2359296 | bytes 2368000 | tf_op jit(solution)/shard_map/stack | solution.py:458
  81.2 1.3 %copy.8 = f32[128,4,2,256]{3,2,1,0:T(2,128)} copy(f32[128,4,2,256]{0,3,2,1:T(8,128)S(1)} %bitcast.22) | data formatting | bytes 2097152 | tf_op jit(solution)/shard_map/jit(_where)/select_n | solution.py:458
  (25 shorter events, 1.5 us)
Async XLA Ops:
  1.0 8.6 %collective-permute-start = (bf16[536,128]{1,0:T(8,128)(2,1)S(1)}, bf16[536,128]{1,0:T(8,128)(2,1)S(1)}, u32[]{:S(2)}, u32[]{:S(2)}) collective-permute-start(bf16[536,128]{1,0:T(8,128)(2,1)S(1)} %tall_design.1), channel_id=1, source_target_pairs={{0,1},{1,0},{4,5},{5,4},{8,9},{9,8},{12,13},{13,12},{2,3},{3,2},{6... | collective-permute-start | bytes 411656 | tf_op jit(solution)/shard_map/ppermute | solution.py:391
  4.1 8.0 %collective-permute-start.1 = (bf16[536,128]{1,0:T(8,128)(2,1)S(1)}, bf16[536,128]{1,0:T(8,128)(2,1)S(1)}, u32[]{:S(2)}, u32[]{:S(2)}) collective-permute-start(bf16[536,128]{1,0:T(8,128)(2,1)S(1)} %tall_design.1), channel_id=1, source_target_pairs={{0,8},{1,9},{4,12},{5,13},{8,0},{9,1},{12,4},{13,5},{2,10},{3,11},... | collective-permute-start | bytes 411656 | tf_op jit(solution)/shard_map/ppermute | solution.py:391
  5.6 6.5 %collective-permute-start.2 = (bf16[536,128]{1,0:T(8,128)(2,1)S(1)}, bf16[536,128]{1,0:T(8,128)(2,1)S(1)}, u32[]{:S(2)}, u32[]{:S(2)}) collective-permute-start(bf16[536,128]{1,0:T(8,128)(2,1)S(1)} %tall_design.1), channel_id=1, source_target_pairs={{0,9},{1,8},{4,13},{5,12},{8,1},{9,0},{12,5},{13,4},{2,11},{3,10},... | collective-permute-start | bytes 411656 | tf_op jit(solution)/shard_map/ppermute | solution.py:391
  12.1 31.9 %all-to-all-start = ((bf16[8,128,1024]{2,1,0:T(8,128)(2,1)}), bf16[8,128,1024]{2,1,0:T(8,128)(2,1)S(1)}, u32[]{:S(2)}, u32[]{:S(2)}) async-start(bf16[8,128,1024]{2,1,0:T(8,128)(2,1)} %smooth.1), calls=%async_computation | async-start | bytes 4194304 | tf_op jit(solution)/shard_map/all_to_all | solution.py:405
  15.8 2.1 %collective-permute-start.3 = (bf16[4,536,128]{2,1,0:T(8,128)(2,1)S(1)}, bf16[4,536,128]{2,1,0:T(8,128)(2,1)S(1)}, u32[]{:S(2)}, u32[]{:S(2)}) collective-permute-start(bf16[4,536,128]{2,1,0:T(8,128)(2,1)S(1)} %pad_maximum_fusion.blocks), channel_id=1, source_target_pairs={{0,4},{1,5},{4,0},{5,1},{8,12},{9,13},{12,8},{13,9},{2,6},{3,7},{6... | collective-permute-start | bytes 1646600 | tf_op jit(solution)/shard_map/ppermute | solution.py:391
  16.3 0.8 copy-start
  18.0 0.8 copy-start.2
  18.8 1.1 %copy-start.1 = (bf16[4,536,128]{2,1,0:T(8,128)(2,1)S(1)}, bf16[4,536,128]{2,1,0:T(8,128)(2,1)}, u32[]{:S(2)}) copy-start(bf16[4,536,128]{2,1,0:T(8,128)(2,1)} %copy-done) | copy-start | bytes 1646596
  19.8 1.1 %copy-start.3 = (bf16[4,536,128]{2,1,0:T(8,128)(2,1)S(1)}, bf16[4,536,128]{2,1,0:T(8,128)(2,1)}, u32[]{:S(2)}) copy-start(bf16[4,536,128]{2,1,0:T(8,128)(2,1)} %copy-done.2) | copy-start | bytes 1646596
  22.6 18.5 %collective-permute-start.4 = (f32[32,640]{1,0:T(8,128)}, f32[32,640]{1,0:T(8,128)S(1)}, u32[]{:S(2)}, u32[]{:S(2)}) collective-permute-start(f32[32,640]{1,0:T(8,128)} %get-tuple-element.35.moment.refs_0_), channel_id=1, source_target_pairs={{0,2},{2,0},{1,3},{3,1},{4,6},{6,4},{5,7},{7,5},{8,10},{10,8},{9,1... | collective-permute-start | bytes 245768 | tf_op jit(solution)/shard_map/ppermute | solution.py:391
  25.2 0.9 %copy-start.6 = (f32[32,640]{1,0:T(8,128)S(1)}, f32[32,640]{1,0:T(8,128)}, u32[]{:S(2)}) copy-start(f32[32,640]{1,0:T(8,128)} %get-tuple-element.35.moment.refs_0_) | copy-start | bytes 245764
  44.5 6.2 %collective-permute-start.5 = (f32[24,1024]{1,0:T(8,128)S(1)}, f32[24,1024]{1,0:T(8,128)}, u32[]{:S(2)}, u32[]{:S(2)}) collective-permute-start(f32[24,1024]{1,0:T(8,128)S(1)} %column_sums.1.stats.refs_0_), channel_id=1, source_target_pairs={{0,2},{2,0},{1,3},{3,1},{4,6},{6,4},{5,7},{7,5},{8,10},{10,8},{9,1... | collective-permute-start | bytes 294920 | tf_op jit(solution)/shard_map/ppermute | solution.py:391
  47.8 10.0 %copy-start.5 = (f32[512,128]{1,0:T(8,128)S(1)}, f32[512,128]{1,0:T(8,128)}, u32[]{:S(2)}) copy-start(f32[512,128]{1,0:T(8,128)} %get-tuple-element.43.coef) | copy-start | bytes 786436
  47.8 10.0 %copy-start.7 = (f32[24,128]{1,0:T(8,128)S(1)}, f32[24,128]{1,0:T(8,128)}, u32[]{:S(2)}) copy-start(f32[24,128]{1,0:T(8,128)} %get-tuple-element.44.inverse) | copy-start | bytes 36868
  51.5 23.5 %collective-permute-start.6 = (f16[128,1024]{1,0:T(8,128)(2,1)}, f16[128,1024]{1,0:T(8,128)(2,1)}, u32[]{:S(2)}, u32[]{:S(2)}) collective-permute-start(f16[128,1024]{1,0:T(8,128)(2,1)} %convert_element_type.18), channel_id=1, source_target_pairs={{0,3},{1,2},{2,1},{3,0},{4,7},{5,6},{6,5},{7,4},{8,11},{9,10},{10,... | collective-permute-start | bytes 786440 | tf_op jit(solution)/shard_map/ppermute | solution.py:391
  57.8 21.1 %collective-permute-start.7 = (f16[128,1024]{1,0:T(8,128)(2,1)}, f16[128,1024]{1,0:T(8,128)(2,1)}, u32[]{:S(2)}, u32[]{:S(2)}) collective-permute-start(f16[128,1024]{1,0:T(8,128)(2,1)} %convert_element_type.19), channel_id=1, source_target_pairs={{0,2},{1,3},{2,0},{3,1},{4,6},{5,7},{6,4},{7,5},{8,10},{9,11},{10,... | collective-permute-start | bytes 786440 | tf_op jit(solution)/shard_map/ppermute | solution.py:391
  60.4 0.8 copy-start.4
  61.2 17.7 %collective-permute-start.8 = (f16[128,1024]{1,0:T(8,128)(2,1)S(1)}, f16[128,1024]{1,0:T(8,128)(2,1)S(1)}, u32[]{:S(2)}, u32[]{:S(2)}) collective-permute-start(f16[128,1024]{1,0:T(8,128)(2,1)S(1)} %convert_element_type.21), channel_id=1, source_target_pairs={{0,1},{1,0},{2,3},{3,2},{4,5},{5,4},{6,7},{7,6},{8,9},{9,8},{10,11... | collective-permute-start | bytes 786440 | tf_op jit(solution)/shard_map/ppermute | solution.py:391
  61.8 13.2 %collective-permute-start.9 = (f32[8,1024]{1,0:T(8,128)S(1)}, f32[8,1024]{1,0:T(8,128)S(1)}, u32[]{:S(2)}, u32[]{:S(2)}) collective-permute-start(f32[8,1024]{1,0:T(8,128)S(1)} %get-tuple-element.50), channel_id=1, source_target_pairs={{0,1},{1,0},{2,3},{3,2},{4,5},{5,4},{6,7},{7,6},{8,9},{9,8},{10,11... | collective-permute-start | bytes 98312 | tf_op jit(solution)/shard_map/ppermute | solution.py:391

commit v13 on v12

--- a/solution.py
+++ b/solution.py
@@ -270,12 +270,11 @@
     lines[...] = jnp.zeros(lines.shape, jnp.float32)
     lines[:DPAD, :] = fitted * -scale
     lines[SCALE_LANE : SCALE_LANE + 1, :] = scale
-    for j in range(len(parts)):
+    for j in range(1, len(parts)):
         _, fit, own_scale = gene_fit(moment[j], snps, design, True)
         lane = SCALE_LANE + 1 + j
         lines[lane : lane + 1, :] = scale / own_scale
-        if j:
-            lines[j * STRIDE : j * STRIDE + DPAD, :] = fit * scale
+        lines[j * STRIDE : j * STRIDE + DPAD, :] = fit * scale
     coef[...] = jnp.transpose(lines[...])
 
 
@@ -431,7 +430,8 @@
     freedom = float(here * n_far - design - 1)
     line = ("far", "near")
     where = [far[None], near[None], n_far, n_near]
-    sent = far_products(genes, columns, pair_coef, stats, *where)
+    sent = list(far_products(genes, columns, pair_coef, stats, *where))
+    sent[0] = sent[0].astype(jnp.float16)
     sent, stat_parts = lax.optimization_barrier((sent, stat_parts))
     sent = [piece.astype(jnp.float16) for piece in sent]
     pieces = {
@@ -450,10 +450,8 @@
             ratio = ratio + pieces[j * n_near + offset].astype(jnp.float32) * weight
         return ratio * jnp.sqrt(freedom / (1.0 - ratio * ratio))
 
-    first = [k for k in pieces if k % n_near]
-    *taken, home = lax.optimization_barrier((*[pieces[k] for k in first], home))
-    pieces.update(zip(first, taken))
     home = t_of(home, factors, 0)
+    away_factors, home = lax.optimization_barrier((away_factors, home))
     away = t_of(away, away_factors, 1)
     both = jnp.where(near == 0, jnp.stack([home, away], 1), jnp.stack([away, home], 1))
     return both.reshape(panel, maps, per_vox, plane)

time: 83 us -> 79.9 us (0.963)
  waiting for transfers between devices: 32.4 us -> 27.4 us
  other arithmetic: 3.54 us -> 4.47 us
  starting transfers between devices: 22.2 us -> 23.1 us
    ppermute x10, waiting for transfers between devices: 32.4 us -> 27.4 us  [permute_xor(): return lax.ppermute(value, axes, [(i, i ^ bits) for i in range(size)])]
    mul x0 -> x1, other arithmetic: none -> 1.45 us  [t_of(): return ratio * jnp.sqrt(freedom / (1.0 - ratio * ratio))]
    ppermute x10, starting transfers between devices: 18.6 us -> 19.5 us  [permute_xor(): return lax.ppermute(value, axes, [(i, i ^ bits) for i in range(size)])]
  transfers between devices with their start and end apart: 11 -> 11, of which waited for: 6 -> 6; matrix products, arithmetic and copies ran while one was open for 2% -> 5% of each run, Pallas kernels for 18% -> 18%
where the time goes in v13:
time: 79.9 us; the launch traced here: 79.4 us
  waiting for transfers between devices  27.4 us (34%)
  starting transfers between devices  23.1 us (29%)
  Pallas kernels  16.1 us (20%)
  local copies, waits for them, and re-layouts  8.06 us (10%)
  other arithmetic  4.47 us (6%)
    ppermute x10, waiting for transfers between devices, permute_xor(): return lax.ppermute(value, axes, [(i, i ^ bits) for i in range(size)])  27.4 us
    ppermute x10, starting transfers between devices, permute_xor(): return lax.ppermute(value, axes, [(i, i ^ bits) for i in range(size)])  19.5 us
    pallas_call x6, Pallas kernels, call(): pl.pallas_call(kernel, out_shape=outs, in_specs=[IN_SMEM] * len(scalars)...  11.2 us
    unnamed x16, local copies, waits for them, and re-layouts  5.41 us
    pallas_call x1, Pallas kernels, smooth(): pl.pallas_call(functools.partial(smooth_kernel, group, planes, per_vox, p...  3.97 us
    all_to_all x1, starting transfers between devices, exchange(): value = lax.all_to_all(value, ('vox', 'near'), 0, 0, tiled=True)  3.6 us
    select_n x2, local copies, waits for them, and re-layouts, on_device(): jnp.where(near == 0, jnp.stack([home, away], 1), jnp.stack([away, home], 1))  1.63 us
  transfers between devices with their start and end apart: 11, of which 6 were waited for; matrix products, arithmetic and copies ran while one was open for 5% of the time, Pallas kernels for 18%

profile of v13, /device:TPU:0, one launch (start us, length us, event | category | flops | bytes accessed | tf_op | source)
XLA Modules:
  0.0 79.4 jit_solution(11920415453362847359)
XLA Ops:
  0.0 1.0 %tall_design.1 = bf16[536,128]{1,0:T(8,128)(2,1)S(1)} custom-call(bf16[128,512]{1,0:T(8,128)(2,1)} %genotypes.1, s32[1,128]{1,0:T(1,128)} %bitcast.30, bf16[16,128]{1,0:T(8,128)(2,1)} %bitcast.29), custom_call_target="tpu_custom_call" | custom-call | tf_op jit(solution)/shard_map/tall_design/pallas_call | solution.py:112
  1.0 3.1 %collective-permute-start = (bf16[536,128]{1,0:T(8,128)(2,1)S(1)}, bf16[536,128]{1,0:T(8,128)(2,1)S(1)}, u32[]{:S(2)}, u32[]{:S(2)}) collective-permute-start(bf16[536,128]{1,0:T(8,128)(2,1)S(1)} %tall_design.1), channel_id=1, source_target_pairs={{0,1},{1,0},{4,5},{5,4},{8,9},{9,8},{12,13},{13,12},{2,3},{3,2},{6... | collective-permute-start | bytes 411656 | tf_op jit(solution)/shard_map/ppermute | solution.py:390
  4.1 1.5 %collective-permute-start.1 = (bf16[536,128]{1,0:T(8,128)(2,1)S(1)}, bf16[536,128]{1,0:T(8,128)(2,1)S(1)}, u32[]{:S(2)}, u32[]{:S(2)}) collective-permute-start(bf16[536,128]{1,0:T(8,128)(2,1)S(1)} %tall_design.1), channel_id=1, source_target_pairs={{0,8},{1,9},{4,12},{5,13},{8,0},{9,1},{12,4},{13,5},{2,10},{3,11},... | collective-permute-start | bytes 411656 | tf_op jit(solution)/shard_map/ppermute | solution.py:390
  5.6 4.0 %smooth.1 = bf16[8,128,1024]{2,1,0:T(8,128)(2,1)} custom-call(bf16[128,32,256]{2,1,0:T(8,128)(2,1)} %bitcast.23, bf16[256,256]{1,0:T(8,128)(2,1)} %constant.29.clone.order, bf16[256,256]{1,0:T(8,128)(2,1)} %constant.30.clone.table), custom_call_target="tpu_custom_call" | custom-call | tf_op jit(solution)/shard_map/smooth/pallas_call | solution.py:167
  9.6 2.5 %collective-permute-done.1 = bf16[536,128]{1,0:T(8,128)(2,1)S(1)} collective-permute-done((bf16[536,128]{1,0:T(8,128)(2,1)S(1)}, bf16[536,128]{1,0:T(8,128)(2,1)S(1)}, u32[]{:S(2)}, u32[]{:S(2)}) %collective-permute-start.1) | collective-permute-done | bytes 137248 | tf_op jit(solution)/shard_map/ppermute | solution.py:390
  12.1 3.6 %all-to-all-start = ((bf16[8,128,1024]{2,1,0:T(8,128)(2,1)}), bf16[8,128,1024]{2,1,0:T(8,128)(2,1)S(1)}, u32[]{:S(2)}, u32[]{:S(2)}) async-start(bf16[8,128,1024]{2,1,0:T(8,128)(2,1)} %smooth.1), calls=%async_computation | async-start | bytes 4194304 | tf_op jit(solution)/shard_map/all_to_all | solution.py:404
  16.3 0.8 %copy-done = bf16[4,536,128]{2,1,0:T(8,128)(2,1)} copy-done((bf16[4,536,128]{2,1,0:T(8,128)(2,1)}, bf16[4,536,128]{2,1,0:T(8,128)(2,1)S(1)}, u32[]{:S(2)}) %copy-start) | copy-done | bytes 548888
  17.1 0.9 %collective-permute-done.3.others = bf16[4,536,128]{2,1,0:T(8,128)(2,1)S(1)} collective-permute-done((bf16[4,536,128]{2,1,0:T(8,128)(2,1)S(1)}, bf16[4,536,128]{2,1,0:T(8,128)(2,1)S(1)}, u32[]{:S(2)}, u32[]{:S(2)}) %collective-permute-start.3) | collective-permute-done | bytes 548896 | tf_op jit(solution)/shard_map/ppermute | solution.py:390
  18.0 0.8 copy-done.2
  18.8 1.0 %copy-done.1 = bf16[4,536,128]{2,1,0:T(8,128)(2,1)S(1)} copy-done((bf16[4,536,128]{2,1,0:T(8,128)(2,1)S(1)}, bf16[4,536,128]{2,1,0:T(8,128)(2,1)}, u32[]{:S(2)}) %copy-start.1) | copy-done | bytes 548888
  19.8 1.0 %copy-done.3 = bf16[4,536,128]{2,1,0:T(8,128)(2,1)S(1)} copy-done((bf16[4,536,128]{2,1,0:T(8,128)(2,1)S(1)}, bf16[4,536,128]{2,1,0:T(8,128)(2,1)}, u32[]{:S(2)}) %copy-start.3) | copy-done | bytes 548888
  20.9 1.7 %moments.1 = (bf16[536,1024]{1,0:T(8,128)(2,1)S(1)}, f32[32,640]{1,0:T(8,128)}) custom-call(s32[1]{0:T(128)} %bitcast.6.me, bf16[4,536,128]{2,1,0:T(8,128)(2,1)S(1)} %copy-done.1, bf16[4,536,128]{2,1,0:T(8,128)(2,1)S(1)} %copy-done.3), custom_call_target="tpu_custom_call" | custom-call | tf_op jit(solution)/shard_map/moments/pallas_call | solution.py:88
  22.6 2.6 %collective-permute-start.4 = (f32[32,640]{1,0:T(8,128)}, f32[32,640]{1,0:T(8,128)S(1)}, u32[]{:S(2)}, u32[]{:S(2)}) collective-permute-start(f32[32,640]{1,0:T(8,128)} %get-tuple-element.34.moment.refs_0_), channel_id=1, source_target_pairs={{0,2},{2,0},{1,3},{3,1},{4,6},{6,4},{5,7},{7,5},{8,10},{10,8},{9,1... | collective-permute-start | bytes 245768 | tf_op jit(solution)/shard_map/ppermute | solution.py:390
  25.2 0.9 %copy-done.6 = f32[32,640]{1,0:T(8,128)S(1)} copy-done((f32[32,640]{1,0:T(8,128)S(1)}, f32[32,640]{1,0:T(8,128)}, u32[]{:S(2)}) %copy-start.6) | copy-done | bytes 81944
  26.1 2.0 %pair_fit.1.coef = f32[512,128]{1,0:T(8,128)S(1)} custom-call(f32[32,640]{1,0:T(8,128)S(1)} %copy-done.6), custom_call_target="tpu_custom_call" | custom-call | tf_op jit(solution)/shard_map/pair_fit/pallas_call | solution.py:88
  28.1 13.0 %collective-permute-done.4.refs_1_ = f32[32,640]{1,0:T(8,128)S(1)} collective-permute-done((f32[32,640]{1,0:T(8,128)}, f32[32,640]{1,0:T(8,128)S(1)}, u32[]{:S(2)}, u32[]{:S(2)}) %collective-permute-start.4) | collective-permute-done | bytes 81952 | tf_op jit(solution)/shard_map/ppermute | solution.py:390
  41.1 2.8 %cohort_fit.1 = (f32[512,128]{1,0:T(8,128)}, f32[24,128]{1,0:T(8,128)}) custom-call(f32[32,640]{1,0:T(8,128)S(1)} %copy-done.6, f32[32,640]{1,0:T(8,128)S(1)} %collective-permute-done.4.refs_1_), custom_call_target="tpu_custom_call" | custom-call | tf_op jit(solution)/shard_map/cohort_fit/pallas_call | solution.py:88
  44.4 3.3 %collective-permute-start.5 = (f32[24,1024]{1,0:T(8,128)S(1)}, f32[24,1024]{1,0:T(8,128)}, u32[]{:S(2)}, u32[]{:S(2)}) collective-permute-start(f32[24,1024]{1,0:T(8,128)S(1)} %column_sums.1.stats.refs_0_), channel_id=1, source_target_pairs={{0,2},{2,0},{1,3},{3,1},{4,6},{6,4},{5,7},{7,5},{8,10},{10,8},{9,1... | collective-permute-start | bytes 294920 | tf_op jit(solution)/shard_map/ppermute | solution.py:390
  47.7 1.5 %far_products.1 = (f32[128,1024]{1,0:T(8,128)S(1)}, f32[128,1024]{1,0:T(8,128)S(1)}) custom-call(s32[1]{0:T(128)} %bitcast.far, s32[1]{0:T(128)} %bitcast.1.near, bf16[536,1024]{1,0:T(8,128)(2,1)S(1)} %get-tuple-element.39.genes, bf16[1024,1024]{1,0:T(8,128)(2,1)S(1)} %bitcast.18, f32[512,128]{1,0:T(8,128)S(1)} %pair_fit.1.coef, ...), custom_call_target="tpu_custom_call" | custom-call | tf_op jit(solution)/shard_map/far_products/pallas_call | solution.py:88
  49.2 0.7 convert_element_type.18
  50.6 2.7 %collective-permute-start.7 = (f16[128,1024]{1,0:T(8,128)(2,1)}, f16[128,1024]{1,0:T(8,128)(2,1)}, u32[]{:S(2)}, u32[]{:S(2)}) collective-permute-start(f16[128,1024]{1,0:T(8,128)(2,1)} %convert_element_type.18), channel_id=1, source_target_pairs={{0,2},{1,3},{2,0},{3,1},{4,6},{5,7},{6,4},{7,5},{8,10},{9,11},{10,... | collective-permute-start | bytes 786440 | tf_op jit(solution)/shard_map/ppermute | solution.py:390
  53.4 0.7 convert_element_type.22
  54.1 3.7 %collective-permute-start.9 = (f16[128,1024]{1,0:T(8,128)(2,1)}, f16[128,1024]{1,0:T(8,128)(2,1)}, u32[]{:S(2)}, u32[]{:S(2)}) collective-permute-start(f16[128,1024]{1,0:T(8,128)(2,1)} %convert_element_type.22), channel_id=1, source_target_pairs={{0,3},{1,2},{2,1},{3,0},{4,7},{5,6},{6,5},{7,4},{8,11},{9,10},{10,... | collective-permute-start | bytes 786440 | tf_op jit(solution)/shard_map/ppermute | solution.py:390
  57.8 2.6 %base_ratio.1 = (f32[128,1024]{1,0:T(8,128)S(1)}, f32[128,1024]{1,0:T(8,128)S(1)}, f32[8,1024]{1,0:T(8,128)S(1)}) custom-call(s32[1]{0:T(128)} %bitcast.far, s32[1]{0:T(128)} %bitcast.1.near, f32[512,128]{1,0:T(8,128)S(1)} %copy-done.5, f32[24,128]{1,0:T(8,128)S(1)} %copy-done.7, bf16[536,1024]{1,0:T(8,128)(2,1)S(1)} %get-tuple-element.39.genes, ...), custom_call_target="tpu_custom_call" | custom-call | tf_op jit(solution)/shard_map/base_ratio/pallas_call | solution.py:88
  60.4 0.8 copy-done.4
  61.3 1.0 %dynamic-slice_reduce_fusion = f32[128]{0:T(128)S(1)} fusion(f32[512,128]{1,0:T(8,128)} %get-tuple-element.37.coef, s32[]{:T(128)S(6)} %select_n.16, s32[]{:T(128)S(6)} %add.21), kind=kLoop, calls=%fused_computation.4 | loop fusion | bytes 1032 | tf_op jit(solution)/shard_map/slice | solution.py:449
  62.3 2.1 %collective-permute-start.6 = (f32[8,1024]{1,0:T(8,128)S(1)}, f32[8,1024]{1,0:T(8,128)S(1)}, u32[]{:S(2)}, u32[]{:S(2)}) collective-permute-start(f32[8,1024]{1,0:T(8,128)S(1)} %get-tuple-element.46), channel_id=1, source_target_pairs={{0,1},{1,0},{2,3},{3,2},{4,5},{5,4},{6,7},{7,6},{8,9},{9,8},{10,11... | collective-permute-start | bytes 98312 | tf_op jit(solution)/shard_map/ppermute | solution.py:390
  64.4 7.9 %collective-permute-done.7 = f16[128,1024]{1,0:T(8,128)(2,1)} collective-permute-done((f16[128,1024]{1,0:T(8,128)(2,1)}, f16[128,1024]{1,0:T(8,128)(2,1)}, u32[]{:S(2)}, u32[]{:S(2)}) %collective-permute-start.7) | collective-permute-done | bytes 262176 | tf_op jit(solution)/shard_map/ppermute | solution.py:390
  72.4 1.5 %sqrt_multiply_fusion = f32[128,1024]{1,0:T(8,128)S(1)} fusion(f32[128,1024]{1,0:T(8,128)} %copy-done.4, f16[128,1024]{1,0:T(8,128)(2,1)} %collective-permute-done.7, f32[1024]{0:T(1024)S(1)} %bitcast.28, f32[128]{0:T(128)S(1)} %dynamic-slice_reduce_fusion), kind=kLoop, calls=%fused_computation.3 | loop fusion | flops 1048576 | bytes 1315328 | tf_op jit(solution)/shard_map/mul | solution.py:451
  73.8 2.4 %collective-permute-done.6 = f32[8,1024]{1,0:T(8,128)S(1)} collective-permute-done((f32[8,1024]{1,0:T(8,128)S(1)}, f32[8,1024]{1,0:T(8,128)S(1)}, u32[]{:S(2)}, u32[]{:S(2)}) %collective-permute-start.6) | collective-permute-done | bytes 32800 | tf_op jit(solution)/shard_map/ppermute | solution.py:390
  76.3 1.3 %multiply_bitcast_fusion = f32[128,1,1024]{2,0,1:T(8,128)S(1)} fusion(f16[128,1024]{1,0:T(8,128)(2,1)} %collective-permute-done.9, f16[128,1024]{1,0:T(8,128)(2,1)S(1)} %collective-permute-done.8, f32[1024]{0:T(1024)S(1)} %bitcast.27, f32[128]{0:T(128)S(1)} %dynamic-slice_reduce_fusion), kind=kLoop, calls=%fused_computation.2 | loop fusion | flops 1310720 | bytes 1053184 | tf_op jit(solution)/shard_map/stack | solution.py:456
  78.1 1.3 %copy.8 = f32[128,4,2,256]{3,2,1,0:T(2,128)} copy(f32[128,4,2,256]{0,3,2,1:T(8,128)S(1)} %bitcast.21) | data formatting | bytes 2097152 | tf_op jit(solution)/shard_map/jit(_where)/select_n | solution.py:456
  (26 shorter events, 2.3 us)
Async XLA Ops:
  1.0 8.6 %collective-permute-start = (bf16[536,128]{1,0:T(8,128)(2,1)S(1)}, bf16[536,128]{1,0:T(8,128)(2,1)S(1)}, u32[]{:S(2)}, u32[]{:S(2)}) collective-permute-start(bf16[536,128]{1,0:T(8,128)(2,1)S(1)} %tall_design.1), channel_id=1, source_target_pairs={{0,1},{1,0},{4,5},{5,4},{8,9},{9,8},{12,13},{13,12},{2,3},{3,2},{6... | collective-permute-start | bytes 411656 | tf_op jit(solution)/shard_map/ppermute | solution.py:390
  4.1 8.0 %collective-permute-start.1 = (bf16[536,128]{1,0:T(8,128)(2,1)S(1)}, bf16[536,128]{1,0:T(8,128)(2,1)S(1)}, u32[]{:S(2)}, u32[]{:S(2)}) collective-permute-start(bf16[536,128]{1,0:T(8,128)(2,1)S(1)} %tall_design.1), channel_id=1, source_target_pairs={{0,8},{1,9},{4,12},{5,13},{8,0},{9,1},{12,4},{13,5},{2,10},{3,11},... | collective-permute-start | bytes 411656 | tf_op jit(solution)/shard_map/ppermute | solution.py:390
  5.6 6.5 %collective-permute-start.2 = (bf16[536,128]{1,0:T(8,128)(2,1)S(1)}, bf16[536,128]{1,0:T(8,128)(2,1)S(1)}, u32[]{:S(2)}, u32[]{:S(2)}) collective-permute-start(bf16[536,128]{1,0:T(8,128)(2,1)S(1)} %tall_design.1), channel_id=1, source_target_pairs={{0,9},{1,8},{4,13},{5,12},{8,1},{9,0},{12,5},{13,4},{2,11},{3,10},... | collective-permute-start | bytes 411656 | tf_op jit(solution)/shard_map/ppermute | solution.py:390
  12.1 31.8 %all-to-all-start = ((bf16[8,128,1024]{2,1,0:T(8,128)(2,1)}), bf16[8,128,1024]{2,1,0:T(8,128)(2,1)S(1)}, u32[]{:S(2)}, u32[]{:S(2)}) async-start(bf16[8,128,1024]{2,1,0:T(8,128)(2,1)} %smooth.1), calls=%async_computation | async-start | bytes 4194304 | tf_op jit(solution)/shard_map/all_to_all | solution.py:404
  15.8 2.1 %collective-permute-start.3 = (bf16[4,536,128]{2,1,0:T(8,128)(2,1)S(1)}, bf16[4,536,128]{2,1,0:T(8,128)(2,1)S(1)}, u32[]{:S(2)}, u32[]{:S(2)}) collective-permute-start(bf16[4,536,128]{2,1,0:T(8,128)(2,1)S(1)} %pad_maximum_fusion.blocks), channel_id=1, source_target_pairs={{0,4},{1,5},{4,0},{5,1},{8,12},{9,13},{12,8},{13,9},{2,6},{3,7},{6... | collective-permute-start | bytes 1646600 | tf_op jit(solution)/shard_map/ppermute | solution.py:390
  16.3 0.8 %copy-start = (bf16[4,536,128]{2,1,0:T(8,128)(2,1)}, bf16[4,536,128]{2,1,0:T(8,128)(2,1)S(1)}, u32[]{:S(2)}) copy-start(bf16[4,536,128]{2,1,0:T(8,128)(2,1)S(1)} %pad_maximum_fusion.blocks) | copy-start | bytes 1646596
  18.0 0.8 copy-start.2
  18.8 1.1 %copy-start.1 = (bf16[4,536,128]{2,1,0:T(8,128)(2,1)S(1)}, bf16[4,536,128]{2,1,0:T(8,128)(2,1)}, u32[]{:S(2)}) copy-start(bf16[4,536,128]{2,1,0:T(8,128)(2,1)} %copy-done) | copy-start | bytes 1646596
  19.8 1.1 %copy-start.3 = (bf16[4,536,128]{2,1,0:T(8,128)(2,1)S(1)}, bf16[4,536,128]{2,1,0:T(8,128)(2,1)}, u32[]{:S(2)}) copy-start(bf16[4,536,128]{2,1,0:T(8,128)(2,1)} %copy-done.2) | copy-start | bytes 1646596
  22.6 18.5 %collective-permute-start.4 = (f32[32,640]{1,0:T(8,128)}, f32[32,640]{1,0:T(8,128)S(1)}, u32[]{:S(2)}, u32[]{:S(2)}) collective-permute-start(f32[32,640]{1,0:T(8,128)} %get-tuple-element.34.moment.refs_0_), channel_id=1, source_target_pairs={{0,2},{2,0},{1,3},{3,1},{4,6},{6,4},{5,7},{7,5},{8,10},{10,8},{9,1... | collective-permute-start | bytes 245768 | tf_op jit(solution)/shard_map/ppermute | solution.py:390
  25.2 0.9 %copy-start.6 = (f32[32,640]{1,0:T(8,128)S(1)}, f32[32,640]{1,0:T(8,128)}, u32[]{:S(2)}) copy-start(f32[32,640]{1,0:T(8,128)} %get-tuple-element.34.moment.refs_0_) | copy-start | bytes 245764
  44.4 6.2 %collective-permute-start.5 = (f32[24,1024]{1,0:T(8,128)S(1)}, f32[24,1024]{1,0:T(8,128)}, u32[]{:S(2)}, u32[]{:S(2)}) collective-permute-start(f32[24,1024]{1,0:T(8,128)S(1)} %column_sums.1.stats.refs_0_), channel_id=1, source_target_pairs={{0,2},{2,0},{1,3},{3,1},{4,6},{6,4},{5,7},{7,5},{8,10},{10,8},{9,1... | collective-permute-start | bytes 294920 | tf_op jit(solution)/shard_map/ppermute | solution.py:390
  47.7 10.1 %copy-start.5 = (f32[512,128]{1,0:T(8,128)S(1)}, f32[512,128]{1,0:T(8,128)}, u32[]{:S(2)}) copy-start(f32[512,128]{1,0:T(8,128)} %get-tuple-element.37.coef) | copy-start | bytes 786436
  47.7 10.1 %copy-start.7 = (f32[24,128]{1,0:T(8,128)S(1)}, f32[24,128]{1,0:T(8,128)}, u32[]{:S(2)}) copy-start(f32[24,128]{1,0:T(8,128)} %get-tuple-element.38.inverse) | copy-start | bytes 36868
  50.6 21.7 %collective-permute-start.7 = (f16[128,1024]{1,0:T(8,128)(2,1)}, f16[128,1024]{1,0:T(8,128)(2,1)}, u32[]{:S(2)}, u32[]{:S(2)}) collective-permute-start(f16[128,1024]{1,0:T(8,128)(2,1)} %convert_element_type.18), channel_id=1, source_target_pairs={{0,2},{1,3},{2,0},{3,1},{4,6},{5,7},{6,4},{7,5},{8,10},{9,11},{10,... | collective-permute-start | bytes 786440 | tf_op jit(solution)/shard_map/ppermute | solution.py:390
  54.1 22.2 %collective-permute-start.9 = (f16[128,1024]{1,0:T(8,128)(2,1)}, f16[128,1024]{1,0:T(8,128)(2,1)}, u32[]{:S(2)}, u32[]{:S(2)}) collective-permute-start(f16[128,1024]{1,0:T(8,128)(2,1)} %convert_element_type.22), channel_id=1, source_target_pairs={{0,3},{1,2},{2,1},{3,0},{4,7},{5,6},{6,5},{7,4},{8,11},{9,10},{10,... | collective-permute-start | bytes 786440 | tf_op jit(solution)/shard_map/ppermute | solution.py:390
  60.4 0.8 %copy-start.4 = (f32[128,1024]{1,0:T(8,128)}, f32[128,1024]{1,0:T(8,128)S(1)}, u32[]{:S(2)}) copy-start(f32[128,1024]{1,0:T(8,128)S(1)} %get-tuple-element.47) | copy-start | bytes 1572868
  61.2 15.0 %collective-permute-start.8 = (f16[128,1024]{1,0:T(8,128)(2,1)S(1)}, f16[128,1024]{1,0:T(8,128)(2,1)S(1)}, u32[]{:S(2)}, u32[]{:S(2)}) collective-permute-start(f16[128,1024]{1,0:T(8,128)(2,1)S(1)} %convert_element_type.20), channel_id=1, source_target_pairs={{0,1},{1,0},{2,3},{3,2},{4,5},{5,4},{6,7},{7,6},{8,9},{9,8},{10,11... | collective-permute-start | bytes 786440 | tf_op jit(solution)/shard_map/ppermute | solution.py:390
  62.3 13.9 %collective-permute-start.6 = (f32[8,1024]{1,0:T(8,128)S(1)}, f32[8,1024]{1,0:T(8,128)S(1)}, u32[]{:S(2)}, u32[]{:S(2)}) collective-permute-start(f32[8,1024]{1,0:T(8,128)S(1)} %get-tuple-element.46), channel_id=1, source_target_pairs={{0,1},{1,0},{2,3},{3,2},{4,5},{5,4},{6,7},{7,6},{8,9},{9,8},{10,11... | collective-permute-start | bytes 98312 | tf_op jit(solution)/shard_map/ppermute | solution.py:390

commit v14 on v13

--- a/solution.py
+++ b/solution.py
@@ -262,27 +262,17 @@
     return call(kernel, "pair_fit", result((snps, LANES), jnp.float32), [], [moment], scratch, 1)
 
 
-def cohort_kernel(snps, design, *refs):
-    parts, (coef, inverse, lines) = refs[:-3], refs[-3:]
-    moment = [part[...] for part in parts]
-    solved, fitted, scale = gene_fit(tree_sum(moment), snps, design, False)
-    inverse[...] = solved
+def cohort_lines(moments, snps, design, lines):
+    solved, fitted, scale = gene_fit(tree_sum(moments), snps, design, False)
     lines[...] = jnp.zeros(lines.shape, jnp.float32)
     lines[:DPAD, :] = fitted * -scale
     lines[SCALE_LANE : SCALE_LANE + 1, :] = scale
-    for j in range(1, len(parts)):
-        _, fit, own_scale = gene_fit(moment[j], snps, design, True)
+    for j in range(1, len(moments)):
+        _, fit, own_scale = gene_fit(moments[j], snps, design, True)
         lane = SCALE_LANE + 1 + j
         lines[lane : lane + 1, :] = scale / own_scale
         lines[j * STRIDE : j * STRIDE + DPAD, :] = fit * scale
-    coef[...] = jnp.transpose(lines[...])
-
-
-def cohort_fit(parts, snps, design):
-    kernel = functools.partial(cohort_kernel, snps, design)
-    outs = (pltpu.HBM((snps, LANES), jnp.float32), pltpu.HBM((DPAD, LANES), jnp.float32))
-    scratch = [pltpu.VMEM((LANES, snps), jnp.float32)]
-    return call(kernel, "cohort_fit", outs, [], parts, scratch, len(parts))
+    return solved
 
 
 def column_norm(sums, here):
@@ -337,9 +327,19 @@
     return call(kernel, "far_products", outs, [far, near], [genes, columns, coef, stats], scratch)
 
 
-def base_kernel(here, count, far, near, genes, columns, coef, inverse, *refs):
-    parts, (home, away, factors, stack, held) = refs[:-5], refs[-5:]
-    stats = [part[...] for part in parts]
+def base_kernel(here, design, count, far, near, genes, columns, *refs):
+    parts, (home, away, factors, weights, stack, held, lines, coef) = refs[:-8], refs[-8:]
+    n_far = len(parts) // 2
+    size = held.shape[0]
+    snps = size * n_far
+    block = pl.ds(pl.multiple_of(far[0] * size, size), size)
+    moments = [
+        jnp.concatenate([part[:, block], part[:, snps : snps + LANES]], axis=1)
+        for part in parts[:n_far]
+    ]
+    inverse = cohort_lines(moments, size, design, lines)
+    coef[...] = jnp.transpose(lines[...])
+    stats = [part[...] for part in parts[n_far:]]
     row = lax.broadcasted_iota(jnp.int32, stats[0].shape, 0)
     total = tree_sum(stats)
     known = row < SQUARE_ROW
@@ -357,32 +357,32 @@
     for j in range(1, len(stats)):
         factors[j : j + 1, :] = column_norm(stats[j], here) * scale
         stack[j * STRIDE : j * STRIDE + DPAD, :] = jnp.where(known, stats[j], 0.0)
-    size = held.shape[0]
-    block = pl.ds(pl.multiple_of(far[0] * size, size), size)
-    line = coef[block, :]
+    line = coef[...]
     sums = jnp.dot(genes[block, :], columns[...], preferred_element_type=jnp.float32)
     terms = jnp.dot(line, stack[...], precision=HIGHEST, preferred_element_type=jnp.float32)
     held[...] = (line[:, SCALE_LANE : SCALE_LANE + 1] * sums + terms) * scale
     panel = size // count
     for k, out in enumerate((home, away)):
-        place = pl.multiple_of(jnp.bitwise_xor(near[0], k) * panel, panel)
-        out[...] = held[pl.ds(place, panel), :] * (WIDE if k else 1.0)
-
-
-def base_ratio(genes, columns, coef, inverse, parts, far, near, n_far, n_near):
+        place = pl.ds(pl.multiple_of(jnp.bitwise_xor(near[0], k) * panel, panel), panel)
+        out[...] = held[place, :] * (WIDE if k else 1.0)
+        if k == 0:
+            weights[...] = coef[place, :]
+
+
+def base_ratio(genes, columns, moments, parts, far, near, n_far, n_near, design):
     here, width = columns.shape
     size = (genes.shape[0] - DPAD) // n_far
     outs = (result((size // n_near, width), jnp.float32),) * 2
-    outs += (result((8, width), jnp.float32),)
-    kernel = functools.partial(base_kernel, float(here), n_near)
-    scratch = [pltpu.VMEM((LANES, width), jnp.float32), pltpu.VMEM((size, width), jnp.float32)]
-    arrays = [coef, inverse, genes, columns, *parts]
-    kernel = functools.partial(reorder, kernel)
-    return call(kernel, "base_ratio", outs, [far, near], arrays, scratch, 2)
-
-
-def reorder(kernel, far, near, coef, inverse, genes, columns, *refs):
-    kernel(far, near, genes, columns, coef, inverse, *refs)
+    outs += (result((8, width), jnp.float32), result((size // n_near, LANES), jnp.float32))
+    kernel = functools.partial(base_kernel, float(here), design, n_near)
+    scratch = [
+        pltpu.VMEM((LANES, width), jnp.float32),
+        pltpu.VMEM((size, width), jnp.float32),
+        pltpu.VMEM((LANES, size), jnp.float32),
+        pltpu.VMEM((size, LANES), jnp.float32),
+    ]
+    arrays = [genes, columns, *moments, *parts]
+    return call(kernel, "base_ratio", outs, [far, near], arrays, scratch)
 
 
 def permute_xor(value, axes, bits):
@@ -418,9 +418,8 @@
     genes, moment = moments(blocks, others, slots, (vox * n_near + near)[None])
     pair_coef = pair_fit(moment, snps, design)
     moment_parts = [moment] + [permute_xor(moment, "far", j) for j in range(1, n_far)]
-    coef, inverse = cohort_fit(moment_parts, snps, design)
-    columns, pair_coef, coef, inverse = lax.optimization_barrier(
-        (columns, pair_coef, coef, inverse)
+    columns, pair_coef, moment_parts = lax.optimization_barrier(
+        (columns, pair_coef, moment_parts)
     )
     stats = column_sums(genes, columns)
     stat_parts = [stats] + [permute_xor(stats, "far", j) for j in range(1, n_far)]
@@ -437,16 +436,16 @@
     pieces = {
         k: permute_xor(sent[k - n_near], line, k) for k in range(n_near, n_far * n_near)
     }
-    home, away, factors = base_ratio(genes, columns, coef, inverse, stat_parts, *where)
+    home, away, factors, weights = base_ratio(
+        genes, columns, moment_parts, stat_parts, *where, design
+    )
     away = permute_xor(away.astype(jnp.float16), "near", 1)
     away = away.astype(jnp.float32) * (1.0 / WIDE)
     away_factors = permute_xor(factors, "near", 1)
-    place = far * n_near + near
-    columns_scale = lax.dynamic_slice_in_dim(coef, place * panel, panel, 0)
 
     def t_of(ratio, factors, offset):
         for j in range(1, n_far):
-            weight = columns_scale[:, SCALE_LANE + 1 + j, None] * factors[None, j]
+            weight = weights[:, SCALE_LANE + 1 + j, None] * factors[None, j]
             ratio = ratio + pieces[j * n_near + offset].astype(jnp.float32) * weight
         return ratio * jnp.sqrt(freedom / (1.0 - ratio * ratio))
 

time: 79.9 us -> 77.9 us (0.975)
  starting transfers between devices: 23.1 us -> 18.9 us
  waiting for transfers between devices: 27.4 us -> 31.4 us
  other arithmetic: 4.47 us -> 3 us
  Pallas kernels: 16.1 us -> 15.1 us
    ppermute x10, starting transfers between devices: 19.5 us -> 15.3 us  [permute_xor(): return lax.ppermute(value, axes, [(i, i ^ bits) for i in range(size)])]
    ppermute x10, waiting for transfers between devices: 27.4 us -> 29.5 us  [permute_xor(): return lax.ppermute(value, axes, [(i, i ^ bits) for i in range(size)])]
    all_to_all x1, waiting for transfers between devices: 0.01 us -> 1.91 us  [exchange(): value = lax.all_to_all(value, ('vox', 'near'), 0, 0, tiled=True)]
    unnamed x16 -> x18, local copies, waits for them, and re-layouts: 5.41 us -> 7.02 us
    pallas_call x6 -> x5, Pallas kernels: 11.2 us -> 10.1 us  [call(): pl.pallas_call(kernel, out_shape=outs, in_specs=[IN_SMEM] * len(scalars)...]
    another operation x1, other arithmetic: 1.33 us -> 0.38 us  [on_device(): jnp.stack([home, away], 1)]
    slice x3, local copies, waits for them, and re-layouts: 1.03 us -> 0.18 us  [t_of(): weight = weights[:, SCALE_LANE + 1 + j, None] * factors[None, j]]
  transfers between devices with their start and end apart: 11 -> 11, of which waited for: 6 -> 7; matrix products, arithmetic and copies ran while one was open for 5% -> 3% of each run, Pallas kernels for 18% -> 18%
where the time goes in v14:
time: 77.9 us; the launch traced here: 77.4 us
  waiting for transfers between devices  31.4 us (40%)
  starting transfers between devices  18.9 us (24%)
  Pallas kernels  15.1 us (19%)
  local copies, waits for them, and re-layouts  8.83 us (11%)
  other arithmetic  3 us (4%)
    ppermute x10, waiting for transfers between devices, permute_xor(): return lax.ppermute(value, axes, [(i, i ^ bits) for i in range(size)])  29.5 us
    ppermute x10, starting transfers between devices, permute_xor(): return lax.ppermute(value, axes, [(i, i ^ bits) for i in range(size)])  15.3 us
    pallas_call x5, Pallas kernels, call(): pl.pallas_call(kernel, out_shape=outs, in_specs=[IN_SMEM] * len(scalars)...  10.1 us
    unnamed x18, local copies, waits for them, and re-layouts  7.02 us
    pallas_call x1, Pallas kernels, smooth(): pl.pallas_call(functools.partial(smooth_kernel, group, planes, per_vox, p...  3.97 us
    all_to_all x1, starting transfers between devices, exchange(): value = lax.all_to_all(value, ('vox', 'near'), 0, 0, tiled=True)  3.6 us
    all_to_all x1, waiting for transfers between devices, exchange(): value = lax.all_to_all(value, ('vox', 'near'), 0, 0, tiled=True)  1.91 us
    select_n x2, local copies, waits for them, and re-layouts, on_device(): jnp.where(near == 0, jnp.stack([home, away], 1), jnp.stack([away, home], 1))  1.63 us
  transfers between devices with their start and end apart: 11, of which 7 were waited for; matrix products, arithmetic and copies ran while one was open for 3% of the time, Pallas kernels for 18%

profile of v14, /device:TPU:0, one launch (start us, length us, event | category | flops | bytes accessed | tf_op | source)
XLA Modules:
  0.0 77.4 jit_solution(7569708290205506579)
XLA Ops:
  0.0 1.0 %tall_design.1 = bf16[536,128]{1,0:T(8,128)(2,1)S(1)} custom-call(bf16[128,512]{1,0:T(8,128)(2,1)} %genotypes.1, s32[1,128]{1,0:T(1,128)} %bitcast.30, bf16[16,128]{1,0:T(8,128)(2,1)} %bitcast.29), custom_call_target="tpu_custom_call" | custom-call | tf_op jit(solution)/shard_map/tall_design/pallas_call | solution.py:112
  1.0 3.1 %collective-permute-start = (bf16[536,128]{1,0:T(8,128)(2,1)S(1)}, bf16[536,128]{1,0:T(8,128)(2,1)S(1)}, u32[]{:S(2)}, u32[]{:S(2)}) collective-permute-start(bf16[536,128]{1,0:T(8,128)(2,1)S(1)} %tall_design.1), channel_id=1, source_target_pairs={{0,1},{1,0},{4,5},{5,4},{8,9},{9,8},{12,13},{13,12},{2,3},{3,2},{6... | collective-permute-start | bytes 411656 | tf_op jit(solution)/shard_map/ppermute | solution.py:390
  4.1 1.5 %collective-permute-start.1 = (bf16[536,128]{1,0:T(8,128)(2,1)S(1)}, bf16[536,128]{1,0:T(8,128)(2,1)S(1)}, u32[]{:S(2)}, u32[]{:S(2)}) collective-permute-start(bf16[536,128]{1,0:T(8,128)(2,1)S(1)} %tall_design.1), channel_id=1, source_target_pairs={{0,8},{1,9},{4,12},{5,13},{8,0},{9,1},{12,4},{13,5},{2,10},{3,11},... | collective-permute-start | bytes 411656 | tf_op jit(solution)/shard_map/ppermute | solution.py:390
  5.6 4.0 %smooth.1 = bf16[8,128,1024]{2,1,0:T(8,128)(2,1)} custom-call(bf16[128,32,256]{2,1,0:T(8,128)(2,1)} %bitcast.23, bf16[256,256]{1,0:T(8,128)(2,1)} %constant.25.clone.order, bf16[256,256]{1,0:T(8,128)(2,1)} %constant.26.clone.table), custom_call_target="tpu_custom_call" | custom-call | tf_op jit(solution)/shard_map/smooth/pallas_call | solution.py:167
  9.6 2.5 %collective-permute-done.1 = bf16[536,128]{1,0:T(8,128)(2,1)S(1)} collective-permute-done((bf16[536,128]{1,0:T(8,128)(2,1)S(1)}, bf16[536,128]{1,0:T(8,128)(2,1)S(1)}, u32[]{:S(2)}, u32[]{:S(2)}) %collective-permute-start.1) | collective-permute-done | bytes 137248 | tf_op jit(solution)/shard_map/ppermute | solution.py:390
  12.1 3.6 %all-to-all-start = ((bf16[8,128,1024]{2,1,0:T(8,128)(2,1)}), bf16[8,128,1024]{2,1,0:T(8,128)(2,1)S(1)}, u32[]{:S(2)}, u32[]{:S(2)}) async-start(bf16[8,128,1024]{2,1,0:T(8,128)(2,1)} %smooth.1), calls=%async_computation | async-start | bytes 4194304 | tf_op jit(solution)/shard_map/all_to_all | solution.py:404
  15.8 0.5 collective-permute-start.3
  16.3 0.8 %copy-done = bf16[4,536,128]{2,1,0:T(8,128)(2,1)} copy-done((bf16[4,536,128]{2,1,0:T(8,128)(2,1)}, bf16[4,536,128]{2,1,0:T(8,128)(2,1)S(1)}, u32[]{:S(2)}) %copy-start) | copy-done | bytes 548888
  17.1 0.9 %collective-permute-done.3.others = bf16[4,536,128]{2,1,0:T(8,128)(2,1)S(1)} collective-permute-done((bf16[4,536,128]{2,1,0:T(8,128)(2,1)S(1)}, bf16[4,536,128]{2,1,0:T(8,128)(2,1)S(1)}, u32[]{:S(2)}, u32[]{:S(2)}) %collective-permute-start.3) | collective-permute-done | bytes 548896 | tf_op jit(solution)/shard_map/ppermute | solution.py:390
  18.0 0.8 %copy-done.2 = bf16[4,536,128]{2,1,0:T(8,128)(2,1)} copy-done((bf16[4,536,128]{2,1,0:T(8,128)(2,1)}, bf16[4,536,128]{2,1,0:T(8,128)(2,1)S(1)}, u32[]{:S(2)}) %copy-start.2) | copy-done | bytes 548888
  18.8 1.0 %copy-done.1 = bf16[4,536,128]{2,1,0:T(8,128)(2,1)S(1)} copy-done((bf16[4,536,128]{2,1,0:T(8,128)(2,1)S(1)}, bf16[4,536,128]{2,1,0:T(8,128)(2,1)}, u32[]{:S(2)}) %copy-start.1) | copy-done | bytes 548888
  19.8 1.0 %copy-done.3 = bf16[4,536,128]{2,1,0:T(8,128)(2,1)S(1)} copy-done((bf16[4,536,128]{2,1,0:T(8,128)(2,1)S(1)}, bf16[4,536,128]{2,1,0:T(8,128)(2,1)}, u32[]{:S(2)}) %copy-start.3) | copy-done | bytes 548888
  20.9 1.7 %moments.1 = (bf16[536,1024]{1,0:T(8,128)(2,1)S(1)}, f32[32,640]{1,0:T(8,128)}) custom-call(s32[1]{0:T(128)} %bitcast.2.me, bf16[4,536,128]{2,1,0:T(8,128)(2,1)S(1)} %copy-done.1, bf16[4,536,128]{2,1,0:T(8,128)(2,1)S(1)} %copy-done.3), custom_call_target="tpu_custom_call" | custom-call | tf_op jit(solution)/shard_map/moments/pallas_call | solution.py:88
  22.6 2.6 %collective-permute-start.4 = (f32[32,640]{1,0:T(8,128)}, f32[32,640]{1,0:T(8,128)S(1)}, u32[]{:S(2)}, u32[]{:S(2)}) collective-permute-start(f32[32,640]{1,0:T(8,128)} %get-tuple-element.36.moment.refs_0_), channel_id=1, source_target_pairs={{0,2},{2,0},{1,3},{3,1},{4,6},{6,4},{5,7},{7,5},{8,10},{10,8},{9,1... | collective-permute-start | bytes 245768 | tf_op jit(solution)/shard_map/ppermute | solution.py:390
  25.1 0.9 %copy-done.5 = f32[32,640]{1,0:T(8,128)S(1)} copy-done((f32[32,640]{1,0:T(8,128)S(1)}, f32[32,640]{1,0:T(8,128)}, u32[]{:S(2)}) %copy-start.5) | copy-done | bytes 81944
  26.1 2.0 %pair_fit.1.coef = f32[512,128]{1,0:T(8,128)S(1)} custom-call(f32[32,640]{1,0:T(8,128)S(1)} %copy-done.5), custom_call_target="tpu_custom_call" | custom-call | tf_op jit(solution)/shard_map/pair_fit/pallas_call | solution.py:88
  28.1 13.0 %collective-permute-done.4.refs_1_ = f32[32,640]{1,0:T(8,128)S(1)} collective-permute-done((f32[32,640]{1,0:T(8,128)}, f32[32,640]{1,0:T(8,128)S(1)}, u32[]{:S(2)}, u32[]{:S(2)}) %collective-permute-start.4) | collective-permute-done | bytes 81952 | tf_op jit(solution)/shard_map/ppermute | solution.py:390
  41.1 0.6 copy-done.7
  41.7 1.9 %all-to-all-done = bf16[8,128,1024]{2,1,0:T(8,128)(2,1)S(1)} async-done(((bf16[8,128,1024]{2,1,0:T(8,128)(2,1)}), bf16[8,128,1024]{2,1,0:T(8,128)(2,1)S(1)}, u32[]{:S(2)}, u32[]{:S(2)}) %all-to-all-start) | async-done | bytes 2097184 | tf_op jit(solution)/shard_map/all_to_all | solution.py:404
  44.1 1.4 %collective-permute-start.5 = (f32[24,1024]{1,0:T(8,128)S(1)}, f32[24,1024]{1,0:T(8,128)}, u32[]{:S(2)}, u32[]{:S(2)}) collective-permute-start(f32[24,1024]{1,0:T(8,128)S(1)} %column_sums.1.stats.refs_2_), channel_id=1, source_target_pairs={{0,2},{2,0},{1,3},{3,1},{4,6},{6,4},{5,7},{7,5},{8,10},{10,8},{9,1... | collective-permute-start | bytes 294920 | tf_op jit(solution)/shard_map/ppermute | solution.py:390
  45.5 1.5 %far_products.1 = (f32[128,1024]{1,0:T(8,128)S(1)}, f32[128,1024]{1,0:T(8,128)S(1)}) custom-call(s32[1]{0:T(128)} %bitcast.far, s32[1]{0:T(128)} %bitcast.1.near, bf16[536,1024]{1,0:T(8,128)(2,1)S(1)} %get-tuple-element.32.genes, bf16[1024,1024]{1,0:T(8,128)(2,1)S(1)} %bitcast.18, f32[512,128]{1,0:T(8,128)S(1)} %pair_fit.1.coef, ...), custom_call_target="tpu_custom_call" | custom-call | tf_op jit(solution)/shard_map/far_products/pallas_call | solution.py:88
  47.1 3.7 %collective-permute-done.5.refs_3_ = f32[24,1024]{1,0:T(8,128)} collective-permute-done((f32[24,1024]{1,0:T(8,128)S(1)}, f32[24,1024]{1,0:T(8,128)}, u32[]{:S(2)}, u32[]{:S(2)}) %collective-permute-start.5) | collective-permute-done | bytes 98336 | tf_op jit(solution)/shard_map/ppermute | solution.py:390
  51.2 1.1 %convert_element_type.22 = f16[128,1024]{1,0:T(8,128)(2,1)S(1)} convert(f32[128,1024]{1,0:T(8,128)} %copy-done.4) | non-fusion elementwise | flops 131072 | bytes 786432 | tf_op jit(solution)/shard_map/convert_element_type | solution.py:435
  52.2 3.7 %collective-permute-start.9 = (f16[128,1024]{1,0:T(8,128)(2,1)S(1)}, f16[128,1024]{1,0:T(8,128)(2,1)S(1)}, u32[]{:S(2)}, u32[]{:S(2)}) collective-permute-start(f16[128,1024]{1,0:T(8,128)(2,1)S(1)} %convert_element_type.22), channel_id=1, source_target_pairs={{0,3},{1,2},{2,1},{3,0},{4,7},{5,6},{6,5},{7,4},{8,11},{9,10},{10,... | collective-permute-start | bytes 786440 | tf_op jit(solution)/shard_map/ppermute | solution.py:390
  56.0 0.9 %copy-done.6 = f32[32,640]{1,0:T(8,128)S(1)} copy-done((f32[32,640]{1,0:T(8,128)S(1)}, f32[32,640]{1,0:T(8,128)}, u32[]{:S(2)}) %copy-start.6) | copy-done | bytes 81944
  56.9 0.9 %copy-done.8 = f32[32,640]{1,0:T(8,128)S(1)} copy-done((f32[32,640]{1,0:T(8,128)S(1)}, f32[32,640]{1,0:T(8,128)}, u32[]{:S(2)}) %copy-start.8) | copy-done | bytes 81944
  57.8 4.4 %base_ratio.1 = (f32[128,1024]{1,0:T(8,128)S(1)}, f32[128,1024]{1,0:T(8,128)S(1)}, f32[8,1024]{1,0:T(8,128)S(1)}, f32[128,128]{1,0:T(8,128)S(1)}) custom-call(s32[1]{0:T(128)} %bitcast.far, s32[1]{0:T(128)} %bitcast.1.near, bf16[536,1024]{1,0:T(8,128)(2,1)S(1)} %get-tuple-element.32.genes, bf16[1024,1024]{1,0:T(8,128)(2,1)S(1)} %bitcast.19, ...), custom_call_target="tpu_custom_call" | custom-call | tf_op jit(solution)/shard_map/base_ratio/pallas_call | solution.py:88
  62.3 2.0 %collective-permute-start.6 = (f32[8,1024]{1,0:T(8,128)S(1)}, f32[8,1024]{1,0:T(8,128)S(1)}, u32[]{:S(2)}, u32[]{:S(2)}) collective-permute-start(f32[8,1024]{1,0:T(8,128)S(1)} %get-tuple-element.43), channel_id=1, source_target_pairs={{0,1},{1,0},{2,3},{3,2},{4,5},{5,4},{6,7},{7,6},{8,9},{9,8},{10,11... | collective-permute-start | bytes 98312 | tf_op jit(solution)/shard_map/ppermute | solution.py:390
  64.5 7.2 %collective-permute-done.7 = f16[128,1024]{1,0:T(8,128)(2,1)} collective-permute-done((f16[128,1024]{1,0:T(8,128)(2,1)S(1)}, f16[128,1024]{1,0:T(8,128)(2,1)}, u32[]{:S(2)}, u32[]{:S(2)}) %collective-permute-start.7) | collective-permute-done | bytes 262176 | tf_op jit(solution)/shard_map/ppermute | solution.py:390
  71.7 1.3 %sqrt_multiply_fusion = f32[128,1024]{1,0:T(8,128)S(1)} fusion(f32[128,1024]{1,0:T(8,128)S(1)} %get-tuple-element.44, f16[128,1024]{1,0:T(8,128)(2,1)} %collective-permute-done.7, f32[1024]{0:T(1024)S(1)} %bitcast.28, f32[128]{0:T(128)S(1)} %slice_reduce_fusion), kind=kLoop, calls=%fused_computation.3 | loop fusion | flops 1048576 | bytes 1315328 | tf_op jit(solution)/shard_map/mul | solution.py:450
  73.0 2.2 %collective-permute-done.6 = f32[8,1024]{1,0:T(8,128)S(1)} collective-permute-done((f32[8,1024]{1,0:T(8,128)S(1)}, f32[8,1024]{1,0:T(8,128)S(1)}, u32[]{:S(2)}, u32[]{:S(2)}) %collective-permute-start.6) | collective-permute-done | bytes 32800 | tf_op jit(solution)/shard_map/ppermute | solution.py:390
  76.0 1.3 %copy.8 = f32[128,4,2,256]{3,2,1,0:T(2,128)} copy(f32[128,4,2,256]{0,3,2,1:T(8,128)S(1)} %bitcast.21) | data formatting | bytes 2097152 | tf_op jit(solution)/shard_map/jit(_where)/select_n | solution.py:455
  (27 shorter events, 2.1 us)
Async XLA Ops:
  1.0 8.6 %collective-permute-start = (bf16[536,128]{1,0:T(8,128)(2,1)S(1)}, bf16[536,128]{1,0:T(8,128)(2,1)S(1)}, u32[]{:S(2)}, u32[]{:S(2)}) collective-permute-start(bf16[536,128]{1,0:T(8,128)(2,1)S(1)} %tall_design.1), channel_id=1, source_target_pairs={{0,1},{1,0},{4,5},{5,4},{8,9},{9,8},{12,13},{13,12},{2,3},{3,2},{6... | collective-permute-start | bytes 411656 | tf_op jit(solution)/shard_map/ppermute | solution.py:390
  4.1 8.0 %collective-permute-start.1 = (bf16[536,128]{1,0:T(8,128)(2,1)S(1)}, bf16[536,128]{1,0:T(8,128)(2,1)S(1)}, u32[]{:S(2)}, u32[]{:S(2)}) collective-permute-start(bf16[536,128]{1,0:T(8,128)(2,1)S(1)} %tall_design.1), channel_id=1, source_target_pairs={{0,8},{1,9},{4,12},{5,13},{8,0},{9,1},{12,4},{13,5},{2,10},{3,11},... | collective-permute-start | bytes 411656 | tf_op jit(solution)/shard_map/ppermute | solution.py:390
  5.6 6.5 %collective-permute-start.2 = (bf16[536,128]{1,0:T(8,128)(2,1)S(1)}, bf16[536,128]{1,0:T(8,128)(2,1)S(1)}, u32[]{:S(2)}, u32[]{:S(2)}) collective-permute-start(bf16[536,128]{1,0:T(8,128)(2,1)S(1)} %tall_design.1), channel_id=1, source_target_pairs={{0,9},{1,8},{4,13},{5,12},{8,1},{9,0},{12,5},{13,4},{2,11},{3,10},... | collective-permute-start | bytes 411656 | tf_op jit(solution)/shard_map/ppermute | solution.py:390
  12.1 31.5 %all-to-all-start = ((bf16[8,128,1024]{2,1,0:T(8,128)(2,1)}), bf16[8,128,1024]{2,1,0:T(8,128)(2,1)S(1)}, u32[]{:S(2)}, u32[]{:S(2)}) async-start(bf16[8,128,1024]{2,1,0:T(8,128)(2,1)} %smooth.1), calls=%async_computation | async-start | bytes 4194304 | tf_op jit(solution)/shard_map/all_to_all | solution.py:404
  15.8 2.1 %collective-permute-start.3 = (bf16[4,536,128]{2,1,0:T(8,128)(2,1)S(1)}, bf16[4,536,128]{2,1,0:T(8,128)(2,1)S(1)}, u32[]{:S(2)}, u32[]{:S(2)}) collective-permute-start(bf16[4,536,128]{2,1,0:T(8,128)(2,1)S(1)} %pad_maximum_fusion.blocks), channel_id=1, source_target_pairs={{0,4},{1,5},{4,0},{5,1},{8,12},{9,13},{12,8},{13,9},{2,6},{3,7},{6... | collective-permute-start | bytes 1646600 | tf_op jit(solution)/shard_map/ppermute | solution.py:390
  16.3 0.8 %copy-start = (bf16[4,536,128]{2,1,0:T(8,128)(2,1)}, bf16[4,536,128]{2,1,0:T(8,128)(2,1)S(1)}, u32[]{:S(2)}) copy-start(bf16[4,536,128]{2,1,0:T(8,128)(2,1)S(1)} %pad_maximum_fusion.blocks) | copy-start | bytes 1646596
  18.0 0.8 %copy-start.2 = (bf16[4,536,128]{2,1,0:T(8,128)(2,1)}, bf16[4,536,128]{2,1,0:T(8,128)(2,1)S(1)}, u32[]{:S(2)}) copy-start(bf16[4,536,128]{2,1,0:T(8,128)(2,1)S(1)} %collective-permute-done.3.others) | copy-start | bytes 1646596
  18.8 1.1 %copy-start.1 = (bf16[4,536,128]{2,1,0:T(8,128)(2,1)S(1)}, bf16[4,536,128]{2,1,0:T(8,128)(2,1)}, u32[]{:S(2)}) copy-start(bf16[4,536,128]{2,1,0:T(8,128)(2,1)} %copy-done) | copy-start | bytes 1646596
  19.8 1.1 %copy-start.3 = (bf16[4,536,128]{2,1,0:T(8,128)(2,1)S(1)}, bf16[4,536,128]{2,1,0:T(8,128)(2,1)}, u32[]{:S(2)}) copy-start(bf16[4,536,128]{2,1,0:T(8,128)(2,1)} %copy-done.2) | copy-start | bytes 1646596
  22.6 18.5 %collective-permute-start.4 = (f32[32,640]{1,0:T(8,128)}, f32[32,640]{1,0:T(8,128)S(1)}, u32[]{:S(2)}, u32[]{:S(2)}) collective-permute-start(f32[32,640]{1,0:T(8,128)} %get-tuple-element.36.moment.refs_0_), channel_id=1, source_target_pairs={{0,2},{2,0},{1,3},{3,1},{4,6},{6,4},{5,7},{7,5},{8,10},{10,8},{9,1... | collective-permute-start | bytes 245768 | tf_op jit(solution)/shard_map/ppermute | solution.py:390
  25.1 0.9 %copy-start.5 = (f32[32,640]{1,0:T(8,128)S(1)}, f32[32,640]{1,0:T(8,128)}, u32[]{:S(2)}) copy-start(f32[32,640]{1,0:T(8,128)} %get-tuple-element.36.moment.refs_0_) | copy-start | bytes 245764
  41.1 0.6 copy-start.7
  44.1 6.7 %collective-permute-start.5 = (f32[24,1024]{1,0:T(8,128)S(1)}, f32[24,1024]{1,0:T(8,128)}, u32[]{:S(2)}, u32[]{:S(2)}) collective-permute-start(f32[24,1024]{1,0:T(8,128)S(1)} %column_sums.1.stats.refs_2_), channel_id=1, source_target_pairs={{0,2},{2,0},{1,3},{3,1},{4,6},{6,4},{5,7},{7,5},{8,10},{10,8},{9,1... | collective-permute-start | bytes 294920 | tf_op jit(solution)/shard_map/ppermute | solution.py:390
  47.0 3.8 %copy-start.4 = (f32[128,1024]{1,0:T(8,128)}, f32[128,1024]{1,0:T(8,128)S(1)}, u32[]{:S(2)}) copy-start(f32[128,1024]{1,0:T(8,128)S(1)} %get-tuple-element.49) | copy-start | bytes 1572868
  50.8 20.9 %collective-permute-start.7 = (f16[128,1024]{1,0:T(8,128)(2,1)S(1)}, f16[128,1024]{1,0:T(8,128)(2,1)}, u32[]{:S(2)}, u32[]{:S(2)}) collective-permute-start(f16[128,1024]{1,0:T(8,128)(2,1)S(1)} %convert_element_type.18), channel_id=1, source_target_pairs={{0,2},{1,3},{2,0},{3,1},{4,6},{5,7},{6,4},{7,5},{8,10},{9,11},{10,... | collective-permute-start | bytes 786440 | tf_op jit(solution)/shard_map/ppermute | solution.py:390
  52.2 23.0 %collective-permute-start.9 = (f16[128,1024]{1,0:T(8,128)(2,1)S(1)}, f16[128,1024]{1,0:T(8,128)(2,1)S(1)}, u32[]{:S(2)}, u32[]{:S(2)}) collective-permute-start(f16[128,1024]{1,0:T(8,128)(2,1)S(1)} %convert_element_type.22), channel_id=1, source_target_pairs={{0,3},{1,2},{2,1},{3,0},{4,7},{5,6},{6,5},{7,4},{8,11},{9,10},{10,... | collective-permute-start | bytes 786440 | tf_op jit(solution)/shard_map/ppermute | solution.py:390
  56.0 0.9 %copy-start.6 = (f32[32,640]{1,0:T(8,128)S(1)}, f32[32,640]{1,0:T(8,128)}, u32[]{:S(2)}) copy-start(f32[32,640]{1,0:T(8,128)} %get-tuple-element.36.moment.refs_0_) | copy-start | bytes 245764
  56.9 0.9 %copy-start.8 = (f32[32,640]{1,0:T(8,128)S(1)}, f32[32,640]{1,0:T(8,128)}, u32[]{:S(2)}) copy-start(f32[32,640]{1,0:T(8,128)} %copy-done.7) | copy-start | bytes 245764
  62.2 13.0 %collective-permute-start.8 = (f16[128,1024]{1,0:T(8,128)(2,1)S(1)}, f16[128,1024]{1,0:T(8,128)(2,1)S(1)}, u32[]{:S(2)}, u32[]{:S(2)}) collective-permute-start(f16[128,1024]{1,0:T(8,128)(2,1)S(1)} %convert_element_type.20), channel_id=1, source_target_pairs={{0,1},{1,0},{2,3},{3,2},{4,5},{5,4},{6,7},{7,6},{8,9},{9,8},{10,11... | collective-permute-start | bytes 786440 | tf_op jit(solution)/shard_map/ppermute | solution.py:390
  62.3 12.9 %collective-permute-start.6 = (f32[8,1024]{1,0:T(8,128)S(1)}, f32[8,1024]{1,0:T(8,128)S(1)}, u32[]{:S(2)}, u32[]{:S(2)}) collective-permute-start(f32[8,1024]{1,0:T(8,128)S(1)} %get-tuple-element.43), channel_id=1, source_target_pairs={{0,1},{1,0},{2,3},{3,2},{4,5},{5,4},{6,7},{7,6},{8,9},{9,8},{10,11... | collective-permute-start | bytes 98312 | tf_op jit(solution)/shard_map/ppermute | solution.py:390

commit v15 on v14

--- a/solution.py
+++ b/solution.py
@@ -449,11 +449,13 @@
             ratio = ratio + pieces[j * n_near + offset].astype(jnp.float32) * weight
         return ratio * jnp.sqrt(freedom / (1.0 - ratio * ratio))
 
+    shape = (panel, maps // n_near, per_vox, plane)
     home = t_of(home, factors, 0)
     away_factors, home = lax.optimization_barrier((away_factors, home))
-    away = t_of(away, away_factors, 1)
-    both = jnp.where(near == 0, jnp.stack([home, away], 1), jnp.stack([away, home], 1))
-    return both.reshape(panel, maps, per_vox, plane)
+    home = home.reshape(shape)
+    away = t_of(away, away_factors, 1).reshape(shape)
+    both = [jnp.concatenate(pair, axis=1) for pair in ([home, away], [away, home])]
+    return jnp.where(near == 0, *both)
 
 
 def solution(mesh):

time: 77.9 us -> 78.8 us (1.012)
  other arithmetic: 3 us -> 4.67 us
    select_n x1, other arithmetic: 0.11 us -> 1.78 us  [on_device(): return jnp.where(near == 0, *both)]
    select_n x2 -> x0, local copies, waits for them, and re-layouts: 1.63 us -> none  [on_device(): jnp.where(near == 0, jnp.stack([home, away], 1), jnp.stack([away, home], 1))]
    reshape x0 -> x2, local copies, waits for them, and re-layouts: none -> 0.88 us  [the longest x1 0.44 us: on_device(): away = t_of(away, away_factors, 1).reshape(shape)]
    mul x1 -> x2, other arithmetic: 1.3 us -> 1.68 us  [t_of(): return ratio * jnp.sqrt(freedom / (1.0 - ratio * ratio))]
  transfers between devices with their start and end apart: 11 -> 11, of which waited for: 7 -> 7; matrix products, arithmetic and copies ran while one was open for 3% -> 3% of each run, Pallas kernels for 18% -> 17%
where the time goes in v15:
time: 78.8 us; the launch traced here: 78.3 us
  waiting for transfers between devices  31.4 us (40%)
  starting transfers between devices  18.9 us (24%)
  Pallas kernels  15.1 us (19%)
  local copies, waits for them, and re-layouts  8.09 us (10%)
  other arithmetic  4.67 us (6%)
    ppermute x10, waiting for transfers between devices, permute_xor(): return lax.ppermute(value, axes, [(i, i ^ bits) for i in range(size)])  29.5 us
    ppermute x10, starting transfers between devices, permute_xor(): return lax.ppermute(value, axes, [(i, i ^ bits) for i in range(size)])  15.3 us
    pallas_call x5, Pallas kernels, call(): pl.pallas_call(kernel, out_shape=outs, in_specs=[IN_SMEM] * len(scalars)...  10.1 us
    unnamed x18, local copies, waits for them, and re-layouts  7.02 us
    pallas_call x1, Pallas kernels, smooth(): pl.pallas_call(functools.partial(smooth_kernel, group, planes, per_vox, p...  3.97 us
    all_to_all x1, starting transfers between devices, exchange(): value = lax.all_to_all(value, ('vox', 'near'), 0, 0, tiled=True)  3.6 us
    all_to_all x1, waiting for transfers between devices, exchange(): value = lax.all_to_all(value, ('vox', 'near'), 0, 0, tiled=True)  1.91 us
    select_n x1, other arithmetic, on_device(): return jnp.where(near == 0, *both)  1.78 us
  transfers between devices with their start and end apart: 11, of which 7 were waited for; matrix products, arithmetic and copies ran while one was open for 3% of the time, Pallas kernels for 17%

profile of v15, /device:TPU:0, one launch (start us, length us, event | category | flops | bytes accessed | tf_op | source)
XLA Modules:
  0.0 78.3 jit_solution(5515586520815423266)
XLA Ops:
  0.0 1.0 %tall_design.1 = bf16[536,128]{1,0:T(8,128)(2,1)S(1)} custom-call(bf16[128,512]{1,0:T(8,128)(2,1)} %genotypes.1, s32[1,128]{1,0:T(1,128)} %bitcast.24, bf16[16,128]{1,0:T(8,128)(2,1)} %bitcast.23), custom_call_target="tpu_custom_call" | custom-call | tf_op jit(solution)/shard_map/tall_design/pallas_call | solution.py:112
  1.0 3.1 %collective-permute-start = (bf16[536,128]{1,0:T(8,128)(2,1)S(1)}, bf16[536,128]{1,0:T(8,128)(2,1)S(1)}, u32[]{:S(2)}, u32[]{:S(2)}) collective-permute-start(bf16[536,128]{1,0:T(8,128)(2,1)S(1)} %tall_design.1), channel_id=1, source_target_pairs={{0,1},{1,0},{4,5},{5,4},{8,9},{9,8},{12,13},{13,12},{2,3},{3,2},{6... | collective-permute-start | bytes 411656 | tf_op jit(solution)/shard_map/ppermute | solution.py:390
  4.1 1.5 %collective-permute-start.1 = (bf16[536,128]{1,0:T(8,128)(2,1)S(1)}, bf16[536,128]{1,0:T(8,128)(2,1)S(1)}, u32[]{:S(2)}, u32[]{:S(2)}) collective-permute-start(bf16[536,128]{1,0:T(8,128)(2,1)S(1)} %tall_design.1), channel_id=1, source_target_pairs={{0,8},{1,9},{4,12},{5,13},{8,0},{9,1},{12,4},{13,5},{2,10},{3,11},... | collective-permute-start | bytes 411656 | tf_op jit(solution)/shard_map/ppermute | solution.py:390
  5.6 4.0 %smooth.1 = bf16[8,128,1024]{2,1,0:T(8,128)(2,1)} custom-call(bf16[128,32,256]{2,1,0:T(8,128)(2,1)} %bitcast.17, bf16[256,256]{1,0:T(8,128)(2,1)} %constant.25.clone.order, bf16[256,256]{1,0:T(8,128)(2,1)} %constant.26.clone.table), custom_call_target="tpu_custom_call" | custom-call | tf_op jit(solution)/shard_map/smooth/pallas_call | solution.py:167
  9.6 2.5 %collective-permute-done.1 = bf16[536,128]{1,0:T(8,128)(2,1)S(1)} collective-permute-done((bf16[536,128]{1,0:T(8,128)(2,1)S(1)}, bf16[536,128]{1,0:T(8,128)(2,1)S(1)}, u32[]{:S(2)}, u32[]{:S(2)}) %collective-permute-start.1) | collective-permute-done | bytes 137248 | tf_op jit(solution)/shard_map/ppermute | solution.py:390
  12.1 3.6 %all-to-all-start = ((bf16[8,128,1024]{2,1,0:T(8,128)(2,1)}), bf16[8,128,1024]{2,1,0:T(8,128)(2,1)S(1)}, u32[]{:S(2)}, u32[]{:S(2)}) async-start(bf16[8,128,1024]{2,1,0:T(8,128)(2,1)} %smooth.1), calls=%async_computation | async-start | bytes 4194304 | tf_op jit(solution)/shard_map/all_to_all | solution.py:404
  15.8 0.5 collective-permute-start.3
  16.3 0.8 %copy-done = bf16[4,536,128]{2,1,0:T(8,128)(2,1)} copy-done((bf16[4,536,128]{2,1,0:T(8,128)(2,1)}, bf16[4,536,128]{2,1,0:T(8,128)(2,1)S(1)}, u32[]{:S(2)}) %copy-start) | copy-done | bytes 548888
  17.1 0.9 %collective-permute-done.3.others = bf16[4,536,128]{2,1,0:T(8,128)(2,1)S(1)} collective-permute-done((bf16[4,536,128]{2,1,0:T(8,128)(2,1)S(1)}, bf16[4,536,128]{2,1,0:T(8,128)(2,1)S(1)}, u32[]{:S(2)}, u32[]{:S(2)}) %collective-permute-start.3) | collective-permute-done | bytes 548896 | tf_op jit(solution)/shard_map/ppermute | solution.py:390
  18.0 0.8 %copy-done.2 = bf16[4,536,128]{2,1,0:T(8,128)(2,1)} copy-done((bf16[4,536,128]{2,1,0:T(8,128)(2,1)}, bf16[4,536,128]{2,1,0:T(8,128)(2,1)S(1)}, u32[]{:S(2)}) %copy-start.2) | copy-done | bytes 548888
  18.8 1.0 %copy-done.1 = bf16[4,536,128]{2,1,0:T(8,128)(2,1)S(1)} copy-done((bf16[4,536,128]{2,1,0:T(8,128)(2,1)S(1)}, bf16[4,536,128]{2,1,0:T(8,128)(2,1)}, u32[]{:S(2)}) %copy-start.1) | copy-done | bytes 548888
  19.8 1.0 %copy-done.3 = bf16[4,536,128]{2,1,0:T(8,128)(2,1)S(1)} copy-done((bf16[4,536,128]{2,1,0:T(8,128)(2,1)S(1)}, bf16[4,536,128]{2,1,0:T(8,128)(2,1)}, u32[]{:S(2)}) %copy-start.3) | copy-done | bytes 548888
  20.9 1.7 %moments.1 = (bf16[536,1024]{1,0:T(8,128)(2,1)S(1)}, f32[32,640]{1,0:T(8,128)}) custom-call(s32[1]{0:T(128)} %bitcast.2.me, bf16[4,536,128]{2,1,0:T(8,128)(2,1)S(1)} %copy-done.1, bf16[4,536,128]{2,1,0:T(8,128)(2,1)S(1)} %copy-done.3), custom_call_target="tpu_custom_call" | custom-call | tf_op jit(solution)/shard_map/moments/pallas_call | solution.py:88
  22.6 2.6 %collective-permute-start.4 = (f32[32,640]{1,0:T(8,128)}, f32[32,640]{1,0:T(8,128)S(1)}, u32[]{:S(2)}, u32[]{:S(2)}) collective-permute-start(f32[32,640]{1,0:T(8,128)} %get-tuple-element.36.moment.refs_0_), channel_id=1, source_target_pairs={{0,2},{2,0},{1,3},{3,1},{4,6},{6,4},{5,7},{7,5},{8,10},{10,8},{9,1... | collective-permute-start | bytes 245768 | tf_op jit(solution)/shard_map/ppermute | solution.py:390
  25.1 0.9 %copy-done.5 = f32[32,640]{1,0:T(8,128)S(1)} copy-done((f32[32,640]{1,0:T(8,128)S(1)}, f32[32,640]{1,0:T(8,128)}, u32[]{:S(2)}) %copy-start.5) | copy-done | bytes 81944
  26.1 2.0 %pair_fit.1.coef = f32[512,128]{1,0:T(8,128)S(1)} custom-call(f32[32,640]{1,0:T(8,128)S(1)} %copy-done.5), custom_call_target="tpu_custom_call" | custom-call | tf_op jit(solution)/shard_map/pair_fit/pallas_call | solution.py:88
  28.1 13.0 %collective-permute-done.4.refs_1_ = f32[32,640]{1,0:T(8,128)S(1)} collective-permute-done((f32[32,640]{1,0:T(8,128)}, f32[32,640]{1,0:T(8,128)S(1)}, u32[]{:S(2)}, u32[]{:S(2)}) %collective-permute-start.4) | collective-permute-done | bytes 81952 | tf_op jit(solution)/shard_map/ppermute | solution.py:390
  41.1 0.6 copy-done.7
  41.7 1.9 %all-to-all-done = bf16[8,128,1024]{2,1,0:T(8,128)(2,1)S(1)} async-done(((bf16[8,128,1024]{2,1,0:T(8,128)(2,1)}), bf16[8,128,1024]{2,1,0:T(8,128)(2,1)S(1)}, u32[]{:S(2)}, u32[]{:S(2)}) %all-to-all-start) | async-done | bytes 2097184 | tf_op jit(solution)/shard_map/all_to_all | solution.py:404
  44.1 1.4 %collective-permute-start.5 = (f32[24,1024]{1,0:T(8,128)S(1)}, f32[24,1024]{1,0:T(8,128)}, u32[]{:S(2)}, u32[]{:S(2)}) collective-permute-start(f32[24,1024]{1,0:T(8,128)S(1)} %column_sums.1.stats.refs_2_), channel_id=1, source_target_pairs={{0,2},{2,0},{1,3},{3,1},{4,6},{6,4},{5,7},{7,5},{8,10},{10,8},{9,1... | collective-permute-start | bytes 294920 | tf_op jit(solution)/shard_map/ppermute | solution.py:390
  45.5 1.5 %far_products.1 = (f32[128,1024]{1,0:T(8,128)S(1)}, f32[128,1024]{1,0:T(8,128)S(1)}) custom-call(s32[1]{0:T(128)} %bitcast.far, s32[1]{0:T(128)} %bitcast.1.near, bf16[536,1024]{1,0:T(8,128)(2,1)S(1)} %get-tuple-element.32.genes, bf16[1024,1024]{1,0:T(8,128)(2,1)S(1)} %bitcast.14, f32[512,128]{1,0:T(8,128)S(1)} %pair_fit.1.coef, ...), custom_call_target="tpu_custom_call" | custom-call | tf_op jit(solution)/shard_map/far_products/pallas_call | solution.py:88
  47.1 3.7 %collective-permute-done.5.refs_3_ = f32[24,1024]{1,0:T(8,128)} collective-permute-done((f32[24,1024]{1,0:T(8,128)S(1)}, f32[24,1024]{1,0:T(8,128)}, u32[]{:S(2)}, u32[]{:S(2)}) %collective-permute-start.5) | collective-permute-done | bytes 98336 | tf_op jit(solution)/shard_map/ppermute | solution.py:390
  51.2 1.1 %convert_element_type.22 = f16[128,1024]{1,0:T(8,128)(2,1)S(1)} convert(f32[128,1024]{1,0:T(8,128)} %copy-done.4) | non-fusion elementwise | flops 131072 | bytes 786432 | tf_op jit(solution)/shard_map/convert_element_type | solution.py:435
  52.2 3.7 %collective-permute-start.9 = (f16[128,1024]{1,0:T(8,128)(2,1)S(1)}, f16[128,1024]{1,0:T(8,128)(2,1)S(1)}, u32[]{:S(2)}, u32[]{:S(2)}) collective-permute-start(f16[128,1024]{1,0:T(8,128)(2,1)S(1)} %convert_element_type.22), channel_id=1, source_target_pairs={{0,3},{1,2},{2,1},{3,0},{4,7},{5,6},{6,5},{7,4},{8,11},{9,10},{10,... | collective-permute-start | bytes 786440 | tf_op jit(solution)/shard_map/ppermute | solution.py:390
  56.0 0.9 %copy-done.6 = f32[32,640]{1,0:T(8,128)S(1)} copy-done((f32[32,640]{1,0:T(8,128)S(1)}, f32[32,640]{1,0:T(8,128)}, u32[]{:S(2)}) %copy-start.6) | copy-done | bytes 81944
  56.9 0.9 %copy-done.8 = f32[32,640]{1,0:T(8,128)S(1)} copy-done((f32[32,640]{1,0:T(8,128)S(1)}, f32[32,640]{1,0:T(8,128)}, u32[]{:S(2)}) %copy-start.8) | copy-done | bytes 81944
  57.8 4.4 %base_ratio.1 = (f32[128,1024]{1,0:T(8,128)S(1)}, f32[128,1024]{1,0:T(8,128)S(1)}, f32[8,1024]{1,0:T(8,128)S(1)}, f32[128,128]{1,0:T(8,128)S(1)}) custom-call(s32[1]{0:T(128)} %bitcast.far, s32[1]{0:T(128)} %bitcast.1.near, bf16[536,1024]{1,0:T(8,128)(2,1)S(1)} %get-tuple-element.32.genes, bf16[1024,1024]{1,0:T(8,128)(2,1)S(1)} %bitcast.15, ...), custom_call_target="tpu_custom_call" | custom-call | tf_op jit(solution)/shard_map/base_ratio/pallas_call | solution.py:88
  62.3 2.0 %collective-permute-start.6 = (f32[8,1024]{1,0:T(8,128)S(1)}, f32[8,1024]{1,0:T(8,128)S(1)}, u32[]{:S(2)}, u32[]{:S(2)}) collective-permute-start(f32[8,1024]{1,0:T(8,128)S(1)} %get-tuple-element.43), channel_id=1, source_target_pairs={{0,1},{1,0},{2,3},{3,2},{4,5},{5,4},{6,7},{7,6},{8,9},{9,8},{10,11... | collective-permute-start | bytes 98312 | tf_op jit(solution)/shard_map/ppermute | solution.py:390
  64.5 7.2 %collective-permute-done.7 = f16[128,1024]{1,0:T(8,128)(2,1)} collective-permute-done((f16[128,1024]{1,0:T(8,128)(2,1)S(1)}, f16[128,1024]{1,0:T(8,128)(2,1)}, u32[]{:S(2)}, u32[]{:S(2)}) %collective-permute-start.7) | collective-permute-done | bytes 262176 | tf_op jit(solution)/shard_map/ppermute | solution.py:390
  71.7 1.3 %sqrt_multiply_fusion.1 = f32[128,1024]{1,0:T(8,128)S(1)} fusion(f32[128,1024]{1,0:T(8,128)S(1)} %get-tuple-element.44, f16[128,1024]{1,0:T(8,128)(2,1)} %collective-permute-done.7, f32[1024]{0:T(1024)S(1)} %bitcast.22, f32[128]{0:T(128)S(1)} %slice_reduce_fusion), kind=kLoop, calls=%fused_computation.3 | loop fusion | flops 1048576 | bytes 1315328 | tf_op jit(solution)/shard_map/mul | solution.py:450
  73.0 2.2 %collective-permute-done.6 = f32[8,1024]{1,0:T(8,128)S(1)} collective-permute-done((f32[8,1024]{1,0:T(8,128)S(1)}, f32[8,1024]{1,0:T(8,128)S(1)}, u32[]{:S(2)}, u32[]{:S(2)}) %collective-permute-start.6) | collective-permute-done | bytes 32800 | tf_op jit(solution)/shard_map/ppermute | solution.py:390
  76.5 1.8 %maximum_select_fusion = f32[128,4,2,256]{3,2,1,0:T(2,128)} fusion(f32[128,2,2,256]{3,2,1,0:T(2,128)S(1)} %reshape.15, f32[128,2,2,256]{3,2,1,0:T(2,128)S(1)} %reshape.14, pred[]{:T(512)S(6)} %eq.3), kind=kLoop, calls=%fused_computation | loop fusion | flops 786432 | bytes 2097153 | tf_op jit(solution)/shard_map/jit(_where)/select_n | solution.py:458
  (27 shorter events, 2.5 us)
Async XLA Ops:
  1.0 8.6 %collective-permute-start = (bf16[536,128]{1,0:T(8,128)(2,1)S(1)}, bf16[536,128]{1,0:T(8,128)(2,1)S(1)}, u32[]{:S(2)}, u32[]{:S(2)}) collective-permute-start(bf16[536,128]{1,0:T(8,128)(2,1)S(1)} %tall_design.1), channel_id=1, source_target_pairs={{0,1},{1,0},{4,5},{5,4},{8,9},{9,8},{12,13},{13,12},{2,3},{3,2},{6... | collective-permute-start | bytes 411656 | tf_op jit(solution)/shard_map/ppermute | solution.py:390
  4.1 8.0 %collective-permute-start.1 = (bf16[536,128]{1,0:T(8,128)(2,1)S(1)}, bf16[536,128]{1,0:T(8,128)(2,1)S(1)}, u32[]{:S(2)}, u32[]{:S(2)}) collective-permute-start(bf16[536,128]{1,0:T(8,128)(2,1)S(1)} %tall_design.1), channel_id=1, source_target_pairs={{0,8},{1,9},{4,12},{5,13},{8,0},{9,1},{12,4},{13,5},{2,10},{3,11},... | collective-permute-start | bytes 411656 | tf_op jit(solution)/shard_map/ppermute | solution.py:390
  5.6 6.5 %collective-permute-start.2 = (bf16[536,128]{1,0:T(8,128)(2,1)S(1)}, bf16[536,128]{1,0:T(8,128)(2,1)S(1)}, u32[]{:S(2)}, u32[]{:S(2)}) collective-permute-start(bf16[536,128]{1,0:T(8,128)(2,1)S(1)} %tall_design.1), channel_id=1, source_target_pairs={{0,9},{1,8},{4,13},{5,12},{8,1},{9,0},{12,5},{13,4},{2,11},{3,10},... | collective-permute-start | bytes 411656 | tf_op jit(solution)/shard_map/ppermute | solution.py:390
  12.1 31.5 %all-to-all-start = ((bf16[8,128,1024]{2,1,0:T(8,128)(2,1)}), bf16[8,128,1024]{2,1,0:T(8,128)(2,1)S(1)}, u32[]{:S(2)}, u32[]{:S(2)}) async-start(bf16[8,128,1024]{2,1,0:T(8,128)(2,1)} %smooth.1), calls=%async_computation | async-start | bytes 4194304 | tf_op jit(solution)/shard_map/all_to_all | solution.py:404
  15.8 2.1 %collective-permute-start.3 = (bf16[4,536,128]{2,1,0:T(8,128)(2,1)S(1)}, bf16[4,536,128]{2,1,0:T(8,128)(2,1)S(1)}, u32[]{:S(2)}, u32[]{:S(2)}) collective-permute-start(bf16[4,536,128]{2,1,0:T(8,128)(2,1)S(1)} %pad_maximum_fusion.blocks), channel_id=1, source_target_pairs={{0,4},{1,5},{4,0},{5,1},{8,12},{9,13},{12,8},{13,9},{2,6},{3,7},{6... | collective-permute-start | bytes 1646600 | tf_op jit(solution)/shard_map/ppermute | solution.py:390
  16.3 0.8 %copy-start = (bf16[4,536,128]{2,1,0:T(8,128)(2,1)}, bf16[4,536,128]{2,1,0:T(8,128)(2,1)S(1)}, u32[]{:S(2)}) copy-start(bf16[4,536,128]{2,1,0:T(8,128)(2,1)S(1)} %pad_maximum_fusion.blocks) | copy-start | bytes 1646596
  18.0 0.8 %copy-start.2 = (bf16[4,536,128]{2,1,0:T(8,128)(2,1)}, bf16[4,536,128]{2,1,0:T(8,128)(2,1)S(1)}, u32[]{:S(2)}) copy-start(bf16[4,536,128]{2,1,0:T(8,128)(2,1)S(1)} %collective-permute-done.3.others) | copy-start | bytes 1646596
  18.8 1.1 %copy-start.1 = (bf16[4,536,128]{2,1,0:T(8,128)(2,1)S(1)}, bf16[4,536,128]{2,1,0:T(8,128)(2,1)}, u32[]{:S(2)}) copy-start(bf16[4,536,128]{2,1,0:T(8,128)(2,1)} %copy-done) | copy-start | bytes 1646596
  19.8 1.1 %copy-start.3 = (bf16[4,536,128]{2,1,0:T(8,128)(2,1)S(1)}, bf16[4,536,128]{2,1,0:T(8,128)(2,1)}, u32[]{:S(2)}) copy-start(bf16[4,536,128]{2,1,0:T(8,128)(2,1)} %copy-done.2) | copy-start | bytes 1646596
  22.6 18.5 %collective-permute-start.4 = (f32[32,640]{1,0:T(8,128)}, f32[32,640]{1,0:T(8,128)S(1)}, u32[]{:S(2)}, u32[]{:S(2)}) collective-permute-start(f32[32,640]{1,0:T(8,128)} %get-tuple-element.36.moment.refs_0_), channel_id=1, source_target_pairs={{0,2},{2,0},{1,3},{3,1},{4,6},{6,4},{5,7},{7,5},{8,10},{10,8},{9,1... | collective-permute-start | bytes 245768 | tf_op jit(solution)/shard_map/ppermute | solution.py:390
  25.1 0.9 %copy-start.5 = (f32[32,640]{1,0:T(8,128)S(1)}, f32[32,640]{1,0:T(8,128)}, u32[]{:S(2)}) copy-start(f32[32,640]{1,0:T(8,128)} %get-tuple-element.36.moment.refs_0_) | copy-start | bytes 245764
  41.1 0.6 copy-start.7
  44.1 6.7 %collective-permute-start.5 = (f32[24,1024]{1,0:T(8,128)S(1)}, f32[24,1024]{1,0:T(8,128)}, u32[]{:S(2)}, u32[]{:S(2)}) collective-permute-start(f32[24,1024]{1,0:T(8,128)S(1)} %column_sums.1.stats.refs_2_), channel_id=1, source_target_pairs={{0,2},{2,0},{1,3},{3,1},{4,6},{6,4},{5,7},{7,5},{8,10},{10,8},{9,1... | collective-permute-start | bytes 294920 | tf_op jit(solution)/shard_map/ppermute | solution.py:390
  47.0 3.8 %copy-start.4 = (f32[128,1024]{1,0:T(8,128)}, f32[128,1024]{1,0:T(8,128)S(1)}, u32[]{:S(2)}) copy-start(f32[128,1024]{1,0:T(8,128)S(1)} %get-tuple-element.49) | copy-start | bytes 1572868
  50.8 20.9 %collective-permute-start.7 = (f16[128,1024]{1,0:T(8,128)(2,1)S(1)}, f16[128,1024]{1,0:T(8,128)(2,1)}, u32[]{:S(2)}, u32[]{:S(2)}) collective-permute-start(f16[128,1024]{1,0:T(8,128)(2,1)S(1)} %convert_element_type.18), channel_id=1, source_target_pairs={{0,2},{1,3},{2,0},{3,1},{4,6},{5,7},{6,4},{7,5},{8,10},{9,11},{10,... | collective-permute-start | bytes 786440 | tf_op jit(solution)/shard_map/ppermute | solution.py:390
  52.2 23.0 %collective-permute-start.9 = (f16[128,1024]{1,0:T(8,128)(2,1)S(1)}, f16[128,1024]{1,0:T(8,128)(2,1)S(1)}, u32[]{:S(2)}, u32[]{:S(2)}) collective-permute-start(f16[128,1024]{1,0:T(8,128)(2,1)S(1)} %convert_element_type.22), channel_id=1, source_target_pairs={{0,3},{1,2},{2,1},{3,0},{4,7},{5,6},{6,5},{7,4},{8,11},{9,10},{10,... | collective-permute-start | bytes 786440 | tf_op jit(solution)/shard_map/ppermute | solution.py:390
  56.0 0.9 %copy-start.6 = (f32[32,640]{1,0:T(8,128)S(1)}, f32[32,640]{1,0:T(8,128)}, u32[]{:S(2)}) copy-start(f32[32,640]{1,0:T(8,128)} %get-tuple-element.36.moment.refs_0_) | copy-start | bytes 245764
  56.9 0.9 %copy-start.8 = (f32[32,640]{1,0:T(8,128)S(1)}, f32[32,640]{1,0:T(8,128)}, u32[]{:S(2)}) copy-start(f32[32,640]{1,0:T(8,128)} %copy-done.7) | copy-start | bytes 245764
  62.2 13.0 %collective-permute-start.8 = (f16[128,1024]{1,0:T(8,128)(2,1)S(1)}, f16[128,1024]{1,0:T(8,128)(2,1)S(1)}, u32[]{:S(2)}, u32[]{:S(2)}) collective-permute-start(f16[128,1024]{1,0:T(8,128)(2,1)S(1)} %convert_element_type.20), channel_id=1, source_target_pairs={{0,1},{1,0},{2,3},{3,2},{4,5},{5,4},{6,7},{7,6},{8,9},{9,8},{10,11... | collective-permute-start | bytes 786440 | tf_op jit(solution)/shard_map/ppermute | solution.py:390
  62.3 12.9 %collective-permute-start.6 = (f32[8,1024]{1,0:T(8,128)S(1)}, f32[8,1024]{1,0:T(8,128)S(1)}, u32[]{:S(2)}, u32[]{:S(2)}) collective-permute-start(f32[8,1024]{1,0:T(8,128)S(1)} %get-tuple-element.43), channel_id=1, source_target_pairs={{0,1},{1,0},{2,3},{3,2},{4,5},{5,4},{6,7},{7,6},{8,9},{9,8},{10,11... | collective-permute-start | bytes 98312 | tf_op jit(solution)/shard_map/ppermute | solution.py:390

commit v16 on v14

--- a/solution.py
+++ b/solution.py
@@ -22,6 +22,7 @@
 VMEM_BASE = 12 * 2**20
 SQUARE_ROW = 20
 WIDE = 2.0**8
+FINE = 2.0**11
 SCALE_LANE = DPAD
 STRIDE = 32
 
@@ -439,9 +440,12 @@
     home, away, factors, weights = base_ratio(
         genes, columns, moment_parts, stat_parts, *where, design
     )
-    away = permute_xor(away.astype(jnp.float16), "near", 1)
-    away = away.astype(jnp.float32) * (1.0 / WIDE)
-    away_factors = permute_xor(factors, "near", 1)
+    coarse = lax.reduce_precision(factors, 5, 10)
+    fine = (factors - coarse) * FINE
+    away = jnp.concatenate([away, coarse, fine], axis=0).astype(jnp.float16)
+    away = permute_xor(away, "near", 1).astype(jnp.float32)
+    away_factors = away[panel : panel + 8] + away[panel + 8 :] * (1.0 / FINE)
+    away = away[:panel] * (1.0 / WIDE)
 
     def t_of(ratio, factors, offset):
         for j in range(1, n_far):

time: 77.9 us -> 76.9 us (0.987)
  waiting for transfers between devices: 31.4 us -> 35.9 us
  other arithmetic: 3 us -> 1.16 us
  local copies, waits for them, and re-layouts: 8.83 us -> 7.06 us
  starting transfers between devices: 18.9 us -> 17.2 us
    ppermute x10 -> x9, waiting for transfers between devices: 29.5 us -> 34 us  [permute_xor(): return lax.ppermute(value, axes, [(i, i ^ bits) for i in range(size)])]
    unnamed x18 -> x16, local copies, waits for them, and re-layouts: 7.02 us -> 5.25 us
    ppermute x10 -> x9, starting transfers between devices: 15.3 us -> 13.6 us  [permute_xor(): return lax.ppermute(value, axes, [(i, i ^ bits) for i in range(size)])]
    convert_element_type x1, other arithmetic: 1.07 us -> 0.03 us  [on_device(): sent = [piece.astype(jnp.float16) for piece in sent]]
    mul x1, other arithmetic: 1.3 us -> 0.35 us  [t_of(): return ratio * jnp.sqrt(freedom / (1.0 - ratio * ratio))]
  transfers between devices with their start and end apart: 11 -> 10, of which waited for: 7 -> 7; matrix products, arithmetic and copies ran while one was open for 3% -> 1% of each run, Pallas kernels for 18% -> 18%
where the time goes in v16:
time: 76.9 us; the launch traced here: 76.6 us
  waiting for transfers between devices  35.9 us (47%)
  starting transfers between devices  17.2 us (22%)
  Pallas kernels  15.1 us (20%)
  local copies, waits for them, and re-layouts  7.06 us (9%)
  other arithmetic  1.16 us (2%)
    ppermute x9, waiting for transfers between devices, permute_xor(): return lax.ppermute(value, axes, [(i, i ^ bits) for i in range(size)])  34 us
    ppermute x9, starting transfers between devices, permute_xor(): return lax.ppermute(value, axes, [(i, i ^ bits) for i in range(size)])  13.6 us
    pallas_call x5, Pallas kernels, call(): pl.pallas_call(kernel, out_shape=outs, in_specs=[IN_SMEM] * len(scalars)...  10.1 us
    unnamed x16, local copies, waits for them, and re-layouts  5.25 us
    pallas_call x1, Pallas kernels, smooth(): pl.pallas_call(functools.partial(smooth_kernel, group, planes, per_vox, p...  3.99 us
    all_to_all x1, starting transfers between devices, exchange(): value = lax.all_to_all(value, ('vox', 'near'), 0, 0, tiled=True)  3.6 us
    all_to_all x1, waiting for transfers between devices, exchange(): value = lax.all_to_all(value, ('vox', 'near'), 0, 0, tiled=True)  1.91 us
    select_n x2, local copies, waits for them, and re-layouts, on_device(): jnp.where(near == 0, jnp.stack([home, away], 1), jnp.stack([away, home], 1))  1.63 us
  transfers between devices with their start and end apart: 10, of which 7 were waited for; matrix products, arithmetic and copies ran while one was open for 1% of the time, Pallas kernels for 18%

profile of v16, /device:TPU:0, one launch (start us, length us, event | category | flops | bytes accessed | tf_op | source)
XLA Modules:
  0.0 76.6 jit_solution(17879955032688426418)
XLA Ops:
  0.0 1.0 %tall_design.1 = bf16[536,128]{1,0:T(8,128)(2,1)S(1)} custom-call(bf16[128,512]{1,0:T(8,128)(2,1)} %genotypes.1, s32[1,128]{1,0:T(1,128)} %bitcast.30, bf16[16,128]{1,0:T(8,128)(2,1)} %bitcast.29), custom_call_target="tpu_custom_call" | custom-call | tf_op jit(solution)/shard_map/tall_design/pallas_call | solution.py:113
  1.0 3.1 %collective-permute-start = (bf16[536,128]{1,0:T(8,128)(2,1)S(1)}, bf16[536,128]{1,0:T(8,128)(2,1)S(1)}, u32[]{:S(2)}, u32[]{:S(2)}) collective-permute-start(bf16[536,128]{1,0:T(8,128)(2,1)S(1)} %tall_design.1), channel_id=1, source_target_pairs={{0,1},{1,0},{4,5},{5,4},{8,9},{9,8},{12,13},{13,12},{2,3},{3,2},{6... | collective-permute-start | bytes 411656 | tf_op jit(solution)/shard_map/ppermute | solution.py:391
  4.1 1.5 %collective-permute-start.1 = (bf16[536,128]{1,0:T(8,128)(2,1)S(1)}, bf16[536,128]{1,0:T(8,128)(2,1)S(1)}, u32[]{:S(2)}, u32[]{:S(2)}) collective-permute-start(bf16[536,128]{1,0:T(8,128)(2,1)S(1)} %tall_design.1), channel_id=1, source_target_pairs={{0,8},{1,9},{4,12},{5,13},{8,0},{9,1},{12,4},{13,5},{2,10},{3,11},... | collective-permute-start | bytes 411656 | tf_op jit(solution)/shard_map/ppermute | solution.py:391
  5.6 4.0 %smooth.1 = bf16[8,128,1024]{2,1,0:T(8,128)(2,1)} custom-call(bf16[128,32,256]{2,1,0:T(8,128)(2,1)} %bitcast.23, bf16[256,256]{1,0:T(8,128)(2,1)} %constant.29.clone.order, bf16[256,256]{1,0:T(8,128)(2,1)} %constant.30.clone.table), custom_call_target="tpu_custom_call" | custom-call | tf_op jit(solution)/shard_map/smooth/pallas_call | solution.py:168
  9.6 2.5 %collective-permute-done.1 = bf16[536,128]{1,0:T(8,128)(2,1)S(1)} collective-permute-done((bf16[536,128]{1,0:T(8,128)(2,1)S(1)}, bf16[536,128]{1,0:T(8,128)(2,1)S(1)}, u32[]{:S(2)}, u32[]{:S(2)}) %collective-permute-start.1) | collective-permute-done | bytes 137248 | tf_op jit(solution)/shard_map/ppermute | solution.py:391
  12.1 3.6 %all-to-all-start = ((bf16[8,128,1024]{2,1,0:T(8,128)(2,1)}), bf16[8,128,1024]{2,1,0:T(8,128)(2,1)S(1)}, u32[]{:S(2)}, u32[]{:S(2)}) async-start(bf16[8,128,1024]{2,1,0:T(8,128)(2,1)} %smooth.1), calls=%async_computation | async-start | bytes 4194304 | tf_op jit(solution)/shard_map/all_to_all | solution.py:405
  15.8 0.5 collective-permute-start.3
  16.3 0.8 %copy-done = bf16[4,536,128]{2,1,0:T(8,128)(2,1)} copy-done((bf16[4,536,128]{2,1,0:T(8,128)(2,1)}, bf16[4,536,128]{2,1,0:T(8,128)(2,1)S(1)}, u32[]{:S(2)}) %copy-start) | copy-done | bytes 548888
  17.1 0.9 %collective-permute-done.3.others = bf16[4,536,128]{2,1,0:T(8,128)(2,1)S(1)} collective-permute-done((bf16[4,536,128]{2,1,0:T(8,128)(2,1)S(1)}, bf16[4,536,128]{2,1,0:T(8,128)(2,1)S(1)}, u32[]{:S(2)}, u32[]{:S(2)}) %collective-permute-start.3) | collective-permute-done | bytes 548896 | tf_op jit(solution)/shard_map/ppermute | solution.py:391
  18.0 0.8 %copy-done.2 = bf16[4,536,128]{2,1,0:T(8,128)(2,1)} copy-done((bf16[4,536,128]{2,1,0:T(8,128)(2,1)}, bf16[4,536,128]{2,1,0:T(8,128)(2,1)S(1)}, u32[]{:S(2)}) %copy-start.2) | copy-done | bytes 548888
  18.8 1.0 %copy-done.1 = bf16[4,536,128]{2,1,0:T(8,128)(2,1)S(1)} copy-done((bf16[4,536,128]{2,1,0:T(8,128)(2,1)S(1)}, bf16[4,536,128]{2,1,0:T(8,128)(2,1)}, u32[]{:S(2)}) %copy-start.1) | copy-done | bytes 548888
  19.8 1.0 %copy-done.3 = bf16[4,536,128]{2,1,0:T(8,128)(2,1)S(1)} copy-done((bf16[4,536,128]{2,1,0:T(8,128)(2,1)S(1)}, bf16[4,536,128]{2,1,0:T(8,128)(2,1)}, u32[]{:S(2)}) %copy-start.3) | copy-done | bytes 548888
  20.9 1.7 %moments.1 = (bf16[536,1024]{1,0:T(8,128)(2,1)S(1)}, f32[32,640]{1,0:T(8,128)}) custom-call(s32[1]{0:T(128)} %bitcast.2.me, bf16[4,536,128]{2,1,0:T(8,128)(2,1)S(1)} %copy-done.1, bf16[4,536,128]{2,1,0:T(8,128)(2,1)S(1)} %copy-done.3), custom_call_target="tpu_custom_call" | custom-call | tf_op jit(solution)/shard_map/moments/pallas_call | solution.py:89
  22.6 2.6 %collective-permute-start.4 = (f32[32,640]{1,0:T(8,128)}, f32[32,640]{1,0:T(8,128)S(1)}, u32[]{:S(2)}, u32[]{:S(2)}) collective-permute-start(f32[32,640]{1,0:T(8,128)} %get-tuple-element.36.moment.refs_0_), channel_id=1, source_target_pairs={{0,2},{2,0},{1,3},{3,1},{4,6},{6,4},{5,7},{7,5},{8,10},{10,8},{9,1... | collective-permute-start | bytes 245768 | tf_op jit(solution)/shard_map/ppermute | solution.py:391
  25.2 0.9 %copy-done.4 = f32[32,640]{1,0:T(8,128)S(1)} copy-done((f32[32,640]{1,0:T(8,128)S(1)}, f32[32,640]{1,0:T(8,128)}, u32[]{:S(2)}) %copy-start.4) | copy-done | bytes 81944
  26.1 2.0 %pair_fit.1.coef = f32[512,128]{1,0:T(8,128)S(1)} custom-call(f32[32,640]{1,0:T(8,128)S(1)} %copy-done.4), custom_call_target="tpu_custom_call" | custom-call | tf_op jit(solution)/shard_map/pair_fit/pallas_call | solution.py:89
  28.1 13.0 %collective-permute-done.4.refs_1_ = f32[32,640]{1,0:T(8,128)S(1)} collective-permute-done((f32[32,640]{1,0:T(8,128)}, f32[32,640]{1,0:T(8,128)S(1)}, u32[]{:S(2)}, u32[]{:S(2)}) %collective-permute-start.4) | collective-permute-done | bytes 81952 | tf_op jit(solution)/shard_map/ppermute | solution.py:391
  41.1 0.6 copy-done.6
  41.7 1.9 %all-to-all-done = bf16[8,128,1024]{2,1,0:T(8,128)(2,1)S(1)} async-done(((bf16[8,128,1024]{2,1,0:T(8,128)(2,1)}), bf16[8,128,1024]{2,1,0:T(8,128)(2,1)S(1)}, u32[]{:S(2)}, u32[]{:S(2)}) %all-to-all-start) | async-done | bytes 2097184 | tf_op jit(solution)/shard_map/all_to_all | solution.py:405
  43.6 0.5 column_sums.1.stats.refs_2_
  44.1 1.4 %collective-permute-start.5 = (f32[24,1024]{1,0:T(8,128)S(1)}, f32[24,1024]{1,0:T(8,128)}, u32[]{:S(2)}, u32[]{:S(2)}) collective-permute-start(f32[24,1024]{1,0:T(8,128)S(1)} %column_sums.1.stats.refs_2_), channel_id=1, source_target_pairs={{0,2},{2,0},{1,3},{3,1},{4,6},{6,4},{5,7},{7,5},{8,10},{10,8},{9,1... | collective-permute-start | bytes 294920 | tf_op jit(solution)/shard_map/ppermute | solution.py:391
  45.5 1.5 %far_products.1 = (f32[128,1024]{1,0:T(8,128)S(1)}, f32[128,1024]{1,0:T(8,128)S(1)}) custom-call(s32[1]{0:T(128)} %bitcast.far, s32[1]{0:T(128)} %bitcast.1.near, bf16[536,1024]{1,0:T(8,128)(2,1)S(1)} %get-tuple-element.32.genes, bf16[1024,1024]{1,0:T(8,128)(2,1)S(1)} %bitcast.18, f32[512,128]{1,0:T(8,128)S(1)} %pair_fit.1.coef, ...), custom_call_target="tpu_custom_call" | custom-call | tf_op jit(solution)/shard_map/far_products/pallas_call | solution.py:89
  47.0 3.7 %collective-permute-done.5.refs_3_ = f32[24,1024]{1,0:T(8,128)} collective-permute-done((f32[24,1024]{1,0:T(8,128)S(1)}, f32[24,1024]{1,0:T(8,128)}, u32[]{:S(2)}, u32[]{:S(2)}) %collective-permute-start.5) | collective-permute-done | bytes 98336 | tf_op jit(solution)/shard_map/ppermute | solution.py:391
  50.8 0.4 collective-permute-start.7
  51.2 4.4 %base_ratio.1 = (f32[128,1024]{1,0:T(8,128)S(1)}, f32[128,1024]{1,0:T(8,128)S(1)}, f32[8,1024]{1,0:T(8,128)S(1)}, f32[128,128]{1,0:T(8,128)S(1)}) custom-call(s32[1]{0:T(128)} %bitcast.far, s32[1]{0:T(128)} %bitcast.1.near, bf16[536,1024]{1,0:T(8,128)(2,1)S(1)} %get-tuple-element.32.genes, bf16[1024,1024]{1,0:T(8,128)(2,1)S(1)} %bitcast.19, ...), custom_call_target="tpu_custom_call" | custom-call | tf_op jit(solution)/shard_map/base_ratio/pallas_call | solution.py:89
  55.7 3.5 %collective-permute-start.6 = (f16[144,1024]{1,0:T(8,128)(2,1)S(1)}, f16[144,1024]{1,0:T(8,128)(2,1)S(1)}, u32[]{:S(2)}, u32[]{:S(2)}) collective-permute-start(f16[144,1024]{1,0:T(8,128)(2,1)S(1)} %pad_maximum_fusion.1), channel_id=1, source_target_pairs={{0,1},{1,0},{2,3},{3,2},{4,5},{5,4},{6,7},{7,6},{8,9},{9,8},{10,11... | collective-permute-start | bytes 884744 | tf_op jit(solution)/shard_map/ppermute | solution.py:391
  59.3 0.7 collective-permute-start.8
  60.1 5.1 %collective-permute-done.7 = f16[128,1024]{1,0:T(8,128)(2,1)S(1)} collective-permute-done((f16[128,1024]{1,0:T(8,128)(2,1)S(1)}, f16[128,1024]{1,0:T(8,128)(2,1)S(1)}, u32[]{:S(2)}, u32[]{:S(2)}) %collective-permute-start.7) | collective-permute-done | bytes 262176 | tf_op jit(solution)/shard_map/ppermute | solution.py:391
  65.2 0.3 sqrt_multiply_fusion
  65.6 8.8 %collective-permute-done.6 = f16[144,1024]{1,0:T(8,128)(2,1)S(1)} collective-permute-done((f16[144,1024]{1,0:T(8,128)(2,1)S(1)}, f16[144,1024]{1,0:T(8,128)(2,1)S(1)}, u32[]{:S(2)}, u32[]{:S(2)}) %collective-permute-start.6) | collective-permute-done | bytes 294944 | tf_op jit(solution)/shard_map/ppermute | solution.py:391
  74.4 0.4 multiply_bitcast_fusion
  75.3 1.3 %copy.8 = f32[128,4,2,256]{3,2,1,0:T(2,128)} copy(f32[128,4,2,256]{0,3,2,1:T(8,128)S(1)} %bitcast.21) | data formatting | bytes 2097152 | tf_op jit(solution)/shard_map/jit(_where)/select_n | solution.py:459
  (27 shorter events, 1.0 us)
Async XLA Ops:
  1.0 8.6 %collective-permute-start = (bf16[536,128]{1,0:T(8,128)(2,1)S(1)}, bf16[536,128]{1,0:T(8,128)(2,1)S(1)}, u32[]{:S(2)}, u32[]{:S(2)}) collective-permute-start(bf16[536,128]{1,0:T(8,128)(2,1)S(1)} %tall_design.1), channel_id=1, source_target_pairs={{0,1},{1,0},{4,5},{5,4},{8,9},{9,8},{12,13},{13,12},{2,3},{3,2},{6... | collective-permute-start | bytes 411656 | tf_op jit(solution)/shard_map/ppermute | solution.py:391
  4.1 8.0 %collective-permute-start.1 = (bf16[536,128]{1,0:T(8,128)(2,1)S(1)}, bf16[536,128]{1,0:T(8,128)(2,1)S(1)}, u32[]{:S(2)}, u32[]{:S(2)}) collective-permute-start(bf16[536,128]{1,0:T(8,128)(2,1)S(1)} %tall_design.1), channel_id=1, source_target_pairs={{0,8},{1,9},{4,12},{5,13},{8,0},{9,1},{12,4},{13,5},{2,10},{3,11},... | collective-permute-start | bytes 411656 | tf_op jit(solution)/shard_map/ppermute | solution.py:391
  5.6 6.5 %collective-permute-start.2 = (bf16[536,128]{1,0:T(8,128)(2,1)S(1)}, bf16[536,128]{1,0:T(8,128)(2,1)S(1)}, u32[]{:S(2)}, u32[]{:S(2)}) collective-permute-start(bf16[536,128]{1,0:T(8,128)(2,1)S(1)} %tall_design.1), channel_id=1, source_target_pairs={{0,9},{1,8},{4,13},{5,12},{8,1},{9,0},{12,5},{13,4},{2,11},{3,10},... | collective-permute-start | bytes 411656 | tf_op jit(solution)/shard_map/ppermute | solution.py:391
  12.1 31.5 %all-to-all-start = ((bf16[8,128,1024]{2,1,0:T(8,128)(2,1)}), bf16[8,128,1024]{2,1,0:T(8,128)(2,1)S(1)}, u32[]{:S(2)}, u32[]{:S(2)}) async-start(bf16[8,128,1024]{2,1,0:T(8,128)(2,1)} %smooth.1), calls=%async_computation | async-start | bytes 4194304 | tf_op jit(solution)/shard_map/all_to_all | solution.py:405
  15.8 2.1 %collective-permute-start.3 = (bf16[4,536,128]{2,1,0:T(8,128)(2,1)S(1)}, bf16[4,536,128]{2,1,0:T(8,128)(2,1)S(1)}, u32[]{:S(2)}, u32[]{:S(2)}) collective-permute-start(bf16[4,536,128]{2,1,0:T(8,128)(2,1)S(1)} %pad_maximum_fusion.blocks), channel_id=1, source_target_pairs={{0,4},{1,5},{4,0},{5,1},{8,12},{9,13},{12,8},{13,9},{2,6},{3,7},{6... | collective-permute-start | bytes 1646600 | tf_op jit(solution)/shard_map/ppermute | solution.py:391
  16.3 0.8 %copy-start = (bf16[4,536,128]{2,1,0:T(8,128)(2,1)}, bf16[4,536,128]{2,1,0:T(8,128)(2,1)S(1)}, u32[]{:S(2)}) copy-start(bf16[4,536,128]{2,1,0:T(8,128)(2,1)S(1)} %pad_maximum_fusion.blocks) | copy-start | bytes 1646596
  18.0 0.8 %copy-start.2 = (bf16[4,536,128]{2,1,0:T(8,128)(2,1)}, bf16[4,536,128]{2,1,0:T(8,128)(2,1)S(1)}, u32[]{:S(2)}) copy-start(bf16[4,536,128]{2,1,0:T(8,128)(2,1)S(1)} %collective-permute-done.3.others) | copy-start | bytes 1646596
  18.8 1.1 %copy-start.1 = (bf16[4,536,128]{2,1,0:T(8,128)(2,1)S(1)}, bf16[4,536,128]{2,1,0:T(8,128)(2,1)}, u32[]{:S(2)}) copy-start(bf16[4,536,128]{2,1,0:T(8,128)(2,1)} %copy-done) | copy-start | bytes 1646596
  19.8 1.1 %copy-start.3 = (bf16[4,536,128]{2,1,0:T(8,128)(2,1)S(1)}, bf16[4,536,128]{2,1,0:T(8,128)(2,1)}, u32[]{:S(2)}) copy-start(bf16[4,536,128]{2,1,0:T(8,128)(2,1)} %copy-done.2) | copy-start | bytes 1646596
  22.6 18.5 %collective-permute-start.4 = (f32[32,640]{1,0:T(8,128)}, f32[32,640]{1,0:T(8,128)S(1)}, u32[]{:S(2)}, u32[]{:S(2)}) collective-permute-start(f32[32,640]{1,0:T(8,128)} %get-tuple-element.36.moment.refs_0_), channel_id=1, source_target_pairs={{0,2},{2,0},{1,3},{3,1},{4,6},{6,4},{5,7},{7,5},{8,10},{10,8},{9,1... | collective-permute-start | bytes 245768 | tf_op jit(solution)/shard_map/ppermute | solution.py:391
  25.2 0.9 %copy-start.4 = (f32[32,640]{1,0:T(8,128)S(1)}, f32[32,640]{1,0:T(8,128)}, u32[]{:S(2)}) copy-start(f32[32,640]{1,0:T(8,128)} %get-tuple-element.36.moment.refs_0_) | copy-start | bytes 245764
  41.1 0.6 copy-start.6
  44.1 6.7 %collective-permute-start.5 = (f32[24,1024]{1,0:T(8,128)S(1)}, f32[24,1024]{1,0:T(8,128)}, u32[]{:S(2)}, u32[]{:S(2)}) collective-permute-start(f32[24,1024]{1,0:T(8,128)S(1)} %column_sums.1.stats.refs_2_), channel_id=1, source_target_pairs={{0,2},{2,0},{1,3},{3,1},{4,6},{6,4},{5,7},{7,5},{8,10},{10,8},{9,1... | collective-permute-start | bytes 294920 | tf_op jit(solution)/shard_map/ppermute | solution.py:391
  45.5 5.7 %copy-start.5 = (f32[32,640]{1,0:T(8,128)S(1)}, f32[32,640]{1,0:T(8,128)}, u32[]{:S(2)}) copy-start(f32[32,640]{1,0:T(8,128)} %get-tuple-element.36.moment.refs_0_) | copy-start | bytes 245764
  45.5 5.7 %copy-start.7 = (f32[32,640]{1,0:T(8,128)S(1)}, f32[32,640]{1,0:T(8,128)}, u32[]{:S(2)}) copy-start(f32[32,640]{1,0:T(8,128)} %copy-done.6) | copy-start | bytes 245764
  50.8 14.4 %collective-permute-start.7 = (f16[128,1024]{1,0:T(8,128)(2,1)S(1)}, f16[128,1024]{1,0:T(8,128)(2,1)S(1)}, u32[]{:S(2)}, u32[]{:S(2)}) collective-permute-start(f16[128,1024]{1,0:T(8,128)(2,1)S(1)} %convert_element_type.16), channel_id=1, source_target_pairs={{0,2},{1,3},{2,0},{3,1},{4,6},{5,7},{6,4},{7,5},{8,10},{9,11},{10,... | collective-permute-start | bytes 786440 | tf_op jit(solution)/shard_map/ppermute | solution.py:391
  55.7 18.6 %collective-permute-start.6 = (f16[144,1024]{1,0:T(8,128)(2,1)S(1)}, f16[144,1024]{1,0:T(8,128)(2,1)S(1)}, u32[]{:S(2)}, u32[]{:S(2)}) collective-permute-start(f16[144,1024]{1,0:T(8,128)(2,1)S(1)} %pad_maximum_fusion.1), channel_id=1, source_target_pairs={{0,1},{1,0},{2,3},{3,2},{4,5},{5,4},{6,7},{7,6},{8,9},{9,8},{10,11... | collective-permute-start | bytes 884744 | tf_op jit(solution)/shard_map/ppermute | solution.py:391
  59.3 15.2 %collective-permute-start.8 = (f16[128,1024]{1,0:T(8,128)(2,1)S(1)}, f16[128,1024]{1,0:T(8,128)(2,1)S(1)}, u32[]{:S(2)}, u32[]{:S(2)}) collective-permute-start(f16[128,1024]{1,0:T(8,128)(2,1)S(1)} %convert_element_type.19), channel_id=1, source_target_pairs={{0,3},{1,2},{2,1},{3,0},{4,7},{5,6},{6,5},{7,4},{8,11},{9,10},{10,... | collective-permute-start | bytes 786440 | tf_op jit(solution)/shard_map/ppermute | solution.py:391

commit v17 on v16

--- a/solution.py
+++ b/solution.py
@@ -443,9 +443,10 @@
     coarse = lax.reduce_precision(factors, 5, 10)
     fine = (factors - coarse) * FINE
     away = jnp.concatenate([away, coarse, fine], axis=0).astype(jnp.float16)
-    away = permute_xor(away, "near", 1).astype(jnp.float32)
-    away_factors = away[panel : panel + 8] + away[panel + 8 :] * (1.0 / FINE)
-    away = away[:panel] * (1.0 / WIDE)
+    away = permute_xor(away, "near", 1)
+    away_factors = away[panel : panel + 8].astype(jnp.float32)
+    away_factors = away_factors + away[panel + 8 :].astype(jnp.float32) * (1.0 / FINE)
+    away = away[:panel].astype(jnp.float32) * (1.0 / WIDE)
 
     def t_of(ratio, factors, offset):
         for j in range(1, n_far):

time: 76.9 us -> 77.5 us (level)
  waiting for transfers between devices: 35.9 us -> 36.8 us
    ppermute x9, waiting for transfers between devices: 34 us -> 34.9 us  [permute_xor(): return lax.ppermute(value, axes, [(i, i ^ bits) for i in range(size)])]
where the time goes in v17:
time: 77.5 us; the launch traced here: 77.1 us
  waiting for transfers between devices  36.8 us (47%)
  starting transfers between devices  16.8 us (22%)
  Pallas kernels  15.1 us (19%)
  local copies, waits for them, and re-layouts  7.07 us (9%)
  other arithmetic  1.13 us (1%)
    ppermute x9, waiting for transfers between devices, permute_xor(): return lax.ppermute(value, axes, [(i, i ^ bits) for i in range(size)])  34.9 us
    ppermute x9, starting transfers between devices, permute_xor(): return lax.ppermute(value, axes, [(i, i ^ bits) for i in range(size)])  13.2 us
    pallas_call x5, Pallas kernels, call(): pl.pallas_call(kernel, out_shape=outs, in_specs=[IN_SMEM] * len(scalars)...  10.1 us
    unnamed x16, local copies, waits for them, and re-layouts  5.25 us
    pallas_call x1, Pallas kernels, smooth(): pl.pallas_call(functools.partial(smooth_kernel, group, planes, per_vox, p...  3.99 us
    all_to_all x1, starting transfers between devices, exchange(): value = lax.all_to_all(value, ('vox', 'near'), 0, 0, tiled=True)  3.6 us
    all_to_all x1, waiting for transfers between devices, exchange(): value = lax.all_to_all(value, ('vox', 'near'), 0, 0, tiled=True)  1.91 us
    select_n x2, local copies, waits for them, and re-layouts, on_device(): jnp.where(near == 0, jnp.stack([home, away], 1), jnp.stack([away, home], 1))  1.63 us
  transfers between devices with their start and end apart: 10, of which 7 were waited for; matrix products, arithmetic and copies ran while one was open for 1% of the time, Pallas kernels for 18%

profile of v17, /device:TPU:0, one launch (start us, length us, event | category | flops | bytes accessed | tf_op | source)
XLA Modules:
  0.0 77.1 jit_solution(16126978836389814761)
XLA Ops:
  0.0 1.0 %tall_design.1 = bf16[536,128]{1,0:T(8,128)(2,1)S(1)} custom-call(bf16[128,512]{1,0:T(8,128)(2,1)} %genotypes.1, s32[1,128]{1,0:T(1,128)} %bitcast.30, bf16[16,128]{1,0:T(8,128)(2,1)} %bitcast.29), custom_call_target="tpu_custom_call" | custom-call | tf_op jit(solution)/shard_map/tall_design/pallas_call | solution.py:113
  1.0 3.1 %collective-permute-start = (bf16[536,128]{1,0:T(8,128)(2,1)S(1)}, bf16[536,128]{1,0:T(8,128)(2,1)S(1)}, u32[]{:S(2)}, u32[]{:S(2)}) collective-permute-start(bf16[536,128]{1,0:T(8,128)(2,1)S(1)} %tall_design.1), channel_id=1, source_target_pairs={{0,1},{1,0},{4,5},{5,4},{8,9},{9,8},{12,13},{13,12},{2,3},{3,2},{6... | collective-permute-start | bytes 411656 | tf_op jit(solution)/shard_map/ppermute | solution.py:391
  4.1 1.5 %collective-permute-start.1 = (bf16[536,128]{1,0:T(8,128)(2,1)S(1)}, bf16[536,128]{1,0:T(8,128)(2,1)S(1)}, u32[]{:S(2)}, u32[]{:S(2)}) collective-permute-start(bf16[536,128]{1,0:T(8,128)(2,1)S(1)} %tall_design.1), channel_id=1, source_target_pairs={{0,8},{1,9},{4,12},{5,13},{8,0},{9,1},{12,4},{13,5},{2,10},{3,11},... | collective-permute-start | bytes 411656 | tf_op jit(solution)/shard_map/ppermute | solution.py:391
  5.6 4.0 %smooth.1 = bf16[8,128,1024]{2,1,0:T(8,128)(2,1)} custom-call(bf16[128,32,256]{2,1,0:T(8,128)(2,1)} %bitcast.23, bf16[256,256]{1,0:T(8,128)(2,1)} %constant.29.clone.order, bf16[256,256]{1,0:T(8,128)(2,1)} %constant.30.clone.table), custom_call_target="tpu_custom_call" | custom-call | tf_op jit(solution)/shard_map/smooth/pallas_call | solution.py:168
  9.6 2.5 %collective-permute-done.1 = bf16[536,128]{1,0:T(8,128)(2,1)S(1)} collective-permute-done((bf16[536,128]{1,0:T(8,128)(2,1)S(1)}, bf16[536,128]{1,0:T(8,128)(2,1)S(1)}, u32[]{:S(2)}, u32[]{:S(2)}) %collective-permute-start.1) | collective-permute-done | bytes 137248 | tf_op jit(solution)/shard_map/ppermute | solution.py:391
  12.1 3.6 %all-to-all-start = ((bf16[8,128,1024]{2,1,0:T(8,128)(2,1)}), bf16[8,128,1024]{2,1,0:T(8,128)(2,1)S(1)}, u32[]{:S(2)}, u32[]{:S(2)}) async-start(bf16[8,128,1024]{2,1,0:T(8,128)(2,1)} %smooth.1), calls=%async_computation | async-start | bytes 4194304 | tf_op jit(solution)/shard_map/all_to_all | solution.py:405
  15.8 0.5 collective-permute-start.3
  16.3 0.8 %copy-done = bf16[4,536,128]{2,1,0:T(8,128)(2,1)} copy-done((bf16[4,536,128]{2,1,0:T(8,128)(2,1)}, bf16[4,536,128]{2,1,0:T(8,128)(2,1)S(1)}, u32[]{:S(2)}) %copy-start) | copy-done | bytes 548888
  17.1 0.9 %collective-permute-done.3.others = bf16[4,536,128]{2,1,0:T(8,128)(2,1)S(1)} collective-permute-done((bf16[4,536,128]{2,1,0:T(8,128)(2,1)S(1)}, bf16[4,536,128]{2,1,0:T(8,128)(2,1)S(1)}, u32[]{:S(2)}, u32[]{:S(2)}) %collective-permute-start.3) | collective-permute-done | bytes 548896 | tf_op jit(solution)/shard_map/ppermute | solution.py:391
  18.0 0.8 %copy-done.2 = bf16[4,536,128]{2,1,0:T(8,128)(2,1)} copy-done((bf16[4,536,128]{2,1,0:T(8,128)(2,1)}, bf16[4,536,128]{2,1,0:T(8,128)(2,1)S(1)}, u32[]{:S(2)}) %copy-start.2) | copy-done | bytes 548888
  18.8 1.0 %copy-done.1 = bf16[4,536,128]{2,1,0:T(8,128)(2,1)S(1)} copy-done((bf16[4,536,128]{2,1,0:T(8,128)(2,1)S(1)}, bf16[4,536,128]{2,1,0:T(8,128)(2,1)}, u32[]{:S(2)}) %copy-start.1) | copy-done | bytes 548888
  19.8 1.0 %copy-done.3 = bf16[4,536,128]{2,1,0:T(8,128)(2,1)S(1)} copy-done((bf16[4,536,128]{2,1,0:T(8,128)(2,1)S(1)}, bf16[4,536,128]{2,1,0:T(8,128)(2,1)}, u32[]{:S(2)}) %copy-start.3) | copy-done | bytes 548888
  20.9 1.7 %moments.1 = (bf16[536,1024]{1,0:T(8,128)(2,1)S(1)}, f32[32,640]{1,0:T(8,128)}) custom-call(s32[1]{0:T(128)} %bitcast.2.me, bf16[4,536,128]{2,1,0:T(8,128)(2,1)S(1)} %copy-done.1, bf16[4,536,128]{2,1,0:T(8,128)(2,1)S(1)} %copy-done.3), custom_call_target="tpu_custom_call" | custom-call | tf_op jit(solution)/shard_map/moments/pallas_call | solution.py:89
  22.6 2.6 %collective-permute-start.4 = (f32[32,640]{1,0:T(8,128)}, f32[32,640]{1,0:T(8,128)S(1)}, u32[]{:S(2)}, u32[]{:S(2)}) collective-permute-start(f32[32,640]{1,0:T(8,128)} %get-tuple-element.36.moment.refs_0_), channel_id=1, source_target_pairs={{0,2},{2,0},{1,3},{3,1},{4,6},{6,4},{5,7},{7,5},{8,10},{10,8},{9,1... | collective-permute-start | bytes 245768 | tf_op jit(solution)/shard_map/ppermute | solution.py:391
  25.2 0.9 %copy-done.4 = f32[32,640]{1,0:T(8,128)S(1)} copy-done((f32[32,640]{1,0:T(8,128)S(1)}, f32[32,640]{1,0:T(8,128)}, u32[]{:S(2)}) %copy-start.4) | copy-done | bytes 81944
  26.1 2.0 %pair_fit.1.coef = f32[512,128]{1,0:T(8,128)S(1)} custom-call(f32[32,640]{1,0:T(8,128)S(1)} %copy-done.4), custom_call_target="tpu_custom_call" | custom-call | tf_op jit(solution)/shard_map/pair_fit/pallas_call | solution.py:89
  28.1 13.0 %collective-permute-done.4.refs_1_ = f32[32,640]{1,0:T(8,128)S(1)} collective-permute-done((f32[32,640]{1,0:T(8,128)}, f32[32,640]{1,0:T(8,128)S(1)}, u32[]{:S(2)}, u32[]{:S(2)}) %collective-permute-start.4) | collective-permute-done | bytes 81952 | tf_op jit(solution)/shard_map/ppermute | solution.py:391
  41.1 0.6 copy-done.6
  41.7 1.9 %all-to-all-done = bf16[8,128,1024]{2,1,0:T(8,128)(2,1)S(1)} async-done(((bf16[8,128,1024]{2,1,0:T(8,128)(2,1)}), bf16[8,128,1024]{2,1,0:T(8,128)(2,1)S(1)}, u32[]{:S(2)}, u32[]{:S(2)}) %all-to-all-start) | async-done | bytes 2097184 | tf_op jit(solution)/shard_map/all_to_all | solution.py:405
  43.6 0.5 column_sums.1.stats.refs_2_
  44.1 1.4 %collective-permute-start.5 = (f32[24,1024]{1,0:T(8,128)S(1)}, f32[24,1024]{1,0:T(8,128)}, u32[]{:S(2)}, u32[]{:S(2)}) collective-permute-start(f32[24,1024]{1,0:T(8,128)S(1)} %column_sums.1.stats.refs_2_), channel_id=1, source_target_pairs={{0,2},{2,0},{1,3},{3,1},{4,6},{6,4},{5,7},{7,5},{8,10},{10,8},{9,1... | collective-permute-start | bytes 294920 | tf_op jit(solution)/shard_map/ppermute | solution.py:391
  45.5 1.5 %far_products.1 = (f32[128,1024]{1,0:T(8,128)S(1)}, f32[128,1024]{1,0:T(8,128)S(1)}) custom-call(s32[1]{0:T(128)} %bitcast.far, s32[1]{0:T(128)} %bitcast.1.near, bf16[536,1024]{1,0:T(8,128)(2,1)S(1)} %get-tuple-element.32.genes, bf16[1024,1024]{1,0:T(8,128)(2,1)S(1)} %bitcast.18, f32[512,128]{1,0:T(8,128)S(1)} %pair_fit.1.coef, ...), custom_call_target="tpu_custom_call" | custom-call | tf_op jit(solution)/shard_map/far_products/pallas_call | solution.py:89
  47.0 3.7 %collective-permute-done.5.refs_3_ = f32[24,1024]{1,0:T(8,128)} collective-permute-done((f32[24,1024]{1,0:T(8,128)S(1)}, f32[24,1024]{1,0:T(8,128)}, u32[]{:S(2)}, u32[]{:S(2)}) %collective-permute-start.5) | collective-permute-done | bytes 98336 | tf_op jit(solution)/shard_map/ppermute | solution.py:391
  50.8 0.4 collective-permute-start.7
  51.2 4.4 %base_ratio.1 = (f32[128,1024]{1,0:T(8,128)S(1)}, f32[128,1024]{1,0:T(8,128)S(1)}, f32[8,1024]{1,0:T(8,128)S(1)}, f32[128,128]{1,0:T(8,128)S(1)}) custom-call(s32[1]{0:T(128)} %bitcast.far, s32[1]{0:T(128)} %bitcast.1.near, bf16[536,1024]{1,0:T(8,128)(2,1)S(1)} %get-tuple-element.32.genes, bf16[1024,1024]{1,0:T(8,128)(2,1)S(1)} %bitcast.19, ...), custom_call_target="tpu_custom_call" | custom-call | tf_op jit(solution)/shard_map/base_ratio/pallas_call | solution.py:89
  55.7 3.7 %collective-permute-start.8 = (f16[128,1024]{1,0:T(8,128)(2,1)S(1)}, f16[128,1024]{1,0:T(8,128)(2,1)S(1)}, u32[]{:S(2)}, u32[]{:S(2)}) collective-permute-start(f16[128,1024]{1,0:T(8,128)(2,1)S(1)} %convert_element_type.27), channel_id=1, source_target_pairs={{0,3},{1,2},{2,1},{3,0},{4,7},{5,6},{6,5},{7,4},{8,11},{9,10},{10,... | collective-permute-start | bytes 786440 | tf_op jit(solution)/shard_map/ppermute | solution.py:391
  59.8 11.8 %collective-permute-done.7 = f16[128,1024]{1,0:T(8,128)(2,1)S(1)} collective-permute-done((f16[128,1024]{1,0:T(8,128)(2,1)S(1)}, f16[128,1024]{1,0:T(8,128)(2,1)S(1)}, u32[]{:S(2)}, u32[]{:S(2)}) %collective-permute-start.7) | collective-permute-done | bytes 262176 | tf_op jit(solution)/shard_map/ppermute | solution.py:391
  71.6 0.3 sqrt_multiply_fusion
  72.0 3.0 %collective-permute-done.6 = f16[144,1024]{1,0:T(8,128)(2,1)S(1)} collective-permute-done((f16[144,1024]{1,0:T(8,128)(2,1)S(1)}, f16[144,1024]{1,0:T(8,128)(2,1)S(1)}, u32[]{:S(2)}, u32[]{:S(2)}) %collective-permute-start.6) | collective-permute-done | bytes 294944 | tf_op jit(solution)/shard_map/ppermute | solution.py:391
  75.0 0.4 multiply_bitcast_fusion
  75.5 0.3 copy.7
  75.8 1.3 %copy.8 = f32[128,4,2,256]{3,2,1,0:T(2,128)} copy(f32[128,4,2,256]{0,3,2,1:T(8,128)S(1)} %bitcast.21) | data formatting | bytes 2097152 | tf_op jit(solution)/shard_map/jit(_where)/select_n | solution.py:460
  (26 shorter events, 0.7 us)
Async XLA Ops:
  1.0 8.6 %collective-permute-start = (bf16[536,128]{1,0:T(8,128)(2,1)S(1)}, bf16[536,128]{1,0:T(8,128)(2,1)S(1)}, u32[]{:S(2)}, u32[]{:S(2)}) collective-permute-start(bf16[536,128]{1,0:T(8,128)(2,1)S(1)} %tall_design.1), channel_id=1, source_target_pairs={{0,1},{1,0},{4,5},{5,4},{8,9},{9,8},{12,13},{13,12},{2,3},{3,2},{6... | collective-permute-start | bytes 411656 | tf_op jit(solution)/shard_map/ppermute | solution.py:391
  4.1 8.0 %collective-permute-start.1 = (bf16[536,128]{1,0:T(8,128)(2,1)S(1)}, bf16[536,128]{1,0:T(8,128)(2,1)S(1)}, u32[]{:S(2)}, u32[]{:S(2)}) collective-permute-start(bf16[536,128]{1,0:T(8,128)(2,1)S(1)} %tall_design.1), channel_id=1, source_target_pairs={{0,8},{1,9},{4,12},{5,13},{8,0},{9,1},{12,4},{13,5},{2,10},{3,11},... | collective-permute-start | bytes 411656 | tf_op jit(solution)/shard_map/ppermute | solution.py:391
  5.6 6.5 %collective-permute-start.2 = (bf16[536,128]{1,0:T(8,128)(2,1)S(1)}, bf16[536,128]{1,0:T(8,128)(2,1)S(1)}, u32[]{:S(2)}, u32[]{:S(2)}) collective-permute-start(bf16[536,128]{1,0:T(8,128)(2,1)S(1)} %tall_design.1), channel_id=1, source_target_pairs={{0,9},{1,8},{4,13},{5,12},{8,1},{9,0},{12,5},{13,4},{2,11},{3,10},... | collective-permute-start | bytes 411656 | tf_op jit(solution)/shard_map/ppermute | solution.py:391
  12.1 31.5 %all-to-all-start = ((bf16[8,128,1024]{2,1,0:T(8,128)(2,1)}), bf16[8,128,1024]{2,1,0:T(8,128)(2,1)S(1)}, u32[]{:S(2)}, u32[]{:S(2)}) async-start(bf16[8,128,1024]{2,1,0:T(8,128)(2,1)} %smooth.1), calls=%async_computation | async-start | bytes 4194304 | tf_op jit(solution)/shard_map/all_to_all | solution.py:405
  15.8 2.1 %collective-permute-start.3 = (bf16[4,536,128]{2,1,0:T(8,128)(2,1)S(1)}, bf16[4,536,128]{2,1,0:T(8,128)(2,1)S(1)}, u32[]{:S(2)}, u32[]{:S(2)}) collective-permute-start(bf16[4,536,128]{2,1,0:T(8,128)(2,1)S(1)} %pad_maximum_fusion.blocks), channel_id=1, source_target_pairs={{0,4},{1,5},{4,0},{5,1},{8,12},{9,13},{12,8},{13,9},{2,6},{3,7},{6... | collective-permute-start | bytes 1646600 | tf_op jit(solution)/shard_map/ppermute | solution.py:391
  16.3 0.8 %copy-start = (bf16[4,536,128]{2,1,0:T(8,128)(2,1)}, bf16[4,536,128]{2,1,0:T(8,128)(2,1)S(1)}, u32[]{:S(2)}) copy-start(bf16[4,536,128]{2,1,0:T(8,128)(2,1)S(1)} %pad_maximum_fusion.blocks) | copy-start | bytes 1646596
  18.0 0.8 %copy-start.2 = (bf16[4,536,128]{2,1,0:T(8,128)(2,1)}, bf16[4,536,128]{2,1,0:T(8,128)(2,1)S(1)}, u32[]{:S(2)}) copy-start(bf16[4,536,128]{2,1,0:T(8,128)(2,1)S(1)} %collective-permute-done.3.others) | copy-start | bytes 1646596
  18.8 1.1 %copy-start.1 = (bf16[4,536,128]{2,1,0:T(8,128)(2,1)S(1)}, bf16[4,536,128]{2,1,0:T(8,128)(2,1)}, u32[]{:S(2)}) copy-start(bf16[4,536,128]{2,1,0:T(8,128)(2,1)} %copy-done) | copy-start | bytes 1646596
  19.8 1.1 %copy-start.3 = (bf16[4,536,128]{2,1,0:T(8,128)(2,1)S(1)}, bf16[4,536,128]{2,1,0:T(8,128)(2,1)}, u32[]{:S(2)}) copy-start(bf16[4,536,128]{2,1,0:T(8,128)(2,1)} %copy-done.2) | copy-start | bytes 1646596
  22.6 18.5 %collective-permute-start.4 = (f32[32,640]{1,0:T(8,128)}, f32[32,640]{1,0:T(8,128)S(1)}, u32[]{:S(2)}, u32[]{:S(2)}) collective-permute-start(f32[32,640]{1,0:T(8,128)} %get-tuple-element.36.moment.refs_0_), channel_id=1, source_target_pairs={{0,2},{2,0},{1,3},{3,1},{4,6},{6,4},{5,7},{7,5},{8,10},{10,8},{9,1... | collective-permute-start | bytes 245768 | tf_op jit(solution)/shard_map/ppermute | solution.py:391
  25.2 0.9 %copy-start.4 = (f32[32,640]{1,0:T(8,128)S(1)}, f32[32,640]{1,0:T(8,128)}, u32[]{:S(2)}) copy-start(f32[32,640]{1,0:T(8,128)} %get-tuple-element.36.moment.refs_0_) | copy-start | bytes 245764
  41.1 0.6 copy-start.6
  44.1 6.7 %collective-permute-start.5 = (f32[24,1024]{1,0:T(8,128)S(1)}, f32[24,1024]{1,0:T(8,128)}, u32[]{:S(2)}, u32[]{:S(2)}) collective-permute-start(f32[24,1024]{1,0:T(8,128)S(1)} %column_sums.1.stats.refs_2_), channel_id=1, source_target_pairs={{0,2},{2,0},{1,3},{3,1},{4,6},{6,4},{5,7},{7,5},{8,10},{10,8},{9,1... | collective-permute-start | bytes 294920 | tf_op jit(solution)/shard_map/ppermute | solution.py:391
  45.5 5.7 %copy-start.5 = (f32[32,640]{1,0:T(8,128)S(1)}, f32[32,640]{1,0:T(8,128)}, u32[]{:S(2)}) copy-start(f32[32,640]{1,0:T(8,128)} %get-tuple-element.36.moment.refs_0_) | copy-start | bytes 245764
  45.5 5.7 %copy-start.7 = (f32[32,640]{1,0:T(8,128)S(1)}, f32[32,640]{1,0:T(8,128)}, u32[]{:S(2)}) copy-start(f32[32,640]{1,0:T(8,128)} %copy-done.6) | copy-start | bytes 245764
  50.8 20.8 %collective-permute-start.7 = (f16[128,1024]{1,0:T(8,128)(2,1)S(1)}, f16[128,1024]{1,0:T(8,128)(2,1)S(1)}, u32[]{:S(2)}, u32[]{:S(2)}) collective-permute-start(f16[128,1024]{1,0:T(8,128)(2,1)S(1)} %convert_element_type.22), channel_id=1, source_target_pairs={{0,2},{1,3},{2,0},{3,1},{4,6},{5,7},{6,4},{7,5},{8,10},{9,11},{10,... | collective-permute-start | bytes 786440 | tf_op jit(solution)/shard_map/ppermute | solution.py:391
  55.7 19.3 %collective-permute-start.8 = (f16[128,1024]{1,0:T(8,128)(2,1)S(1)}, f16[128,1024]{1,0:T(8,128)(2,1)S(1)}, u32[]{:S(2)}, u32[]{:S(2)}) collective-permute-start(f16[128,1024]{1,0:T(8,128)(2,1)S(1)} %convert_element_type.27), channel_id=1, source_target_pairs={{0,3},{1,2},{2,1},{3,0},{4,7},{5,6},{6,5},{7,4},{8,11},{9,10},{10,... | collective-permute-start | bytes 786440 | tf_op jit(solution)/shard_map/ppermute | solution.py:391
  59.5 15.4 %collective-permute-start.6 = (f16[144,1024]{1,0:T(8,128)(2,1)S(1)}, f16[144,1024]{1,0:T(8,128)(2,1)S(1)}, u32[]{:S(2)}, u32[]{:S(2)}) collective-permute-start(f16[144,1024]{1,0:T(8,128)(2,1)S(1)} %pad_maximum_fusion.1), channel_id=1, source_target_pairs={{0,1},{1,0},{2,3},{3,2},{4,5},{5,4},{6,7},{7,6},{8,9},{9,8},{10,11... | collective-permute-start | bytes 884744 | tf_op jit(solution)/shard_map/ppermute | solution.py:391
